TPU v7x, 32 devices: a whole 2x2x4 slice. The times are simulated.
32 devices in a mesh: wide: 8 (over y, x, core), narrow: 4 (over z).
Axes of the slice: x: 2, y: 2, z: 4, core: 2. Of those that a mesh axis runs over, the one named last changes fastest.
Arguments:
- hidden_in: bfloat16 [4096, 1536], P('wide'), may hold values from -64 to 64
- segment_ids: int32 [4096], P('wide'), may hold values from 0 to 7, as said below
- seg_lengths: int32 [8], replicated, may hold values from 1 to 2048, as said below
- seg_offsets: int32 [8], replicated, may hold values from 0 to 4095, as said below
- block_table: int32 [8, 16], replicated, may hold values from -1 to 39, as said below
- attn_gain: bfloat16 [1536], replicated, may hold values from 0.099609375 to 1.8984375
- w_query: bfloat16 [1536, 1536], P('wide', 'narrow'), may hold values from -0.15625 to 0.15625
- b_query: bfloat16 [1536], P('narrow'), may hold values from -128 to 128
- w_keyval: bfloat16 [1536, 512], P('wide'), may hold values from -0.15625 to 0.15625
- b_keyval: bfloat16 [512], replicated, may hold values from -128 to 128
- w_out: bfloat16 [1536, 1536], P('narrow', 'wide'), may hold values from -0.15625 to 0.15625
- mlp_gain: bfloat16 [1536], replicated, may hold values from 0.099609375 to 1.8984375
- w_gate: bfloat16 [1536, 8960], P('wide', 'narrow'), may hold values from -0.15625 to 0.15625
- w_up: bfloat16 [1536, 8960], P('wide', 'narrow'), may hold values from -0.15625 to 0.15625
- w_down: bfloat16 [8960, 1536], P('narrow', 'wide'), may hold values from -0.0625 to 0.0625
- next_gain: bfloat16 [1536], replicated, may hold values from 0.099609375 to 1.8984375
- w_query2: bfloat16 [1536, 1536], P('wide', 'narrow'), may hold values from -0.15625 to 0.15625
- b_query2: bfloat16 [1536], P('narrow'), may hold values from -3 to 3
- w_keyval2: bfloat16 [1536, 512], P('wide'), may hold values from -0.15625 to 0.15625
- b_keyval2: bfloat16 [512], replicated, may hold values from -3 to 3
Outputs:
- hidden_out: bfloat16 [4096, 1536], P('wide')
- next_query: bfloat16 [4096, 1536], P('wide', 'narrow')
- next_keyval: bfloat16 [4096, 512], P('wide', 'narrow')
- kv_cache: bfloat16 [4, 40, 128, 128], P('narrow', 'wide')
Inputs may be any that keep to these rules, and one draw needn't show every extreme that they name: `segment_ids`: segment s covers tokens seg_offsets[s] to seg_offsets[s] + seg_lengths[s] - 1. `seg_lengths`: they sum to 4096. seg_offsets[0] = 0 and seg_offsets[s + 1] = seg_offsets[s] + seg_lengths[s]. `block_table`: entry j of row s is a page for j below ceil(seg_lengths[s] / 128) and -1 beyond; no page appears twice.
All inputs are finite; a program needn't handle non-finite values.
Results may differ from a plain program's by a relative error of at most 0.017.
Values may be sent and summed in bfloat16 or wider, within the bound.
No kernel may reach another device: no remote copies, remote signals or barrier semaphores. Data moves between devices by JAX's collectives and lax.ppermute only.
A program may use at most 128 MiB of HBM per device.

v0:
```python
import math

import jax
import jax.numpy as jnp
from jax import lax
from jax.sharding import PartitionSpec as P

HD = 128
PAGE_LEN = 128


norm_eps = 1e-06
rope_base = 1000000.0
masked_score = -1e30


def rms_norm(activations, gain_vector):
    values = activations.astype(jnp.float32)
    row_scale = lax.rsqrt(jnp.mean(values * values, axis=-1, keepdims=True) + norm_eps)
    return (values * row_scale * gain_vector.astype(jnp.float32)).astype(jnp.bfloat16)


def rotate(values, positions):
    half_dim = values.shape[-1] // 2
    frequency = rope_base ** (-(jnp.arange(half_dim, dtype=jnp.float32) * 2.0 / values.shape[-1]))
    angles = positions.astype(jnp.float32)[:, None, None] * frequency
    cosine = jnp.cos(angles)
    sine_part = jnp.sin(angles)
    lower_half = values[..., :half_dim]
    upper_half = values[..., half_dim:]
    return jnp.concatenate(
        [
            lower_half * cosine - upper_half * sine_part,
            upper_half * cosine + lower_half * sine_part,
        ],
        axis=-1,
    )


def lookup(table, indices):
    table_match = indices[..., None] == jnp.arange(table.shape[0], dtype=jnp.int32)
    return jnp.sum(jnp.where(table_match, table, 0), axis=-1)


def fold_rows(normed, first_weight, second_weight):
    return (
        jnp.dot(
            normed,
            lax.all_gather(first_weight, "wide", axis=0, tiled=True),
            preferred_element_type=jnp.float32,
        ),
        jnp.dot(
            normed,
            lax.all_gather(second_weight, "wide", axis=0, tiled=True),
            preferred_element_type=jnp.float32,
        ),
    )


def column_terms(left_rows, weight_block):
    return jnp.dot(
        left_rows,
        lax.all_gather(weight_block, "wide", axis=1, tiled=True),
        preferred_element_type=jnp.float32,
    )


def keyval_block(w_keyval, b_keyval, head_pair):
    pair_width = 2 * HD
    pair_offset = head_pair * pair_width
    return (w_keyval, b_keyval, pair_offset)


def add_branch(partial_terms, base_rows, narrow_index):
    share_sum = lax.psum_scatter(
        partial_terms.astype(jnp.bfloat16), "narrow", scatter_dimension=1, tiled=True
    ).astype(jnp.float32)
    share_width = share_sum.shape[1]
    base_share = lax.dynamic_slice_in_dim(base_rows, narrow_index * share_width, share_width, 1)
    updated = (base_share.astype(jnp.float32) + share_sum).astype(jnp.bfloat16)
    result_rows = lax.all_gather(updated, "narrow", axis=1, tiled=True)
    return result_rows


def attend(queries, keys_all, values_all, segment_ids, seg_offsets, row_base):
    tok_rows = queries.shape[0]
    local_heads = queries.shape[1] // HD
    total_rows = keys_all.shape[0]
    key_block = math.gcd(total_rows, 512)
    score_scale = HD ** (-0.5)
    stacked = (
        queries.reshape(tok_rows, local_heads, HD)
        .transpose(1, 0, 2)
        .reshape(local_heads * tok_rows, HD)
    )
    query_pos = row_base + jnp.arange(tok_rows, dtype=jnp.int32)
    query_pos_all = jnp.tile(query_pos, local_heads)
    query_seg_all = jnp.tile(segment_ids, local_heads)
    lowest = lookup(seg_offsets, segment_ids[:1])[0]
    first_block = lowest // key_block
    last_block = (row_base + tok_rows - 1) // key_block

    def visit_block(block_number, state_now):
        running_max, running_sum, accumulated = state_now
        key_start = block_number * key_block
        keys_here = lax.dynamic_slice_in_dim(keys_all, key_start, key_block, 0)
        values_here = lax.dynamic_slice_in_dim(values_all, key_start, key_block, 0)
        key_pos = key_start + jnp.arange(key_block, dtype=jnp.int32)
        key_seg = jnp.sum((key_pos[:, None] >= seg_offsets[None, 1:]).astype(jnp.int32), axis=1)
        visible = (
            (key_seg[None, :] == query_seg_all[:, None])
            & (key_pos[None, :] <= query_pos_all[:, None])
            & (key_pos[None, :] >= 0)
        )
        scores = (
            jnp.einsum("qd,kd->qk", stacked, keys_here, preferred_element_type=jnp.float32)
            * score_scale
        )
        scores = jnp.where(visible, scores, masked_score)
        new_max = jnp.maximum(running_max, jnp.max(scores, axis=1))
        weights = jnp.where(visible, jnp.exp(scores - new_max[:, None]), 0.0)
        factor = jnp.exp(running_max - new_max)
        running_sum = running_sum * factor + jnp.sum(weights, axis=1)
        accumulated = accumulated * factor[:, None] + jnp.dot(
            weights.astype(jnp.bfloat16), values_here, preferred_element_type=jnp.float32
        )
        return (new_max, running_sum, accumulated)

    row_count = stacked.shape[0]
    initial = (
        jnp.full((row_count,), masked_score, jnp.float32),
        jnp.zeros((row_count,), jnp.float32),
        jnp.zeros((row_count, HD), jnp.float32),
    )
    final_max, final_sum, accumulated = lax.fori_loop(
        first_block, last_block + 1, visit_block, initial
    )
    mixed_heads = (
        (accumulated / final_sum[:, None]).reshape(local_heads, tok_rows, HD).transpose(1, 0, 2)
    )
    return mixed_heads.reshape(tok_rows, local_heads * HD).astype(jnp.bfloat16)


def fill_pages(source, seg_lengths, seg_offsets, block_table, first_page, page_count):
    pages_here = first_page + jnp.arange(page_count, dtype=jnp.int32)
    page_match = block_table[None, :, :] == pages_here[:, None, None]
    seg_grid = jnp.arange(block_table.shape[0], dtype=jnp.int32)[None, :, None]
    page_grid = jnp.arange(block_table.shape[1], dtype=jnp.int32)[None, None, :]
    page_owner = jnp.sum(jnp.where(page_match, seg_grid, 0), axis=(1, 2))
    logical = jnp.sum(jnp.where(page_match, page_grid, 0), axis=(1, 2))
    in_use = jnp.any(page_match, axis=(1, 2))
    first_token = lookup(seg_offsets, page_owner) + logical * PAGE_LEN
    filled = lookup(seg_lengths, page_owner) - logical * PAGE_LEN
    slot_index = jnp.arange(PAGE_LEN, dtype=jnp.int32)
    row_ids = jnp.clip(first_token[:, None] + slot_index[None, :], 0, source.shape[0] - 1)
    keep_slot = in_use[:, None] & (slot_index[None, :] < filled[:, None])
    taken_rows = jnp.take(source, row_ids.reshape(-1), axis=0).reshape(
        page_count, PAGE_LEN, source.shape[1]
    )
    return jnp.where(keep_slot[:, :, None], taken_rows, jnp.zeros((), source.dtype))


def local(
    hidden_in,
    segment_ids,
    seg_lengths,
    seg_offsets,
    block_table,
    attn_gain,
    w_query,
    b_query,
    w_keyval,
    b_keyval,
    w_out,
    mlp_gain,
    w_gate,
    w_up,
    w_down,
    next_gain,
    w_query2,
    b_query2,
    w_keyval2,
    b_keyval2,
):
    tok_rows = hidden_in.shape[0]
    wide_index = lax.axis_index("wide")
    narrow_index = lax.axis_index("narrow")
    head_pair = narrow_index // 2
    kind_index = narrow_index % 2
    row_base = wide_index * tok_rows
    positions = row_base + jnp.arange(tok_rows, dtype=jnp.int32) - lookup(seg_offsets, segment_ids)
    normed = rms_norm(hidden_in, attn_gain)
    kv_weight, kv_bias, pair_offset = keyval_block(w_keyval, b_keyval, head_pair)
    query_sum, keyval_sum = fold_rows(normed, w_query, kv_weight)
    queries = query_sum + b_query.astype(jnp.float32)
    local_heads = queries.shape[1] // HD
    queries = (
        rotate(queries.reshape(tok_rows, local_heads, HD), positions)
        .reshape(tok_rows, local_heads * HD)
        .astype(jnp.bfloat16)
    )
    keyvals = (keyval_sum + kv_bias.astype(jnp.float32)).reshape(tok_rows, -1, 2, HD)
    keyvals = jnp.stack([rotate(keyvals[:, :, 0, :], positions), keyvals[:, :, 1, :]], axis=2)
    keyvals = keyvals.reshape(tok_rows, kv_weight.shape[1]).astype(jnp.bfloat16)
    gathered = lax.all_gather(keyvals, "wide", axis=0, tiled=True)
    source = lax.dynamic_slice_in_dim(gathered, pair_offset + kind_index * HD, HD, 1)
    keys_all = lax.dynamic_slice_in_dim(gathered, pair_offset, HD, 1)
    values_all = lax.dynamic_slice_in_dim(gathered, pair_offset + HD, HD, 1)
    mixed_heads = attend(queries, keys_all, values_all, segment_ids, seg_offsets, row_base)
    residual = add_branch(column_terms(mixed_heads, w_out), hidden_in, narrow_index)
    normed_mlp = rms_norm(residual, mlp_gain)
    gate_sum, up_sum = fold_rows(normed_mlp, w_gate, w_up)
    hidden_units = (jax.nn.silu(gate_sum) * up_sum).astype(jnp.bfloat16)
    hidden_out = add_branch(column_terms(hidden_units, w_down), residual, narrow_index)
    normed_next = rms_norm(hidden_out, next_gain)
    kv_weight_next, kv_bias_next, pair_offset_next = keyval_block(w_keyval2, b_keyval2, head_pair)
    query_next, keyval_next = fold_rows(normed_next, w_query2, kv_weight_next)
    next_query = (query_next + b_query2.astype(jnp.float32)).astype(jnp.bfloat16)
    keyval_next = keyval_next + kv_bias_next.astype(jnp.float32)
    next_keyval = lax.dynamic_slice_in_dim(
        keyval_next, pair_offset_next + kind_index * HD, HD, 1
    ).astype(jnp.bfloat16)
    page_count = tok_rows // PAGE_LEN + 1
    cache_block = fill_pages(
        source, seg_lengths, seg_offsets, block_table, wide_index * page_count, page_count
    )
    return (hidden_out, next_query, next_keyval, cache_block[None])


def solution(mesh):
    placed = (
        P("wide", None),
        P("wide"),
        P(),
        P(),
        P(),
        P(),
        P("wide", "narrow"),
        P("narrow"),
        P("wide", None),
        P(),
        P("narrow", "wide"),
        P(),
        P("wide", "narrow"),
        P("wide", "narrow"),
        P("narrow", "wide"),
        P(),
        P("wide", "narrow"),
        P("narrow"),
        P("wide", None),
        P(),
    )
    return jax.shard_map(
        local,
        mesh=mesh,
        in_specs=placed,
        out_specs=(
            P("wide", None),
            P("wide", "narrow"),
            P("wide", "narrow"),
            P("narrow", "wide", None, None),
        ),
        check_vma=False,
    )
```

profile of v0, /device:TPU:10, one launch (start us, length us, event | category | flops | bytes accessed | tf_op | source)
XLA Modules:
  0.0 519.7 jit_solution(14658357420002267087)
XLA Ops:
  7.2 0.7 all-gather.12.cloned.1.call-update
  7.9 0.7 all-gather.16.cloned.1.call-update
  8.7 0.7 convert_element_type.106
  9.4 0.7 convert_element_type.108
  10.1 0.8 select_reduce_fusion
  10.9 1.8 fusion.17
  12.7 0.5 multiply_cosine_fusion
  13.2 23.5 %all-gather.12.cloned.1.call-done = bf16[1536,512]{1,0:T(8,128)(2,1)} async-done(((bf16[192,512]{1,0:T(8,128)(2,1)}), bf16[1536,512]{1,0:T(8,128)(2,1)}) %all-gather.12.cloned.1.call-update) | async-done | bytes 1572880 | tf_op jit(solution)/shard_map/all_gather | solution.py:54
  36.7 3.0 convolution_add_fusion.1
  40.1 1.0 copy.42
  41.2 0.5 all-gather.18.cloned.1.call-update
  41.8 0.5 slice.25
  42.3 1.3 fusion.44
  46.2 16.5 %all-gather.16.cloned.1.call-done = bf16[1536,384]{1,0:T(8,128)(2,1)} async-done(((bf16[192,384]{1,0:T(8,128)(2,1)}), bf16[1536,384]{1,0:T(8,128)(2,1)}) %all-gather.16.cloned.1.call-update) | async-done | bytes 1179664 | tf_op jit(solution)/shard_map/all_gather | solution.py:49
  62.7 2.2 convolution_add_fusion.3
  64.9 0.1 subtract_convert_fusion
  65.1 0.2 copy.40
  65.3 36.6 %all-gather.14.cloned.1.call-done = bf16[4096,512]{1,0:T(8,128)(2,1)} async-done(((bf16[512,512]{1,0:T(8,128)(2,1)}), bf16[4096,512]{1,0:T(8,128)(2,1)}) %all-gather.14.cloned.1.call-update) | async-done | bytes 4194320 | tf_op jit(solution)/shard_map/all_gather | solution.py:205
  101.9 3.1 constant_dynamic-slice_fusion
  105.1 11.5 %while.15 = (s32[]{:T(128)}, f32[1536]{0:T(1024)S(1)}, f32[1536]{0:T(1024)S(1)}, f32[1536,128]{1,0:T(8,128)S(1)}, s32[]{:T(128)}, /*index=5*/s32[8]{0:T(128)S(1)...) while((s32[]{:T(128)}, f32[1536]{0:T(1024)S(1)}, ...), condition=%wide.region_7.8_spmd.clone, body=%wide.region_3.7_spmd.clone.sunk | while | flops 419576320 | bytes 11870495 | solution.py:135
  105.4 2.2 fusion.73
  107.6 1.4 fusion.74
  109.0 1.8 convolution_add_fusion.5
  111.1 2.2 fusion.73
  113.3 1.4 fusion.74
  114.7 1.8 convolution_add_fusion.5
  116.6 0.3 divide_convert_fusion
  116.9 0.2 copy.41
  117.1 10.7 %all-gather.18.cloned.1.call-done = bf16[384,1536]{0,1:T(8,128)(2,1)} async-done(((bf16[384,192]{0,1:T(8,128)(2,1)}), bf16[384,1536]{0,1:T(8,128)(2,1)}) %all-gather.18.cloned.1.call-update) | async-done | bytes 1179664 | tf_op jit(solution)/shard_map/all_gather | solution.py:63
  127.8 2.3 convolution_convert_fusion.1
  130.1 1.6 copy.43
  131.7 40.9 %reduce-scatter.7.cloned.1.call-done = bf16[384,512]{1,0:T(8,128)(2,1)} async-done(((bf16[1536,512]{1,0:T(8,128)(2,1)}), bf16[384,512]{1,0:T(8,128)(2,1)}) %reduce-scatter.7.cloned.1.call-update) | async-done | bytes 393232
  172.6 1.2 copy.44
  173.8 1.8 add_convert_fusion.1
  175.7 0.7 all-gather.22.cloned.1.call-update
  176.5 0.7 all-gather.24.cloned.1.call-update
  177.2 0.7 all-gather.26.cloned.1.call-update
  177.9 0.2 reduce-scatter.9.cloned.1.call-start
  178.2 34.2 %all-gather.20.cloned.1.call-done = bf16[512,1536]{1,0:T(8,128)(2,1)} async-done(((bf16[512,384]{1,0:T(8,128)(2,1)}), bf16[512,1536]{1,0:T(8,128)(2,1)}) %all-gather.20.cloned.1.call-update) | async-done | bytes 1572880 | tf_op jit(solution)/shard_map/all_gather | solution.py:81
  212.4 1.8 fusion.20
  214.2 48.5 %all-gather.22.cloned.1.call-done = bf16[1536,2240]{1,0:T(8,128)(2,1)} async-done(((bf16[192,2240]{1,0:T(8,128)(2,1)}), bf16[1536,2240]{1,0:T(8,128)(2,1)}) %all-gather.22.cloned.1.call-update) | async-done | bytes 6881296 | tf_op jit(solution)/shard_map/all_gather | solution.py:49
  262.7 9.5 %fusion.28 = f32[512,2240]{0,1:T(8,128)} fusion(bf16[1536,2240]{1,0:T(8,128)(2,1)} %all-gather.22.cloned.1.call-done, bf16[512,1536]{1,0:T(8,128)(2,1)} %all-gather.20.cloned.1.call-done, f32[1536]{0:T(1024)S(1)} %convert_element_type.121, f32[512]{0:T(512)S(1)} %add_rsqrt_fusion.1), kind=kOutput, calls=%fused_computation.52 | convolution fusion | flops 3526361088 | bytes 13049856 | tf_op jit(solution)/shard_map/dot_general | solution.py:47
  272.2 41.3 %all-gather.24.cloned.1.call-done = bf16[1536,2240]{1,0:T(8,128)(2,1)} async-done(((bf16[192,2240]{1,0:T(8,128)(2,1)}), bf16[1536,2240]{1,0:T(8,128)(2,1)}) %all-gather.24.cloned.1.call-update) | async-done | bytes 6881296 | tf_op jit(solution)/shard_map/all_gather | solution.py:54
  313.5 50.8 %all-gather.26.cloned.1.call-done = bf16[2240,1536]{0,1:T(8,128)(2,1)} async-done(((bf16[2240,192]{0,1:T(8,128)(2,1)}), bf16[2240,1536]{0,1:T(8,128)(2,1)}) %all-gather.26.cloned.1.call-update) | async-done | bytes 6881296 | tf_op jit(solution)/shard_map/all_gather | solution.py:63
  364.2 15.9 %convolution_convert_fusion = bf16[512,1536]{1,0:T(8,128)(2,1)} fusion(bf16[2240,1536]{0,1:T(8,128)(2,1)} %all-gather.26.cloned.1.call-done, bf16[1536,2240]{1,0:T(8,128)(2,1)} %all-gather.24.cloned.1.call-done, f32[512,2240]{0,1:T(8,128)} %fusion.28, bf16[512,1536]{1,0:T(8,128)(2,1)S(1)} %copy-done.2, f32[1536]{0:T(1024)S(1)} %convert_element_type.121, ...), kind=kOutput, calls=%fused_computation.40 | convolution fusion | flops 7057244160 | bytes 21504000 | tf_op jit(solution)/shard_map/dot_general | solution.py:61
  380.2 2.7 copy.45
  382.9 34.3 %reduce-scatter.9.cloned.1.call-done = bf16[384,512]{1,0:T(8,128)(2,1)} async-done(((bf16[1536,512]{1,0:T(8,128)(2,1)}), bf16[384,512]{1,0:T(8,128)(2,1)}) %reduce-scatter.9.cloned.1.call-update) | async-done | bytes 393232
  417.2 1.2 copy.46
  418.4 0.9 add_convert_fusion
  419.4 0.5 all-gather.32.cloned.1.call-update
  419.9 0.7 all-gather.30.cloned.1.call-update
  420.7 0.3 fusion.37
  421.0 0.2 select_reduce_fusion.2
  421.4 0.3 compare_reduce_fusion
  421.8 2.0 gather_fusion
  423.8 0.9 select_select_fusion
  424.7 31.4 %all-gather.28.cloned.1.call-done = bf16[512,1536]{1,0:T(8,128)(2,1)} async-done(((bf16[512,384]{1,0:T(8,128)(2,1)}), bf16[512,1536]{1,0:T(8,128)(2,1)}) %all-gather.28.cloned.1.call-update) | async-done | bytes 1572880 | tf_op jit(solution)/shard_map/all_gather | solution.py:81
  456.0 1.8 fusion.23
  457.8 25.2 %all-gather.32.cloned.1.call-done = bf16[1536,512]{1,0:T(8,128)(2,1)} async-done(((bf16[192,512]{1,0:T(8,128)(2,1)}), bf16[1536,512]{1,0:T(8,128)(2,1)}) %all-gather.32.cloned.1.call-update) | async-done | bytes 1572880 | tf_op jit(solution)/shard_map/all_gather | solution.py:54
  483.1 2.9 fusion.30
  486.0 0.7 fusion.35
  486.7 22.4 %all-gather.30.cloned.1.call-done = bf16[1536,384]{1,0:T(8,128)(2,1)} async-done(((bf16[192,384]{1,0:T(8,128)(2,1)}), bf16[1536,384]{1,0:T(8,128)(2,1)}) %all-gather.30.cloned.1.call-update) | async-done | bytes 1179664 | tf_op jit(solution)/shard_map/all_gather | solution.py:49
  509.0 3.0 fusion.26
  512.1 1.1 copy.63
  (89 shorter events, 1.7 us)
Async XLA Ops:
  7.2 29.6 %all-gather.12.cloned.1.call-start = ((), (), s32[]{:S(2)}) async-start(), calls=%async_computation.2 | async-start | bytes 1769472 | tf_op jit(solution)/shard_map/all_gather | solution.py:54
  7.9 54.8 %all-gather.16.cloned.1.call-start = ((), (), s32[]{:S(2)}) async-start(), calls=%async_computation.4 | async-start | bytes 1327104 | tf_op jit(solution)/shard_map/all_gather | solution.py:49
  8.6 93.3 %all-gather.14.cloned.1.call-start = ((), (), s32[]{:S(2)}) async-start(), calls=%async_computation.3 | async-start | bytes 4718592 | tf_op jit(solution)/shard_map/all_gather | solution.py:205
  39.8 2.0 copy-start.3
  39.8 2.5 copy-start.7
  39.8 6.4 %copy-start.8 = (bf16[384]{0:T(512)(128)(2,1)S(1)}, bf16[384]{0:T(512)(128)(2,1)}, u32[]{:S(2)}) copy-start(bf16[384]{0:T(512)(128)(2,1)} %param.29) | copy-start | bytes 2308
  39.8 22.9 %copy-start.1 = (bf16[512,1536]{1,0:T(8,128)(2,1)S(1)}, bf16[512,1536]{1,0:T(8,128)(2,1)}, u32[]{:S(2)}) copy-start(bf16[512,1536]{1,0:T(8,128)(2,1)} %param.22) | copy-start | bytes 4718596
  41.1 86.7 %all-gather.18.cloned.1.call-start = ((), (), s32[]{:S(2)}) async-start(), calls=%async_computation.5 | async-start | bytes 1327104 | tf_op jit(solution)/shard_map/all_gather | solution.py:63
  41.7 130.9 %reduce-scatter.7.cloned.1.call-start = ((), (), s32[]{:S(2)}) async-start(), calls=%async_computation.13 | async-start | bytes 1966080
  131.7 46.5 %copy-start.5 = (bf16[1536]{0:T(1024)(128)(2,1)S(1)}, bf16[1536]{0:T(1024)(128)(2,1)}, u32[]{:S(2)}) copy-start(bf16[1536]{0:T(1024)(128)(2,1)} %param.33) | copy-start | bytes 9220
  131.7 80.7 %all-gather.20.cloned.1.call-start = ((), (), s32[]{:S(2)}) async-start(), calls=%async_computation.6 | async-start | bytes 1966080 | tf_op jit(solution)/shard_map/all_gather | solution.py:81
  175.7 87.0 %all-gather.22.cloned.1.call-start = ((), (), s32[]{:S(2)}) async-start(), calls=%async_computation.7 | async-start | bytes 7962624 | tf_op jit(solution)/shard_map/all_gather | solution.py:49
  176.4 137.0 %all-gather.24.cloned.1.call-start = ((), (), s32[]{:S(2)}) async-start(), calls=%async_computation.8 | async-start | bytes 7962624 | tf_op jit(solution)/shard_map/all_gather | solution.py:54
  177.2 187.1 %all-gather.26.cloned.1.call-start = ((), (), s32[]{:S(2)}) async-start(), calls=%async_computation.9 | async-start | bytes 7962624 | tf_op jit(solution)/shard_map/all_gather | solution.py:63
  177.9 239.3 %reduce-scatter.9.cloned.1.call-start = ((), (), s32[]{:S(2)}) async-start(), calls=%async_computation.14 | async-start | bytes 1966080
  214.2 150.1 %copy-start.2 = (bf16[512,1536]{1,0:T(8,128)(2,1)S(1)}, bf16[512,1536]{1,0:T(8,128)(2,1)}, u32[]{:S(2)}) copy-start(bf16[512,1536]{1,0:T(8,128)(2,1)} %all-gather.20.cloned.1.call-done) | copy-start | bytes 4718596
  380.1 40.5 %copy-start.4 = (s32[8,16]{1,0:T(8,128)S(1)}, s32[8,16]{1,0:T(8,128)}, u32[]{:S(2)}) copy-start(s32[8,16]{1,0:T(8,128)} %param.26) | copy-start | bytes 1540
  380.1 40.9 %copy-start.10 = (s32[8]{0:T(128)S(1)}, s32[8]{0:T(128)}, u32[]{:S(2)}) copy-start(s32[8]{0:T(128)} %param.24) | copy-start | bytes 100
  380.1 41.1 %copy-start.6 = (bf16[1536]{0:T(1024)(128)(2,1)S(1)}, bf16[1536]{0:T(1024)(128)(2,1)}, u32[]{:S(2)}) copy-start(bf16[1536]{0:T(1024)(128)(2,1)} %param.37) | copy-start | bytes 9220
  380.1 41.1 %copy-start.11 = (bf16[512]{0:T(512)(128)(2,1)S(1)}, bf16[512]{0:T(512)(128)(2,1)}, u32[]{:S(2)}) copy-start(bf16[512]{0:T(512)(128)(2,1)} %param.41) | copy-start | bytes 3076
  380.1 41.2 %copy-start.9 = (bf16[384]{0:T(512)(128)(2,1)S(1)}, bf16[384]{0:T(512)(128)(2,1)}, u32[]{:S(2)}) copy-start(bf16[384]{0:T(512)(128)(2,1)} %param.39) | copy-start | bytes 2308
  382.9 73.2 %all-gather.28.cloned.1.call-start = ((), (), s32[]{:S(2)}) async-start(), calls=%async_computation.10 | async-start | bytes 1966080 | tf_op jit(solution)/shard_map/all_gather | solution.py:81
  419.3 63.7 %all-gather.32.cloned.1.call-start = ((), (), s32[]{:S(2)}) async-start(), calls=%async_computation.12 | async-start | bytes 1769472 | tf_op jit(solution)/shard_map/all_gather | solution.py:54
  419.9 89.1 %all-gather.30.cloned.1.call-start = ((), (), s32[]{:S(2)}) async-start(), calls=%async_computation.11 | async-start | bytes 1327104 | tf_op jit(solution)/shard_map/all_gather | solution.py:49
  457.8 51.2 %copy-start = (bf16[512,1536]{1,0:T(8,128)(2,1)S(1)}, bf16[512,1536]{1,0:T(8,128)(2,1)}, u32[]{:S(2)}) copy-start(bf16[512,1536]{1,0:T(8,128)(2,1)} %all-gather.28.cloned.1.call-done) | copy-start | bytes 4718596
Sparse Core Ops, SparseCore 0:
  9.9 26.8 all-gather.11
  38.6 24.0 all-gather.15
  65.2 36.7 all-gather.13
  103.7 24.0 all-gather.17
  131.8 40.7 reduce-scatter.6
  175.8 36.5 all-gather.19
  214.2 48.3 all-gather.21
  264.6 48.8 all-gather.23
  315.4 48.8 all-gather.25
  383.0 34.1 reduce-scatter.8
  419.4 36.5 all-gather.27
  457.8 25.2 all-gather.31
  484.9 24.0 all-gather.29
where the time goes:
time: 522 us; the launch traced here: 520 us
  waiting for transfers between devices  421 us (81%)
  matrix products  46.8 us (9%)
  other arithmetic  18.3 us (4%)
  between operations  16.9 us (3%)
  local copies, waits for them, and re-layouts  15.3 us (3%)
    all_gather x3, waiting for transfers between devices, fold_rows(): lax.all_gather(second_weight, 'wide', axis=0, tiled=True)  90 us
    all_gather x3, waiting for transfers between devices, fold_rows(): lax.all_gather(first_weight, 'wide', axis=0, tiled=True)  87.4 us
    unnamed x15, waiting for transfers between devices  80.4 us
    all_gather x2, waiting for transfers between devices, add_branch(): result_rows = lax.all_gather(updated, 'narrow', axis=1, tiled=True)  65.6 us
    all_gather x2, waiting for transfers between devices, column_terms(): lax.all_gather(weight_block, 'wide', axis=1, tiled=True)  61.5 us
    all_gather x1, waiting for transfers between devices, local(): gathered = lax.all_gather(keyvals, 'wide', axis=0, tiled=True)  36.6 us
    dot_general x2, matrix products, column_terms(): jnp.dot(left_rows, lax.all_gather(weight_block, 'wide', axis=1, tiled=Tru...  18.2 us
    dot_general x3, matrix products, fold_rows(): jnp.dot(normed, lax.all_gather(first_weight, 'wide', axis=0, tiled=True),...  14.7 us
  transfers between devices with their start and end apart: 13, of which 13 were waited for; matrix products, arithmetic and copies ran while one was open for 9% of the time, Pallas kernels for 0%

commit v1 on v0

v1 whole, which is shorter than its diff:
```python
import functools
import math

import jax
import jax.numpy as jnp
from jax import lax
from jax.experimental import pallas as pl
from jax.experimental.pallas import tpu as pltpu
from jax.sharding import PartitionSpec as P

HD = 128
PAGE_LEN = 128

norm_eps = 1e-06
rope_base = 1000000.0
masked_score = -1e30

f32 = jnp.float32
bf16 = jnp.bfloat16
VMEM = pltpu.VMEM
ANY = pl.ANY
SMEM = pltpu.SMEM


def vmem_spec():
    return pl.BlockSpec(memory_space=VMEM)


def any_spec():
    return pl.BlockSpec(memory_space=ANY)


def smem_spec():
    return pl.BlockSpec(memory_space=SMEM)


def params(mib):
    return pltpu.CompilerParams(vmem_limit_bytes=mib << 20)


def norm_rows(values, gain_row):
    row_scale = lax.rsqrt(jnp.mean(values * values, axis=-1, keepdims=True) + norm_eps)
    return (values * row_scale * gain_row).astype(bf16)


def lookup(table, indices):
    table_match = indices[..., None] == jnp.arange(table.shape[0], dtype=jnp.int32)
    return jnp.sum(jnp.where(table_match, table, 0), axis=-1)


def exchange(value, axis, size, mask):
    return lax.ppermute(value, axis, [(i, i ^ mask) for i in range(size)])


def wide_pieces(value, size):
    pieces = {0: value}
    for mask in range(2, size, 2):
        pieces[mask] = exchange(value, "wide", size, mask)
    for mask in range(0, size, 2):
        pieces[mask + 1] = exchange(pieces[mask], "wide", size, 1)
    return [pieces[m] for m in range(size)]


def narrow_swap(pieces, size):
    return [pieces[0]] + [exchange(pieces[k], "narrow", size, k) for k in range(1, size)]


def place_copies(piece_refs, target, sems, wide_index):
    rows = piece_refs[0].shape[0]
    copies = []
    for m, piece in enumerate(piece_refs):
        start = pl.multiple_of((wide_index ^ m) * rows, rows)
        copies.append(pltpu.make_async_copy(piece, target.at[pl.ds(start, rows)], sems.at[m]))
    return copies


def contract_last(left, right):
    return lax.dot_general(left, right, (((1,), (1,)), ((), ())), preferred_element_type=f32)


def qkv_kernel(wide, index_ref, hidden_ref, gain_ref, bias_ref, cos_ref, sin_ref, *rest):
    pieces, (q_ref, kv_ref, weight, sems) = rest[:wide], rest[wide:]
    copies = place_copies(pieces, weight, sems, index_ref[0])
    for c in copies:
        c.start()
    normed = norm_rows(hidden_ref[...].astype(f32), gain_ref[...])
    cosine, sine = cos_ref[...], sin_ref[...]
    for c in copies:
        c.wait()
    heads = weight.shape[1] // HD
    for h in range(heads):
        lanes = slice(h * HD, (h + 1) * HD)
        if h % 2 == 0:
            wider = slice(h * HD, min(h + 2, heads) * HD)
            both = jnp.dot(normed, weight[:, wider], preferred_element_type=f32)
        value = both[:, (h % 2) * HD : (h % 2 + 1) * HD] + bias_ref[:, lanes]
        if h < heads - 1:
            value = value * cosine + pltpu.roll(value, HD // 2, 1) * sine
        value = value.astype(bf16)
        if h < heads - 2:
            q_ref[:, lanes] = value
        else:
            kv_ref[:, (h - heads + 2) * HD : (h - heads + 3) * HD] = value


def attend_kernel(wide, narrow, key_block, scalar_ref, starts_ref, q_ref, *rest):
    kv_pieces, out_pieces = rest[:wide], rest[wide : 2 * wide]
    rest = rest[2 * wide :]
    part_refs, (kv_out, keyvals, w_out, mix, kv_sems, out_sems, flush_sem) = rest[:narrow], rest[narrow:]
    wide_index, narrow_index = scalar_ref[0], scalar_ref[1]
    kv_copies = place_copies(kv_pieces, keyvals, kv_sems, wide_index)
    out_copies = place_copies(out_pieces, w_out, out_sems, wide_index)
    for c in kv_copies:
        c.start()
    for c in out_copies:
        c.start()
    for c in kv_copies:
        c.wait()
    flush = pltpu.make_async_copy(keyvals, kv_out, flush_sem)
    flush.start()
    tok_rows = q_ref.shape[0]
    heads = q_ref.shape[1] // HD
    tile = key_block
    row_base = wide_index * tok_rows
    factor = HD ** (-0.5) * math.log2(math.e)
    for t in range(tok_rows // tile):
        rows = slice(t * tile, (t + 1) * tile)
        stacked = jnp.concatenate(
            [q_ref[rows, h * HD : (h + 1) * HD] for h in range(heads)], axis=0
        )
        first = row_base + t * tile
        diagonal = first // tile
        lowest = scalar_ref[2 + 2 * t] // tile
        whole_from = (scalar_ref[3 + 2 * t] + tile - 1) // tile
        starts = jnp.concatenate([starts_ref[rows, :]] * heads, axis=0)
        own = first + lax.broadcasted_iota(jnp.int32, (tile, 1), 0)
        own = jnp.concatenate([own] * heads, axis=0)

        def visit(block, state, masked, stacked=stacked, starts=starts, own=own):
            top, total, mixed = state
            begin = pl.multiple_of(block * tile, tile)
            keys = keyvals[pl.ds(begin, tile), :HD]
            values = keyvals[pl.ds(begin, tile), HD:]
            scores = contract_last(stacked, keys) * factor
            if masked:
                spot = begin + lax.broadcasted_iota(jnp.int32, (1, tile), 1)
                scores = jnp.where((spot >= starts) & (spot <= own), scores, masked_score)
            new_top = jnp.maximum(top, jnp.max(scores, axis=1, keepdims=True))
            weights = jnp.exp2(scores - new_top)
            scale = jnp.exp2(top - new_top)
            total = total * scale + jnp.sum(weights, axis=1, keepdims=True)
            mixed = mixed * scale + jnp.dot(
                weights.astype(bf16), values, preferred_element_type=f32
            )
            return new_top, total, mixed

        count = heads * tile
        state = (
            jnp.full((count, 1), masked_score, f32),
            jnp.zeros((count, 1), f32),
            jnp.zeros((count, HD), f32),
        )
        state = visit(diagonal, state, True)
        split = jnp.minimum(whole_from, diagonal)
        state = lax.fori_loop(lowest, split, lambda b, s: visit(b, s, True), state)
        split = jnp.maximum(split, lowest)
        _, total, mixed = lax.fori_loop(split, diagonal, lambda b, s: visit(b, s, False), state)
        mixed = (mixed / total).astype(bf16)
        for h in range(heads):
            mix[rows, h * HD : (h + 1) * HD] = mixed[h * tile : (h + 1) * tile]
    for c in out_copies:
        c.wait()
    share = tok_rows // narrow
    for k in range(narrow):
        start = pl.multiple_of((narrow_index ^ k) * share, share)
        part_refs[k][...] = contract_last(mix[pl.ds(start, share), :], w_out[...]).astype(bf16)
    flush.wait()


def join_kernel(narrow, base_ref, gain_ref, *rest):
    parts, (sum_ref, norm_ref) = rest[:narrow], rest[narrow:]
    total = parts[0][...].astype(f32)
    for part in parts[1:]:
        total = total + part[...].astype(f32)
    rounded = (base_ref[...].astype(f32) + total).astype(bf16)
    sum_ref[...] = rounded
    if norm_ref is not None:
        norm_ref[...] = norm_rows(rounded.astype(f32), gain_ref[...])


def ffn_kernel(narrow, *rest):
    x_refs, weights_ref = rest[:narrow], rest[narrow]
    rest = rest[narrow + 1 :]
    part_refs, (x, held, gate, hidden, sems) = rest[:narrow], rest[narrow:]
    copies = [
        pltpu.make_async_copy(weights_ref.at[:, j], held.at[j], sems.at[j]) for j in range(3)
    ]
    for c in copies:
        c.start()
    share = x_refs[0].shape[0]
    for k in range(narrow):
        x[k * share : (k + 1) * share, :] = x_refs[k][...]
    width = hidden.shape[1]
    depth = x.shape[1]
    tile = 256
    whole = width // tile

    def each_tile(body):
        @pl.loop(0, whole)
        def _(j):
            body(pl.ds(pl.multiple_of(j * tile, tile), tile), tile)

        if width % tile:
            body(slice(whole * tile, width), width - whole * tile)

    def gate_tile(lanes, size):
        block = held[0, :, :, lanes].reshape(depth, size)
        gate[:, lanes] = jnp.dot(x[...], block, preferred_element_type=f32)

    def up_tile(lanes, size):
        block = held[1, :, :, lanes].reshape(depth, size)
        up = jnp.dot(x[...], block, preferred_element_type=f32)
        value = gate[:, lanes]
        hidden[:, lanes] = (value / (1.0 + jnp.exp(-value)) * up).astype(bf16)

    copies[0].wait()
    each_tile(gate_tile)
    copies[1].wait()
    each_tile(up_tile)
    copies[2].wait()
    pieces, rows = held.shape[1], held.shape[2]
    group = 768 // rows
    for g in range(pieces // group):
        block = held[2, g * group : (g + 1) * group].reshape(group * rows, width)
        product = contract_last(hidden[...], block)
        lanes = slice(g * group * rows, (g + 1) * group * rows)
        for k in range(narrow):
            part_refs[k][:, lanes] = product[k * share : (k + 1) * share].astype(bf16)


def next_kernel(wide, narrow, scalar_ref, gain_ref, bias_ref, *rest):
    h_refs, pieces = rest[:narrow], rest[narrow : narrow + wide]
    out_ref, query_ref, keyval_ref, weight, sems = rest[narrow + wide :]
    wide_index, narrow_index = scalar_ref[0], scalar_ref[1]
    copies = place_copies(pieces, weight, sems, wide_index)
    for c in copies:
        c.start()
    share = h_refs[0].shape[0]
    queries = query_ref.shape[1]
    for c in copies:
        c.wait()
    for k in range(narrow):
        rows = pl.ds(pl.multiple_of((narrow_index ^ k) * share, share), share)
        value = h_refs[k][...]
        out_ref[rows, :] = value
        normed = norm_rows(value.astype(f32), gain_ref[...])
        product = jnp.dot(normed, weight[...], preferred_element_type=f32) + bias_ref[...]
        query_ref[rows, :] = product[:, :queries].astype(bf16)
        keyval_ref[rows, :] = product[:, queries:].astype(bf16)


def fill_pages(source, seg_lengths, seg_offsets, block_table, first_page, page_count):
    pages_here = first_page + jnp.arange(page_count, dtype=jnp.int32)
    page_match = block_table[None, :, :] == pages_here[:, None, None]
    seg_grid = jnp.arange(block_table.shape[0], dtype=jnp.int32)[None, :, None]
    page_grid = jnp.arange(block_table.shape[1], dtype=jnp.int32)[None, None, :]
    page_owner = jnp.sum(jnp.where(page_match, seg_grid, 0), axis=(1, 2))
    logical = jnp.sum(jnp.where(page_match, page_grid, 0), axis=(1, 2))
    in_use = jnp.any(page_match, axis=(1, 2))
    first_token = lookup(seg_offsets, page_owner) + logical * PAGE_LEN
    filled = lookup(seg_lengths, page_owner) - logical * PAGE_LEN
    slot_index = jnp.arange(PAGE_LEN, dtype=jnp.int32)
    row_ids = jnp.clip(first_token[:, None] + slot_index[None, :], 0, source.shape[0] - 1)
    keep_slot = in_use[:, None] & (slot_index[None, :] < filled[:, None])
    taken_rows = jnp.take(source, row_ids.reshape(-1), axis=0).reshape(
        page_count, PAGE_LEN, source.shape[1]
    )
    return jnp.where(keep_slot[:, :, None], taken_rows, jnp.zeros((), source.dtype))


def local(
    wide,
    narrow,
    hidden_in,
    segment_ids,
    seg_lengths,
    seg_offsets,
    block_table,
    attn_gain,
    w_query,
    b_query,
    w_keyval,
    b_keyval,
    w_out,
    mlp_gain,
    w_gate,
    w_up,
    w_down,
    next_gain,
    w_query2,
    b_query2,
    w_keyval2,
    b_keyval2,
):
    tok_rows, depth = hidden_in.shape
    piece_rows = w_query.shape[0]
    query_width = w_query.shape[1]
    width = w_gate.shape[1]
    wide_index = lax.axis_index("wide")
    narrow_index = lax.axis_index("narrow")
    head_pair = narrow_index // 2
    kind_index = narrow_index % 2
    pair_offset = head_pair * 2 * HD
    share = tok_rows // narrow
    row_base = wide_index * tok_rows

    packed = jnp.stack([w_gate, w_up, w_down.T])
    ffn_weights = lax.all_gather(packed, "wide", axis=0, tiled=False)

    qkv_weight = jnp.concatenate(
        [w_query, lax.dynamic_slice_in_dim(w_keyval, pair_offset, 2 * HD, 1)], axis=1
    )
    qkv_bias = jnp.concatenate(
        [b_query, lax.dynamic_slice_in_dim(b_keyval, pair_offset, 2 * HD, 0)]
    ).astype(f32)[None]
    qkv_pieces = wide_pieces(qkv_weight, wide)

    token_start = lookup(seg_offsets, segment_ids)
    positions = row_base + jnp.arange(tok_rows, dtype=jnp.int32) - token_start
    half = HD // 2
    frequency = rope_base ** (-(jnp.arange(half, dtype=f32) * 2.0 / HD))
    angles = positions.astype(f32)[:, None] * frequency
    cosine, sine = jnp.cos(angles), jnp.sin(angles)
    cosine = jnp.concatenate([cosine, cosine], axis=1)
    sine = jnp.concatenate([-sine, sine], axis=1)

    qkv_width = query_width + 2 * HD
    queries, keyvals = pl.pallas_call(
        functools.partial(qkv_kernel, wide),
        out_shape=(
            jax.ShapeDtypeStruct((tok_rows, query_width), bf16),
            jax.ShapeDtypeStruct((tok_rows, 2 * HD), bf16),
        ),
        in_specs=[smem_spec()] + [vmem_spec()] * 5 + [any_spec()] * wide,
        out_specs=(vmem_spec(), vmem_spec()),
        scratch_shapes=[VMEM((depth, qkv_width), bf16), pltpu.SemaphoreType.DMA((wide,))],
        compiler_params=params(32),
        cost_estimate=pl.CostEstimate(
            flops=2 * tok_rows * depth * qkv_width,
            bytes_accessed=2 * depth * (tok_rows + qkv_width),
            transcendentals=0,
        ),
        name="qkv",
    )(
        wide_index[None],
        hidden_in,
        attn_gain.astype(f32)[None],
        qkv_bias,
        cosine,
        sine,
        *qkv_pieces,
    )

    kv_pieces = wide_pieces(keyvals, wide)
    out_pieces = wide_pieces(w_out.T, wide)

    tile = 256
    ends = []
    for t in range(tok_rows // tile):
        ends += [token_start[t * tile], token_start[(t + 1) * tile - 1]]
    scalars = jnp.stack([wide_index, narrow_index] + ends)
    total_rows = wide * tok_rows
    *parts, kv_all = pl.pallas_call(
        functools.partial(attend_kernel, wide, narrow, tile),
        out_shape=[jax.ShapeDtypeStruct((share, depth), bf16)] * narrow
        + [jax.ShapeDtypeStruct((total_rows, 2 * HD), bf16)],
        in_specs=[smem_spec(), vmem_spec(), vmem_spec()] + [any_spec()] * (2 * wide),
        out_specs=[vmem_spec()] * narrow + [any_spec()],
        scratch_shapes=[
            VMEM((total_rows, 2 * HD), bf16),
            VMEM((depth, query_width), bf16),
            VMEM((tok_rows, query_width), bf16),
            pltpu.SemaphoreType.DMA((wide,)),
            pltpu.SemaphoreType.DMA((wide,)),
            pltpu.SemaphoreType.DMA,
        ],
        compiler_params=params(40),
        cost_estimate=pl.CostEstimate(
            flops=8 * tok_rows * query_width * depth,
            bytes_accessed=4 * total_rows * HD,
            transcendentals=tok_rows * depth,
        ),
        name="attend",
    )(scalars, token_start[:, None], queries, *kv_pieces, *out_pieces)

    def join(parts, base_rows, gain, with_norm):
        shape = jax.ShapeDtypeStruct((share, depth), bf16)
        kernel = functools.partial(join_kernel, narrow)
        if not with_norm:
            body = kernel
            kernel = lambda *refs: body(*refs, None)
        return pl.pallas_call(
            kernel,
            out_shape=[shape, shape] if with_norm else [shape],
            in_specs=[vmem_spec()] * (2 + narrow),
            out_specs=[vmem_spec()] * (2 if with_norm else 1),
            compiler_params=params(24),
            name="join",
        )(base_rows, gain, *parts)

    base_rows = lax.dynamic_slice_in_dim(hidden_in, narrow_index * share, share, 0)
    residual, normed = join(
        narrow_swap(parts, narrow), base_rows, mlp_gain.astype(f32)[None], True
    )
    normed_pieces = [normed] + [exchange(normed, "narrow", narrow, k) for k in range(1, narrow)]

    parts = pl.pallas_call(
        functools.partial(ffn_kernel, narrow),
        out_shape=[jax.ShapeDtypeStruct((share, depth), bf16)] * narrow,
        in_specs=[vmem_spec()] * narrow + [any_spec()],
        out_specs=[vmem_spec()] * narrow,
        scratch_shapes=[
            VMEM((tok_rows, depth), bf16),
            VMEM((3, wide, piece_rows, width), bf16),
            VMEM((tok_rows, width), f32),
            VMEM((tok_rows, width), bf16),
            pltpu.SemaphoreType.DMA((3,)),
        ],
        compiler_params=params(52),
        cost_estimate=pl.CostEstimate(
            flops=6 * tok_rows * depth * width,
            bytes_accessed=6 * depth * width,
            transcendentals=tok_rows * width,
        ),
        name="ffn",
    )(*normed_pieces, ffn_weights)

    (hidden_rows,) = join(
        narrow_swap(parts, narrow), residual, mlp_gain.astype(f32)[None], False
    )
    hidden_pieces = [hidden_rows] + [
        exchange(hidden_rows, "narrow", narrow, k) for k in range(1, narrow)
    ]

    one_offset = pair_offset + kind_index * HD
    next_weight = jnp.concatenate(
        [w_query2, lax.dynamic_slice_in_dim(w_keyval2, one_offset, HD, 1)], axis=1
    )
    next_bias = jnp.concatenate(
        [b_query2, lax.dynamic_slice_in_dim(b_keyval2, one_offset, HD, 0)]
    ).astype(f32)[None]
    next_pieces = wide_pieces(next_weight, wide)
    next_width = query_width + HD
    hidden_out, next_query, next_keyval = pl.pallas_call(
        functools.partial(next_kernel, wide, narrow),
        out_shape=(
            jax.ShapeDtypeStruct((tok_rows, depth), bf16),
            jax.ShapeDtypeStruct((tok_rows, query_width), bf16),
            jax.ShapeDtypeStruct((tok_rows, HD), bf16),
        ),
        in_specs=[smem_spec()] + [vmem_spec()] * (2 + narrow) + [any_spec()] * wide,
        out_specs=(vmem_spec(),) * 3,
        scratch_shapes=[VMEM((depth, next_width), bf16), pltpu.SemaphoreType.DMA((wide,))],
        compiler_params=params(32),
        cost_estimate=pl.CostEstimate(
            flops=2 * tok_rows * depth * next_width,
            bytes_accessed=2 * depth * (2 * tok_rows + next_width),
            transcendentals=0,
        ),
        name="next",
    )(
        scalars[:2],
        next_gain.astype(f32)[None],
        next_bias,
        *hidden_pieces,
        *next_pieces,
    )

    source = lax.dynamic_slice_in_dim(kv_all, kind_index * HD, HD, 1)
    page_count = tok_rows // PAGE_LEN + 1
    cache_block = fill_pages(
        source, seg_lengths, seg_offsets, block_table, wide_index * page_count, page_count
    )
    return (hidden_out, next_query, next_keyval, cache_block[None])


def solution(mesh):
    placed = (
        P("wide", None),
        P("wide"),
        P(),
        P(),
        P(),
        P(),
        P("wide", "narrow"),
        P("narrow"),
        P("wide", None),
        P(),
        P("narrow", "wide"),
        P(),
        P("wide", "narrow"),
        P("wide", "narrow"),
        P("narrow", "wide"),
        P(),
        P("wide", "narrow"),
        P("narrow"),
        P("wide", None),
        P(),
    )
    return jax.shard_map(
        functools.partial(local, mesh.shape["wide"], mesh.shape["narrow"]),
        mesh=mesh,
        in_specs=placed,
        out_specs=(
            P("wide", None),
            P("wide", "narrow"),
            P("wide", "narrow"),
            P("narrow", "wide", None, None),
        ),
        check_vma=False,
    )
```

time: 522 us -> 271 us (0.52)
  the two profiles are of different devices: /device:TPU:10 before, /device:TPU:4 now
where the time goes in v1:
time: 271 us; the launch traced here: 267 us
  waiting for transfers between devices  116 us (43%)
  starting transfers between devices  70.4 us (26%)
  Pallas kernels  38.7 us (14%)
  local copies, waits for them, and re-layouts  17.1 us (6%)
  between operations  14.5 us (5%)
  other arithmetic  10.2 us (4%)
    ppermute x40, waiting for transfers between devices, exchange(): return lax.ppermute(value, axis, [(i, i ^ mask) for i in range(size)])  116 us
    ppermute x40, starting transfers between devices, exchange(): return lax.ppermute(value, axis, [(i, i ^ mask) for i in range(size)])  70.4 us
    pallas_call x1, Pallas kernels, local(): pl.pallas_call(functools.partial(ffn_kernel, narrow), out_shape=[jax.Shap...  18.5 us
    pallas_call x1, Pallas kernels, local(): pl.pallas_call(functools.partial(attend_kernel, wide, narrow, tile), out_...  9.17 us
    unnamed x66, local copies, waits for them, and re-layouts  8.07 us
    pallas_call x1, Pallas kernels, local(): pl.pallas_call(functools.partial(qkv_kernel, wide), out_shape=(jax.ShapeD...  5.53 us
  transfers between devices with their start and end apart: 41, of which 13 were waited for; matrix products, arithmetic and copies ran while one was open for 6% of the time, Pallas kernels for 13%

profile of v1, /device:TPU:4, one launch (start us, length us, event | category | flops | bytes accessed | tf_op | source)
XLA Modules:
  0.0 267.0 jit_solution(14486204434180446384)
XLA Ops:
  7.2 3.5 %pad_maximum_fusion = bf16[3,192,2240]{2,1,0:T(8,128)(2,1)} fusion(bf16[1,192,2240]{2,1,0:T(8,128)(2,1)} %bitcast.24, bf16[1,192,2240]{2,1,0:T(8,128)(2,1)} %bitcast.25, bf16[1,192,2240]{2,1,0:T(8,128)(2,1)} %bitcast.26), kind=kLoop, calls=%fused_computation.1 | loop fusion | flops 2580480 | bytes 5160960 | tf_op jit(solution)/shard_map/stack | solution.py:317
  10.9 0.8 copy-done.14
  11.7 1.5 collective-permute-start.5
  13.2 1.5 collective-permute-start.3
  14.7 0.5 collective-permute-start.1
  15.3 1.4 collective-permute-start.19
  16.8 1.0 fusion
  17.8 3.7 %collective-permute-done.5.rest_6_ = bf16[192,640]{1,0:T(8,128)(2,1)S(1)} collective-permute-done((bf16[192,640]{1,0:T(8,128)(2,1)S(1)}, bf16[192,640]{1,0:T(8,128)(2,1)S(1)}, u32[]{:S(2)}, u32[]{:S(2)}) %collective-permute-start.5) | collective-permute-done | bytes 245792 | tf_op jit(solution)/shard_map/ppermute | solution.py:52
  21.6 6.7 %collective-permute-done.3.rest_4_ = bf16[192,640]{1,0:T(8,128)(2,1)S(1)} collective-permute-done((bf16[192,640]{1,0:T(8,128)(2,1)S(1)}, bf16[192,640]{1,0:T(8,128)(2,1)S(1)}, u32[]{:S(2)}, u32[]{:S(2)}) %collective-permute-start.3) | collective-permute-done | bytes 245792 | tf_op jit(solution)/shard_map/ppermute | solution.py:52
  28.3 0.5 collective-permute-start.2
  29.5 0.8 collective-permute-start.17
  30.3 2.5 collective-permute-start.15
  32.9 5.5 %qkv.1 = (bf16[512,384]{1,0:T(8,128)(2,1)S(1)}, bf16[512,256]{1,0:T(8,128)(2,1)}) custom-call(s32[1]{0:T(128)} %bitcast.index_ref, bf16[512,1536]{1,0:T(8,128)(2,1)S(1)} %copy-done.1, f32[1,1536]{1,0:T(1,128)S(1)} %reshape.200.gain_ref, f32[1,640]{1,0:T(1,128)S(1)} %maximum_convert_fusion.bias_ref, f32[512,128]{1,0:T(8,128)S(1)} %get-tuple-element.47.cos_ref, ...), custom_call_target="tpu_custom_call" | custom-call | flops 1006632960 | bytes 3538944 | tf_op jit(solution)/shard_map/qkv/pallas_call | solution.py:338
  38.8 1.5 collective-permute-start.10
  40.3 1.7 collective-permute-start.8
  42.3 0.7 copy-done.8
  43.0 0.5 collective-permute-start.18
  43.5 0.5 multiply_subtract_fusion
  44.0 10.4 %collective-permute-done.12.rest_6_ = bf16[512,256]{1,0:T(8,128)(2,1)S(1)} collective-permute-done((bf16[512,256]{1,0:T(8,128)(2,1)}, bf16[512,256]{1,0:T(8,128)(2,1)S(1)}, u32[]{:S(2)}, u32[]{:S(2)}) %collective-permute-start.12) | collective-permute-done | bytes 262176 | tf_op jit(solution)/shard_map/ppermute | solution.py:52
  54.4 4.7 %collective-permute-done.10.rest_4_ = bf16[512,256]{1,0:T(8,128)(2,1)S(1)} collective-permute-done((bf16[512,256]{1,0:T(8,128)(2,1)}, bf16[512,256]{1,0:T(8,128)(2,1)S(1)}, u32[]{:S(2)}, u32[]{:S(2)}) %collective-permute-start.10) | collective-permute-done | bytes 262176 | tf_op jit(solution)/shard_map/ppermute | solution.py:52
  59.1 5.1 %collective-permute-done.8.rest_2_ = bf16[512,256]{1,0:T(8,128)(2,1)} collective-permute-done((bf16[512,256]{1,0:T(8,128)(2,1)}, bf16[512,256]{1,0:T(8,128)(2,1)}, u32[]{:S(2)}, u32[]{:S(2)}) %collective-permute-start.8) | collective-permute-done | bytes 262176 | tf_op jit(solution)/shard_map/ppermute | solution.py:52
  64.3 0.8 constant_dynamic-slice_fusion.1
  65.1 0.7 copy-done.12
  65.8 0.5 collective-permute-start.16
  66.3 0.6 fusion.9
  67.1 1.3 stack.26.scalar_ref
  68.4 0.9 pad_maximum_fusion.4.rest_4_
  69.4 1.6 collective-permute-start.38
  71.0 0.7 collective-permute-start.36
  71.7 0.9 copy-done.6
  72.7 0.9 copy-done.9
  73.6 0.9 copy-done.11
  74.5 0.9 copy-done.13
  75.4 9.2 %attend.1 = (bf16[128,1536]{1,0:T(8,128)(2,1)S(1)}, bf16[128,1536]{1,0:T(8,128)(2,1)}, bf16[128,1536]{1,0:T(8,128)(2,1)}, bf16[128,1536]{1,0:T(8,128)(2,1)}, bf16[4096,256]{1,0:T(8,128)(2,1)S(1)}) custom-call(s32[6]{0:T(128)S(1)} %stack.26.scalar_ref, s32[512,1]{1,0:T(8,128)S(1)} %copy.26.starts_ref, bf16[512,384]{1,0:T(8,128)(2,1)S(1)} %get-tuple-element.20.q_ref, ...), custom_call_target="tpu_custom_call" | custom-call | flops 2415919104 | bytes 2097152 | tf_op jit(solution)/shard_map/attend/pallas_call | solution.py:373
  84.6 1.4 copy-done.2
  86.0 1.4 collective-permute-start.21
  87.3 2.8 %collective-permute-start.22 = (bf16[128,1536]{1,0:T(8,128)(2,1)}, bf16[128,1536]{1,0:T(8,128)(2,1)S(1)}, u32[]{:S(2)}, u32[]{:S(2)}) collective-permute-start(bf16[128,1536]{1,0:T(8,128)(2,1)} %get-tuple-element.24), channel_id=1, source_target_pairs={{0,2},{1,3},{2,0},{3,1},{4,6},{5,7},{6,4},{7,5},{8,10},{9,11},{10,... | collective-permute-start | bytes 1179656 | tf_op jit(solution)/shard_map/ppermute | solution.py:52
  90.4 0.6 dynamic-slice_bitcast_fusion
  91.0 0.6 concatenate.41
  91.5 0.7 reshape.198.gain_ref
  92.2 1.3 maximum_convert_fusion.1.bias_ref
  93.5 11.1 %collective-permute-done.21.rest_1_ = bf16[128,1536]{1,0:T(8,128)(2,1)S(1)} collective-permute-done((bf16[128,1536]{1,0:T(8,128)(2,1)}, bf16[128,1536]{1,0:T(8,128)(2,1)S(1)}, u32[]{:S(2)}, u32[]{:S(2)}) %collective-permute-start.21) | collective-permute-done | bytes 393248 | tf_op jit(solution)/shard_map/ppermute | solution.py:52
  104.6 11.2 %collective-permute-done.23.rest_3_ = bf16[128,1536]{1,0:T(8,128)(2,1)S(1)} collective-permute-done((bf16[128,1536]{1,0:T(8,128)(2,1)}, bf16[128,1536]{1,0:T(8,128)(2,1)S(1)}, u32[]{:S(2)}, u32[]{:S(2)}) %collective-permute-start.23) | collective-permute-done | bytes 393248 | tf_op jit(solution)/shard_map/ppermute | solution.py:52
  115.8 0.4 join.2
  116.2 3.3 %collective-permute-start.26 = (bf16[128,1536]{1,0:T(8,128)(2,1)S(1)}, bf16[128,1536]{1,0:T(8,128)(2,1)S(1)}, u32[]{:S(2)}, u32[]{:S(2)}) collective-permute-start(bf16[128,1536]{1,0:T(8,128)(2,1)S(1)} %get-tuple-element.27.rest_0_), channel_id=1, source_target_pairs={{0,3},{1,2},{2,1},{3,0},{4,7},{5,6},{6,5},{7,4},{8,11},{9,10},{10,... | collective-permute-start | bytes 1179656 | tf_op jit(solution)/shard_map/ppermute | solution.py:52
  119.4 16.1 %collective-permute-start.25 = (bf16[128,1536]{1,0:T(8,128)(2,1)S(1)}, bf16[128,1536]{1,0:T(8,128)(2,1)S(1)}, u32[]{:S(2)}, u32[]{:S(2)}) collective-permute-start(bf16[128,1536]{1,0:T(8,128)(2,1)S(1)} %get-tuple-element.27.rest_0_), channel_id=1, source_target_pairs={{0,2},{1,3},{2,0},{3,1},{4,6},{5,7},{6,4},{7,5},{8,10},{9,11},{10,... | collective-permute-start | bytes 1179656 | tf_op jit(solution)/shard_map/ppermute | solution.py:52
  135.5 0.4 collective-permute-start.24
  136.0 0.7 fusion.3
  136.7 25.3 %collective-permute-done.25.rest_2_ = bf16[128,1536]{1,0:T(8,128)(2,1)S(1)} collective-permute-done((bf16[128,1536]{1,0:T(8,128)(2,1)S(1)}, bf16[128,1536]{1,0:T(8,128)(2,1)S(1)}, u32[]{:S(2)}, u32[]{:S(2)}) %collective-permute-start.25) | collective-permute-done | bytes 393248 | tf_op jit(solution)/shard_map/ppermute | solution.py:52
  162.1 0.7 copy-done.29
  162.9 18.5 %ffn.1 = (bf16[128,1536]{1,0:T(8,128)(2,1)S(1)}, bf16[128,1536]{1,0:T(8,128)(2,1)S(1)}, bf16[128,1536]{1,0:T(8,128)(2,1)S(1)}, bf16[128,1536]{1,0:T(8,128)(2,1)S(1)}) custom-call(bf16[128,1536]{1,0:T(8,128)(2,1)S(1)} %get-tuple-element.27.rest_0_, bf16[128,1536]{1,0:T(8,128)(2,1)} %copy-done.30, bf16[128,1536]{1,0:T(8,128)(2,1)} %copy-done.29, ...), custom_call_target="tpu_custom_call" | custom-call | flops 10569646080 | bytes 20643840 | tf_op jit(solution)/shard_map/ffn/pallas_call | solution.py:417
  181.6 3.4 %collective-permute-start.28 = (bf16[128,1536]{1,0:T(8,128)(2,1)S(1)}, bf16[128,1536]{1,0:T(8,128)(2,1)S(1)}, u32[]{:S(2)}, u32[]{:S(2)}) collective-permute-start(bf16[128,1536]{1,0:T(8,128)(2,1)S(1)} %get-tuple-element.30), channel_id=1, source_target_pairs={{0,2},{1,3},{2,0},{3,1},{4,6},{5,7},{6,4},{7,5},{8,10},{9,11},{10,... | collective-permute-start | bytes 1179656 | tf_op jit(solution)/shard_map/ppermute | solution.py:52
  184.9 0.9 collective-permute-start.29
  186.2 7.1 %collective-permute-start.34 = (bf16[192,512]{1,0:T(8,128)(2,1)S(1)}, bf16[192,512]{1,0:T(8,128)(2,1)S(1)}, u32[]{:S(2)}, u32[]{:S(2)}) collective-permute-start(bf16[192,512]{1,0:T(8,128)(2,1)S(1)} %pad_maximum_fusion.4.rest_4_), channel_id=1, source_target_pairs={{0,8},{4,12},{8,0},{12,4},{16,24},{20,28},{24,16},{28,20},{1,9},{5... | collective-permute-start | bytes 589832 | tf_op jit(solution)/shard_map/ppermute | solution.py:52
  193.4 7.1 %collective-permute-done.27.refs_3_ = bf16[128,1536]{1,0:T(8,128)(2,1)S(1)} collective-permute-done((bf16[128,1536]{1,0:T(8,128)(2,1)S(1)}, bf16[128,1536]{1,0:T(8,128)(2,1)S(1)}, u32[]{:S(2)}, u32[]{:S(2)}) %collective-permute-start.27) | collective-permute-done | bytes 393248 | tf_op jit(solution)/shard_map/ppermute | solution.py:52
  200.6 11.2 %collective-permute-done.28.refs_4_ = bf16[128,1536]{1,0:T(8,128)(2,1)S(1)} collective-permute-done((bf16[128,1536]{1,0:T(8,128)(2,1)S(1)}, bf16[128,1536]{1,0:T(8,128)(2,1)S(1)}, u32[]{:S(2)}, u32[]{:S(2)}) %collective-permute-start.28) | collective-permute-done | bytes 393248 | tf_op jit(solution)/shard_map/ppermute | solution.py:52
  212.1 2.5 collective-permute-start.32
  214.6 15.6 %collective-permute-start.31 = (bf16[128,1536]{1,0:T(8,128)(2,1)S(1)}, bf16[128,1536]{1,0:T(8,128)(2,1)S(1)}, u32[]{:S(2)}, u32[]{:S(2)}) collective-permute-start(bf16[128,1536]{1,0:T(8,128)(2,1)S(1)} %join.3.rest_0_), channel_id=1, source_target_pairs={{0,2},{1,3},{2,0},{3,1},{4,6},{5,7},{6,4},{7,5},{8,10},{9,11},{10,... | collective-permute-start | bytes 1179656 | tf_op jit(solution)/shard_map/ppermute | solution.py:52
  230.3 1.0 constant_dynamic-slice_fusion
  231.3 3.1 %gather_fusion = bf16[640,128]{1,0:T(8,128)(2,1)S(1)} fusion(bf16[4096,128]{1,0:T(8,128)(2,1)} %constant_dynamic-slice_fusion, s32[1024]{0:T(1024)S(1)} %pad_clamp_fusion), kind=kCustom, calls=%fused_computation | custom fusion | bytes 330240 | tf_op jit(solution)/shard_map/jit(_take)/gather | solution.py:275
  234.5 0.5 collective-permute-start.35
  235.0 0.9 select_select_fusion
  236.2 19.1 %collective-permute-done.31.rest_2_ = bf16[128,1536]{1,0:T(8,128)(2,1)S(1)} collective-permute-done((bf16[128,1536]{1,0:T(8,128)(2,1)S(1)}, bf16[128,1536]{1,0:T(8,128)(2,1)S(1)}, u32[]{:S(2)}, u32[]{:S(2)}) %collective-permute-start.31) | collective-permute-done | bytes 393248 | tf_op jit(solution)/shard_map/ppermute | solution.py:52
  255.3 4.9 %next.1 = (bf16[512,1536]{1,0:T(8,128)(2,1)}, bf16[512,384]{1,0:T(8,128)(2,1)}, bf16[512,128]{1,0:T(8,128)(2,1)}) custom-call(s32[2]{0:T(128)S(1)} %pad_add_fusion.scalar_ref, f32[1,1536]{1,0:T(1,128)S(1)} %reshape.198.gain_ref, f32[1,512]{1,0:T(1,128)S(1)} %copy-done.4, bf16[128,1536]{1,0:T(8,128)(2,1)S(1)} %join.3.rest_0_, ...), custom_call_target="tpu_custom_call" | custom-call | flops 805306368 | bytes 4718592 | tf_op jit(solution)/shard_map/next/pallas_call | solution.py:454
  (129 shorter events, 3.6 us)
Async XLA Ops:
  7.2 3.7 %copy-start = (bf16[192,512]{1,0:T(8,128)(2,1)S(1)}, bf16[192,512]{1,0:T(8,128)(2,1)}, u32[]{:S(2)}) copy-start(bf16[192,512]{1,0:T(8,128)(2,1)} %param.28) | copy-start | bytes 589828
  7.2 154.9 %all-gather.3.cloned.1.call-start = ((), (), s32[]{:S(2)}) async-start(), calls=%async_computation | async-start | bytes 23887872 | tf_op jit(solution)/shard_map/all_gather | solution.py:318
  10.8 4.5 %copy-start.7 = (bf16[384,192]{0,1:T(8,128)(2,1)S(1)}, bf16[384,192]{0,1:T(8,128)(2,1)}, u32[]{:S(2)}) copy-start(bf16[384,192]{0,1:T(8,128)(2,1)} %param.30) | copy-start | bytes 442372
  10.8 5.9 %copy-start.20 = (s32[8]{0:T(128)S(1)}, s32[8]{0:T(128)}, u32[]{:S(2)}) copy-start(s32[8]{0:T(128)} %param.23) | copy-start | bytes 100
  10.8 5.9 %copy-start.22 = (s32[512]{0:T(512)S(1)}, s32[512]{0:T(512)}, u32[]{:S(2)}) copy-start(s32[512]{0:T(512)} %param.21) | copy-start | bytes 6148
  10.8 18.0 %copy-start.15 = (s32[8,16]{1,0:T(8,128)S(1)}, s32[8,16]{1,0:T(8,128)}, u32[]{:S(2)}) copy-start(s32[8,16]{1,0:T(8,128)} %param.24) | copy-start | bytes 1540
  10.8 18.4 %copy-start.31 = (bf16[512]{0:T(512)(128)(2,1)S(1)}, bf16[512]{0:T(512)(128)(2,1)}, u32[]{:S(2)}) copy-start(bf16[512]{0:T(512)(128)(2,1)} %param.29) | copy-start | bytes 3076
  10.8 18.4 %copy-start.25 = (bf16[384]{0:T(512)(128)(2,1)S(1)}, bf16[384]{0:T(512)(128)(2,1)}, u32[]{:S(2)}) copy-start(bf16[384]{0:T(512)(128)(2,1)} %param.27) | copy-start | bytes 2308
  10.8 19.5 %copy-start.18 = (bf16[1536]{0:T(1024)(128)(2,1)S(1)}, bf16[1536]{0:T(1024)(128)(2,1)}, u32[]{:S(2)}) copy-start(bf16[1536]{0:T(1024)(128)(2,1)} %param.25) | copy-start | bytes 9220
  10.8 22.1 %copy-start.1 = (bf16[512,1536]{1,0:T(8,128)(2,1)S(1)}, bf16[512,1536]{1,0:T(8,128)(2,1)}, u32[]{:S(2)}) copy-start(bf16[512,1536]{1,0:T(8,128)(2,1)} %hidden_ref.1) | copy-start | bytes 4718596
  11.7 9.8 %collective-permute-start.5 = (bf16[192,640]{1,0:T(8,128)(2,1)S(1)}, bf16[192,640]{1,0:T(8,128)(2,1)S(1)}, u32[]{:S(2)}, u32[]{:S(2)}) collective-permute-start(bf16[192,640]{1,0:T(8,128)(2,1)S(1)} %pad_maximum_fusion.3.rest_0_), channel_id=1, source_target_pairs={{0,24},{4,28},{8,16},{12,20},{16,8},{20,12},{24,0},{28,4},{1,25},{... | collective-permute-start | bytes 737288 | tf_op jit(solution)/shard_map/ppermute | solution.py:52
  13.2 15.1 %collective-permute-start.3 = (bf16[192,640]{1,0:T(8,128)(2,1)S(1)}, bf16[192,640]{1,0:T(8,128)(2,1)S(1)}, u32[]{:S(2)}, u32[]{:S(2)}) collective-permute-start(bf16[192,640]{1,0:T(8,128)(2,1)S(1)} %pad_maximum_fusion.3.rest_0_), channel_id=1, source_target_pairs={{0,16},{4,20},{8,24},{12,28},{16,0},{20,4},{24,8},{28,12},{1,17},{... | collective-permute-start | bytes 737288 | tf_op jit(solution)/shard_map/ppermute | solution.py:52
  14.7 13.6 %collective-permute-start.1 = (bf16[192,640]{1,0:T(8,128)(2,1)S(1)}, bf16[192,640]{1,0:T(8,128)(2,1)S(1)}, u32[]{:S(2)}, u32[]{:S(2)}) collective-permute-start(bf16[192,640]{1,0:T(8,128)(2,1)S(1)} %pad_maximum_fusion.3.rest_0_), channel_id=1, source_target_pairs={{0,8},{4,12},{8,0},{12,4},{16,24},{20,28},{24,16},{28,20},{1,9},{5... | collective-permute-start | bytes 737288 | tf_op jit(solution)/shard_map/ppermute | solution.py:52
  15.3 14.2 %collective-permute-start = (bf16[192,640]{1,0:T(8,128)(2,1)S(1)}, bf16[192,640]{1,0:T(8,128)(2,1)S(1)}, u32[]{:S(2)}, u32[]{:S(2)}) collective-permute-start(bf16[192,640]{1,0:T(8,128)(2,1)S(1)} %pad_maximum_fusion.3.rest_0_), channel_id=1, source_target_pairs={{0,4},{4,0},{8,12},{12,8},{16,20},{20,16},{24,28},{28,24},{1,5},{5... | collective-permute-start | bytes 737288 | tf_op jit(solution)/shard_map/ppermute | solution.py:52
  15.3 23.5 %collective-permute-start.19 = (bf16[192,384]{1,0:T(8,128)(2,1)S(1)}, bf16[192,384]{1,0:T(8,128)(2,1)}, u32[]{:S(2)}, u32[]{:S(2)}) collective-permute-start(bf16[192,384]{1,0:T(8,128)(2,1)S(1)} %bitcast.19), channel_id=1, source_target_pairs={{0,24},{4,28},{8,16},{12,20},{16,8},{20,12},{24,0},{28,4},{1,25},{... | collective-permute-start | bytes 442376 | tf_op jit(solution)/shard_map/ppermute | solution.py:52
  17.8 15.1 %copy-start.23 = (s32[5]{0:T(128)}, s32[5]{0:T(128)S(1)}, u32[]{:S(2)}) copy-start(s32[5]{0:T(128)S(1)} %iota_add_fusion) | copy-start | bytes 64
  21.5 8.8 %collective-permute-start.6 = (bf16[192,640]{1,0:T(8,128)(2,1)S(1)}, bf16[192,640]{1,0:T(8,128)(2,1)S(1)}, u32[]{:S(2)}, u32[]{:S(2)}) collective-permute-start(bf16[192,640]{1,0:T(8,128)(2,1)S(1)} %collective-permute-done.5.rest_6_), channel_id=1, source_target_pairs={{0,4},{4,0},{8,12},{12,8},{16,20},{20,16},{24,28},{28,24},{1,5},{5... | collective-permute-start | bytes 737288 | tf_op jit(solution)/shard_map/ppermute | solution.py:52
  28.3 4.6 %collective-permute-start.4 = (bf16[192,640]{1,0:T(8,128)(2,1)S(1)}, bf16[192,640]{1,0:T(8,128)(2,1)S(1)}, u32[]{:S(2)}, u32[]{:S(2)}) collective-permute-start(bf16[192,640]{1,0:T(8,128)(2,1)S(1)} %collective-permute-done.3.rest_4_), channel_id=1, source_target_pairs={{0,4},{4,0},{8,12},{12,8},{16,20},{20,16},{24,28},{28,24},{1,5},{5... | collective-permute-start | bytes 737288 | tf_op jit(solution)/shard_map/ppermute | solution.py:52
  28.3 4.6 %collective-permute-start.2 = (bf16[192,640]{1,0:T(8,128)(2,1)S(1)}, bf16[192,640]{1,0:T(8,128)(2,1)S(1)}, u32[]{:S(2)}, u32[]{:S(2)}) collective-permute-start(bf16[192,640]{1,0:T(8,128)(2,1)S(1)} %collective-permute-done.1.rest_2_), channel_id=1, source_target_pairs={{0,4},{4,0},{8,12},{12,8},{16,20},{20,16},{24,28},{28,24},{1,5},{5... | collective-permute-start | bytes 737288 | tf_op jit(solution)/shard_map/ppermute | solution.py:52
  29.2 12.8 %copy-start.27 = (s32[8]{0:T(128)S(1)}, s32[8]{0:T(128)}, u32[]{:S(2)}) copy-start(s32[8]{0:T(128)} %param.22) | copy-start | bytes 100
  29.5 10.8 %collective-permute-start.17 = (bf16[192,384]{1,0:T(8,128)(2,1)S(1)}, bf16[192,384]{1,0:T(8,128)(2,1)}, u32[]{:S(2)}, u32[]{:S(2)}) collective-permute-start(bf16[192,384]{1,0:T(8,128)(2,1)S(1)} %bitcast.20), channel_id=1, source_target_pairs={{0,16},{4,20},{8,24},{12,28},{16,0},{20,4},{24,8},{28,12},{1,17},{... | collective-permute-start | bytes 442376 | tf_op jit(solution)/shard_map/ppermute | solution.py:52
  30.3 11.9 %collective-permute-start.15 = (bf16[192,384]{1,0:T(8,128)(2,1)S(1)}, bf16[192,384]{1,0:T(8,128)(2,1)}, u32[]{:S(2)}, u32[]{:S(2)}) collective-permute-start(bf16[192,384]{1,0:T(8,128)(2,1)S(1)} %bitcast.21), channel_id=1, source_target_pairs={{0,8},{4,12},{8,0},{12,4},{16,24},{20,28},{24,16},{28,20},{1,9},{5... | collective-permute-start | bytes 442376 | tf_op jit(solution)/shard_map/ppermute | solution.py:52
  32.9 9.4 %collective-permute-start.14 = (bf16[192,384]{1,0:T(8,128)(2,1)S(1)}, bf16[192,384]{1,0:T(8,128)(2,1)S(1)}, u32[]{:S(2)}, u32[]{:S(2)}) collective-permute-start(bf16[192,384]{1,0:T(8,128)(2,1)S(1)} %bitcast.22), channel_id=1, source_target_pairs={{0,4},{4,0},{8,12},{12,8},{16,20},{20,16},{24,28},{28,24},{1,5},{5... | collective-permute-start | bytes 442376 | tf_op jit(solution)/shard_map/ppermute | solution.py:52
  38.5 15.9 %collective-permute-start.12 = (bf16[512,256]{1,0:T(8,128)(2,1)}, bf16[512,256]{1,0:T(8,128)(2,1)S(1)}, u32[]{:S(2)}, u32[]{:S(2)}) collective-permute-start(bf16[512,256]{1,0:T(8,128)(2,1)} %get-tuple-element.21.rest_0_), channel_id=1, source_target_pairs={{0,24},{4,28},{8,16},{12,20},{16,8},{20,12},{24,0},{28,4},{1,25},{... | collective-permute-start | bytes 786440 | tf_op jit(solution)/shard_map/ppermute | solution.py:52
  38.8 20.4 %collective-permute-start.10 = (bf16[512,256]{1,0:T(8,128)(2,1)}, bf16[512,256]{1,0:T(8,128)(2,1)S(1)}, u32[]{:S(2)}, u32[]{:S(2)}) collective-permute-start(bf16[512,256]{1,0:T(8,128)(2,1)} %get-tuple-element.21.rest_0_), channel_id=1, source_target_pairs={{0,16},{4,20},{8,24},{12,28},{16,0},{20,4},{24,8},{28,12},{1,17},{... | collective-permute-start | bytes 786440 | tf_op jit(solution)/shard_map/ppermute | solution.py:52
  40.3 24.0 %collective-permute-start.8 = (bf16[512,256]{1,0:T(8,128)(2,1)}, bf16[512,256]{1,0:T(8,128)(2,1)}, u32[]{:S(2)}, u32[]{:S(2)}) collective-permute-start(bf16[512,256]{1,0:T(8,128)(2,1)} %get-tuple-element.21.rest_0_), channel_id=1, source_target_pairs={{0,8},{4,12},{8,0},{12,4},{16,24},{20,28},{24,16},{28,20},{1,9},{5... | collective-permute-start | bytes 786440 | tf_op jit(solution)/shard_map/ppermute | solution.py:52
  42.2 1.8 collective-permute-start.20
  43.0 22.1 %collective-permute-start.18 = (bf16[192,384]{1,0:T(8,128)(2,1)}, bf16[192,384]{1,0:T(8,128)(2,1)S(1)}, u32[]{:S(2)}, u32[]{:S(2)}) collective-permute-start(bf16[192,384]{1,0:T(8,128)(2,1)} %collective-permute-done.17.rest_12_), channel_id=1, source_target_pairs={{0,4},{4,0},{8,12},{12,8},{16,20},{20,16},{24,28},{28,24},{1,5},{5... | collective-permute-start | bytes 442376 | tf_op jit(solution)/shard_map/ppermute | solution.py:52
  44.0 23.1 %copy-start.10 = (bf16[192,384]{1,0:T(8,128)(2,1)}, bf16[192,384]{1,0:T(8,128)(2,1)S(1)}, u32[]{:S(2)}) copy-start(bf16[192,384]{1,0:T(8,128)(2,1)S(1)} %collective-permute-done.20.rest_15_) | copy-start | bytes 442372
  44.0 27.0 %collective-permute-start.7 = (bf16[512,256]{1,0:T(8,128)(2,1)}, bf16[512,256]{1,0:T(8,128)(2,1)}, u32[]{:S(2)}, u32[]{:S(2)}) collective-permute-start(bf16[512,256]{1,0:T(8,128)(2,1)} %get-tuple-element.21.rest_0_), channel_id=1, source_target_pairs={{0,4},{4,0},{8,12},{12,8},{16,20},{20,16},{24,28},{28,24},{1,5},{5... | collective-permute-start | bytes 786440 | tf_op jit(solution)/shard_map/ppermute | solution.py:52
  54.4 17.3 %collective-permute-start.13 = (bf16[512,256]{1,0:T(8,128)(2,1)S(1)}, bf16[512,256]{1,0:T(8,128)(2,1)}, u32[]{:S(2)}, u32[]{:S(2)}) collective-permute-start(bf16[512,256]{1,0:T(8,128)(2,1)S(1)} %collective-permute-done.12.rest_6_), channel_id=1, source_target_pairs={{0,4},{4,0},{8,12},{12,8},{16,20},{20,16},{24,28},{28,24},{1,5},{5... | collective-permute-start | bytes 786440 | tf_op jit(solution)/shard_map/ppermute | solution.py:52
  59.1 12.6 %copy-start.5 = (bf16[512,256]{1,0:T(8,128)(2,1)}, bf16[512,256]{1,0:T(8,128)(2,1)S(1)}, u32[]{:S(2)}) copy-start(bf16[512,256]{1,0:T(8,128)(2,1)S(1)} %collective-permute-done.10.rest_4_) | copy-start | bytes 786436
  59.1 12.6 %collective-permute-start.11 = (bf16[512,256]{1,0:T(8,128)(2,1)S(1)}, bf16[512,256]{1,0:T(8,128)(2,1)}, u32[]{:S(2)}, u32[]{:S(2)}) collective-permute-start(bf16[512,256]{1,0:T(8,128)(2,1)S(1)} %collective-permute-done.10.rest_4_), channel_id=1, source_target_pairs={{0,4},{4,0},{8,12},{12,8},{16,20},{20,16},{24,28},{28,24},{1,5},{5... | collective-permute-start | bytes 786440 | tf_op jit(solution)/shard_map/ppermute | solution.py:52
  64.3 7.4 %collective-permute-start.9 = (bf16[512,256]{1,0:T(8,128)(2,1)}, bf16[512,256]{1,0:T(8,128)(2,1)}, u32[]{:S(2)}, u32[]{:S(2)}) collective-permute-start(bf16[512,256]{1,0:T(8,128)(2,1)} %collective-permute-done.8.rest_2_), channel_id=1, source_target_pairs={{0,4},{4,0},{8,12},{12,8},{16,20},{20,16},{24,28},{28,24},{1,5},{5... | collective-permute-start | bytes 786440 | tf_op jit(solution)/shard_map/ppermute | solution.py:52
  65.8 3.6 %collective-permute-start.16 = (bf16[192,384]{1,0:T(8,128)(2,1)}, bf16[192,384]{1,0:T(8,128)(2,1)}, u32[]{:S(2)}, u32[]{:S(2)}) collective-permute-start(bf16[192,384]{1,0:T(8,128)(2,1)} %collective-permute-done.15.rest_10_), channel_id=1, source_target_pairs={{0,4},{4,0},{8,12},{12,8},{16,20},{20,16},{24,28},{28,24},{1,5},{5... | collective-permute-start | bytes 442376 | tf_op jit(solution)/shard_map/ppermute | solution.py:52
  69.4 116.8 %collective-permute-start.38 = (bf16[192,512]{1,0:T(8,128)(2,1)S(1)}, bf16[192,512]{1,0:T(8,128)(2,1)}, u32[]{:S(2)}, u32[]{:S(2)}) collective-permute-start(bf16[192,512]{1,0:T(8,128)(2,1)S(1)} %pad_maximum_fusion.4.rest_4_), channel_id=1, source_target_pairs={{0,24},{4,28},{8,16},{12,20},{16,8},{20,12},{24,0},{28,4},{1,25},{... | collective-permute-start | bytes 589832 | tf_op jit(solution)/shard_map/ppermute | solution.py:52
  71.0 143.6 %collective-permute-start.36 = (bf16[192,512]{1,0:T(8,128)(2,1)S(1)}, bf16[192,512]{1,0:T(8,128)(2,1)}, u32[]{:S(2)}, u32[]{:S(2)}) collective-permute-start(bf16[192,512]{1,0:T(8,128)(2,1)S(1)} %pad_maximum_fusion.4.rest_4_), channel_id=1, source_target_pairs={{0,16},{4,20},{8,24},{12,28},{16,0},{20,4},{24,8},{28,12},{1,17},{... | collective-permute-start | bytes 589832 | tf_op jit(solution)/shard_map/ppermute | solution.py:52
  75.4 15.0 %copy-start.32 = (bf16[512]{0:T(512)(128)(2,1)S(1)}, bf16[512]{0:T(512)(128)(2,1)}, u32[]{:S(2)}) copy-start(bf16[512]{0:T(512)(128)(2,1)} %param.39) | copy-start | bytes 3076
  75.4 15.6 %copy-start.26 = (bf16[384]{0:T(512)(128)(2,1)S(1)}, bf16[384]{0:T(512)(128)(2,1)}, u32[]{:S(2)}) copy-start(bf16[384]{0:T(512)(128)(2,1)} %param.37) | copy-start | bytes 2308
  75.4 16.1 %copy-start.19 = (bf16[1536]{0:T(1024)(128)(2,1)S(1)}, bf16[1536]{0:T(1024)(128)(2,1)}, u32[]{:S(2)}) copy-start(bf16[1536]{0:T(1024)(128)(2,1)} %param.31) | copy-start | bytes 9220
  86.0 18.6 %collective-permute-start.21 = (bf16[128,1536]{1,0:T(8,128)(2,1)}, bf16[128,1536]{1,0:T(8,128)(2,1)S(1)}, u32[]{:S(2)}, u32[]{:S(2)}) collective-permute-start(bf16[128,1536]{1,0:T(8,128)(2,1)} %get-tuple-element.23), channel_id=1, source_target_pairs={{0,1},{1,0},{2,3},{3,2},{4,5},{5,4},{6,7},{7,6},{8,9},{9,8},{10,11... | collective-permute-start | bytes 1179656 | tf_op jit(solution)/shard_map/ppermute | solution.py:52
  87.3 17.3 %collective-permute-start.22 = (bf16[128,1536]{1,0:T(8,128)(2,1)}, bf16[128,1536]{1,0:T(8,128)(2,1)S(1)}, u32[]{:S(2)}, u32[]{:S(2)}) collective-permute-start(bf16[128,1536]{1,0:T(8,128)(2,1)} %get-tuple-element.24), channel_id=1, source_target_pairs={{0,2},{1,3},{2,0},{3,1},{4,6},{5,7},{6,4},{7,5},{8,10},{9,11},{10,... | collective-permute-start | bytes 1179656 | tf_op jit(solution)/shard_map/ppermute | solution.py:52
  90.2 25.6 %collective-permute-start.23 = (bf16[128,1536]{1,0:T(8,128)(2,1)}, bf16[128,1536]{1,0:T(8,128)(2,1)S(1)}, u32[]{:S(2)}, u32[]{:S(2)}) collective-permute-start(bf16[128,1536]{1,0:T(8,128)(2,1)} %get-tuple-element.25), channel_id=1, source_target_pairs={{0,3},{1,2},{2,1},{3,0},{4,7},{5,6},{6,5},{7,4},{8,11},{9,10},{10,... | collective-permute-start | bytes 1179656 | tf_op jit(solution)/shard_map/ppermute | solution.py:52
  116.2 20.5 %collective-permute-start.26 = (bf16[128,1536]{1,0:T(8,128)(2,1)S(1)}, bf16[128,1536]{1,0:T(8,128)(2,1)S(1)}, u32[]{:S(2)}, u32[]{:S(2)}) collective-permute-start(bf16[128,1536]{1,0:T(8,128)(2,1)S(1)} %get-tuple-element.27.rest_0_), channel_id=1, source_target_pairs={{0,3},{1,2},{2,1},{3,0},{4,7},{5,6},{6,5},{7,4},{8,11},{9,10},{10,... | collective-permute-start | bytes 1179656 | tf_op jit(solution)/shard_map/ppermute | solution.py:52
  119.4 42.6 %collective-permute-start.25 = (bf16[128,1536]{1,0:T(8,128)(2,1)S(1)}, bf16[128,1536]{1,0:T(8,128)(2,1)S(1)}, u32[]{:S(2)}, u32[]{:S(2)}) collective-permute-start(bf16[128,1536]{1,0:T(8,128)(2,1)S(1)} %get-tuple-element.27.rest_0_), channel_id=1, source_target_pairs={{0,2},{1,3},{2,0},{3,1},{4,6},{5,7},{6,4},{7,5},{8,10},{9,11},{10,... | collective-permute-start | bytes 1179656 | tf_op jit(solution)/shard_map/ppermute | solution.py:52
  135.5 26.5 %collective-permute-start.24 = (bf16[128,1536]{1,0:T(8,128)(2,1)S(1)}, bf16[128,1536]{1,0:T(8,128)(2,1)S(1)}, u32[]{:S(2)}, u32[]{:S(2)}) collective-permute-start(bf16[128,1536]{1,0:T(8,128)(2,1)S(1)} %get-tuple-element.27.rest_0_), channel_id=1, source_target_pairs={{0,1},{1,0},{2,3},{3,2},{4,5},{5,4},{6,7},{7,6},{8,9},{9,8},{10,11... | collective-permute-start | bytes 1179656 | tf_op jit(solution)/shard_map/ppermute | solution.py:52
  136.7 25.4 %copy-start.28 = (bf16[128,1536]{1,0:T(8,128)(2,1)}, bf16[128,1536]{1,0:T(8,128)(2,1)S(1)}, u32[]{:S(2)}) copy-start(bf16[128,1536]{1,0:T(8,128)(2,1)S(1)} %collective-permute-done.26.rest_3_) | copy-start | bytes 1179652
  162.9 23.1 %copy-start.16 = (s32[8,16]{1,0:T(8,128)S(1)}, s32[8,16]{1,0:T(8,128)}, u32[]{:S(2)}) copy-start(s32[8,16]{1,0:T(8,128)} %param.24) | copy-start | bytes 1540
  162.9 23.1 %copy-start.24 = (s32[5]{0:T(128)S(1)}, s32[5]{0:T(128)}, u32[]{:S(2)}) copy-start(s32[5]{0:T(128)} %copy-done.23) | copy-start | bytes 64
  162.9 30.4 %copy-start.17 = (s32[5]{0:T(128)S(1)}, s32[5]{0:T(128)}, u32[]{:S(2)}) copy-start(s32[5]{0:T(128)} %get-tuple-element.46) | copy-start | bytes 64
  162.9 30.4 %copy-start.21 = (s32[5]{0:T(128)S(1)}, s32[5]{0:T(128)}, u32[]{:S(2)}) copy-start(s32[5]{0:T(128)} %get-tuple-element.45) | copy-start | bytes 64
  181.4 48.9 %copy-start.3 = (bf16[4096,256]{1,0:T(8,128)(2,1)S(1)}, bf16[4096,256]{1,0:T(8,128)(2,1)}, u32[]{:S(2)}) copy-start(bf16[4096,256]{1,0:T(8,128)(2,1)} %copy-done.2) | copy-start | bytes 6291460
  181.4 19.1 %collective-permute-start.27 = (bf16[128,1536]{1,0:T(8,128)(2,1)S(1)}, bf16[128,1536]{1,0:T(8,128)(2,1)S(1)}, u32[]{:S(2)}, u32[]{:S(2)}) collective-permute-start(bf16[128,1536]{1,0:T(8,128)(2,1)S(1)} %get-tuple-element.29), channel_id=1, source_target_pairs={{0,1},{1,0},{2,3},{3,2},{4,5},{5,4},{6,7},{7,6},{8,9},{9,8},{10,11... | collective-permute-start | bytes 1179656 | tf_op jit(solution)/shard_map/ppermute | solution.py:52
  181.6 30.2 %collective-permute-start.28 = (bf16[128,1536]{1,0:T(8,128)(2,1)S(1)}, bf16[128,1536]{1,0:T(8,128)(2,1)S(1)}, u32[]{:S(2)}, u32[]{:S(2)}) collective-permute-start(bf16[128,1536]{1,0:T(8,128)(2,1)S(1)} %get-tuple-element.30), channel_id=1, source_target_pairs={{0,2},{1,3},{2,0},{3,1},{4,6},{5,7},{6,4},{7,5},{8,10},{9,11},{10,... | collective-permute-start | bytes 1179656 | tf_op jit(solution)/shard_map/ppermute | solution.py:52
  184.9 26.8 %collective-permute-start.29 = (bf16[128,1536]{1,0:T(8,128)(2,1)S(1)}, bf16[128,1536]{1,0:T(8,128)(2,1)S(1)}, u32[]{:S(2)}, u32[]{:S(2)}) collective-permute-start(bf16[128,1536]{1,0:T(8,128)(2,1)S(1)} %get-tuple-element.31), channel_id=1, source_target_pairs={{0,3},{1,2},{2,1},{3,0},{4,7},{5,6},{6,5},{7,4},{8,11},{9,10},{10,... | collective-permute-start | bytes 1179656 | tf_op jit(solution)/shard_map/ppermute | solution.py:52
  186.2 43.9 %collective-permute-start.34 = (bf16[192,512]{1,0:T(8,128)(2,1)S(1)}, bf16[192,512]{1,0:T(8,128)(2,1)S(1)}, u32[]{:S(2)}, u32[]{:S(2)}) collective-permute-start(bf16[192,512]{1,0:T(8,128)(2,1)S(1)} %pad_maximum_fusion.4.rest_4_), channel_id=1, source_target_pairs={{0,8},{4,12},{8,0},{12,4},{16,24},{20,28},{24,16},{28,20},{1,9},{5... | collective-permute-start | bytes 589832 | tf_op jit(solution)/shard_map/ppermute | solution.py:52
  200.6 33.9 %collective-permute-start.33 = (bf16[192,512]{1,0:T(8,128)(2,1)S(1)}, bf16[192,512]{1,0:T(8,128)(2,1)S(1)}, u32[]{:S(2)}, u32[]{:S(2)}) collective-permute-start(bf16[192,512]{1,0:T(8,128)(2,1)S(1)} %pad_maximum_fusion.4.rest_4_), channel_id=1, source_target_pairs={{0,4},{4,0},{8,12},{12,8},{16,20},{20,16},{24,28},{28,24},{1,5},{5... | collective-permute-start | bytes 589832 | tf_op jit(solution)/shard_map/ppermute | solution.py:52
  211.8 22.7 %collective-permute-start.39 = (bf16[192,512]{1,0:T(8,128)(2,1)}, bf16[192,512]{1,0:T(8,128)(2,1)S(1)}, u32[]{:S(2)}, u32[]{:S(2)}) collective-permute-start(bf16[192,512]{1,0:T(8,128)(2,1)} %collective-permute-done.38.rest_10_), channel_id=1, source_target_pairs={{0,4},{4,0},{8,12},{12,8},{16,20},{20,16},{24,28},{28,24},{1,5},{5... | collective-permute-start | bytes 589832 | tf_op jit(solution)/shard_map/ppermute | solution.py:52
  211.8 43.5 %copy-start.4 = (f32[1,512]{1,0:T(1,128)S(1)}, f32[1,512]{1,0:T(1,128)}, u32[]{:S(2)}) copy-start(f32[1,512]{1,0:T(1,128)} %maximum_convert_fusion.1.bias_ref) | copy-start | bytes 6148
  212.1 24.2 %collective-permute-start.32 = (bf16[128,1536]{1,0:T(8,128)(2,1)S(1)}, bf16[128,1536]{1,0:T(8,128)(2,1)S(1)}, u32[]{:S(2)}, u32[]{:S(2)}) collective-permute-start(bf16[128,1536]{1,0:T(8,128)(2,1)S(1)} %join.3.rest_0_), channel_id=1, source_target_pairs={{0,3},{1,2},{2,1},{3,0},{4,7},{5,6},{6,5},{7,4},{8,11},{9,10},{10,... | collective-permute-start | bytes 1179656 | tf_op jit(solution)/shard_map/ppermute | solution.py:52
  214.6 40.7 %collective-permute-start.31 = (bf16[128,1536]{1,0:T(8,128)(2,1)S(1)}, bf16[128,1536]{1,0:T(8,128)(2,1)S(1)}, u32[]{:S(2)}, u32[]{:S(2)}) collective-permute-start(bf16[128,1536]{1,0:T(8,128)(2,1)S(1)} %join.3.rest_0_), channel_id=1, source_target_pairs={{0,2},{1,3},{2,0},{3,1},{4,6},{5,7},{6,4},{7,5},{8,10},{9,11},{10,... | collective-permute-start | bytes 1179656 | tf_op jit(solution)/shard_map/ppermute | solution.py:52
  230.2 25.1 %collective-permute-start.30 = (bf16[128,1536]{1,0:T(8,128)(2,1)S(1)}, bf16[128,1536]{1,0:T(8,128)(2,1)S(1)}, u32[]{:S(2)}, u32[]{:S(2)}) collective-permute-start(bf16[128,1536]{1,0:T(8,128)(2,1)S(1)} %join.3.rest_0_), channel_id=1, source_target_pairs={{0,1},{1,0},{2,3},{3,2},{4,5},{5,4},{6,7},{7,6},{8,9},{9,8},{10,11... | collective-permute-start | bytes 1179656 | tf_op jit(solution)/shard_map/ppermute | solution.py:52
  234.4 1.7 collective-permute-start.37
  234.5 1.7 collective-permute-start.35
  (10 other events, 8.9 us)
Sparse Core Ops, SparseCore 0:
  11.0 130.1 all-gather.2

commit v2 on v1

--- a/solution.py
+++ b/solution.py
@@ -18,7 +18,6 @@
 f32 = jnp.float32
 bf16 = jnp.bfloat16
 VMEM = pltpu.VMEM
-ANY = pl.ANY
 SMEM = pltpu.SMEM
 
 
@@ -27,7 +26,7 @@
 
 
 def any_spec():
-    return pl.BlockSpec(memory_space=ANY)
+    return pl.BlockSpec(memory_space=pltpu.HBM)
 
 
 def smem_spec():
@@ -103,11 +102,11 @@
             kv_ref[:, (h - heads + 2) * HD : (h - heads + 3) * HD] = value
 
 
-def attend_kernel(wide, narrow, key_block, scalar_ref, starts_ref, q_ref, *rest):
+def attend_kernel(wide, narrow, key_block, wide_ref, narrow_ref, spots_ref, starts_ref, q_ref, *rest):
     kv_pieces, out_pieces = rest[:wide], rest[wide : 2 * wide]
     rest = rest[2 * wide :]
     part_refs, (kv_out, keyvals, w_out, mix, kv_sems, out_sems, flush_sem) = rest[:narrow], rest[narrow:]
-    wide_index, narrow_index = scalar_ref[0], scalar_ref[1]
+    wide_index, narrow_index = wide_ref[0], narrow_ref[0]
     kv_copies = place_copies(kv_pieces, keyvals, kv_sems, wide_index)
     out_copies = place_copies(out_pieces, w_out, out_sems, wide_index)
     for c in kv_copies:
@@ -130,8 +129,8 @@
         )
         first = row_base + t * tile
         diagonal = first // tile
-        lowest = scalar_ref[2 + 2 * t] // tile
-        whole_from = (scalar_ref[3 + 2 * t] + tile - 1) // tile
+        lowest = spots_ref[t * tile] // tile
+        whole_from = (spots_ref[(t + 1) * tile - 1] + tile - 1) // tile
         starts = jnp.concatenate([starts_ref[rows, :]] * heads, axis=0)
         own = first + lax.broadcasted_iota(jnp.int32, (tile, 1), 0)
         own = jnp.concatenate([own] * heads, axis=0)
@@ -178,14 +177,16 @@
 
 
 def join_kernel(narrow, base_ref, gain_ref, *rest):
-    parts, (sum_ref, norm_ref) = rest[:narrow], rest[narrow:]
+    parts, outs = rest[:narrow], rest[narrow:]
     total = parts[0][...].astype(f32)
     for part in parts[1:]:
         total = total + part[...].astype(f32)
     rounded = (base_ref[...].astype(f32) + total).astype(bf16)
-    sum_ref[...] = rounded
-    if norm_ref is not None:
-        norm_ref[...] = norm_rows(rounded.astype(f32), gain_ref[...])
+    if len(outs) > narrow:
+        outs[narrow][...] = rounded
+        rounded = norm_rows(rounded.astype(f32), gain_ref[...])
+    for out in outs[:narrow]:
+        out[...] = rounded
 
 
 def ffn_kernel(narrow, *rest):
@@ -238,10 +239,10 @@
             part_refs[k][:, lanes] = product[k * share : (k + 1) * share].astype(bf16)
 
 
-def next_kernel(wide, narrow, scalar_ref, gain_ref, bias_ref, *rest):
+def next_kernel(wide, narrow, wide_ref, narrow_ref, gain_ref, bias_ref, *rest):
     h_refs, pieces = rest[:narrow], rest[narrow : narrow + wide]
     out_ref, query_ref, keyval_ref, weight, sems = rest[narrow + wide :]
-    wide_index, narrow_index = scalar_ref[0], scalar_ref[1]
+    wide_index, narrow_index = wide_ref[0], narrow_ref[0]
     copies = place_copies(pieces, weight, sems, wide_index)
     for c in copies:
         c.start()
@@ -365,16 +366,12 @@
     out_pieces = wide_pieces(w_out.T, wide)
 
     tile = 256
-    ends = []
-    for t in range(tok_rows // tile):
-        ends += [token_start[t * tile], token_start[(t + 1) * tile - 1]]
-    scalars = jnp.stack([wide_index, narrow_index] + ends)
     total_rows = wide * tok_rows
     *parts, kv_all = pl.pallas_call(
         functools.partial(attend_kernel, wide, narrow, tile),
         out_shape=[jax.ShapeDtypeStruct((share, depth), bf16)] * narrow
         + [jax.ShapeDtypeStruct((total_rows, 2 * HD), bf16)],
-        in_specs=[smem_spec(), vmem_spec(), vmem_spec()] + [any_spec()] * (2 * wide),
+        in_specs=[smem_spec()] * 3 + [vmem_spec()] * 2 + [any_spec()] * (2 * wide),
         out_specs=[vmem_spec()] * narrow + [any_spec()],
         scratch_shapes=[
             VMEM((total_rows, 2 * HD), bf16),
@@ -391,28 +388,32 @@
             transcendentals=tok_rows * depth,
         ),
         name="attend",
-    )(scalars, token_start[:, None], queries, *kv_pieces, *out_pieces)
+    )(
+        wide_index[None],
+        narrow_index[None],
+        token_start,
+        token_start[:, None],
+        queries,
+        *kv_pieces,
+        *out_pieces,
+    )
 
     def join(parts, base_rows, gain, with_norm):
         shape = jax.ShapeDtypeStruct((share, depth), bf16)
-        kernel = functools.partial(join_kernel, narrow)
-        if not with_norm:
-            body = kernel
-            kernel = lambda *refs: body(*refs, None)
+        count = narrow + 1 if with_norm else narrow
         return pl.pallas_call(
-            kernel,
-            out_shape=[shape, shape] if with_norm else [shape],
+            functools.partial(join_kernel, narrow),
+            out_shape=[shape] * count,
             in_specs=[vmem_spec()] * (2 + narrow),
-            out_specs=[vmem_spec()] * (2 if with_norm else 1),
+            out_specs=[vmem_spec()] * count,
             compiler_params=params(24),
             name="join",
         )(base_rows, gain, *parts)
 
     base_rows = lax.dynamic_slice_in_dim(hidden_in, narrow_index * share, share, 0)
-    residual, normed = join(
-        narrow_swap(parts, narrow), base_rows, mlp_gain.astype(f32)[None], True
-    )
-    normed_pieces = [normed] + [exchange(normed, "narrow", narrow, k) for k in range(1, narrow)]
+    mlp_row = mlp_gain.astype(f32)[None]
+    *normed, residual = join(narrow_swap(parts, narrow), base_rows, mlp_row, True)
+    normed_pieces = narrow_swap(normed, narrow)
 
     parts = pl.pallas_call(
         functools.partial(ffn_kernel, narrow),
@@ -435,12 +436,8 @@
         name="ffn",
     )(*normed_pieces, ffn_weights)
 
-    (hidden_rows,) = join(
-        narrow_swap(parts, narrow), residual, mlp_gain.astype(f32)[None], False
-    )
-    hidden_pieces = [hidden_rows] + [
-        exchange(hidden_rows, "narrow", narrow, k) for k in range(1, narrow)
-    ]
+    hidden_rows = join(narrow_swap(parts, narrow), residual, mlp_row, False)
+    hidden_pieces = narrow_swap(hidden_rows, narrow)
 
     one_offset = pair_offset + kind_index * HD
     next_weight = jnp.concatenate(
@@ -449,6 +446,7 @@
     next_bias = jnp.concatenate(
         [b_query2, lax.dynamic_slice_in_dim(b_keyval2, one_offset, HD, 0)]
     ).astype(f32)[None]
+    next_weight, _ = lax.optimization_barrier((next_weight, residual))
     next_pieces = wide_pieces(next_weight, wide)
     next_width = query_width + HD
     hidden_out, next_query, next_keyval = pl.pallas_call(
@@ -458,7 +456,7 @@
             jax.ShapeDtypeStruct((tok_rows, query_width), bf16),
             jax.ShapeDtypeStruct((tok_rows, HD), bf16),
         ),
-        in_specs=[smem_spec()] + [vmem_spec()] * (2 + narrow) + [any_spec()] * wide,
+        in_specs=[smem_spec()] * 2 + [vmem_spec()] * (2 + narrow) + [any_spec()] * wide,
         out_specs=(vmem_spec(),) * 3,
         scratch_shapes=[VMEM((depth, next_width), bf16), pltpu.SemaphoreType.DMA((wide,))],
         compiler_params=params(32),
@@ -469,7 +467,8 @@
         ),
         name="next",
     )(
-        scalars[:2],
+        wide_index[None],
+        narrow_index[None],
         next_gain.astype(f32)[None],
         next_bias,
         *hidden_pieces,

time: 271 us -> 275 us (1.015)
  the two profiles are of different devices: /device:TPU:4 before, /device:TPU:10 now
where the time goes in v2:
time: 275 us; the launch traced here: 274 us
  waiting for transfers between devices  164 us (60%)
  Pallas kernels  47.3 us (17%)
  starting transfers between devices  25.6 us (9%)
  local copies, waits for them, and re-layouts  15.9 us (6%)
  between operations  14.6 us (5%)
  other arithmetic  7.25 us (3%)
    ppermute x40, waiting for transfers between devices, exchange(): return lax.ppermute(value, axis, [(i, i ^ mask) for i in range(size)])  163 us
    ppermute x40, starting transfers between devices, exchange(): return lax.ppermute(value, axis, [(i, i ^ mask) for i in range(size)])  25.6 us
    pallas_call x1, Pallas kernels, local(): pl.pallas_call(functools.partial(ffn_kernel, narrow), out_shape=[jax.Shap...  19.6 us
    pallas_call x1, Pallas kernels, local(): pl.pallas_call(functools.partial(attend_kernel, wide, narrow, tile), out_...  13 us
    unnamed x72, local copies, waits for them, and re-layouts  10.6 us
    pallas_call x1, Pallas kernels, local(): pl.pallas_call(functools.partial(qkv_kernel, wide), out_shape=(jax.ShapeD...  5.57 us
  transfers between devices with their start and end apart: 41, of which 23 were waited for; matrix products, arithmetic and copies ran while one was open for 3% of the time, Pallas kernels for 15%

profile of v2, /device:TPU:10, one launch (start us, length us, event | category | flops | bytes accessed | tf_op | source)
XLA Modules:
  0.0 274.1 jit_solution(12278190925143813546)
XLA Ops:
  7.2 3.5 %pad_maximum_fusion = bf16[3,192,2240]{2,1,0:T(8,128)(2,1)} fusion(bf16[1,192,2240]{2,1,0:T(8,128)(2,1)} %bitcast.25, bf16[1,192,2240]{2,1,0:T(8,128)(2,1)} %bitcast.26, bf16[1,192,2240]{2,1,0:T(8,128)(2,1)} %bitcast.27), kind=kLoop, calls=%fused_computation.1 | loop fusion | flops 2580480 | bytes 5160960 | tf_op jit(solution)/shard_map/stack | solution.py:318
  10.9 0.8 copy-done.18
  11.7 1.6 collective-permute-start.5
  13.2 0.5 collective-permute-start.3
  13.8 1.5 collective-permute-start.1
  15.2 1.5 collective-permute-start.19
  16.9 4.7 %collective-permute-done.5.rest_6_ = bf16[192,640]{1,0:T(8,128)(2,1)S(1)} collective-permute-done((bf16[192,640]{1,0:T(8,128)(2,1)S(1)}, bf16[192,640]{1,0:T(8,128)(2,1)S(1)}, u32[]{:S(2)}, u32[]{:S(2)}) %collective-permute-start.5) | collective-permute-done | bytes 245792 | tf_op jit(solution)/shard_map/ppermute | solution.py:51
  21.5 5.5 %collective-permute-done.3.rest_4_ = bf16[192,640]{1,0:T(8,128)(2,1)S(1)} collective-permute-done((bf16[192,640]{1,0:T(8,128)(2,1)S(1)}, bf16[192,640]{1,0:T(8,128)(2,1)S(1)}, u32[]{:S(2)}, u32[]{:S(2)}) %collective-permute-start.3) | collective-permute-done | bytes 245792 | tf_op jit(solution)/shard_map/ppermute | solution.py:51
  27.0 2.9 %collective-permute-done.1.rest_2_ = bf16[192,640]{1,0:T(8,128)(2,1)S(1)} collective-permute-done((bf16[192,640]{1,0:T(8,128)(2,1)S(1)}, bf16[192,640]{1,0:T(8,128)(2,1)S(1)}, u32[]{:S(2)}, u32[]{:S(2)}) %collective-permute-start.1) | collective-permute-done | bytes 245792 | tf_op jit(solution)/shard_map/ppermute | solution.py:51
  29.9 1.0 fusion
  31.4 0.7 collective-permute-start.15
  32.1 5.6 %qkv.1 = (bf16[512,384]{1,0:T(8,128)(2,1)S(1)}, bf16[512,256]{1,0:T(8,128)(2,1)}) custom-call(s32[1]{0:T(128)} %bitcast.index_ref.wide_ref, bf16[512,1536]{1,0:T(8,128)(2,1)S(1)} %copy-done.1, f32[1,1536]{1,0:T(1,128)S(1)} %reshape.200.gain_ref, f32[1,640]{1,0:T(1,128)S(1)} %maximum_convert_fusion.bias_ref, f32[512,128]{1,0:T(8,128)S(1)} %get-tuple-element.61.cos_ref, ...), custom_call_target="tpu_custom_call" | custom-call | flops 1006632960 | bytes 3538944 | tf_op jit(solution)/shard_map/qkv/pallas_call | solution.py:339
  37.7 2.8 %collective-permute-start.12 = (bf16[512,256]{1,0:T(8,128)(2,1)}, bf16[512,256]{1,0:T(8,128)(2,1)S(1)}, u32[]{:S(2)}, u32[]{:S(2)}) collective-permute-start(bf16[512,256]{1,0:T(8,128)(2,1)} %get-tuple-element.29.rest_0_), channel_id=1, source_target_pairs={{0,24},{4,28},{8,16},{12,20},{16,8},{20,12},{24,0},{28,4},{1,25},{... | collective-permute-start | bytes 786440 | tf_op jit(solution)/shard_map/ppermute | solution.py:51
  40.6 0.6 collective-permute-start.8
  41.2 0.3 collective-permute-done.15.rest_10_
  41.8 0.9 collective-permute-done.14.rest_9_
  42.6 0.7 copy-done.13
  43.4 0.3 fusion.2
  43.8 0.7 copy-done.15
  44.4 0.4 collective-permute-start.7
  44.8 9.1 %collective-permute-done.12.rest_6_ = bf16[512,256]{1,0:T(8,128)(2,1)S(1)} collective-permute-done((bf16[512,256]{1,0:T(8,128)(2,1)}, bf16[512,256]{1,0:T(8,128)(2,1)S(1)}, u32[]{:S(2)}, u32[]{:S(2)}) %collective-permute-start.12) | collective-permute-done | bytes 262176 | tf_op jit(solution)/shard_map/ppermute | solution.py:51
  53.9 5.9 %collective-permute-done.10.rest_4_ = bf16[512,256]{1,0:T(8,128)(2,1)S(1)} collective-permute-done((bf16[512,256]{1,0:T(8,128)(2,1)}, bf16[512,256]{1,0:T(8,128)(2,1)S(1)}, u32[]{:S(2)}, u32[]{:S(2)}) %collective-permute-start.10) | collective-permute-done | bytes 262176 | tf_op jit(solution)/shard_map/ppermute | solution.py:51
  59.8 4.6 %collective-permute-done.8.rest_2_ = bf16[512,256]{1,0:T(8,128)(2,1)S(1)} collective-permute-done((bf16[512,256]{1,0:T(8,128)(2,1)}, bf16[512,256]{1,0:T(8,128)(2,1)S(1)}, u32[]{:S(2)}, u32[]{:S(2)}) %collective-permute-start.8) | collective-permute-done | bytes 262176 | tf_op jit(solution)/shard_map/ppermute | solution.py:51
  64.8 0.6 collective-permute-start.16
  65.4 0.5 multiply_subtract_fusion
  65.9 0.7 collective-permute-done.16.rest_11_
  66.7 0.9 copy-done.11
  67.6 0.9 copy-done.14
  68.5 0.9 copy-done.16
  69.4 13.0 %attend.1 = (bf16[128,1536]{1,0:T(8,128)(2,1)S(1)}, bf16[128,1536]{1,0:T(8,128)(2,1)}, bf16[128,1536]{1,0:T(8,128)(2,1)}, bf16[128,1536]{1,0:T(8,128)(2,1)}, bf16[4096,256]{1,0:T(8,128)(2,1)S(1)}) custom-call(s32[1]{0:T(128)} %bitcast.index_ref.wide_ref, s32[1]{0:T(128)} %bitcast.1.narrow_ref, s32[512]{0:T(512)S(1)} %select_reduce_fusion.spots_ref, ...), custom_call_target="tpu_custom_call" | custom-call | flops 2415919104 | bytes 2097152 | tf_op jit(solution)/shard_map/attend/pallas_call | solution.py:370
  82.4 1.4 copy-done.2
  83.8 0.6 collective-permute-start.21
  84.4 2.5 collective-permute-start.22
  86.9 0.4 collective-permute-start.23
  87.4 11.9 %collective-permute-done.21.rest_1_ = bf16[128,1536]{1,0:T(8,128)(2,1)S(1)} collective-permute-done((bf16[128,1536]{1,0:T(8,128)(2,1)}, bf16[128,1536]{1,0:T(8,128)(2,1)S(1)}, u32[]{:S(2)}, u32[]{:S(2)}) %collective-permute-start.21) | collective-permute-done | bytes 393248 | tf_op jit(solution)/shard_map/ppermute | solution.py:51
  99.4 4.1 %collective-permute-done.22.rest_2_ = bf16[128,1536]{1,0:T(8,128)(2,1)S(1)} collective-permute-done((bf16[128,1536]{1,0:T(8,128)(2,1)}, bf16[128,1536]{1,0:T(8,128)(2,1)S(1)}, u32[]{:S(2)}, u32[]{:S(2)}) %collective-permute-start.22) | collective-permute-done | bytes 393248 | tf_op jit(solution)/shard_map/ppermute | solution.py:51
  103.4 0.7 copy-done.4
  104.2 16.8 %collective-permute-done.23.rest_3_ = bf16[128,1536]{1,0:T(8,128)(2,1)} collective-permute-done((bf16[128,1536]{1,0:T(8,128)(2,1)}, bf16[128,1536]{1,0:T(8,128)(2,1)}, u32[]{:S(2)}, u32[]{:S(2)}) %collective-permute-start.23) | collective-permute-done | bytes 393248 | tf_op jit(solution)/shard_map/ppermute | solution.py:51
  121.0 1.0 copy-done.5
  122.0 1.4 join.2
  123.5 3.2 %collective-permute-start.25 = (bf16[128,1536]{1,0:T(8,128)(2,1)S(1)}, bf16[128,1536]{1,0:T(8,128)(2,1)S(1)}, u32[]{:S(2)}, u32[]{:S(2)}) collective-permute-start(bf16[128,1536]{1,0:T(8,128)(2,1)S(1)} %get-tuple-element.37), channel_id=1, source_target_pairs={{0,2},{1,3},{2,0},{3,1},{4,6},{5,7},{6,4},{7,5},{8,10},{9,11},{10,... | collective-permute-start | bytes 1179656 | tf_op jit(solution)/shard_map/ppermute | solution.py:51
  127.0 0.8 constant_dynamic-slice_fusion
  128.0 11.4 %collective-permute-done.24.rest_1_ = bf16[128,1536]{1,0:T(8,128)(2,1)S(1)} collective-permute-done((bf16[128,1536]{1,0:T(8,128)(2,1)S(1)}, bf16[128,1536]{1,0:T(8,128)(2,1)S(1)}, u32[]{:S(2)}, u32[]{:S(2)}) %collective-permute-start.24) | collective-permute-done | bytes 393248 | tf_op jit(solution)/shard_map/ppermute | solution.py:51
  139.4 13.0 %collective-permute-done.25.rest_2_ = bf16[128,1536]{1,0:T(8,128)(2,1)S(1)} collective-permute-done((bf16[128,1536]{1,0:T(8,128)(2,1)S(1)}, bf16[128,1536]{1,0:T(8,128)(2,1)S(1)}, u32[]{:S(2)}, u32[]{:S(2)}) %collective-permute-start.25) | collective-permute-done | bytes 393248 | tf_op jit(solution)/shard_map/ppermute | solution.py:51
  152.4 9.0 %collective-permute-done.26.rest_3_ = bf16[128,1536]{1,0:T(8,128)(2,1)S(1)} collective-permute-done((bf16[128,1536]{1,0:T(8,128)(2,1)S(1)}, bf16[128,1536]{1,0:T(8,128)(2,1)S(1)}, u32[]{:S(2)}, u32[]{:S(2)}) %collective-permute-start.26) | collective-permute-done | bytes 393248 | tf_op jit(solution)/shard_map/ppermute | solution.py:51
  161.4 0.8 copy-done.33
  162.2 1.0 copy-done.9
  163.2 19.6 %ffn.1 = (bf16[128,1536]{1,0:T(8,128)(2,1)S(1)}, bf16[128,1536]{1,0:T(8,128)(2,1)}, bf16[128,1536]{1,0:T(8,128)(2,1)}, bf16[128,1536]{1,0:T(8,128)(2,1)}) custom-call(bf16[128,1536]{1,0:T(8,128)(2,1)S(1)} %copy-done.9, bf16[128,1536]{1,0:T(8,128)(2,1)} %copy-done.31, bf16[128,1536]{1,0:T(8,128)(2,1)} %copy-done.32, bf16[128,1536]{1,0:T(8,128)(2,1)} %copy-done.33, ...), custom_call_target="tpu_custom_call" | custom-call | flops 10569646080 | bytes 20643840 | tf_op jit(solution)/shard_map/ffn/pallas_call | solution.py:418
  182.8 3.4 %collective-permute-start.28 = (bf16[128,1536]{1,0:T(8,128)(2,1)}, bf16[128,1536]{1,0:T(8,128)(2,1)}, u32[]{:S(2)}, u32[]{:S(2)}) collective-permute-start(bf16[128,1536]{1,0:T(8,128)(2,1)} %get-tuple-element.41), channel_id=1, source_target_pairs={{0,2},{1,3},{2,0},{3,1},{4,6},{5,7},{6,4},{7,5},{8,10},{9,11},{10,... | collective-permute-start | bytes 1179656 | tf_op jit(solution)/shard_map/ppermute | solution.py:51
  186.9 13.9 %collective-permute-done.27.rest_1_ = bf16[128,1536]{1,0:T(8,128)(2,1)} collective-permute-done((bf16[128,1536]{1,0:T(8,128)(2,1)}, bf16[128,1536]{1,0:T(8,128)(2,1)}, u32[]{:S(2)}, u32[]{:S(2)}) %collective-permute-start.27) | collective-permute-done | bytes 393248 | tf_op jit(solution)/shard_map/ppermute | solution.py:51
  200.9 12.0 %collective-permute-done.28.rest_2_ = bf16[128,1536]{1,0:T(8,128)(2,1)} collective-permute-done((bf16[128,1536]{1,0:T(8,128)(2,1)}, bf16[128,1536]{1,0:T(8,128)(2,1)}, u32[]{:S(2)}, u32[]{:S(2)}) %collective-permute-start.28) | collective-permute-done | bytes 393248 | tf_op jit(solution)/shard_map/ppermute | solution.py:51
  212.9 8.4 %collective-permute-done.29.rest_3_ = bf16[128,1536]{1,0:T(8,128)(2,1)} collective-permute-done((bf16[128,1536]{1,0:T(8,128)(2,1)}, bf16[128,1536]{1,0:T(8,128)(2,1)}, u32[]{:S(2)}, u32[]{:S(2)}) %collective-permute-start.29) | collective-permute-done | bytes 393248 | tf_op jit(solution)/shard_map/ppermute | solution.py:51
  221.3 2.5 join.3
  223.8 0.7 copy-done.6
  224.6 3.2 %collective-permute-start.31 = (bf16[128,1536]{1,0:T(8,128)(2,1)}, bf16[128,1536]{1,0:T(8,128)(2,1)}, u32[]{:S(2)}, u32[]{:S(2)}) collective-permute-start(bf16[128,1536]{1,0:T(8,128)(2,1)} %get-tuple-element.45), channel_id=1, source_target_pairs={{0,2},{1,3},{2,0},{3,1},{4,6},{5,7},{6,4},{7,5},{8,10},{9,11},{10,... | collective-permute-start | bytes 1179656 | tf_op jit(solution)/shard_map/ppermute | solution.py:51
  227.8 0.3 collective-permute-start.32
  228.1 1.0 constant_dynamic-slice_fusion.2
  229.1 3.1 %gather_fusion = bf16[640,128]{1,0:T(8,128)(2,1)S(1)} fusion(bf16[4096,128]{1,0:T(8,128)(2,1)} %constant_dynamic-slice_fusion.2, s32[1024]{0:T(1024)S(1)} %pad_clamp_fusion), kind=kCustom, calls=%fused_computation | custom fusion | bytes 330240 | tf_op jit(solution)/shard_map/jit(_take)/gather | solution.py:276
  232.3 0.5 collective-permute-start.35
  232.8 0.9 select_select_fusion
  234.2 6.6 %collective-permute-done.30.rest_1_ = bf16[128,1536]{1,0:T(8,128)(2,1)S(1)} collective-permute-done((bf16[128,1536]{1,0:T(8,128)(2,1)}, bf16[128,1536]{1,0:T(8,128)(2,1)S(1)}, u32[]{:S(2)}, u32[]{:S(2)}) %collective-permute-start.30) | collective-permute-done | bytes 393248 | tf_op jit(solution)/shard_map/ppermute | solution.py:51
  240.8 13.7 %collective-permute-done.31.rest_2_ = bf16[128,1536]{1,0:T(8,128)(2,1)} collective-permute-done((bf16[128,1536]{1,0:T(8,128)(2,1)}, bf16[128,1536]{1,0:T(8,128)(2,1)}, u32[]{:S(2)}, u32[]{:S(2)}) %collective-permute-start.31) | collective-permute-done | bytes 393248 | tf_op jit(solution)/shard_map/ppermute | solution.py:51
  254.5 7.5 %collective-permute-done.32.rest_3_ = bf16[128,1536]{1,0:T(8,128)(2,1)} collective-permute-done((bf16[128,1536]{1,0:T(8,128)(2,1)}, bf16[128,1536]{1,0:T(8,128)(2,1)}, u32[]{:S(2)}, u32[]{:S(2)}) %collective-permute-start.32) | collective-permute-done | bytes 393248 | tf_op jit(solution)/shard_map/ppermute | solution.py:51
  262.0 5.2 %next.1 = (bf16[512,1536]{1,0:T(8,128)(2,1)}, bf16[512,384]{1,0:T(8,128)(2,1)}, bf16[512,128]{1,0:T(8,128)(2,1)}) custom-call(s32[1]{0:T(128)} %bitcast.index_ref.wide_ref, s32[1]{0:T(128)} %bitcast.1.narrow_ref, f32[1,1536]{1,0:T(1,128)S(1)} %reshape.198.gain_ref, f32[1,512]{1,0:T(1,128)S(1)} %maximum_convert_fusion.1.bias_ref, ...), custom_call_target="tpu_custom_call" | custom-call | flops 805306368 | bytes 4718592 | tf_op jit(solution)/shard_map/next/pallas_call | solution.py:452
  (131 shorter events, 3.6 us)
Async XLA Ops:
  7.2 3.7 %copy-start = (bf16[192,512]{1,0:T(8,128)(2,1)S(1)}, bf16[192,512]{1,0:T(8,128)(2,1)}, u32[]{:S(2)}) copy-start(bf16[192,512]{1,0:T(8,128)(2,1)} %param.28) | copy-start | bytes 589828
  7.2 154.2 %all-gather.3.cloned.1.call-start = ((), (), s32[]{:S(2)}) async-start(), calls=%async_computation | async-start | bytes 23887872 | tf_op jit(solution)/shard_map/all_gather | solution.py:319
  10.8 4.5 %copy-start.12 = (bf16[384,192]{0,1:T(8,128)(2,1)S(1)}, bf16[384,192]{0,1:T(8,128)(2,1)}, u32[]{:S(2)}) copy-start(bf16[384,192]{0,1:T(8,128)(2,1)} %param.30) | copy-start | bytes 442372
  10.8 6.0 %copy-start.23 = (s32[8]{0:T(128)S(1)}, s32[8]{0:T(128)}, u32[]{:S(2)}) copy-start(s32[8]{0:T(128)} %param.23) | copy-start | bytes 100
  10.8 6.0 %copy-start.25 = (s32[512]{0:T(512)S(1)}, s32[512]{0:T(512)}, u32[]{:S(2)}) copy-start(s32[512]{0:T(512)} %param.21) | copy-start | bytes 6148
  10.8 20.2 %copy-start.34 = (bf16[512]{0:T(512)(128)(2,1)S(1)}, bf16[512]{0:T(512)(128)(2,1)}, u32[]{:S(2)}) copy-start(bf16[512]{0:T(512)(128)(2,1)} %param.29) | copy-start | bytes 3076
  10.8 20.2 %copy-start.28 = (bf16[384]{0:T(512)(128)(2,1)S(1)}, bf16[384]{0:T(512)(128)(2,1)}, u32[]{:S(2)}) copy-start(bf16[384]{0:T(512)(128)(2,1)} %param.27) | copy-start | bytes 2308
  10.8 21.3 %copy-start.20 = (bf16[1536]{0:T(1024)(128)(2,1)S(1)}, bf16[1536]{0:T(1024)(128)(2,1)}, u32[]{:S(2)}) copy-start(bf16[1536]{0:T(1024)(128)(2,1)} %param.25) | copy-start | bytes 9220
  10.8 21.3 %copy-start.1 = (bf16[512,1536]{1,0:T(8,128)(2,1)S(1)}, bf16[512,1536]{1,0:T(8,128)(2,1)}, u32[]{:S(2)}) copy-start(bf16[512,1536]{1,0:T(8,128)(2,1)} %hidden_ref.1) | copy-start | bytes 4718596
  11.7 9.8 %collective-permute-start.5 = (bf16[192,640]{1,0:T(8,128)(2,1)S(1)}, bf16[192,640]{1,0:T(8,128)(2,1)S(1)}, u32[]{:S(2)}, u32[]{:S(2)}) collective-permute-start(bf16[192,640]{1,0:T(8,128)(2,1)S(1)} %pad_maximum_fusion.3.rest_0_), channel_id=1, source_target_pairs={{0,24},{4,28},{8,16},{12,20},{16,8},{20,12},{24,0},{28,4},{1,25},{... | collective-permute-start | bytes 737288 | tf_op jit(solution)/shard_map/ppermute | solution.py:51
  13.2 13.8 %collective-permute-start.3 = (bf16[192,640]{1,0:T(8,128)(2,1)S(1)}, bf16[192,640]{1,0:T(8,128)(2,1)S(1)}, u32[]{:S(2)}, u32[]{:S(2)}) collective-permute-start(bf16[192,640]{1,0:T(8,128)(2,1)S(1)} %pad_maximum_fusion.3.rest_0_), channel_id=1, source_target_pairs={{0,16},{4,20},{8,24},{12,28},{16,0},{20,4},{24,8},{28,12},{1,17},{... | collective-permute-start | bytes 737288 | tf_op jit(solution)/shard_map/ppermute | solution.py:51
  13.8 16.2 %collective-permute-start.1 = (bf16[192,640]{1,0:T(8,128)(2,1)S(1)}, bf16[192,640]{1,0:T(8,128)(2,1)S(1)}, u32[]{:S(2)}, u32[]{:S(2)}) collective-permute-start(bf16[192,640]{1,0:T(8,128)(2,1)S(1)} %pad_maximum_fusion.3.rest_0_), channel_id=1, source_target_pairs={{0,8},{4,12},{8,0},{12,4},{16,24},{20,28},{24,16},{28,20},{1,9},{5... | collective-permute-start | bytes 737288 | tf_op jit(solution)/shard_map/ppermute | solution.py:51
  15.2 16.0 %collective-permute-start = (bf16[192,640]{1,0:T(8,128)(2,1)S(1)}, bf16[192,640]{1,0:T(8,128)(2,1)S(1)}, u32[]{:S(2)}, u32[]{:S(2)}) collective-permute-start(bf16[192,640]{1,0:T(8,128)(2,1)S(1)} %pad_maximum_fusion.3.rest_0_), channel_id=1, source_target_pairs={{0,4},{4,0},{8,12},{12,8},{16,20},{20,16},{24,28},{28,24},{1,5},{5... | collective-permute-start | bytes 737288 | tf_op jit(solution)/shard_map/ppermute | solution.py:51
  15.2 25.4 %collective-permute-start.19 = (bf16[192,384]{1,0:T(8,128)(2,1)S(1)}, bf16[192,384]{1,0:T(8,128)(2,1)}, u32[]{:S(2)}, u32[]{:S(2)}) collective-permute-start(bf16[192,384]{1,0:T(8,128)(2,1)S(1)} %bitcast.20), channel_id=1, source_target_pairs={{0,24},{4,28},{8,16},{12,20},{16,8},{20,12},{24,0},{28,4},{1,25},{... | collective-permute-start | bytes 442376 | tf_op jit(solution)/shard_map/ppermute | solution.py:51
  21.5 9.8 %collective-permute-start.6 = (bf16[192,640]{1,0:T(8,128)(2,1)S(1)}, bf16[192,640]{1,0:T(8,128)(2,1)S(1)}, u32[]{:S(2)}, u32[]{:S(2)}) collective-permute-start(bf16[192,640]{1,0:T(8,128)(2,1)S(1)} %collective-permute-done.5.rest_6_), channel_id=1, source_target_pairs={{0,4},{4,0},{8,12},{12,8},{16,20},{20,16},{24,28},{28,24},{1,5},{5... | collective-permute-start | bytes 737288 | tf_op jit(solution)/shard_map/ppermute | solution.py:51
  27.0 5.1 %collective-permute-start.4 = (bf16[192,640]{1,0:T(8,128)(2,1)S(1)}, bf16[192,640]{1,0:T(8,128)(2,1)S(1)}, u32[]{:S(2)}, u32[]{:S(2)}) collective-permute-start(bf16[192,640]{1,0:T(8,128)(2,1)S(1)} %collective-permute-done.3.rest_4_), channel_id=1, source_target_pairs={{0,4},{4,0},{8,12},{12,8},{16,20},{20,16},{24,28},{28,24},{1,5},{5... | collective-permute-start | bytes 737288 | tf_op jit(solution)/shard_map/ppermute | solution.py:51
  29.9 2.2 collective-permute-start.2
  31.0 12.4 %copy-start.19 = (s32[8,16]{1,0:T(8,128)S(1)}, s32[8,16]{1,0:T(8,128)}, u32[]{:S(2)}) copy-start(s32[8,16]{1,0:T(8,128)} %param.24) | copy-start | bytes 1540
  31.0 33.4 %copy-start.30 = (s32[8]{0:T(128)S(1)}, s32[8]{0:T(128)}, u32[]{:S(2)}) copy-start(s32[8]{0:T(128)} %param.22) | copy-start | bytes 100
  31.3 10.0 %collective-permute-start.17 = (bf16[192,384]{1,0:T(8,128)(2,1)S(1)}, bf16[192,384]{1,0:T(8,128)(2,1)}, u32[]{:S(2)}, u32[]{:S(2)}) collective-permute-start(bf16[192,384]{1,0:T(8,128)(2,1)S(1)} %bitcast.21), channel_id=1, source_target_pairs={{0,16},{4,20},{8,24},{12,28},{16,0},{20,4},{24,8},{28,12},{1,17},{... | collective-permute-start | bytes 442376 | tf_op jit(solution)/shard_map/ppermute | solution.py:51
  31.4 10.2 %collective-permute-start.15 = (bf16[192,384]{1,0:T(8,128)(2,1)S(1)}, bf16[192,384]{1,0:T(8,128)(2,1)}, u32[]{:S(2)}, u32[]{:S(2)}) collective-permute-start(bf16[192,384]{1,0:T(8,128)(2,1)S(1)} %bitcast.22), channel_id=1, source_target_pairs={{0,8},{4,12},{8,0},{12,4},{16,24},{20,28},{24,16},{28,20},{1,9},{5... | collective-permute-start | bytes 442376 | tf_op jit(solution)/shard_map/ppermute | solution.py:51
  37.7 16.2 %collective-permute-start.12 = (bf16[512,256]{1,0:T(8,128)(2,1)}, bf16[512,256]{1,0:T(8,128)(2,1)S(1)}, u32[]{:S(2)}, u32[]{:S(2)}) collective-permute-start(bf16[512,256]{1,0:T(8,128)(2,1)} %get-tuple-element.29.rest_0_), channel_id=1, source_target_pairs={{0,24},{4,28},{8,16},{12,20},{16,8},{20,12},{24,0},{28,4},{1,25},{... | collective-permute-start | bytes 786440 | tf_op jit(solution)/shard_map/ppermute | solution.py:51
  40.5 19.3 %collective-permute-start.10 = (bf16[512,256]{1,0:T(8,128)(2,1)}, bf16[512,256]{1,0:T(8,128)(2,1)S(1)}, u32[]{:S(2)}, u32[]{:S(2)}) collective-permute-start(bf16[512,256]{1,0:T(8,128)(2,1)} %get-tuple-element.29.rest_0_), channel_id=1, source_target_pairs={{0,16},{4,20},{8,24},{12,28},{16,0},{20,4},{24,8},{28,12},{1,17},{... | collective-permute-start | bytes 786440 | tf_op jit(solution)/shard_map/ppermute | solution.py:51
  40.6 23.8 %collective-permute-start.8 = (bf16[512,256]{1,0:T(8,128)(2,1)}, bf16[512,256]{1,0:T(8,128)(2,1)S(1)}, u32[]{:S(2)}, u32[]{:S(2)}) collective-permute-start(bf16[512,256]{1,0:T(8,128)(2,1)} %get-tuple-element.29.rest_0_), channel_id=1, source_target_pairs={{0,8},{4,12},{8,0},{12,4},{16,24},{20,28},{24,16},{28,20},{1,9},{5... | collective-permute-start | bytes 786440 | tf_op jit(solution)/shard_map/ppermute | solution.py:51
  41.2 1.4 collective-permute-start.14
  41.6 2.2 collective-permute-start.20
  41.8 22.7 %copy-start.26 = (s32[5]{0:T(128)}, s32[5]{0:T(128)S(1)}, u32[]{:S(2)}) copy-start(s32[5]{0:T(128)S(1)} %iota_add_fusion) | copy-start | bytes 64
  43.3 21.5 %collective-permute-start.18 = (bf16[192,384]{1,0:T(8,128)(2,1)}, bf16[192,384]{1,0:T(8,128)(2,1)}, u32[]{:S(2)}, u32[]{:S(2)}) collective-permute-start(bf16[192,384]{1,0:T(8,128)(2,1)} %collective-permute-done.17.rest_12_), channel_id=1, source_target_pairs={{0,4},{4,0},{8,12},{12,8},{16,20},{20,16},{24,28},{28,24},{1,5},{5... | collective-permute-start | bytes 442376 | tf_op jit(solution)/shard_map/ppermute | solution.py:51
  44.4 22.2 %collective-permute-start.7 = (bf16[512,256]{1,0:T(8,128)(2,1)}, bf16[512,256]{1,0:T(8,128)(2,1)}, u32[]{:S(2)}, u32[]{:S(2)}) collective-permute-start(bf16[512,256]{1,0:T(8,128)(2,1)} %get-tuple-element.29.rest_0_), channel_id=1, source_target_pairs={{0,4},{4,0},{8,12},{12,8},{16,20},{20,16},{24,28},{28,24},{1,5},{5... | collective-permute-start | bytes 786440 | tf_op jit(solution)/shard_map/ppermute | solution.py:51
  53.9 12.7 %collective-permute-start.13 = (bf16[512,256]{1,0:T(8,128)(2,1)S(1)}, bf16[512,256]{1,0:T(8,128)(2,1)}, u32[]{:S(2)}, u32[]{:S(2)}) collective-permute-start(bf16[512,256]{1,0:T(8,128)(2,1)S(1)} %collective-permute-done.12.rest_6_), channel_id=1, source_target_pairs={{0,4},{4,0},{8,12},{12,8},{16,20},{20,16},{24,28},{28,24},{1,5},{5... | collective-permute-start | bytes 786440 | tf_op jit(solution)/shard_map/ppermute | solution.py:51
  59.8 6.8 %collective-permute-start.11 = (bf16[512,256]{1,0:T(8,128)(2,1)S(1)}, bf16[512,256]{1,0:T(8,128)(2,1)}, u32[]{:S(2)}, u32[]{:S(2)}) collective-permute-start(bf16[512,256]{1,0:T(8,128)(2,1)S(1)} %collective-permute-done.10.rest_4_), channel_id=1, source_target_pairs={{0,4},{4,0},{8,12},{12,8},{16,20},{20,16},{24,28},{28,24},{1,5},{5... | collective-permute-start | bytes 786440 | tf_op jit(solution)/shard_map/ppermute | solution.py:51
  64.5 2.2 collective-permute-start.9
  64.8 1.8 collective-permute-start.16
  69.4 17.9 %copy-start.21 = (bf16[1536]{0:T(1024)(128)(2,1)S(1)}, bf16[1536]{0:T(1024)(128)(2,1)}, u32[]{:S(2)}) copy-start(bf16[1536]{0:T(1024)(128)(2,1)} %param.31) | copy-start | bytes 9220
  83.8 43.2 %copy-start.35 = (bf16[512]{0:T(512)(128)(2,1)S(1)}, bf16[512]{0:T(512)(128)(2,1)}, u32[]{:S(2)}) copy-start(bf16[512]{0:T(512)(128)(2,1)} %param.39) | copy-start | bytes 3076
  83.8 43.2 %copy-start.29 = (bf16[384]{0:T(512)(128)(2,1)S(1)}, bf16[384]{0:T(512)(128)(2,1)}, u32[]{:S(2)}) copy-start(bf16[384]{0:T(512)(128)(2,1)} %param.37) | copy-start | bytes 2308
  83.8 44.1 %copy-start.17 = (bf16[192,384]{1,0:T(8,128)(2,1)S(1)}, bf16[192,384]{1,0:T(8,128)(2,1)}, u32[]{:S(2)}) copy-start(bf16[192,384]{1,0:T(8,128)(2,1)} %param.36) | copy-start | bytes 442372
  83.8 15.6 %collective-permute-start.21 = (bf16[128,1536]{1,0:T(8,128)(2,1)}, bf16[128,1536]{1,0:T(8,128)(2,1)S(1)}, u32[]{:S(2)}, u32[]{:S(2)}) collective-permute-start(bf16[128,1536]{1,0:T(8,128)(2,1)} %get-tuple-element.31), channel_id=1, source_target_pairs={{0,1},{1,0},{2,3},{3,2},{4,5},{5,4},{6,7},{7,6},{8,9},{9,8},{10,11... | collective-permute-start | bytes 1179656 | tf_op jit(solution)/shard_map/ppermute | solution.py:51
  84.4 19.1 %collective-permute-start.22 = (bf16[128,1536]{1,0:T(8,128)(2,1)}, bf16[128,1536]{1,0:T(8,128)(2,1)S(1)}, u32[]{:S(2)}, u32[]{:S(2)}) collective-permute-start(bf16[128,1536]{1,0:T(8,128)(2,1)} %get-tuple-element.32), channel_id=1, source_target_pairs={{0,2},{1,3},{2,0},{3,1},{4,6},{5,7},{6,4},{7,5},{8,10},{9,11},{10,... | collective-permute-start | bytes 1179656 | tf_op jit(solution)/shard_map/ppermute | solution.py:51
  86.9 34.1 %collective-permute-start.23 = (bf16[128,1536]{1,0:T(8,128)(2,1)}, bf16[128,1536]{1,0:T(8,128)(2,1)}, u32[]{:S(2)}, u32[]{:S(2)}) collective-permute-start(bf16[128,1536]{1,0:T(8,128)(2,1)} %get-tuple-element.33), channel_id=1, source_target_pairs={{0,3},{1,2},{2,1},{3,0},{4,7},{5,6},{6,5},{7,4},{8,11},{9,10},{10,... | collective-permute-start | bytes 1179656 | tf_op jit(solution)/shard_map/ppermute | solution.py:51
  123.4 4.5 %copy-start.8 = (bf16[128,1536]{1,0:T(8,128)(2,1)}, bf16[128,1536]{1,0:T(8,128)(2,1)S(1)}, u32[]{:S(2)}) copy-start(bf16[128,1536]{1,0:T(8,128)(2,1)S(1)} %get-tuple-element.35.rest_0_) | copy-start | bytes 1179652
  123.4 16.0 %collective-permute-start.24 = (bf16[128,1536]{1,0:T(8,128)(2,1)S(1)}, bf16[128,1536]{1,0:T(8,128)(2,1)S(1)}, u32[]{:S(2)}, u32[]{:S(2)}) collective-permute-start(bf16[128,1536]{1,0:T(8,128)(2,1)S(1)} %get-tuple-element.36), channel_id=1, source_target_pairs={{0,1},{1,0},{2,3},{3,2},{4,5},{5,4},{6,7},{7,6},{8,9},{9,8},{10,11... | collective-permute-start | bytes 1179656 | tf_op jit(solution)/shard_map/ppermute | solution.py:51
  123.5 28.9 %collective-permute-start.25 = (bf16[128,1536]{1,0:T(8,128)(2,1)S(1)}, bf16[128,1536]{1,0:T(8,128)(2,1)S(1)}, u32[]{:S(2)}, u32[]{:S(2)}) collective-permute-start(bf16[128,1536]{1,0:T(8,128)(2,1)S(1)} %get-tuple-element.37), channel_id=1, source_target_pairs={{0,2},{1,3},{2,0},{3,1},{4,6},{5,7},{6,4},{7,5},{8,10},{9,11},{10,... | collective-permute-start | bytes 1179656 | tf_op jit(solution)/shard_map/ppermute | solution.py:51
  126.6 34.8 %collective-permute-start.26 = (bf16[128,1536]{1,0:T(8,128)(2,1)S(1)}, bf16[128,1536]{1,0:T(8,128)(2,1)S(1)}, u32[]{:S(2)}, u32[]{:S(2)}) collective-permute-start(bf16[128,1536]{1,0:T(8,128)(2,1)S(1)} %get-tuple-element.38), channel_id=1, source_target_pairs={{0,3},{1,2},{2,1},{3,0},{4,7},{5,6},{6,5},{7,4},{8,11},{9,10},{10,... | collective-permute-start | bytes 1179656 | tf_op jit(solution)/shard_map/ppermute | solution.py:51
  127.9 58.8 %collective-permute-start.38 = (bf16[192,512]{1,0:T(8,128)(2,1)S(1)}, bf16[192,512]{1,0:T(8,128)(2,1)S(1)}, u32[]{:S(2)}, u32[]{:S(2)}) collective-permute-start(bf16[192,512]{1,0:T(8,128)(2,1)S(1)} %pad_maximum_fusion.4.rest_4_), channel_id=1, source_target_pairs={{0,24},{4,28},{8,16},{12,20},{16,8},{20,12},{24,0},{28,4},{1,25},{... | collective-permute-start | bytes 589832 | tf_op jit(solution)/shard_map/ppermute | solution.py:51
  139.4 22.0 %copy-start.31 = (bf16[128,1536]{1,0:T(8,128)(2,1)}, bf16[128,1536]{1,0:T(8,128)(2,1)S(1)}, u32[]{:S(2)}) copy-start(bf16[128,1536]{1,0:T(8,128)(2,1)S(1)} %collective-permute-done.24.rest_1_) | copy-start | bytes 1179652
  152.4 9.0 %copy-start.32 = (bf16[128,1536]{1,0:T(8,128)(2,1)}, bf16[128,1536]{1,0:T(8,128)(2,1)S(1)}, u32[]{:S(2)}) copy-start(bf16[128,1536]{1,0:T(8,128)(2,1)S(1)} %collective-permute-done.25.rest_2_) | copy-start | bytes 1179652
  163.2 23.2 %copy-start.22 = (bf16[1536]{0:T(1024)(128)(2,1)S(1)}, bf16[1536]{0:T(1024)(128)(2,1)}, u32[]{:S(2)}) copy-start(bf16[1536]{0:T(1024)(128)(2,1)} %param.35) | copy-start | bytes 9220
  163.2 23.2 %copy-start.27 = (s32[5]{0:T(128)S(1)}, s32[5]{0:T(128)}, u32[]{:S(2)}) copy-start(s32[5]{0:T(128)} %copy-done.26) | copy-start | bytes 64
  163.2 23.6 %copy-start.24 = (s32[5]{0:T(128)S(1)}, s32[5]{0:T(128)}, u32[]{:S(2)}) copy-start(s32[5]{0:T(128)} %get-tuple-element.59) | copy-start | bytes 64
  163.2 64.9 %copy-start.3 = (bf16[4096,256]{1,0:T(8,128)(2,1)S(1)}, bf16[4096,256]{1,0:T(8,128)(2,1)}, u32[]{:S(2)}) copy-start(bf16[4096,256]{1,0:T(8,128)(2,1)} %copy-done.2) | copy-start | bytes 6291460
  182.8 18.0 %collective-permute-start.27 = (bf16[128,1536]{1,0:T(8,128)(2,1)}, bf16[128,1536]{1,0:T(8,128)(2,1)}, u32[]{:S(2)}, u32[]{:S(2)}) collective-permute-start(bf16[128,1536]{1,0:T(8,128)(2,1)} %get-tuple-element.40), channel_id=1, source_target_pairs={{0,1},{1,0},{2,3},{3,2},{4,5},{5,4},{6,7},{7,6},{8,9},{9,8},{10,11... | collective-permute-start | bytes 1179656 | tf_op jit(solution)/shard_map/ppermute | solution.py:51
  182.8 30.0 %collective-permute-start.28 = (bf16[128,1536]{1,0:T(8,128)(2,1)}, bf16[128,1536]{1,0:T(8,128)(2,1)}, u32[]{:S(2)}, u32[]{:S(2)}) collective-permute-start(bf16[128,1536]{1,0:T(8,128)(2,1)} %get-tuple-element.41), channel_id=1, source_target_pairs={{0,2},{1,3},{2,0},{3,1},{4,6},{5,7},{6,4},{7,5},{8,10},{9,11},{10,... | collective-permute-start | bytes 1179656 | tf_op jit(solution)/shard_map/ppermute | solution.py:51
  186.2 35.1 %collective-permute-start.29 = (bf16[128,1536]{1,0:T(8,128)(2,1)}, bf16[128,1536]{1,0:T(8,128)(2,1)}, u32[]{:S(2)}, u32[]{:S(2)}) collective-permute-start(bf16[128,1536]{1,0:T(8,128)(2,1)} %get-tuple-element.42), channel_id=1, source_target_pairs={{0,3},{1,2},{2,1},{3,0},{4,7},{5,6},{6,5},{7,4},{8,11},{9,10},{10,... | collective-permute-start | bytes 1179656 | tf_op jit(solution)/shard_map/ppermute | solution.py:51
  186.6 37.9 %collective-permute-start.36 = (bf16[192,512]{1,0:T(8,128)(2,1)S(1)}, bf16[192,512]{1,0:T(8,128)(2,1)}, u32[]{:S(2)}, u32[]{:S(2)}) collective-permute-start(bf16[192,512]{1,0:T(8,128)(2,1)S(1)} %pad_maximum_fusion.4.rest_4_), channel_id=1, source_target_pairs={{0,16},{4,20},{8,24},{12,28},{16,0},{20,4},{24,8},{28,12},{1,17},{... | collective-permute-start | bytes 589832 | tf_op jit(solution)/shard_map/ppermute | solution.py:51
  186.7 41.0 %collective-permute-start.34 = (bf16[192,512]{1,0:T(8,128)(2,1)S(1)}, bf16[192,512]{1,0:T(8,128)(2,1)}, u32[]{:S(2)}, u32[]{:S(2)}) collective-permute-start(bf16[192,512]{1,0:T(8,128)(2,1)S(1)} %pad_maximum_fusion.4.rest_4_), channel_id=1, source_target_pairs={{0,8},{4,12},{8,0},{12,4},{16,24},{20,28},{24,16},{28,20},{1,9},{5... | collective-permute-start | bytes 589832 | tf_op jit(solution)/shard_map/ppermute | solution.py:51
  200.8 31.4 %collective-permute-start.33 = (bf16[192,512]{1,0:T(8,128)(2,1)S(1)}, bf16[192,512]{1,0:T(8,128)(2,1)}, u32[]{:S(2)}, u32[]{:S(2)}) collective-permute-start(bf16[192,512]{1,0:T(8,128)(2,1)S(1)} %pad_maximum_fusion.4.rest_4_), channel_id=1, source_target_pairs={{0,4},{4,0},{8,12},{12,8},{16,20},{20,16},{24,28},{28,24},{1,5},{5... | collective-permute-start | bytes 589832 | tf_op jit(solution)/shard_map/ppermute | solution.py:51
  212.9 19.4 %collective-permute-start.39 = (bf16[192,512]{1,0:T(8,128)(2,1)S(1)}, bf16[192,512]{1,0:T(8,128)(2,1)}, u32[]{:S(2)}, u32[]{:S(2)}) collective-permute-start(bf16[192,512]{1,0:T(8,128)(2,1)S(1)} %collective-permute-done.38.rest_10_), channel_id=1, source_target_pairs={{0,4},{4,0},{8,12},{12,8},{16,20},{20,16},{24,28},{28,24},{1,5},{5... | collective-permute-start | bytes 589832 | tf_op jit(solution)/shard_map/ppermute | solution.py:51
  224.6 37.4 %copy-start.7 = (bf16[128,1536]{1,0:T(8,128)(2,1)S(1)}, bf16[128,1536]{1,0:T(8,128)(2,1)}, u32[]{:S(2)}) copy-start(bf16[128,1536]{1,0:T(8,128)(2,1)} %copy-done.6) | copy-start | bytes 1179652
  224.6 16.2 %collective-permute-start.30 = (bf16[128,1536]{1,0:T(8,128)(2,1)}, bf16[128,1536]{1,0:T(8,128)(2,1)S(1)}, u32[]{:S(2)}, u32[]{:S(2)}) collective-permute-start(bf16[128,1536]{1,0:T(8,128)(2,1)} %get-tuple-element.44), channel_id=1, source_target_pairs={{0,1},{1,0},{2,3},{3,2},{4,5},{5,4},{6,7},{7,6},{8,9},{9,8},{10,11... | collective-permute-start | bytes 1179656 | tf_op jit(solution)/shard_map/ppermute | solution.py:51
  224.6 29.9 %collective-permute-start.31 = (bf16[128,1536]{1,0:T(8,128)(2,1)}, bf16[128,1536]{1,0:T(8,128)(2,1)}, u32[]{:S(2)}, u32[]{:S(2)}) collective-permute-start(bf16[128,1536]{1,0:T(8,128)(2,1)} %get-tuple-element.45), channel_id=1, source_target_pairs={{0,2},{1,3},{2,0},{3,1},{4,6},{5,7},{6,4},{7,5},{8,10},{9,11},{10,... | collective-permute-start | bytes 1179656 | tf_op jit(solution)/shard_map/ppermute | solution.py:51
  227.8 34.2 %collective-permute-start.32 = (bf16[128,1536]{1,0:T(8,128)(2,1)}, bf16[128,1536]{1,0:T(8,128)(2,1)}, u32[]{:S(2)}, u32[]{:S(2)}) collective-permute-start(bf16[128,1536]{1,0:T(8,128)(2,1)} %get-tuple-element.46), channel_id=1, source_target_pairs={{0,3},{1,2},{2,1},{3,0},{4,7},{5,6},{6,5},{7,4},{8,11},{9,10},{10,... | collective-permute-start | bytes 1179656 | tf_op jit(solution)/shard_map/ppermute | solution.py:51
  232.2 1.7 collective-permute-start.37
  232.3 1.9 collective-permute-start.35
  (13 other events, 12.8 us)
Sparse Core Ops, SparseCore 0:
  11.0 132.6 all-gather.2

commit v3 on v2

--- a/solution.py
+++ b/solution.py
@@ -315,9 +315,6 @@
     share = tok_rows // narrow
     row_base = wide_index * tok_rows
 
-    packed = jnp.stack([w_gate, w_up, w_down.T])
-    ffn_weights = lax.all_gather(packed, "wide", axis=0, tiled=False)
-
     qkv_weight = jnp.concatenate(
         [w_query, lax.dynamic_slice_in_dim(w_keyval, pair_offset, 2 * HD, 1)], axis=1
     )
@@ -325,6 +322,7 @@
         [b_query, lax.dynamic_slice_in_dim(b_keyval, pair_offset, 2 * HD, 0)]
     ).astype(f32)[None]
     qkv_pieces = wide_pieces(qkv_weight, wide)
+
 
     token_start = lookup(seg_offsets, segment_ids)
     positions = row_base + jnp.arange(tok_rows, dtype=jnp.int32) - token_start
@@ -334,6 +332,12 @@
     cosine, sine = jnp.cos(angles), jnp.sin(angles)
     cosine = jnp.concatenate([cosine, cosine], axis=1)
     sine = jnp.concatenate([-sine, sine], axis=1)
+
+    packed = jnp.stack([w_gate, w_up, w_down.T])
+    packed, cosine, sine, qkv_bias, *qkv_pieces = lax.optimization_barrier(
+        (packed, cosine, sine, qkv_bias, *qkv_pieces)
+    )
+    ffn_weights = lax.all_gather(packed, "wide", axis=0, tiled=False)
 
     qkv_width = query_width + 2 * HD
     queries, keyvals = pl.pallas_call(

time: 275 us -> 282 us (1.025); the launches traced: 274 us -> 277 us
  waiting for transfers between devices: 164 us -> 147 us
  local copies, waits for them, and re-layouts: 15.9 us -> 28.4 us
  starting transfers between devices: 25.6 us -> 35.4 us
  Pallas kernels: 47.3 us -> 42.6 us
    ppermute x40, waiting for transfers between devices: 163 us -> 147 us  [exchange(): return lax.ppermute(value, axis, [(i, i ^ mask) for i in range(size)])]
    unnamed x72 -> x90, local copies, waits for them, and re-layouts: 10.6 us -> 23.1 us
    ppermute x40, starting transfers between devices: 25.6 us -> 35.4 us  [exchange(): return lax.ppermute(value, axis, [(i, i ^ mask) for i in range(size)])]
    pallas_call x1, Pallas kernels: 13 us -> 8.83 us  [local(): pl.pallas_call(functools.partial(attend_kernel, wide, narrow, tile), out_...]
  transfers between devices with their start and end apart: 41 -> 41, of which waited for: 23 -> 21; matrix products, arithmetic and copies ran while one was open for 3% -> 5% of each run, Pallas kernels for 15% -> 14%
where the time goes in v3:
time: 282 us; the launch traced here: 277 us
  waiting for transfers between devices  147 us (52%)
  Pallas kernels  42.6 us (15%)
  starting transfers between devices  35.4 us (13%)
  local copies, waits for them, and re-layouts  28.4 us (10%)
  between operations  14.5 us (5%)
  other arithmetic  9.25 us (3%)
    ppermute x40, waiting for transfers between devices, exchange(): return lax.ppermute(value, axis, [(i, i ^ mask) for i in range(size)])  147 us
    ppermute x40, starting transfers between devices, exchange(): return lax.ppermute(value, axis, [(i, i ^ mask) for i in range(size)])  35.4 us
    unnamed x90, local copies, waits for them, and re-layouts  23.1 us
    pallas_call x1, Pallas kernels, local(): pl.pallas_call(functools.partial(ffn_kernel, narrow), out_shape=[jax.Shap...  19.6 us
    pallas_call x1, Pallas kernels, local(): pl.pallas_call(functools.partial(attend_kernel, wide, narrow, tile), out_...  8.83 us
  transfers between devices with their start and end apart: 41, of which 21 were waited for; matrix products, arithmetic and copies ran while one was open for 5% of the time, Pallas kernels for 14%

profile of v3, /device:TPU:10, one launch (start us, length us, event | category | flops | bytes accessed | tf_op | source)
XLA Modules:
  0.0 277.4 jit_solution(17367339249747199227)
XLA Ops:
  7.2 0.8 copy-done
  8.1 0.9 pad_maximum_fusion.3.rest_0_
  9.6 1.5 collective-permute-start.3
  11.2 1.4 collective-permute-start.5
  12.6 0.8 select_reduce_fusion.spots_ref
  13.4 3.5 %pad_maximum_fusion = bf16[3,192,2240]{2,1,0:T(8,128)(2,1)} fusion(bf16[1,192,2240]{2,1,0:T(8,128)(2,1)} %bitcast.20, bf16[1,192,2240]{2,1,0:T(8,128)(2,1)} %bitcast.21, bf16[1,192,2240]{2,1,0:T(8,128)(2,1)} %bitcast.22), kind=kLoop, calls=%fused_computation.1 | loop fusion | flops 2580480 | bytes 5160960 | tf_op jit(solution)/shard_map/stack | solution.py:336
  16.9 1.0 collective-permute-done.1.rest_2_
  18.0 3.4 %collective-permute-done.3.rest_4_ = bf16[192,640]{1,0:T(8,128)(2,1)S(1)} collective-permute-done((bf16[192,640]{1,0:T(8,128)(2,1)S(1)}, bf16[192,640]{1,0:T(8,128)(2,1)S(1)}, u32[]{:S(2)}, u32[]{:S(2)}) %collective-permute-start.3) | collective-permute-done | bytes 245792 | tf_op jit(solution)/shard_map/ppermute | solution.py:51
  21.4 1.6 collective-permute-done.5.rest_6_
  23.0 1.0 fusion
  26.6 1.4 collective-permute-start.15
  27.9 1.5 collective-permute-start.17
  30.1 0.9 copy-done.9
  31.1 0.9 copy-done.11
  32.0 0.9 copy-done.13
  33.0 5.5 %qkv.1 = (bf16[512,384]{1,0:T(8,128)(2,1)S(1)}, bf16[512,256]{1,0:T(8,128)(2,1)}) custom-call(s32[1]{0:T(128)} %bitcast.index_ref.wide_ref, bf16[512,1536]{1,0:T(8,128)(2,1)S(1)} %copy-done.1, f32[1,1536]{1,0:T(1,128)S(1)} %reshape.200.gain_ref, f32[1,640]{1,0:T(1,128)S(1)} %maximum_convert_fusion.bias_ref, f32[512,128]{1,0:T(8,128)S(1)} %get-tuple-element.41.cos_ref, ...), custom_call_target="tpu_custom_call" | custom-call | flops 1006632960 | bytes 3538944 | tf_op jit(solution)/shard_map/qkv/pallas_call | solution.py:343
  39.2 1.3 collective-permute-start.10
  40.6 1.4 collective-permute-start.12
  43.2 1.1 collective-permute-done.14.rest_9_
  46.5 12.8 %collective-permute-done.10.rest_4_ = bf16[512,256]{1,0:T(8,128)(2,1)S(1)} collective-permute-done((bf16[512,256]{1,0:T(8,128)(2,1)}, bf16[512,256]{1,0:T(8,128)(2,1)S(1)}, u32[]{:S(2)}, u32[]{:S(2)}) %collective-permute-start.10) | collective-permute-done | bytes 262176 | tf_op jit(solution)/shard_map/ppermute | solution.py:51
  59.8 6.6 %collective-permute-done.8.rest_2_ = bf16[512,256]{1,0:T(8,128)(2,1)S(1)} collective-permute-done((bf16[512,256]{1,0:T(8,128)(2,1)}, bf16[512,256]{1,0:T(8,128)(2,1)S(1)}, u32[]{:S(2)}, u32[]{:S(2)}) %collective-permute-start.8) | collective-permute-done | bytes 262176 | tf_op jit(solution)/shard_map/ppermute | solution.py:51
  67.3 1.2 collective-permute-done.20.rest_15_
  69.9 1.0 copy-done.19
  70.9 0.9 copy-done.23
  71.9 0.9 copy-done.25
  72.8 0.9 copy-done.27
  73.8 0.9 copy-done.29
  74.7 0.9 copy-done.31
  75.6 8.8 %attend.1 = (bf16[128,1536]{1,0:T(8,128)(2,1)S(1)}, bf16[128,1536]{1,0:T(8,128)(2,1)}, bf16[128,1536]{1,0:T(8,128)(2,1)}, bf16[128,1536]{1,0:T(8,128)(2,1)S(1)}, bf16[4096,256]{1,0:T(8,128)(2,1)S(1)}) custom-call(s32[1]{0:T(128)} %bitcast.index_ref.wide_ref, s32[1]{0:T(128)} %bitcast.1.narrow_ref, s32[512]{0:T(512)S(1)} %select_reduce_fusion.spots_ref, ...), custom_call_target="tpu_custom_call" | custom-call | flops 2415919104 | bytes 2097152 | tf_op jit(solution)/shard_map/attend/pallas_call | solution.py:374
  84.5 1.4 copy-done.2
  86.3 2.6 collective-permute-start.22
  89.5 11.6 %collective-permute-done.21.rest_1_ = bf16[128,1536]{1,0:T(8,128)(2,1)S(1)} collective-permute-done((bf16[128,1536]{1,0:T(8,128)(2,1)}, bf16[128,1536]{1,0:T(8,128)(2,1)S(1)}, u32[]{:S(2)}, u32[]{:S(2)}) %collective-permute-start.21) | collective-permute-done | bytes 393248 | tf_op jit(solution)/shard_map/ppermute | solution.py:51
  101.0 4.3 %collective-permute-done.22.rest_2_ = bf16[128,1536]{1,0:T(8,128)(2,1)S(1)} collective-permute-done((bf16[128,1536]{1,0:T(8,128)(2,1)}, bf16[128,1536]{1,0:T(8,128)(2,1)S(1)}, u32[]{:S(2)}, u32[]{:S(2)}) %collective-permute-start.22) | collective-permute-done | bytes 393248 | tf_op jit(solution)/shard_map/ppermute | solution.py:51
  105.4 0.7 copy-done.4
  106.1 16.9 %collective-permute-done.23.rest_3_ = bf16[128,1536]{1,0:T(8,128)(2,1)} collective-permute-done((bf16[128,1536]{1,0:T(8,128)(2,1)S(1)}, bf16[128,1536]{1,0:T(8,128)(2,1)}, u32[]{:S(2)}, u32[]{:S(2)}) %collective-permute-start.23) | collective-permute-done | bytes 393248 | tf_op jit(solution)/shard_map/ppermute | solution.py:51
  123.1 1.0 copy-done.5
  124.1 1.4 join.2
  125.6 3.0 %collective-permute-start.25 = (bf16[128,1536]{1,0:T(8,128)(2,1)S(1)}, bf16[128,1536]{1,0:T(8,128)(2,1)S(1)}, u32[]{:S(2)}, u32[]{:S(2)}) collective-permute-start(bf16[128,1536]{1,0:T(8,128)(2,1)S(1)} %get-tuple-element.60), channel_id=1, source_target_pairs={{0,2},{1,3},{2,0},{3,1},{4,6},{5,7},{6,4},{7,5},{8,10},{9,11},{10,... | collective-permute-start | bytes 1179656 | tf_op jit(solution)/shard_map/ppermute | solution.py:51
  129.2 0.8 constant_dynamic-slice_fusion
  130.0 0.9 pad_maximum_fusion.4.rest_4_
  130.9 1.4 collective-permute-start.34
  132.3 9.4 %collective-permute-done.24.rest_1_ = bf16[128,1536]{1,0:T(8,128)(2,1)S(1)} collective-permute-done((bf16[128,1536]{1,0:T(8,128)(2,1)S(1)}, bf16[128,1536]{1,0:T(8,128)(2,1)S(1)}, u32[]{:S(2)}, u32[]{:S(2)}) %collective-permute-start.24) | collective-permute-done | bytes 393248 | tf_op jit(solution)/shard_map/ppermute | solution.py:51
  141.7 12.7 %collective-permute-done.25.rest_2_ = bf16[128,1536]{1,0:T(8,128)(2,1)S(1)} collective-permute-done((bf16[128,1536]{1,0:T(8,128)(2,1)S(1)}, bf16[128,1536]{1,0:T(8,128)(2,1)S(1)}, u32[]{:S(2)}, u32[]{:S(2)}) %collective-permute-start.25) | collective-permute-done | bytes 393248 | tf_op jit(solution)/shard_map/ppermute | solution.py:51
  154.4 9.3 %collective-permute-done.26.rest_3_ = bf16[128,1536]{1,0:T(8,128)(2,1)S(1)} collective-permute-done((bf16[128,1536]{1,0:T(8,128)(2,1)S(1)}, bf16[128,1536]{1,0:T(8,128)(2,1)S(1)}, u32[]{:S(2)}, u32[]{:S(2)}) %collective-permute-start.26) | collective-permute-done | bytes 393248 | tf_op jit(solution)/shard_map/ppermute | solution.py:51
  163.7 0.7 copy-done.42
  164.5 1.0 copy-done.21
  165.5 19.6 %ffn.1 = (bf16[128,1536]{1,0:T(8,128)(2,1)S(1)}, bf16[128,1536]{1,0:T(8,128)(2,1)}, bf16[128,1536]{1,0:T(8,128)(2,1)}, bf16[128,1536]{1,0:T(8,128)(2,1)}) custom-call(bf16[128,1536]{1,0:T(8,128)(2,1)S(1)} %copy-done.21, bf16[128,1536]{1,0:T(8,128)(2,1)} %copy-done.40, bf16[128,1536]{1,0:T(8,128)(2,1)} %copy-done.41, bf16[128,1536]{1,0:T(8,128)(2,1)} %copy-done.42, ...), custom_call_target="tpu_custom_call" | custom-call | flops 10569646080 | bytes 20643840 | tf_op jit(solution)/shard_map/ffn/pallas_call | solution.py:422
  185.1 3.0 %collective-permute-start.28 = (bf16[128,1536]{1,0:T(8,128)(2,1)}, bf16[128,1536]{1,0:T(8,128)(2,1)}, u32[]{:S(2)}, u32[]{:S(2)}) collective-permute-start(bf16[128,1536]{1,0:T(8,128)(2,1)} %get-tuple-element.65), channel_id=1, source_target_pairs={{0,2},{1,3},{2,0},{3,1},{4,6},{5,7},{6,4},{7,5},{8,10},{9,11},{10,... | collective-permute-start | bytes 1179656 | tf_op jit(solution)/shard_map/ppermute | solution.py:51
  188.9 6.7 %collective-permute-start.36 = (bf16[192,512]{1,0:T(8,128)(2,1)S(1)}, bf16[192,512]{1,0:T(8,128)(2,1)S(1)}, u32[]{:S(2)}, u32[]{:S(2)}) collective-permute-start(bf16[192,512]{1,0:T(8,128)(2,1)S(1)} %pad_maximum_fusion.4.rest_4_), channel_id=1, source_target_pairs={{0,16},{4,20},{8,24},{12,28},{16,0},{20,4},{24,8},{28,12},{1,17},{... | collective-permute-start | bytes 589832 | tf_op jit(solution)/shard_map/ppermute | solution.py:51
  195.6 7.1 %collective-permute-done.27.rest_1_ = bf16[128,1536]{1,0:T(8,128)(2,1)} collective-permute-done((bf16[128,1536]{1,0:T(8,128)(2,1)}, bf16[128,1536]{1,0:T(8,128)(2,1)}, u32[]{:S(2)}, u32[]{:S(2)}) %collective-permute-start.27) | collective-permute-done | bytes 393248 | tf_op jit(solution)/shard_map/ppermute | solution.py:51
  202.7 12.1 %collective-permute-done.28.rest_2_ = bf16[128,1536]{1,0:T(8,128)(2,1)} collective-permute-done((bf16[128,1536]{1,0:T(8,128)(2,1)}, bf16[128,1536]{1,0:T(8,128)(2,1)}, u32[]{:S(2)}, u32[]{:S(2)}) %collective-permute-start.28) | collective-permute-done | bytes 393248 | tf_op jit(solution)/shard_map/ppermute | solution.py:51
  214.8 8.6 %collective-permute-done.29.rest_3_ = bf16[128,1536]{1,0:T(8,128)(2,1)} collective-permute-done((bf16[128,1536]{1,0:T(8,128)(2,1)}, bf16[128,1536]{1,0:T(8,128)(2,1)}, u32[]{:S(2)}, u32[]{:S(2)}) %collective-permute-start.29) | collective-permute-done | bytes 393248 | tf_op jit(solution)/shard_map/ppermute | solution.py:51
  223.4 2.5 join.3
  225.9 0.8 copy-done.6
  226.7 3.0 %collective-permute-start.31 = (bf16[128,1536]{1,0:T(8,128)(2,1)}, bf16[128,1536]{1,0:T(8,128)(2,1)}, u32[]{:S(2)}, u32[]{:S(2)}) collective-permute-start(bf16[128,1536]{1,0:T(8,128)(2,1)} %get-tuple-element.69), channel_id=1, source_target_pairs={{0,2},{1,3},{2,0},{3,1},{4,6},{5,7},{6,4},{7,5},{8,10},{9,11},{10,... | collective-permute-start | bytes 1179656 | tf_op jit(solution)/shard_map/ppermute | solution.py:51
  230.8 1.0 constant_dynamic-slice_fusion.2
  231.9 3.1 %gather_fusion = bf16[640,128]{1,0:T(8,128)(2,1)S(1)} fusion(bf16[4096,128]{1,0:T(8,128)(2,1)} %constant_dynamic-slice_fusion.2, s32[1024]{0:T(1024)S(1)} %pad_clamp_fusion), kind=kCustom, calls=%fused_computation | custom fusion | bytes 330240 | tf_op jit(solution)/shard_map/jit(_take)/gather | solution.py:276
  235.5 0.9 select_select_fusion
  237.0 5.6 %collective-permute-done.30.rest_1_ = bf16[128,1536]{1,0:T(8,128)(2,1)S(1)} collective-permute-done((bf16[128,1536]{1,0:T(8,128)(2,1)}, bf16[128,1536]{1,0:T(8,128)(2,1)S(1)}, u32[]{:S(2)}, u32[]{:S(2)}) %collective-permute-start.30) | collective-permute-done | bytes 393248 | tf_op jit(solution)/shard_map/ppermute | solution.py:51
  242.6 13.9 %collective-permute-done.31.rest_2_ = bf16[128,1536]{1,0:T(8,128)(2,1)} collective-permute-done((bf16[128,1536]{1,0:T(8,128)(2,1)}, bf16[128,1536]{1,0:T(8,128)(2,1)}, u32[]{:S(2)}, u32[]{:S(2)}) %collective-permute-start.31) | collective-permute-done | bytes 393248 | tf_op jit(solution)/shard_map/ppermute | solution.py:51
  256.4 7.4 %collective-permute-done.32.rest_3_ = bf16[128,1536]{1,0:T(8,128)(2,1)} collective-permute-done((bf16[128,1536]{1,0:T(8,128)(2,1)}, bf16[128,1536]{1,0:T(8,128)(2,1)}, u32[]{:S(2)}, u32[]{:S(2)}) %collective-permute-start.32) | collective-permute-done | bytes 393248 | tf_op jit(solution)/shard_map/ppermute | solution.py:51
  263.9 0.9 copy-done.15
  264.8 0.9 copy-done.17
  265.7 4.8 %next.1 = (bf16[512,1536]{1,0:T(8,128)(2,1)}, bf16[512,384]{1,0:T(8,128)(2,1)}, bf16[512,128]{1,0:T(8,128)(2,1)}) custom-call(s32[1]{0:T(128)} %bitcast.index_ref.wide_ref, s32[1]{0:T(128)} %bitcast.1.narrow_ref, f32[1,1536]{1,0:T(1,128)S(1)} %reshape.198.gain_ref, f32[1,512]{1,0:T(1,128)S(1)} %maximum_convert_fusion.1.bias_ref, ...), custom_call_target="tpu_custom_call" | custom-call | flops 805306368 | bytes 4718592 | tf_op jit(solution)/shard_map/next/pallas_call | solution.py:456
  (149 shorter events, 15.6 us)
Async XLA Ops:
  7.2 156.5 %all-gather.3.cloned.1.call-start = ((), (), s32[]{:S(2)}) async-start(), calls=%async_computation | async-start | bytes 23887872 | tf_op jit(solution)/shard_map/all_gather | solution.py:340
  9.0 8.9 %collective-permute-start.1 = (bf16[192,640]{1,0:T(8,128)(2,1)S(1)}, bf16[192,640]{1,0:T(8,128)(2,1)S(1)}, u32[]{:S(2)}, u32[]{:S(2)}) collective-permute-start(bf16[192,640]{1,0:T(8,128)(2,1)S(1)} %pad_maximum_fusion.3.rest_0_), channel_id=1, source_target_pairs={{0,8},{4,12},{8,0},{12,4},{16,24},{20,28},{24,16},{28,20},{1,9},{5... | collective-permute-start | bytes 737288 | tf_op jit(solution)/shard_map/ppermute | solution.py:51
  9.6 11.8 %collective-permute-start.3 = (bf16[192,640]{1,0:T(8,128)(2,1)S(1)}, bf16[192,640]{1,0:T(8,128)(2,1)S(1)}, u32[]{:S(2)}, u32[]{:S(2)}) collective-permute-start(bf16[192,640]{1,0:T(8,128)(2,1)S(1)} %pad_maximum_fusion.3.rest_0_), channel_id=1, source_target_pairs={{0,16},{4,20},{8,24},{12,28},{16,0},{20,4},{24,8},{28,12},{1,17},{... | collective-permute-start | bytes 737288 | tf_op jit(solution)/shard_map/ppermute | solution.py:51
  11.2 11.9 %collective-permute-start.5 = (bf16[192,640]{1,0:T(8,128)(2,1)S(1)}, bf16[192,640]{1,0:T(8,128)(2,1)S(1)}, u32[]{:S(2)}, u32[]{:S(2)}) collective-permute-start(bf16[192,640]{1,0:T(8,128)(2,1)S(1)} %pad_maximum_fusion.3.rest_0_), channel_id=1, source_target_pairs={{0,24},{4,28},{8,16},{12,20},{16,8},{20,12},{24,0},{28,4},{1,25},{... | collective-permute-start | bytes 737288 | tf_op jit(solution)/shard_map/ppermute | solution.py:51
  12.6 11.8 %collective-permute-start = (bf16[192,640]{1,0:T(8,128)(2,1)S(1)}, bf16[192,640]{1,0:T(8,128)(2,1)S(1)}, u32[]{:S(2)}, u32[]{:S(2)}) collective-permute-start(bf16[192,640]{1,0:T(8,128)(2,1)S(1)} %pad_maximum_fusion.3.rest_0_), channel_id=1, source_target_pairs={{0,4},{4,0},{8,12},{12,8},{16,20},{20,16},{24,28},{28,24},{1,5},{5... | collective-permute-start | bytes 737288 | tf_op jit(solution)/shard_map/ppermute | solution.py:51
  13.4 10.6 %copy-start.43 = (bf16[512]{0:T(512)(128)(2,1)S(1)}, bf16[512]{0:T(512)(128)(2,1)}, u32[]{:S(2)}) copy-start(bf16[512]{0:T(512)(128)(2,1)} %param.29) | copy-start | bytes 3076
  13.4 10.7 %copy-start.37 = (bf16[384]{0:T(512)(128)(2,1)S(1)}, bf16[384]{0:T(512)(128)(2,1)}, u32[]{:S(2)}) copy-start(bf16[384]{0:T(512)(128)(2,1)} %param.27) | copy-start | bytes 2308
  16.9 13.2 %copy-start.33 = (bf16[1536]{0:T(1024)(128)(2,1)S(1)}, bf16[1536]{0:T(1024)(128)(2,1)}, u32[]{:S(2)}) copy-start(bf16[1536]{0:T(1024)(128)(2,1)} %param.25) | copy-start | bytes 9220
  16.9 13.2 %copy-start.1 = (bf16[512,1536]{1,0:T(8,128)(2,1)S(1)}, bf16[512,1536]{1,0:T(8,128)(2,1)}, u32[]{:S(2)}) copy-start(bf16[512,1536]{1,0:T(8,128)(2,1)} %hidden_ref.1) | copy-start | bytes 4718596
  18.0 6.4 %collective-permute-start.2 = (bf16[192,640]{1,0:T(8,128)(2,1)S(1)}, bf16[192,640]{1,0:T(8,128)(2,1)S(1)}, u32[]{:S(2)}, u32[]{:S(2)}) collective-permute-start(bf16[192,640]{1,0:T(8,128)(2,1)S(1)} %collective-permute-done.1.rest_2_), channel_id=1, source_target_pairs={{0,4},{4,0},{8,12},{12,8},{16,20},{20,16},{24,28},{28,24},{1,5},{5... | collective-permute-start | bytes 737288 | tf_op jit(solution)/shard_map/ppermute | solution.py:51
  21.4 3.7 %collective-permute-start.4 = (bf16[192,640]{1,0:T(8,128)(2,1)S(1)}, bf16[192,640]{1,0:T(8,128)(2,1)S(1)}, u32[]{:S(2)}, u32[]{:S(2)}) collective-permute-start(bf16[192,640]{1,0:T(8,128)(2,1)S(1)} %collective-permute-done.3.rest_4_), channel_id=1, source_target_pairs={{0,4},{4,0},{8,12},{12,8},{16,20},{20,16},{24,28},{28,24},{1,5},{5... | collective-permute-start | bytes 737288 | tf_op jit(solution)/shard_map/ppermute | solution.py:51
  23.0 2.7 collective-permute-start.6
  26.5 18.6 %copy-start.32 = (s32[8,16]{1,0:T(8,128)S(1)}, s32[8,16]{1,0:T(8,128)}, u32[]{:S(2)}) copy-start(s32[8,16]{1,0:T(8,128)} %param.24) | copy-start | bytes 1540
  26.5 39.8 %copy-start.36 = (s32[8]{0:T(128)S(1)}, s32[8]{0:T(128)}, u32[]{:S(2)}) copy-start(s32[8]{0:T(128)} %param.23) | copy-start | bytes 100
  26.5 39.8 %copy-start.39 = (s32[8]{0:T(128)S(1)}, s32[8]{0:T(128)}, u32[]{:S(2)}) copy-start(s32[8]{0:T(128)} %param.22) | copy-start | bytes 100
  26.6 15.4 %collective-permute-start.15 = (bf16[192,384]{1,0:T(8,128)(2,1)}, bf16[192,384]{1,0:T(8,128)(2,1)}, u32[]{:S(2)}, u32[]{:S(2)}) collective-permute-start(bf16[192,384]{1,0:T(8,128)(2,1)} %bitcast.8.rest_8_), channel_id=1, source_target_pairs={{0,8},{4,12},{8,0},{12,4},{16,24},{20,28},{24,16},{28,20},{1,9},{5... | collective-permute-start | bytes 442376 | tf_op jit(solution)/shard_map/ppermute | solution.py:51
  27.9 14.8 %collective-permute-start.17 = (bf16[192,384]{1,0:T(8,128)(2,1)}, bf16[192,384]{1,0:T(8,128)(2,1)}, u32[]{:S(2)}, u32[]{:S(2)}) collective-permute-start(bf16[192,384]{1,0:T(8,128)(2,1)} %bitcast.8.rest_8_), channel_id=1, source_target_pairs={{0,16},{4,20},{8,24},{12,28},{16,0},{20,4},{24,8},{28,12},{1,17},{... | collective-permute-start | bytes 442376 | tf_op jit(solution)/shard_map/ppermute | solution.py:51
  29.4 13.3 %collective-permute-start.19 = (bf16[192,384]{1,0:T(8,128)(2,1)}, bf16[192,384]{1,0:T(8,128)(2,1)}, u32[]{:S(2)}, u32[]{:S(2)}) collective-permute-start(bf16[192,384]{1,0:T(8,128)(2,1)} %bitcast.8.rest_8_), channel_id=1, source_target_pairs={{0,24},{4,28},{8,16},{12,20},{16,8},{20,12},{24,0},{28,4},{1,25},{... | collective-permute-start | bytes 442376 | tf_op jit(solution)/shard_map/ppermute | solution.py:51
  39.2 20.1 %collective-permute-start.10 = (bf16[512,256]{1,0:T(8,128)(2,1)}, bf16[512,256]{1,0:T(8,128)(2,1)S(1)}, u32[]{:S(2)}, u32[]{:S(2)}) collective-permute-start(bf16[512,256]{1,0:T(8,128)(2,1)} %get-tuple-element.52.rest_0_), channel_id=1, source_target_pairs={{0,16},{4,20},{8,24},{12,28},{16,0},{20,4},{24,8},{28,12},{1,17},{... | collective-permute-start | bytes 786440 | tf_op jit(solution)/shard_map/ppermute | solution.py:51
  40.6 18.7 %collective-permute-start.12 = (bf16[512,256]{1,0:T(8,128)(2,1)}, bf16[512,256]{1,0:T(8,128)(2,1)S(1)}, u32[]{:S(2)}, u32[]{:S(2)}) collective-permute-start(bf16[512,256]{1,0:T(8,128)(2,1)} %get-tuple-element.52.rest_0_), channel_id=1, source_target_pairs={{0,24},{4,28},{8,16},{12,20},{16,8},{20,12},{24,0},{28,4},{1,25},{... | collective-permute-start | bytes 786440 | tf_op jit(solution)/shard_map/ppermute | solution.py:51
  42.0 24.4 %collective-permute-start.8 = (bf16[512,256]{1,0:T(8,128)(2,1)}, bf16[512,256]{1,0:T(8,128)(2,1)S(1)}, u32[]{:S(2)}, u32[]{:S(2)}) collective-permute-start(bf16[512,256]{1,0:T(8,128)(2,1)} %get-tuple-element.52.rest_0_), channel_id=1, source_target_pairs={{0,8},{4,12},{8,0},{12,4},{16,24},{20,28},{24,16},{28,20},{1,9},{5... | collective-permute-start | bytes 786440 | tf_op jit(solution)/shard_map/ppermute | solution.py:51
  42.7 1.6 collective-permute-start.14
  42.7 2.7 collective-permute-start.16
  45.0 21.8 %collective-permute-start.18 = (bf16[192,384]{1,0:T(8,128)(2,1)}, bf16[192,384]{1,0:T(8,128)(2,1)}, u32[]{:S(2)}, u32[]{:S(2)}) collective-permute-start(bf16[192,384]{1,0:T(8,128)(2,1)} %collective-permute-done.17.rest_12_), channel_id=1, source_target_pairs={{0,4},{4,0},{8,12},{12,8},{16,20},{20,16},{24,28},{28,24},{1,5},{5... | collective-permute-start | bytes 442376 | tf_op jit(solution)/shard_map/ppermute | solution.py:51
  46.1 22.4 %collective-permute-start.7 = (bf16[512,256]{1,0:T(8,128)(2,1)}, bf16[512,256]{1,0:T(8,128)(2,1)S(1)}, u32[]{:S(2)}, u32[]{:S(2)}) collective-permute-start(bf16[512,256]{1,0:T(8,128)(2,1)} %get-tuple-element.52.rest_0_), channel_id=1, source_target_pairs={{0,4},{4,0},{8,12},{12,8},{16,20},{20,16},{24,28},{28,24},{1,5},{5... | collective-permute-start | bytes 786440 | tf_op jit(solution)/shard_map/ppermute | solution.py:51
  59.3 9.9 %collective-permute-start.11 = (bf16[512,256]{1,0:T(8,128)(2,1)S(1)}, bf16[512,256]{1,0:T(8,128)(2,1)S(1)}, u32[]{:S(2)}, u32[]{:S(2)}) collective-permute-start(bf16[512,256]{1,0:T(8,128)(2,1)S(1)} %collective-permute-done.10.rest_4_), channel_id=1, source_target_pairs={{0,4},{4,0},{8,12},{12,8},{16,20},{20,16},{24,28},{28,24},{1,5},{5... | collective-permute-start | bytes 786440 | tf_op jit(solution)/shard_map/ppermute | solution.py:51
  59.3 10.6 %collective-permute-start.13 = (bf16[512,256]{1,0:T(8,128)(2,1)S(1)}, bf16[512,256]{1,0:T(8,128)(2,1)}, u32[]{:S(2)}, u32[]{:S(2)}) collective-permute-start(bf16[512,256]{1,0:T(8,128)(2,1)S(1)} %collective-permute-done.12.rest_6_), channel_id=1, source_target_pairs={{0,4},{4,0},{8,12},{12,8},{16,20},{20,16},{24,28},{28,24},{1,5},{5... | collective-permute-start | bytes 786440 | tf_op jit(solution)/shard_map/ppermute | solution.py:51
  66.4 3.6 %copy-start.22 = (bf16[512,256]{1,0:T(8,128)(2,1)}, bf16[512,256]{1,0:T(8,128)(2,1)S(1)}, u32[]{:S(2)}) copy-start(bf16[512,256]{1,0:T(8,128)(2,1)S(1)} %collective-permute-done.8.rest_2_) | copy-start | bytes 786436
  66.4 3.6 %collective-permute-start.9 = (bf16[512,256]{1,0:T(8,128)(2,1)S(1)}, bf16[512,256]{1,0:T(8,128)(2,1)}, u32[]{:S(2)}, u32[]{:S(2)}) collective-permute-start(bf16[512,256]{1,0:T(8,128)(2,1)S(1)} %collective-permute-done.8.rest_2_), channel_id=1, source_target_pairs={{0,4},{4,0},{8,12},{12,8},{16,20},{20,16},{24,28},{28,24},{1,5},{5... | collective-permute-start | bytes 786440 | tf_op jit(solution)/shard_map/ppermute | solution.py:51
  66.7 1.8 collective-permute-start.20
  69.9 1.0 copy-start.19
  70.9 0.9 copy-start.23
  75.6 13.8 %copy-start.34 = (bf16[1536]{0:T(1024)(128)(2,1)S(1)}, bf16[1536]{0:T(1024)(128)(2,1)}, u32[]{:S(2)}) copy-start(bf16[1536]{0:T(1024)(128)(2,1)} %param.31) | copy-start | bytes 9220
  84.4 1.4 copy-start.2
  85.8 43.3 %copy-start.44 = (bf16[512]{0:T(512)(128)(2,1)S(1)}, bf16[512]{0:T(512)(128)(2,1)}, u32[]{:S(2)}) copy-start(bf16[512]{0:T(512)(128)(2,1)} %param.39) | copy-start | bytes 3076
  85.8 43.3 %copy-start.38 = (bf16[384]{0:T(512)(128)(2,1)S(1)}, bf16[384]{0:T(512)(128)(2,1)}, u32[]{:S(2)}) copy-start(bf16[384]{0:T(512)(128)(2,1)} %param.37) | copy-start | bytes 2308
  85.8 15.2 %collective-permute-start.21 = (bf16[128,1536]{1,0:T(8,128)(2,1)}, bf16[128,1536]{1,0:T(8,128)(2,1)S(1)}, u32[]{:S(2)}, u32[]{:S(2)}) collective-permute-start(bf16[128,1536]{1,0:T(8,128)(2,1)} %get-tuple-element.54), channel_id=1, source_target_pairs={{0,1},{1,0},{2,3},{3,2},{4,5},{5,4},{6,7},{7,6},{8,9},{9,8},{10,11... | collective-permute-start | bytes 1179656 | tf_op jit(solution)/shard_map/ppermute | solution.py:51
  86.3 19.1 %collective-permute-start.22 = (bf16[128,1536]{1,0:T(8,128)(2,1)}, bf16[128,1536]{1,0:T(8,128)(2,1)S(1)}, u32[]{:S(2)}, u32[]{:S(2)}) collective-permute-start(bf16[128,1536]{1,0:T(8,128)(2,1)} %get-tuple-element.55), channel_id=1, source_target_pairs={{0,2},{1,3},{2,0},{3,1},{4,6},{5,7},{6,4},{7,5},{8,10},{9,11},{10,... | collective-permute-start | bytes 1179656 | tf_op jit(solution)/shard_map/ppermute | solution.py:51
  88.9 34.2 %collective-permute-start.23 = (bf16[128,1536]{1,0:T(8,128)(2,1)S(1)}, bf16[128,1536]{1,0:T(8,128)(2,1)}, u32[]{:S(2)}, u32[]{:S(2)}) collective-permute-start(bf16[128,1536]{1,0:T(8,128)(2,1)S(1)} %get-tuple-element.56), channel_id=1, source_target_pairs={{0,3},{1,2},{2,1},{3,0},{4,7},{5,6},{6,5},{7,4},{8,11},{9,10},{10,... | collective-permute-start | bytes 1179656 | tf_op jit(solution)/shard_map/ppermute | solution.py:51
  123.1 1.0 copy-start.5
  125.5 38.2 %copy-start.20 = (bf16[128,1536]{1,0:T(8,128)(2,1)}, bf16[128,1536]{1,0:T(8,128)(2,1)S(1)}, u32[]{:S(2)}) copy-start(bf16[128,1536]{1,0:T(8,128)(2,1)S(1)} %get-tuple-element.58.rest_0_) | copy-start | bytes 1179652
  125.5 16.2 %collective-permute-start.24 = (bf16[128,1536]{1,0:T(8,128)(2,1)S(1)}, bf16[128,1536]{1,0:T(8,128)(2,1)S(1)}, u32[]{:S(2)}, u32[]{:S(2)}) collective-permute-start(bf16[128,1536]{1,0:T(8,128)(2,1)S(1)} %get-tuple-element.59), channel_id=1, source_target_pairs={{0,1},{1,0},{2,3},{3,2},{4,5},{5,4},{6,7},{7,6},{8,9},{9,8},{10,11... | collective-permute-start | bytes 1179656 | tf_op jit(solution)/shard_map/ppermute | solution.py:51
  125.6 28.8 %collective-permute-start.25 = (bf16[128,1536]{1,0:T(8,128)(2,1)S(1)}, bf16[128,1536]{1,0:T(8,128)(2,1)S(1)}, u32[]{:S(2)}, u32[]{:S(2)}) collective-permute-start(bf16[128,1536]{1,0:T(8,128)(2,1)S(1)} %get-tuple-element.60), channel_id=1, source_target_pairs={{0,2},{1,3},{2,0},{3,1},{4,6},{5,7},{6,4},{7,5},{8,10},{9,11},{10,... | collective-permute-start | bytes 1179656 | tf_op jit(solution)/shard_map/ppermute | solution.py:51
  128.6 35.1 %collective-permute-start.26 = (bf16[128,1536]{1,0:T(8,128)(2,1)S(1)}, bf16[128,1536]{1,0:T(8,128)(2,1)S(1)}, u32[]{:S(2)}, u32[]{:S(2)}) collective-permute-start(bf16[128,1536]{1,0:T(8,128)(2,1)S(1)} %get-tuple-element.61), channel_id=1, source_target_pairs={{0,3},{1,2},{2,1},{3,0},{4,7},{5,6},{6,5},{7,4},{8,11},{9,10},{10,... | collective-permute-start | bytes 1179656 | tf_op jit(solution)/shard_map/ppermute | solution.py:51
  130.9 64.6 %collective-permute-start.34 = (bf16[192,512]{1,0:T(8,128)(2,1)S(1)}, bf16[192,512]{1,0:T(8,128)(2,1)S(1)}, u32[]{:S(2)}, u32[]{:S(2)}) collective-permute-start(bf16[192,512]{1,0:T(8,128)(2,1)S(1)} %pad_maximum_fusion.4.rest_4_), channel_id=1, source_target_pairs={{0,8},{4,12},{8,0},{12,4},{16,24},{20,28},{24,16},{28,20},{1,9},{5... | collective-permute-start | bytes 589832 | tf_op jit(solution)/shard_map/ppermute | solution.py:51
  141.7 22.0 %copy-start.40 = (bf16[128,1536]{1,0:T(8,128)(2,1)}, bf16[128,1536]{1,0:T(8,128)(2,1)S(1)}, u32[]{:S(2)}) copy-start(bf16[128,1536]{1,0:T(8,128)(2,1)S(1)} %collective-permute-done.24.rest_1_) | copy-start | bytes 1179652
  154.4 9.3 %copy-start.41 = (bf16[128,1536]{1,0:T(8,128)(2,1)}, bf16[128,1536]{1,0:T(8,128)(2,1)S(1)}, u32[]{:S(2)}) copy-start(bf16[128,1536]{1,0:T(8,128)(2,1)S(1)} %collective-permute-done.25.rest_2_) | copy-start | bytes 1179652
  164.5 1.0 copy-start.21
  165.5 23.1 %copy-start.35 = (bf16[1536]{0:T(1024)(128)(2,1)S(1)}, bf16[1536]{0:T(1024)(128)(2,1)}, u32[]{:S(2)}) copy-start(bf16[1536]{0:T(1024)(128)(2,1)} %param.35) | copy-start | bytes 9220
  165.5 65.4 %copy-start.3 = (bf16[4096,256]{1,0:T(8,128)(2,1)S(1)}, bf16[4096,256]{1,0:T(8,128)(2,1)}, u32[]{:S(2)}) copy-start(bf16[4096,256]{1,0:T(8,128)(2,1)} %copy-done.2) | copy-start | bytes 6291460
  185.0 17.7 %collective-permute-start.27 = (bf16[128,1536]{1,0:T(8,128)(2,1)}, bf16[128,1536]{1,0:T(8,128)(2,1)}, u32[]{:S(2)}, u32[]{:S(2)}) collective-permute-start(bf16[128,1536]{1,0:T(8,128)(2,1)} %get-tuple-element.64), channel_id=1, source_target_pairs={{0,1},{1,0},{2,3},{3,2},{4,5},{5,4},{6,7},{7,6},{8,9},{9,8},{10,11... | collective-permute-start | bytes 1179656 | tf_op jit(solution)/shard_map/ppermute | solution.py:51
  185.1 29.7 %collective-permute-start.28 = (bf16[128,1536]{1,0:T(8,128)(2,1)}, bf16[128,1536]{1,0:T(8,128)(2,1)}, u32[]{:S(2)}, u32[]{:S(2)}) collective-permute-start(bf16[128,1536]{1,0:T(8,128)(2,1)} %get-tuple-element.65), channel_id=1, source_target_pairs={{0,2},{1,3},{2,0},{3,1},{4,6},{5,7},{6,4},{7,5},{8,10},{9,11},{10,... | collective-permute-start | bytes 1179656 | tf_op jit(solution)/shard_map/ppermute | solution.py:51
  188.1 35.3 %collective-permute-start.29 = (bf16[128,1536]{1,0:T(8,128)(2,1)}, bf16[128,1536]{1,0:T(8,128)(2,1)}, u32[]{:S(2)}, u32[]{:S(2)}) collective-permute-start(bf16[128,1536]{1,0:T(8,128)(2,1)} %get-tuple-element.66), channel_id=1, source_target_pairs={{0,3},{1,2},{2,1},{3,0},{4,7},{5,6},{6,5},{7,4},{8,11},{9,10},{10,... | collective-permute-start | bytes 1179656 | tf_op jit(solution)/shard_map/ppermute | solution.py:51
  188.9 37.8 %collective-permute-start.36 = (bf16[192,512]{1,0:T(8,128)(2,1)S(1)}, bf16[192,512]{1,0:T(8,128)(2,1)S(1)}, u32[]{:S(2)}, u32[]{:S(2)}) collective-permute-start(bf16[192,512]{1,0:T(8,128)(2,1)S(1)} %pad_maximum_fusion.4.rest_4_), channel_id=1, source_target_pairs={{0,16},{4,20},{8,24},{12,28},{16,0},{20,4},{24,8},{28,12},{1,17},{... | collective-permute-start | bytes 589832 | tf_op jit(solution)/shard_map/ppermute | solution.py:51
  195.6 34.2 %collective-permute-start.38 = (bf16[192,512]{1,0:T(8,128)(2,1)S(1)}, bf16[192,512]{1,0:T(8,128)(2,1)S(1)}, u32[]{:S(2)}, u32[]{:S(2)}) collective-permute-start(bf16[192,512]{1,0:T(8,128)(2,1)S(1)} %pad_maximum_fusion.4.rest_4_), channel_id=1, source_target_pairs={{0,24},{4,28},{8,16},{12,20},{16,8},{20,12},{24,0},{28,4},{1,25},{... | collective-permute-start | bytes 589832 | tf_op jit(solution)/shard_map/ppermute | solution.py:51
  202.7 32.2 %collective-permute-start.33 = (bf16[192,512]{1,0:T(8,128)(2,1)S(1)}, bf16[192,512]{1,0:T(8,128)(2,1)}, u32[]{:S(2)}, u32[]{:S(2)}) collective-permute-start(bf16[192,512]{1,0:T(8,128)(2,1)S(1)} %pad_maximum_fusion.4.rest_4_), channel_id=1, source_target_pairs={{0,4},{4,0},{8,12},{12,8},{16,20},{20,16},{24,28},{28,24},{1,5},{5... | collective-permute-start | bytes 589832 | tf_op jit(solution)/shard_map/ppermute | solution.py:51
  214.8 20.2 %collective-permute-start.35 = (bf16[192,512]{1,0:T(8,128)(2,1)S(1)}, bf16[192,512]{1,0:T(8,128)(2,1)}, u32[]{:S(2)}, u32[]{:S(2)}) collective-permute-start(bf16[192,512]{1,0:T(8,128)(2,1)S(1)} %collective-permute-done.34.rest_6_), channel_id=1, source_target_pairs={{0,4},{4,0},{8,12},{12,8},{16,20},{20,16},{24,28},{28,24},{1,5},{5... | collective-permute-start | bytes 589832 | tf_op jit(solution)/shard_map/ppermute | solution.py:51
  226.7 37.2 %copy-start.7 = (bf16[128,1536]{1,0:T(8,128)(2,1)S(1)}, bf16[128,1536]{1,0:T(8,128)(2,1)}, u32[]{:S(2)}) copy-start(bf16[128,1536]{1,0:T(8,128)(2,1)} %copy-done.6) | copy-start | bytes 1179652
  226.7 15.9 %collective-permute-start.30 = (bf16[128,1536]{1,0:T(8,128)(2,1)}, bf16[128,1536]{1,0:T(8,128)(2,1)S(1)}, u32[]{:S(2)}, u32[]{:S(2)}) collective-permute-start(bf16[128,1536]{1,0:T(8,128)(2,1)} %get-tuple-element.68), channel_id=1, source_target_pairs={{0,1},{1,0},{2,3},{3,2},{4,5},{5,4},{6,7},{7,6},{8,9},{9,8},{10,11... | collective-permute-start | bytes 1179656 | tf_op jit(solution)/shard_map/ppermute | solution.py:51
  226.7 3.0 %copy-start.14 = (bf16[192,512]{1,0:T(8,128)(2,1)}, bf16[192,512]{1,0:T(8,128)(2,1)S(1)}, u32[]{:S(2)}) copy-start(bf16[192,512]{1,0:T(8,128)(2,1)S(1)} %collective-permute-done.36.rest_8_) | copy-start | bytes 589828
  226.7 29.8 %collective-permute-start.31 = (bf16[128,1536]{1,0:T(8,128)(2,1)}, bf16[128,1536]{1,0:T(8,128)(2,1)}, u32[]{:S(2)}, u32[]{:S(2)}) collective-permute-start(bf16[128,1536]{1,0:T(8,128)(2,1)} %get-tuple-element.69), channel_id=1, source_target_pairs={{0,2},{1,3},{2,0},{3,1},{4,6},{5,7},{6,4},{7,5},{8,10},{9,11},{10,... | collective-permute-start | bytes 1179656 | tf_op jit(solution)/shard_map/ppermute | solution.py:51
  230.4 33.5 %collective-permute-start.32 = (bf16[128,1536]{1,0:T(8,128)(2,1)}, bf16[128,1536]{1,0:T(8,128)(2,1)}, u32[]{:S(2)}, u32[]{:S(2)}) collective-permute-start(bf16[128,1536]{1,0:T(8,128)(2,1)} %get-tuple-element.70), channel_id=1, source_target_pairs={{0,3},{1,2},{2,1},{3,0},{4,7},{5,6},{6,5},{7,4},{8,11},{9,10},{10,... | collective-permute-start | bytes 1179656 | tf_op jit(solution)/shard_map/ppermute | solution.py:51
  235.0 1.7 collective-permute-start.37
  235.0 1.9 collective-permute-start.39
  (22 other events, 17.9 us)
Sparse Core Ops, SparseCore 0:
  26.6 123.2 all-gather.2

commit v4 on v2

--- a/solution.py
+++ b/solution.py
@@ -26,6 +26,10 @@
 
 
 def any_spec():
+    return pl.BlockSpec(memory_space=pl.ANY)
+
+
+def hbm_spec():
     return pl.BlockSpec(memory_space=pltpu.HBM)
 
 
@@ -60,6 +64,32 @@
     return [pieces[m] for m in range(size)]
 
 
+def after(values, *tokens):
+    return lax.optimization_barrier((tuple(values), tokens))[0]
+
+
+class Relay:
+    def __init__(self, value, size):
+        self.size = size
+        if size != 8:
+            self.pieces = [(m, 0, piece) for m, piece in enumerate(wide_pieces(value, size))]
+            return
+        self.across = exchange(value, "wide", 8, 2)
+        self.along = exchange(value, "wide", 8, 4)
+        self.pieces = [(0, 0, value), (1, 0, exchange(value, "wide", 8, 1))]
+
+    def pass_on(self, *tokens):
+        if self.size != 8:
+            return
+        across, along = after([self.across, self.along], *tokens)
+        half = across.shape[0] // 2
+        top = exchange(across[:half], "wide", 8, 4)
+        low = exchange(along[half:], "wide", 8, 2)
+        for mask, offset, piece in ((2, 0, across), (4, 0, along), (6, 0, top), (6, half, low)):
+            self.pieces.append((mask, offset, piece))
+            self.pieces.append((mask | 1, offset, exchange(piece, "wide", 8, 1)))
+
+
 def narrow_swap(pieces, size):
     return [pieces[0]] + [exchange(pieces[k], "narrow", size, k) for k in range(1, size)]
 
@@ -78,7 +108,7 @@
 
 
 def qkv_kernel(wide, index_ref, hidden_ref, gain_ref, bias_ref, cos_ref, sin_ref, *rest):
-    pieces, (q_ref, kv_ref, weight, sems) = rest[:wide], rest[wide:]
+    pieces, (q_ref, kv_ref, out_ref, weight, sems) = rest[:wide], rest[wide:]
     copies = place_copies(pieces, weight, sems, index_ref[0])
     for c in copies:
         c.start()
@@ -86,7 +116,7 @@
     cosine, sine = cos_ref[...], sin_ref[...]
     for c in copies:
         c.wait()
-    heads = weight.shape[1] // HD
+    heads = q_ref.shape[1] // HD + 2
     for h in range(heads):
         lanes = slice(h * HD, (h + 1) * HD)
         if h % 2 == 0:
@@ -100,18 +130,15 @@
             q_ref[:, lanes] = value
         else:
             kv_ref[:, (h - heads + 2) * HD : (h - heads + 3) * HD] = value
-
-
-def attend_kernel(wide, narrow, key_block, wide_ref, narrow_ref, spots_ref, starts_ref, q_ref, *rest):
-    kv_pieces, out_pieces = rest[:wide], rest[wide : 2 * wide]
-    rest = rest[2 * wide :]
-    part_refs, (kv_out, keyvals, w_out, mix, kv_sems, out_sems, flush_sem) = rest[:narrow], rest[narrow:]
+    out_ref[...] = weight[:, heads * HD :]
+
+
+def attend_kernel(wide, narrow, key_block, wide_ref, narrow_ref, spots_ref, starts_ref, q_ref, w_out, *rest):
+    kv_pieces, rest = rest[:wide], rest[wide:]
+    part_refs, (kv_out, keyvals, mix, kv_sems, flush_sem) = rest[:narrow], rest[narrow:]
     wide_index, narrow_index = wide_ref[0], narrow_ref[0]
     kv_copies = place_copies(kv_pieces, keyvals, kv_sems, wide_index)
-    out_copies = place_copies(out_pieces, w_out, out_sems, wide_index)
     for c in kv_copies:
-        c.start()
-    for c in out_copies:
         c.start()
     for c in kv_copies:
         c.wait()
@@ -167,8 +194,6 @@
         mixed = (mixed / total).astype(bf16)
         for h in range(heads):
             mix[rows, h * HD : (h + 1) * HD] = mixed[h * tile : (h + 1) * tile]
-    for c in out_copies:
-        c.wait()
     share = tok_rows // narrow
     for k in range(narrow):
         start = pl.multiple_of((narrow_index ^ k) * share, share)
@@ -189,52 +214,60 @@
         out[...] = rounded
 
 
-def ffn_kernel(narrow, *rest):
-    x_refs, weights_ref = rest[:narrow], rest[narrow]
-    rest = rest[narrow + 1 :]
+def ffn_kernel(narrow, piece_rows, spots, wide_ref, *rest):
+    x_refs, rest = rest[:narrow], rest[narrow:]
+    piece_refs, rest = rest[: len(spots)], rest[len(spots) :]
     part_refs, (x, held, gate, hidden, sems) = rest[:narrow], rest[narrow:]
-    copies = [
-        pltpu.make_async_copy(weights_ref.at[:, j], held.at[j], sems.at[j]) for j in range(3)
-    ]
-    for c in copies:
+    copies = [[], [], []]
+    for j in range(3):
+        for (mask, offset), piece in zip(spots, piece_refs):
+            low = max(offset, j * piece_rows)
+            high = min(offset + piece.shape[0], (j + 1) * piece_rows)
+            if low >= high:
+                continue
+            start = (wide_ref[0] ^ mask) * piece_rows + low - j * piece_rows
+            target = held.at[j, pl.ds(pl.multiple_of(start, 16), high - low)]
+            source = piece.at[pl.ds(low - offset, high - low)]
+            sem = sems.at[j, len(copies[j])]
+            copies[j].append(pltpu.make_async_copy(source, target, sem))
+    for c in copies[0] + copies[1] + copies[2]:
         c.start()
     share = x_refs[0].shape[0]
     for k in range(narrow):
         x[k * share : (k + 1) * share, :] = x_refs[k][...]
-    width = hidden.shape[1]
-    depth = x.shape[1]
+    depth, width = held.shape[1:]
     tile = 256
     whole = width // tile
+
+    def arrive(j):
+        for c in copies[j]:
+            c.wait()
 
     def each_tile(body):
         @pl.loop(0, whole)
         def _(j):
-            body(pl.ds(pl.multiple_of(j * tile, tile), tile), tile)
+            body(pl.ds(pl.multiple_of(j * tile, tile), tile))
 
         if width % tile:
-            body(slice(whole * tile, width), width - whole * tile)
-
-    def gate_tile(lanes, size):
-        block = held[0, :, :, lanes].reshape(depth, size)
-        gate[:, lanes] = jnp.dot(x[...], block, preferred_element_type=f32)
-
-    def up_tile(lanes, size):
-        block = held[1, :, :, lanes].reshape(depth, size)
-        up = jnp.dot(x[...], block, preferred_element_type=f32)
+            body(slice(whole * tile, width))
+
+    def gate_tile(lanes):
+        gate[:, lanes] = jnp.dot(x[...], held[0, :, lanes], preferred_element_type=f32)
+
+    def up_tile(lanes):
+        up = jnp.dot(x[...], held[1, :, lanes], preferred_element_type=f32)
         value = gate[:, lanes]
         hidden[:, lanes] = (value / (1.0 + jnp.exp(-value)) * up).astype(bf16)
 
-    copies[0].wait()
+    arrive(0)
     each_tile(gate_tile)
-    copies[1].wait()
+    arrive(1)
     each_tile(up_tile)
-    copies[2].wait()
-    pieces, rows = held.shape[1], held.shape[2]
-    group = 768 // rows
-    for g in range(pieces // group):
-        block = held[2, g * group : (g + 1) * group].reshape(group * rows, width)
-        product = contract_last(hidden[...], block)
-        lanes = slice(g * group * rows, (g + 1) * group * rows)
+    arrive(2)
+    group = 768
+    for g in range(depth // group):
+        lanes = slice(g * group, (g + 1) * group)
+        product = contract_last(hidden[...], held[2, lanes, :])
         for k in range(narrow):
             part_refs[k][:, lanes] = product[k * share : (k + 1) * share].astype(bf16)
 
@@ -315,16 +348,14 @@
     share = tok_rows // narrow
     row_base = wide_index * tok_rows
 
-    packed = jnp.stack([w_gate, w_up, w_down.T])
-    ffn_weights = lax.all_gather(packed, "wide", axis=0, tiled=False)
-
     qkv_weight = jnp.concatenate(
-        [w_query, lax.dynamic_slice_in_dim(w_keyval, pair_offset, 2 * HD, 1)], axis=1
+        [w_query, lax.dynamic_slice_in_dim(w_keyval, pair_offset, 2 * HD, 1), w_out.T], axis=1
     )
     qkv_bias = jnp.concatenate(
         [b_query, lax.dynamic_slice_in_dim(b_keyval, pair_offset, 2 * HD, 0)]
     ).astype(f32)[None]
     qkv_pieces = wide_pieces(qkv_weight, wide)
+
 
     token_start = lookup(seg_offsets, segment_ids)
     positions = row_base + jnp.arange(tok_rows, dtype=jnp.int32) - token_start
@@ -335,17 +366,46 @@
     cosine = jnp.concatenate([cosine, cosine], axis=1)
     sine = jnp.concatenate([-sine, sine], axis=1)
 
+    one_offset = pair_offset + kind_index * HD
+    next_weight = jnp.concatenate(
+        [w_query2, lax.dynamic_slice_in_dim(w_keyval2, one_offset, HD, 1)], axis=1
+    )
+    next_bias = jnp.concatenate(
+        [b_query2, lax.dynamic_slice_in_dim(b_keyval2, one_offset, HD, 0)]
+    ).astype(f32)[None]
+    base_rows = lax.dynamic_slice_in_dim(hidden_in, narrow_index * share, share, 0)
+    mlp_row = mlp_gain.astype(f32)[None]
+    next_row = next_gain.astype(f32)[None]
+    starts_column = token_start[:, None]
+    packed = jnp.concatenate([w_gate, w_up, w_down.T])
+    early = (
+        packed,
+        cosine,
+        sine,
+        qkv_bias,
+        next_weight,
+        next_bias,
+        base_rows,
+        mlp_row,
+        next_row,
+        starts_column,
+    )
+    early, qkv_pieces = lax.optimization_barrier((early, qkv_pieces))
+    packed, cosine, sine, qkv_bias, next_weight, next_bias, base_rows = early[:7]
+    mlp_row, next_row, starts_column = early[7:]
+
     qkv_width = query_width + 2 * HD
-    queries, keyvals = pl.pallas_call(
+    queries, keyvals, out_weight = pl.pallas_call(
         functools.partial(qkv_kernel, wide),
         out_shape=(
             jax.ShapeDtypeStruct((tok_rows, query_width), bf16),
             jax.ShapeDtypeStruct((tok_rows, 2 * HD), bf16),
+            jax.ShapeDtypeStruct((depth, query_width), bf16),
         ),
         in_specs=[smem_spec()] + [vmem_spec()] * 5 + [any_spec()] * wide,
-        out_specs=(vmem_spec(), vmem_spec()),
-        scratch_shapes=[VMEM((depth, qkv_width), bf16), pltpu.SemaphoreType.DMA((wide,))],
-        compiler_params=params(32),
+        out_specs=(vmem_spec(),) * 3,
+        scratch_shapes=[VMEM((depth, qkv_width + query_width), bf16), pltpu.SemaphoreType.DMA((wide,))],
+        compiler_params=params(60),
         cost_estimate=pl.CostEstimate(
             flops=2 * tok_rows * depth * qkv_width,
             bytes_accessed=2 * depth * (tok_rows + qkv_width),
@@ -363,7 +423,9 @@
     )
 
     kv_pieces = wide_pieces(keyvals, wide)
-    out_pieces = wide_pieces(w_out.T, wide)
+
+    (packed,) = after([packed], *kv_pieces[2::2])
+    relay = Relay(packed, wide)
 
     tile = 256
     total_rows = wide * tok_rows
@@ -371,17 +433,15 @@
         functools.partial(attend_kernel, wide, narrow, tile),
         out_shape=[jax.ShapeDtypeStruct((share, depth), bf16)] * narrow
         + [jax.ShapeDtypeStruct((total_rows, 2 * HD), bf16)],
-        in_specs=[smem_spec()] * 3 + [vmem_spec()] * 2 + [any_spec()] * (2 * wide),
-        out_specs=[vmem_spec()] * narrow + [any_spec()],
+        in_specs=[smem_spec()] * 3 + [vmem_spec()] * 3 + [any_spec()] * wide,
+        out_specs=[vmem_spec()] * narrow + [hbm_spec()],
         scratch_shapes=[
             VMEM((total_rows, 2 * HD), bf16),
-            VMEM((depth, query_width), bf16),
             VMEM((tok_rows, query_width), bf16),
-            pltpu.SemaphoreType.DMA((wide,)),
             pltpu.SemaphoreType.DMA((wide,)),
             pltpu.SemaphoreType.DMA,
         ],
-        compiler_params=params(40),
+        compiler_params=params(60),
         cost_estimate=pl.CostEstimate(
             flops=8 * tok_rows * query_width * depth,
             bytes_accessed=4 * total_rows * HD,
@@ -392,10 +452,10 @@
         wide_index[None],
         narrow_index[None],
         token_start,
-        token_start[:, None],
+        starts_column,
         queries,
+        out_weight,
         *kv_pieces,
-        *out_pieces,
     )
 
     def join(parts, base_rows, gain, with_norm):
@@ -406,47 +466,47 @@
             out_shape=[shape] * count,
             in_specs=[vmem_spec()] * (2 + narrow),
             out_specs=[vmem_spec()] * count,
-            compiler_params=params(24),
+            compiler_params=params(60),
             name="join",
         )(base_rows, gain, *parts)
 
-    base_rows = lax.dynamic_slice_in_dim(hidden_in, narrow_index * share, share, 0)
-    mlp_row = mlp_gain.astype(f32)[None]
     *normed, residual = join(narrow_swap(parts, narrow), base_rows, mlp_row, True)
     normed_pieces = narrow_swap(normed, narrow)
 
+    source = lax.dynamic_slice_in_dim(kv_all, kind_index * HD, HD, 1)
+    page_count = tok_rows // PAGE_LEN + 1
+    cache_block = fill_pages(
+        source, seg_lengths, seg_offsets, block_table, wide_index * page_count, page_count
+    )
+    relay.pass_on(normed_pieces[1])
+    normed_pieces = after(normed_pieces, cache_block)
+    spots = [(mask, offset) for mask, offset, _ in relay.pieces]
+    bulk = [piece for _, _, piece in relay.pieces]
     parts = pl.pallas_call(
-        functools.partial(ffn_kernel, narrow),
+        functools.partial(ffn_kernel, narrow, piece_rows, spots),
         out_shape=[jax.ShapeDtypeStruct((share, depth), bf16)] * narrow,
-        in_specs=[vmem_spec()] * narrow + [any_spec()],
+        in_specs=[smem_spec()] + [vmem_spec()] * narrow + [hbm_spec()] * len(bulk),
         out_specs=[vmem_spec()] * narrow,
         scratch_shapes=[
             VMEM((tok_rows, depth), bf16),
-            VMEM((3, wide, piece_rows, width), bf16),
+            VMEM((3, depth, width), bf16),
             VMEM((tok_rows, width), f32),
             VMEM((tok_rows, width), bf16),
-            pltpu.SemaphoreType.DMA((3,)),
+            pltpu.SemaphoreType.DMA((3, len(spots))),
         ],
-        compiler_params=params(52),
+        compiler_params=params(60),
         cost_estimate=pl.CostEstimate(
             flops=6 * tok_rows * depth * width,
             bytes_accessed=6 * depth * width,
             transcendentals=tok_rows * width,
         ),
         name="ffn",
-    )(*normed_pieces, ffn_weights)
+    )(wide_index[None], *normed_pieces, *bulk)
 
     hidden_rows = join(narrow_swap(parts, narrow), residual, mlp_row, False)
     hidden_pieces = narrow_swap(hidden_rows, narrow)
 
-    one_offset = pair_offset + kind_index * HD
-    next_weight = jnp.concatenate(
-        [w_query2, lax.dynamic_slice_in_dim(w_keyval2, one_offset, HD, 1)], axis=1
-    )
-    next_bias = jnp.concatenate(
-        [b_query2, lax.dynamic_slice_in_dim(b_keyval2, one_offset, HD, 0)]
-    ).astype(f32)[None]
-    next_weight, _ = lax.optimization_barrier((next_weight, residual))
+    (next_weight,) = after([next_weight], parts[0])
     next_pieces = wide_pieces(next_weight, wide)
     next_width = query_width + HD
     hidden_out, next_query, next_keyval = pl.pallas_call(
@@ -459,7 +519,7 @@
         in_specs=[smem_spec()] * 2 + [vmem_spec()] * (2 + narrow) + [any_spec()] * wide,
         out_specs=(vmem_spec(),) * 3,
         scratch_shapes=[VMEM((depth, next_width), bf16), pltpu.SemaphoreType.DMA((wide,))],
-        compiler_params=params(32),
+        compiler_params=params(60),
         cost_estimate=pl.CostEstimate(
             flops=2 * tok_rows * depth * next_width,
             bytes_accessed=2 * depth * (2 * tok_rows + next_width),
@@ -469,17 +529,12 @@
     )(
         wide_index[None],
         narrow_index[None],
-        next_gain.astype(f32)[None],
+        next_row,
         next_bias,
         *hidden_pieces,
         *next_pieces,
     )
 
-    source = lax.dynamic_slice_in_dim(kv_all, kind_index * HD, HD, 1)
-    page_count = tok_rows // PAGE_LEN + 1
-    cache_block = fill_pages(
-        source, seg_lengths, seg_offsets, block_table, wide_index * page_count, page_count
-    )
     return (hidden_out, next_query, next_keyval, cache_block[None])
 
 

time: 275 us -> 290 us (1.055)
  between operations: 14.6 us -> 1.18 us
  starting transfers between devices: 25.6 us -> 35.9 us
  waiting for transfers between devices: 164 us -> 173 us
  local copies, waits for them, and re-layouts: 15.9 us -> 19.5 us
    ppermute x40 -> x42, starting transfers between devices: 25.6 us -> 35.9 us  [exchange(): return lax.ppermute(value, axis, [(i, i ^ mask) for i in range(size)])]
    ppermute x40 -> x42, waiting for transfers between devices: 163 us -> 173 us  [exchange(): return lax.ppermute(value, axis, [(i, i ^ mask) for i in range(size)])]
    unnamed x72 -> x56, local copies, waits for them, and re-layouts: 10.6 us -> 3.25 us
    another operation x1 -> x0, other arithmetic: 3.52 us -> none  [local(): packed = jnp.stack([w_gate, w_up, w_down.T])]
    pallas_call x1, Pallas kernels: 13 us -> 10 us  [local(): pl.pallas_call(functools.partial(attend_kernel, wide, narrow, tile), out_...]
  transfers between devices with their start and end apart: 41 -> 42, of which waited for: 23 -> 25; matrix products, arithmetic and copies ran while one was open for 3% -> 9% of each run, Pallas kernels for 15% -> 6%
where the time goes in v4:
time: 290 us; the launch traced here: 287 us
  waiting for transfers between devices  173 us (60%)
  Pallas kernels  47.5 us (16%)
  starting transfers between devices  35.9 us (12%)
  local copies, waits for them, and re-layouts  19.5 us (7%)
  other arithmetic  9.16 us (3%)
    ppermute x42, waiting for transfers between devices, exchange(): return lax.ppermute(value, axis, [(i, i ^ mask) for i in range(size)])  173 us
    ppermute x42, starting transfers between devices, exchange(): return lax.ppermute(value, axis, [(i, i ^ mask) for i in range(size)])  35.9 us
    pallas_call x1, Pallas kernels, local(): pl.pallas_call(functools.partial(ffn_kernel, narrow, piece_rows, spots),...  20 us
    pallas_call x1, Pallas kernels, local(): pl.pallas_call(functools.partial(attend_kernel, wide, narrow, tile), out_...  10 us
    pallas_call x1, Pallas kernels, local(): pl.pallas_call(functools.partial(qkv_kernel, wide), out_shape=(jax.ShapeD...  6.38 us
    pallas_call x2, Pallas kernels, join(): pl.pallas_call(functools.partial(join_kernel, narrow), out_shape=[shape]...  6.14 us
  transfers between devices with their start and end apart: 42, of which 25 were waited for; matrix products, arithmetic and copies ran while one was open for 9% of the time, Pallas kernels for 6%

profile of v4, /device:TPU:10, one launch (start us, length us, event | category | flops | bytes accessed | tf_op | source)
XLA Modules:
  0.0 286.7 jit_solution(4447577967028480168)
XLA Ops:
  0.7 0.9 copy-done
  1.6 1.0 pad_maximum_fusion.1.rest_0_
  2.6 1.6 collective-permute-start.5
  4.7 1.5 collective-permute-start.1
  6.2 0.8 dynamic_slice.18
  7.0 0.7 concatenate.46
  7.6 0.7 concatenate.50
  8.3 0.8 dynamic-slice_bitcast_fusion
  9.1 0.8 constant_dynamic-slice_fusion.2
  10.5 0.8 select_reduce_fusion.spots_ref
  11.3 0.9 pad_maximum_fusion.4.rest_4_
  12.2 1.0 fusion
  13.8 1.3 reshape.202.gain_ref
  15.1 1.3 reshape.200.gain_ref
  16.4 1.3 reshape.201.gain_ref
  17.6 1.0 pad_maximum_fusion.2
  18.6 1.8 constant_dynamic-slice_fusion.1.base_ref
  20.9 2.1 collective-permute-done.3.rest_4_
  23.5 1.4 pad_maximum_fusion.rest_4_
  25.7 6.4 %qkv.1 = (bf16[512,384]{1,0:T(8,128)(2,1)}, bf16[512,256]{1,0:T(8,128)(2,1)}, bf16[1536,384]{1,0:T(8,128)(2,1)}) custom-call(s32[1]{0:T(128)} %bitcast.index_ref.wide_ref, bf16[512,1536]{1,0:T(8,128)(2,1)} %hidden_ref.1, f32[1,1536]{1,0:T(1,128)} %reshape.202.gain_ref, f32[1,640]{1,0:T(1,128)} %maximum_convert_fusion.bias_ref, ...), custom_call_target="tpu_custom_call" | custom-call | flops 1006632960 | bytes 3538944 | tf_op jit(solution)/shard_map/qkv/pallas_call | solution.py:398
  32.1 1.6 collective-permute-start.12
  34.1 1.5 collective-permute-start.8
  35.6 6.8 %collective-permute-done.12.rest_6_ = bf16[512,256]{1,0:T(8,128)(2,1)S(1)} collective-permute-done((bf16[512,256]{1,0:T(8,128)(2,1)}, bf16[512,256]{1,0:T(8,128)(2,1)S(1)}, u32[]{:S(2)}, u32[]{:S(2)}) %collective-permute-start.12) | collective-permute-done | bytes 262176 | tf_op jit(solution)/shard_map/ppermute | solution.py:55
  42.5 4.8 %collective-permute-done.10.rest_4_ = bf16[512,256]{1,0:T(8,128)(2,1)} collective-permute-done((bf16[512,256]{1,0:T(8,128)(2,1)}, bf16[512,256]{1,0:T(8,128)(2,1)}, u32[]{:S(2)}, u32[]{:S(2)}) %collective-permute-start.10) | collective-permute-done | bytes 262176 | tf_op jit(solution)/shard_map/ppermute | solution.py:55
  47.3 0.7 collective-permute-start.22
  48.0 1.2 collective-permute-start.21
  49.8 1.7 collective-permute-done.7.rest_1_
  51.6 0.8 copy.25.starts_ref
  52.5 0.9 collective-permute-done.9.rest_3_
  53.4 10.0 %attend.1 = (bf16[128,1536]{1,0:T(8,128)(2,1)}, bf16[128,1536]{1,0:T(8,128)(2,1)}, bf16[128,1536]{1,0:T(8,128)(2,1)}, bf16[128,1536]{1,0:T(8,128)(2,1)}, bf16[4096,256]{1,0:T(8,128)(2,1)}) custom-call(s32[1]{0:T(128)} %bitcast.index_ref.wide_ref, s32[1]{0:T(128)} %bitcast.1.narrow_ref, s32[512]{0:T(512)} %copy-done.20, s32[512,1]{1,0:T(8,128)} %copy.25.starts_ref, ...), custom_call_target="tpu_custom_call" | custom-call | flops 2415919104 | bytes 2097152 | tf_op jit(solution)/shard_map/attend/pallas_call | solution.py:432
  63.9 2.6 collective-permute-start.15
  66.9 13.8 %collective-permute-done.14.rest_1_ = bf16[128,1536]{1,0:T(8,128)(2,1)S(1)} collective-permute-done((bf16[128,1536]{1,0:T(8,128)(2,1)}, bf16[128,1536]{1,0:T(8,128)(2,1)S(1)}, u32[]{:S(2)}, u32[]{:S(2)}) %collective-permute-start.14) | collective-permute-done | bytes 393248 | tf_op jit(solution)/shard_map/ppermute | solution.py:55
  80.7 12.5 %collective-permute-done.15.rest_2_ = bf16[128,1536]{1,0:T(8,128)(2,1)S(1)} collective-permute-done((bf16[128,1536]{1,0:T(8,128)(2,1)}, bf16[128,1536]{1,0:T(8,128)(2,1)S(1)}, u32[]{:S(2)}, u32[]{:S(2)}) %collective-permute-start.15) | collective-permute-done | bytes 393248 | tf_op jit(solution)/shard_map/ppermute | solution.py:55
  93.2 8.2 %collective-permute-done.16.rest_3_ = bf16[128,1536]{1,0:T(8,128)(2,1)} collective-permute-done((bf16[128,1536]{1,0:T(8,128)(2,1)}, bf16[128,1536]{1,0:T(8,128)(2,1)}, u32[]{:S(2)}, u32[]{:S(2)}) %collective-permute-start.16) | collective-permute-done | bytes 393248 | tf_op jit(solution)/shard_map/ppermute | solution.py:55
  101.4 3.3 %join.2 = (bf16[128,1536]{1,0:T(8,128)(2,1)}, bf16[128,1536]{1,0:T(8,128)(2,1)}, bf16[128,1536]{1,0:T(8,128)(2,1)}, bf16[128,1536]{1,0:T(8,128)(2,1)}, bf16[128,1536]{1,0:T(8,128)(2,1)}) custom-call(bf16[128,1536]{1,0:T(8,128)(2,1)} %constant_dynamic-slice_fusion.1.base_ref, f32[1,1536]{1,0:T(1,128)} %reshape.200.gain_ref, ...), custom_call_target="tpu_custom_call" | custom-call | tf_op jit(solution)/shard_map/join/pallas_call | solution.py:464
  104.7 3.0 %collective-permute-start.18 = (bf16[128,1536]{1,0:T(8,128)(2,1)}, bf16[128,1536]{1,0:T(8,128)(2,1)S(1)}, u32[]{:S(2)}, u32[]{:S(2)}) collective-permute-start(bf16[128,1536]{1,0:T(8,128)(2,1)} %get-tuple-element.80), channel_id=1, source_target_pairs={{0,2},{1,3},{2,0},{3,1},{4,6},{5,7},{6,4},{7,5},{8,10},{9,11},{10,... | collective-permute-start | bytes 1179656 | tf_op jit(solution)/shard_map/ppermute | solution.py:55
  108.2 11.9 %collective-permute-done.17.rest_1_ = bf16[128,1536]{1,0:T(8,128)(2,1)S(1)} collective-permute-done((bf16[128,1536]{1,0:T(8,128)(2,1)}, bf16[128,1536]{1,0:T(8,128)(2,1)S(1)}, u32[]{:S(2)}, u32[]{:S(2)}) %collective-permute-start.17) | collective-permute-done | bytes 393248 | tf_op jit(solution)/shard_map/ppermute | solution.py:55
  120.1 0.7 copy-done.24
  120.9 1.4 slice.6
  122.4 1.4 slice.7
  124.3 10.2 %collective-permute-done.18.rest_2_ = bf16[128,1536]{1,0:T(8,128)(2,1)S(1)} collective-permute-done((bf16[128,1536]{1,0:T(8,128)(2,1)}, bf16[128,1536]{1,0:T(8,128)(2,1)S(1)}, u32[]{:S(2)}, u32[]{:S(2)}) %collective-permute-start.18) | collective-permute-done | bytes 393248 | tf_op jit(solution)/shard_map/ppermute | solution.py:55
  134.5 7.0 %collective-permute-done.19.rest_3_ = bf16[128,1536]{1,0:T(8,128)(2,1)S(1)} collective-permute-done((bf16[128,1536]{1,0:T(8,128)(2,1)}, bf16[128,1536]{1,0:T(8,128)(2,1)S(1)}, u32[]{:S(2)}, u32[]{:S(2)}) %collective-permute-start.19) | collective-permute-done | bytes 393248 | tf_op jit(solution)/shard_map/ppermute | solution.py:55
  141.5 7.6 %collective-permute-start.25 = (bf16[288,2240]{1,0:T(8,128)(2,1)S(1)}, bf16[288,2240]{1,0:T(8,128)(2,1)}, u32[]{:S(2)}, u32[]{:S(2)}) collective-permute-start(bf16[288,2240]{1,0:T(8,128)(2,1)S(1)} %slice.6), channel_id=1, source_target_pairs={{0,16},{4,20},{8,24},{12,28},{16,0},{20,4},{24,8},{28,12},{1,17},{... | collective-permute-start | bytes 3870728 | tf_op jit(solution)/shard_map/ppermute | solution.py:55
  149.1 6.5 %collective-permute-done.27.rest_12_ = bf16[288,2240]{1,0:T(8,128)(2,1)} collective-permute-done((bf16[288,2240]{1,0:T(8,128)(2,1)S(1)}, bf16[288,2240]{1,0:T(8,128)(2,1)}, u32[]{:S(2)}, u32[]{:S(2)}) %collective-permute-start.27) | collective-permute-done | bytes 1290272 | tf_op jit(solution)/shard_map/ppermute | solution.py:55
  155.6 23.5 %collective-permute-done.25.rest_10_ = bf16[288,2240]{1,0:T(8,128)(2,1)} collective-permute-done((bf16[288,2240]{1,0:T(8,128)(2,1)S(1)}, bf16[288,2240]{1,0:T(8,128)(2,1)}, u32[]{:S(2)}, u32[]{:S(2)}) %collective-permute-start.25) | collective-permute-done | bytes 1290272 | tf_op jit(solution)/shard_map/ppermute | solution.py:55
  179.8 2.7 collective-permute-done.26.rest_11_
  182.5 20.0 %ffn.1 = (bf16[128,1536]{1,0:T(8,128)(2,1)}, bf16[128,1536]{1,0:T(8,128)(2,1)}, bf16[128,1536]{1,0:T(8,128)(2,1)}, bf16[128,1536]{1,0:T(8,128)(2,1)}) custom-call(s32[1]{0:T(128)} %bitcast.index_ref.wide_ref, bf16[128,1536]{1,0:T(8,128)(2,1)} %get-tuple-element.82.rest_0_, bf16[128,1536]{1,0:T(8,128)(2,1)} %copy-done.24, bf16[128,1536]{1,0:T(8,128)(2,1)} %copy-done.25, ...), custom_call_target="tpu_custom_call" | custom-call | flops 10569646080 | bytes 20643840 | tf_op jit(solution)/shard_map/ffn/pallas_call | solution.py:485
  202.6 3.0 %collective-permute-start.30 = (bf16[128,1536]{1,0:T(8,128)(2,1)}, bf16[128,1536]{1,0:T(8,128)(2,1)S(1)}, u32[]{:S(2)}, u32[]{:S(2)}) collective-permute-start(bf16[128,1536]{1,0:T(8,128)(2,1)} %get-tuple-element.92), channel_id=1, source_target_pairs={{0,2},{1,3},{2,0},{3,1},{4,6},{5,7},{6,4},{7,5},{8,10},{9,11},{10,... | collective-permute-start | bytes 1179656 | tf_op jit(solution)/shard_map/ppermute | solution.py:55
  206.4 1.8 collective-permute-start.38
  208.2 2.3 collective-permute-done.40.rest_10_
  211.0 8.7 %collective-permute-done.29.rest_1_ = bf16[128,1536]{1,0:T(8,128)(2,1)S(1)} collective-permute-done((bf16[128,1536]{1,0:T(8,128)(2,1)}, bf16[128,1536]{1,0:T(8,128)(2,1)S(1)}, u32[]{:S(2)}, u32[]{:S(2)}) %collective-permute-start.29) | collective-permute-done | bytes 393248 | tf_op jit(solution)/shard_map/ppermute | solution.py:55
  219.7 12.6 %collective-permute-done.30.rest_2_ = bf16[128,1536]{1,0:T(8,128)(2,1)S(1)} collective-permute-done((bf16[128,1536]{1,0:T(8,128)(2,1)}, bf16[128,1536]{1,0:T(8,128)(2,1)S(1)}, u32[]{:S(2)}, u32[]{:S(2)}) %collective-permute-start.30) | collective-permute-done | bytes 393248 | tf_op jit(solution)/shard_map/ppermute | solution.py:55
  232.3 8.2 %collective-permute-done.31.rest_3_ = bf16[128,1536]{1,0:T(8,128)(2,1)S(1)} collective-permute-done((bf16[128,1536]{1,0:T(8,128)(2,1)}, bf16[128,1536]{1,0:T(8,128)(2,1)S(1)}, u32[]{:S(2)}, u32[]{:S(2)}) %collective-permute-start.31) | collective-permute-done | bytes 393248 | tf_op jit(solution)/shard_map/ppermute | solution.py:55
  240.5 0.7 copy-done.9
  241.2 2.9 %join.3 = (bf16[128,1536]{1,0:T(8,128)(2,1)}, bf16[128,1536]{1,0:T(8,128)(2,1)}, bf16[128,1536]{1,0:T(8,128)(2,1)}, bf16[128,1536]{1,0:T(8,128)(2,1)}) custom-call(bf16[128,1536]{1,0:T(8,128)(2,1)} %get-tuple-element.77.base_ref, f32[1,1536]{1,0:T(1,128)} %reshape.200.gain_ref, bf16[128,1536]{1,0:T(8,128)(2,1)} %get-tuple-element.90.rest_0_, ...), custom_call_target="tpu_custom_call" | custom-call | tf_op jit(solution)/shard_map/join/pallas_call | solution.py:464
  244.1 3.0 %collective-permute-start.33 = (bf16[128,1536]{1,0:T(8,128)(2,1)}, bf16[128,1536]{1,0:T(8,128)(2,1)S(1)}, u32[]{:S(2)}, u32[]{:S(2)}) collective-permute-start(bf16[128,1536]{1,0:T(8,128)(2,1)} %get-tuple-element.96), channel_id=1, source_target_pairs={{0,2},{1,3},{2,0},{3,1},{4,6},{5,7},{6,4},{7,5},{8,10},{9,11},{10,... | collective-permute-start | bytes 1179656 | tf_op jit(solution)/shard_map/ppermute | solution.py:55
  247.6 1.3 constant_dynamic-slice_fusion.3
  248.9 2.0 gather_fusion
  251.5 0.9 select_select_fusion
  252.7 6.8 %collective-permute-done.32.rest_1_ = bf16[128,1536]{1,0:T(8,128)(2,1)S(1)} collective-permute-done((bf16[128,1536]{1,0:T(8,128)(2,1)}, bf16[128,1536]{1,0:T(8,128)(2,1)S(1)}, u32[]{:S(2)}, u32[]{:S(2)}) %collective-permute-start.32) | collective-permute-done | bytes 393248 | tf_op jit(solution)/shard_map/ppermute | solution.py:55
  259.5 14.4 %collective-permute-done.33.rest_2_ = bf16[128,1536]{1,0:T(8,128)(2,1)S(1)} collective-permute-done((bf16[128,1536]{1,0:T(8,128)(2,1)}, bf16[128,1536]{1,0:T(8,128)(2,1)S(1)}, u32[]{:S(2)}, u32[]{:S(2)}) %collective-permute-start.33) | collective-permute-done | bytes 393248 | tf_op jit(solution)/shard_map/ppermute | solution.py:55
  273.9 7.0 %collective-permute-done.34.rest_3_ = bf16[128,1536]{1,0:T(8,128)(2,1)S(1)} collective-permute-done((bf16[128,1536]{1,0:T(8,128)(2,1)}, bf16[128,1536]{1,0:T(8,128)(2,1)S(1)}, u32[]{:S(2)}, u32[]{:S(2)}) %collective-permute-start.34) | collective-permute-done | bytes 393248 | tf_op jit(solution)/shard_map/ppermute | solution.py:55
  281.0 0.7 copy-done.14
  281.6 4.9 %next.1 = (bf16[512,1536]{1,0:T(8,128)(2,1)}, bf16[512,384]{1,0:T(8,128)(2,1)}, bf16[512,128]{1,0:T(8,128)(2,1)}) custom-call(s32[1]{0:T(128)} %bitcast.index_ref.wide_ref, s32[1]{0:T(128)} %bitcast.1.narrow_ref, f32[1,1536]{1,0:T(1,128)} %reshape.201.gain_ref, f32[1,512]{1,0:T(1,128)} %maximum_convert_fusion.1.bias_ref, ...), custom_call_target="tpu_custom_call" | custom-call | flops 805306368 | bytes 4718592 | tf_op jit(solution)/shard_map/next/pallas_call | solution.py:512
  (118 shorter events, 10.2 us)
Async XLA Ops:
  2.6 22.2 %copy-start.2 = (bf16[192,1024]{1,0:T(8,128)(2,1)}, bf16[192,1024]{1,0:T(8,128)(2,1)S(1)}, u32[]{:S(2)}) copy-start(bf16[192,1024]{1,0:T(8,128)(2,1)S(1)} %pad_maximum_fusion.1.rest_0_) | copy-start | bytes 1179652
  2.6 17.8 %collective-permute-start.5 = (bf16[192,1024]{1,0:T(8,128)(2,1)S(1)}, bf16[192,1024]{1,0:T(8,128)(2,1)}, u32[]{:S(2)}, u32[]{:S(2)}) collective-permute-start(bf16[192,1024]{1,0:T(8,128)(2,1)S(1)} %pad_maximum_fusion.1.rest_0_), channel_id=1, source_target_pairs={{0,24},{4,28},{8,16},{12,20},{16,8},{20,12},{24,0},{28,4},{1,25},{... | collective-permute-start | bytes 1179656 | tf_op jit(solution)/shard_map/ppermute | solution.py:55
  4.2 18.8 %collective-permute-start.3 = (bf16[192,1024]{1,0:T(8,128)(2,1)S(1)}, bf16[192,1024]{1,0:T(8,128)(2,1)}, u32[]{:S(2)}, u32[]{:S(2)}) collective-permute-start(bf16[192,1024]{1,0:T(8,128)(2,1)S(1)} %pad_maximum_fusion.1.rest_0_), channel_id=1, source_target_pairs={{0,16},{4,20},{8,24},{12,28},{16,0},{20,4},{24,8},{28,12},{1,17},{... | collective-permute-start | bytes 1179656 | tf_op jit(solution)/shard_map/ppermute | solution.py:55
  4.7 18.4 %collective-permute-start.1 = (bf16[192,1024]{1,0:T(8,128)(2,1)S(1)}, bf16[192,1024]{1,0:T(8,128)(2,1)}, u32[]{:S(2)}, u32[]{:S(2)}) collective-permute-start(bf16[192,1024]{1,0:T(8,128)(2,1)S(1)} %pad_maximum_fusion.1.rest_0_), channel_id=1, source_target_pairs={{0,8},{4,12},{8,0},{12,4},{16,24},{20,28},{24,16},{28,20},{1,9},{5... | collective-permute-start | bytes 1179656 | tf_op jit(solution)/shard_map/ppermute | solution.py:55
  6.2 18.7 %collective-permute-start = (bf16[192,1024]{1,0:T(8,128)(2,1)S(1)}, bf16[192,1024]{1,0:T(8,128)(2,1)}, u32[]{:S(2)}, u32[]{:S(2)}) collective-permute-start(bf16[192,1024]{1,0:T(8,128)(2,1)S(1)} %pad_maximum_fusion.1.rest_0_), channel_id=1, source_target_pairs={{0,4},{4,0},{8,12},{12,8},{16,20},{20,16},{24,28},{28,24},{1,5},{5... | collective-permute-start | bytes 1179656 | tf_op jit(solution)/shard_map/ppermute | solution.py:55
  11.2 40.4 %copy-start.20 = (s32[512]{0:T(512)}, s32[512]{0:T(512)S(1)}, u32[]{:S(2)}) copy-start(s32[512]{0:T(512)S(1)} %select_reduce_fusion.spots_ref) | copy-start | bytes 6148
  12.2 207.5 %copy-start.5 = (bf16[192,512]{1,0:T(8,128)(2,1)}, bf16[192,512]{1,0:T(8,128)(2,1)S(1)}, u32[]{:S(2)}) copy-start(bf16[192,512]{1,0:T(8,128)(2,1)S(1)} %pad_maximum_fusion.4.rest_4_) | copy-start | bytes 589828
  17.6 5.9 %copy-start.4 = (bf16[192,2240]{1,0:T(8,128)(2,1)S(1)}, bf16[192,2240]{1,0:T(8,128)(2,1)}, u32[]{:S(2)}) copy-start(bf16[192,2240]{1,0:T(8,128)(2,1)} %param.33) | copy-start | bytes 2580484
  20.4 4.5 %collective-permute-start.6 = (bf16[192,1024]{1,0:T(8,128)(2,1)}, bf16[192,1024]{1,0:T(8,128)(2,1)S(1)}, u32[]{:S(2)}, u32[]{:S(2)}) collective-permute-start(bf16[192,1024]{1,0:T(8,128)(2,1)} %collective-permute-done.5.rest_6_), channel_id=1, source_target_pairs={{0,4},{4,0},{8,12},{12,8},{16,20},{20,16},{24,28},{28,24},{1,5},{5... | collective-permute-start | bytes 1179656 | tf_op jit(solution)/shard_map/ppermute | solution.py:55
  23.0 2.1 collective-permute-start.4
  23.1 2.5 collective-permute-start.2
  24.9 95.3 %copy-start.1 = (bf16[576,2240]{1,0:T(8,128)(2,1)}, bf16[576,2240]{1,0:T(8,128)(2,1)S(1)}, u32[]{:S(2)}) copy-start(bf16[576,2240]{1,0:T(8,128)(2,1)S(1)} %pad_maximum_fusion.rest_4_) | copy-start | bytes 7741444
  32.1 10.4 %collective-permute-start.12 = (bf16[512,256]{1,0:T(8,128)(2,1)}, bf16[512,256]{1,0:T(8,128)(2,1)S(1)}, u32[]{:S(2)}, u32[]{:S(2)}) collective-permute-start(bf16[512,256]{1,0:T(8,128)(2,1)} %get-tuple-element.72.rest_0_), channel_id=1, source_target_pairs={{0,24},{4,28},{8,16},{12,20},{16,8},{20,12},{24,0},{28,4},{1,25},{... | collective-permute-start | bytes 786440 | tf_op jit(solution)/shard_map/ppermute | solution.py:55
  33.6 13.6 %collective-permute-start.10 = (bf16[512,256]{1,0:T(8,128)(2,1)}, bf16[512,256]{1,0:T(8,128)(2,1)}, u32[]{:S(2)}, u32[]{:S(2)}) collective-permute-start(bf16[512,256]{1,0:T(8,128)(2,1)} %get-tuple-element.72.rest_0_), channel_id=1, source_target_pairs={{0,16},{4,20},{8,24},{12,28},{16,0},{20,4},{24,8},{28,12},{1,17},{... | collective-permute-start | bytes 786440 | tf_op jit(solution)/shard_map/ppermute | solution.py:55
  34.1 13.1 %collective-permute-start.8 = (bf16[512,256]{1,0:T(8,128)(2,1)}, bf16[512,256]{1,0:T(8,128)(2,1)}, u32[]{:S(2)}, u32[]{:S(2)}) collective-permute-start(bf16[512,256]{1,0:T(8,128)(2,1)} %get-tuple-element.72.rest_0_), channel_id=1, source_target_pairs={{0,8},{4,12},{8,0},{12,4},{16,24},{20,28},{24,16},{28,20},{1,9},{5... | collective-permute-start | bytes 786440 | tf_op jit(solution)/shard_map/ppermute | solution.py:55
  42.4 10.9 %copy-start.27 = (bf16[512,256]{1,0:T(8,128)(2,1)}, bf16[512,256]{1,0:T(8,128)(2,1)S(1)}, u32[]{:S(2)}) copy-start(bf16[512,256]{1,0:T(8,128)(2,1)S(1)} %collective-permute-done.12.rest_6_) | copy-start | bytes 786436
  47.3 72.8 %collective-permute-start.22 = (bf16[576,2240]{1,0:T(8,128)(2,1)S(1)}, bf16[576,2240]{1,0:T(8,128)(2,1)}, u32[]{:S(2)}, u32[]{:S(2)}) collective-permute-start(bf16[576,2240]{1,0:T(8,128)(2,1)S(1)} %pad_maximum_fusion.rest_4_), channel_id=1, source_target_pairs={{0,16},{4,20},{8,24},{12,28},{16,0},{20,4},{24,8},{28,12},{1,17},{... | collective-permute-start | bytes 7741448 | tf_op jit(solution)/shard_map/ppermute | solution.py:55
  48.0 72.8 %collective-permute-start.21 = (bf16[576,2240]{1,0:T(8,128)(2,1)S(1)}, bf16[576,2240]{1,0:T(8,128)(2,1)}, u32[]{:S(2)}, u32[]{:S(2)}) collective-permute-start(bf16[576,2240]{1,0:T(8,128)(2,1)S(1)} %pad_maximum_fusion.rest_4_), channel_id=1, source_target_pairs={{0,8},{4,12},{8,0},{12,4},{16,24},{20,28},{24,16},{28,20},{1,9},{5... | collective-permute-start | bytes 7741448 | tf_op jit(solution)/shard_map/ppermute | solution.py:55
  49.3 2.2 collective-permute-start.7
  49.3 3.2 %collective-permute-start.13 = (bf16[512,256]{1,0:T(8,128)(2,1)S(1)}, bf16[512,256]{1,0:T(8,128)(2,1)}, u32[]{:S(2)}, u32[]{:S(2)}) collective-permute-start(bf16[512,256]{1,0:T(8,128)(2,1)S(1)} %collective-permute-done.12.rest_6_), channel_id=1, source_target_pairs={{0,4},{4,0},{8,12},{12,8},{16,20},{20,16},{24,28},{28,24},{1,5},{5... | collective-permute-start | bytes 786440 | tf_op jit(solution)/shard_map/ppermute | solution.py:55
  49.8 2.7 collective-permute-start.11
  51.5 1.9 collective-permute-start.9
  63.4 17.3 %collective-permute-start.14 = (bf16[128,1536]{1,0:T(8,128)(2,1)}, bf16[128,1536]{1,0:T(8,128)(2,1)S(1)}, u32[]{:S(2)}, u32[]{:S(2)}) collective-permute-start(bf16[128,1536]{1,0:T(8,128)(2,1)} %get-tuple-element.74), channel_id=1, source_target_pairs={{0,1},{1,0},{2,3},{3,2},{4,5},{5,4},{6,7},{7,6},{8,9},{9,8},{10,11... | collective-permute-start | bytes 1179656 | tf_op jit(solution)/shard_map/ppermute | solution.py:55
  63.9 29.3 %collective-permute-start.15 = (bf16[128,1536]{1,0:T(8,128)(2,1)}, bf16[128,1536]{1,0:T(8,128)(2,1)S(1)}, u32[]{:S(2)}, u32[]{:S(2)}) collective-permute-start(bf16[128,1536]{1,0:T(8,128)(2,1)} %get-tuple-element.75), channel_id=1, source_target_pairs={{0,2},{1,3},{2,0},{3,1},{4,6},{5,7},{6,4},{7,5},{8,10},{9,11},{10,... | collective-permute-start | bytes 1179656 | tf_op jit(solution)/shard_map/ppermute | solution.py:55
  66.5 34.9 %collective-permute-start.16 = (bf16[128,1536]{1,0:T(8,128)(2,1)}, bf16[128,1536]{1,0:T(8,128)(2,1)}, u32[]{:S(2)}, u32[]{:S(2)}) collective-permute-start(bf16[128,1536]{1,0:T(8,128)(2,1)} %get-tuple-element.76), channel_id=1, source_target_pairs={{0,3},{1,2},{2,1},{3,0},{4,7},{5,6},{6,5},{7,4},{8,11},{9,10},{10,... | collective-permute-start | bytes 1179656 | tf_op jit(solution)/shard_map/ppermute | solution.py:55
  80.7 20.7 %copy-start.10 = (bf16[128,1536]{1,0:T(8,128)(2,1)}, bf16[128,1536]{1,0:T(8,128)(2,1)S(1)}, u32[]{:S(2)}) copy-start(bf16[128,1536]{1,0:T(8,128)(2,1)S(1)} %collective-permute-done.14.rest_1_) | copy-start | bytes 1179652
  93.2 8.3 %copy-start.11 = (bf16[128,1536]{1,0:T(8,128)(2,1)}, bf16[128,1536]{1,0:T(8,128)(2,1)S(1)}, u32[]{:S(2)}) copy-start(bf16[128,1536]{1,0:T(8,128)(2,1)S(1)} %collective-permute-done.15.rest_2_) | copy-start | bytes 1179652
  104.7 15.4 %collective-permute-start.17 = (bf16[128,1536]{1,0:T(8,128)(2,1)}, bf16[128,1536]{1,0:T(8,128)(2,1)S(1)}, u32[]{:S(2)}, u32[]{:S(2)}) collective-permute-start(bf16[128,1536]{1,0:T(8,128)(2,1)} %get-tuple-element.79), channel_id=1, source_target_pairs={{0,1},{1,0},{2,3},{3,2},{4,5},{5,4},{6,7},{7,6},{8,9},{9,8},{10,11... | collective-permute-start | bytes 1179656 | tf_op jit(solution)/shard_map/ppermute | solution.py:55
  104.7 29.8 %collective-permute-start.18 = (bf16[128,1536]{1,0:T(8,128)(2,1)}, bf16[128,1536]{1,0:T(8,128)(2,1)S(1)}, u32[]{:S(2)}, u32[]{:S(2)}) collective-permute-start(bf16[128,1536]{1,0:T(8,128)(2,1)} %get-tuple-element.80), channel_id=1, source_target_pairs={{0,2},{1,3},{2,0},{3,1},{4,6},{5,7},{6,4},{7,5},{8,10},{9,11},{10,... | collective-permute-start | bytes 1179656 | tf_op jit(solution)/shard_map/ppermute | solution.py:55
  107.7 71.3 %copy-start.21 = (s32[8,16]{1,0:T(8,128)S(1)}, s32[8,16]{1,0:T(8,128)}, u32[]{:S(2)}) copy-start(s32[8,16]{1,0:T(8,128)} %param.24) | copy-start | bytes 1540
  107.7 71.7 %copy-start.22 = (s32[8]{0:T(128)S(1)}, s32[8]{0:T(128)}, u32[]{:S(2)}) copy-start(s32[8]{0:T(128)} %param.23) | copy-start | bytes 100
  107.7 71.7 %copy-start.23 = (s32[8]{0:T(128)S(1)}, s32[8]{0:T(128)}, u32[]{:S(2)}) copy-start(s32[8]{0:T(128)} %param.22) | copy-start | bytes 100
  107.8 33.7 %collective-permute-start.19 = (bf16[128,1536]{1,0:T(8,128)(2,1)}, bf16[128,1536]{1,0:T(8,128)(2,1)S(1)}, u32[]{:S(2)}, u32[]{:S(2)}) collective-permute-start(bf16[128,1536]{1,0:T(8,128)(2,1)} %get-tuple-element.81), channel_id=1, source_target_pairs={{0,3},{1,2},{2,1},{3,0},{4,7},{5,6},{6,5},{7,4},{8,11},{9,10},{10,... | collective-permute-start | bytes 1179656 | tf_op jit(solution)/shard_map/ppermute | solution.py:55
  120.1 59.6 %collective-permute-start.20 = (bf16[576,2240]{1,0:T(8,128)(2,1)S(1)}, bf16[576,2240]{1,0:T(8,128)(2,1)}, u32[]{:S(2)}, u32[]{:S(2)}) collective-permute-start(bf16[576,2240]{1,0:T(8,128)(2,1)S(1)} %pad_maximum_fusion.rest_4_), channel_id=1, source_target_pairs={{0,4},{4,0},{8,12},{12,8},{16,20},{20,16},{24,28},{28,24},{1,5},{5... | collective-permute-start | bytes 7741448 | tf_op jit(solution)/shard_map/ppermute | solution.py:55
  122.3 57.5 %collective-permute-start.23 = (bf16[576,2240]{1,0:T(8,128)(2,1)}, bf16[576,2240]{1,0:T(8,128)(2,1)}, u32[]{:S(2)}, u32[]{:S(2)}) collective-permute-start(bf16[576,2240]{1,0:T(8,128)(2,1)} %collective-permute-done.21.rest_6_), channel_id=1, source_target_pairs={{0,4},{4,0},{8,12},{12,8},{16,20},{20,16},{24,28},{28,24},{1,5},{5... | collective-permute-start | bytes 7741448 | tf_op jit(solution)/shard_map/ppermute | solution.py:55
  123.8 56.0 %collective-permute-start.24 = (bf16[576,2240]{1,0:T(8,128)(2,1)}, bf16[576,2240]{1,0:T(8,128)(2,1)}, u32[]{:S(2)}, u32[]{:S(2)}) collective-permute-start(bf16[576,2240]{1,0:T(8,128)(2,1)} %collective-permute-done.22.rest_8_), channel_id=1, source_target_pairs={{0,4},{4,0},{8,12},{12,8},{16,20},{20,16},{24,28},{28,24},{1,5},{5... | collective-permute-start | bytes 7741448 | tf_op jit(solution)/shard_map/ppermute | solution.py:55
  134.5 44.6 %copy-start.25 = (bf16[128,1536]{1,0:T(8,128)(2,1)}, bf16[128,1536]{1,0:T(8,128)(2,1)S(1)}, u32[]{:S(2)}) copy-start(bf16[128,1536]{1,0:T(8,128)(2,1)S(1)} %collective-permute-done.18.rest_2_) | copy-start | bytes 1179652
  134.5 21.1 %collective-permute-start.27 = (bf16[288,2240]{1,0:T(8,128)(2,1)S(1)}, bf16[288,2240]{1,0:T(8,128)(2,1)}, u32[]{:S(2)}, u32[]{:S(2)}) collective-permute-start(bf16[288,2240]{1,0:T(8,128)(2,1)S(1)} %slice.7), channel_id=1, source_target_pairs={{0,8},{4,12},{8,0},{12,4},{16,24},{20,28},{24,16},{28,20},{1,9},{5... | collective-permute-start | bytes 3870728 | tf_op jit(solution)/shard_map/ppermute | solution.py:55
  141.5 37.6 %copy-start.26 = (bf16[128,1536]{1,0:T(8,128)(2,1)}, bf16[128,1536]{1,0:T(8,128)(2,1)S(1)}, u32[]{:S(2)}) copy-start(bf16[128,1536]{1,0:T(8,128)(2,1)S(1)} %collective-permute-done.19.rest_3_) | copy-start | bytes 1179652
  141.5 37.6 %collective-permute-start.25 = (bf16[288,2240]{1,0:T(8,128)(2,1)S(1)}, bf16[288,2240]{1,0:T(8,128)(2,1)}, u32[]{:S(2)}, u32[]{:S(2)}) collective-permute-start(bf16[288,2240]{1,0:T(8,128)(2,1)S(1)} %slice.6), channel_id=1, source_target_pairs={{0,16},{4,20},{8,24},{12,28},{16,0},{20,4},{24,8},{28,12},{1,17},{... | collective-permute-start | bytes 3870728 | tf_op jit(solution)/shard_map/ppermute | solution.py:55
  155.6 24.2 %collective-permute-start.28 = (bf16[288,2240]{1,0:T(8,128)(2,1)}, bf16[288,2240]{1,0:T(8,128)(2,1)}, u32[]{:S(2)}, u32[]{:S(2)}) collective-permute-start(bf16[288,2240]{1,0:T(8,128)(2,1)} %collective-permute-done.27.rest_12_), channel_id=1, source_target_pairs={{0,4},{4,0},{8,12},{12,8},{16,20},{20,16},{24,28},{28,24},{1,5},{5... | collective-permute-start | bytes 3870728 | tf_op jit(solution)/shard_map/ppermute | solution.py:55
  179.1 3.4 %collective-permute-start.26 = (bf16[288,2240]{1,0:T(8,128)(2,1)}, bf16[288,2240]{1,0:T(8,128)(2,1)}, u32[]{:S(2)}, u32[]{:S(2)}) collective-permute-start(bf16[288,2240]{1,0:T(8,128)(2,1)} %collective-permute-done.25.rest_10_), channel_id=1, source_target_pairs={{0,4},{4,0},{8,12},{12,8},{16,20},{20,16},{24,28},{28,24},{1,5},{5... | collective-permute-start | bytes 3870728 | tf_op jit(solution)/shard_map/ppermute | solution.py:55
  202.5 8.0 %collective-permute-start.40 = (bf16[192,512]{1,0:T(8,128)(2,1)S(1)}, bf16[192,512]{1,0:T(8,128)(2,1)S(1)}, u32[]{:S(2)}, u32[]{:S(2)}) collective-permute-start(bf16[192,512]{1,0:T(8,128)(2,1)S(1)} %pad_maximum_fusion.4.rest_4_), channel_id=1, source_target_pairs={{0,24},{4,28},{8,16},{12,20},{16,8},{20,12},{24,0},{28,4},{1,25},{... | collective-permute-start | bytes 589832 | tf_op jit(solution)/shard_map/ppermute | solution.py:55
  202.5 17.2 %collective-permute-start.29 = (bf16[128,1536]{1,0:T(8,128)(2,1)}, bf16[128,1536]{1,0:T(8,128)(2,1)S(1)}, u32[]{:S(2)}, u32[]{:S(2)}) collective-permute-start(bf16[128,1536]{1,0:T(8,128)(2,1)} %get-tuple-element.91), channel_id=1, source_target_pairs={{0,1},{1,0},{2,3},{3,2},{4,5},{5,4},{6,7},{7,6},{8,9},{9,8},{10,11... | collective-permute-start | bytes 1179656 | tf_op jit(solution)/shard_map/ppermute | solution.py:55
  202.6 29.7 %collective-permute-start.30 = (bf16[128,1536]{1,0:T(8,128)(2,1)}, bf16[128,1536]{1,0:T(8,128)(2,1)S(1)}, u32[]{:S(2)}, u32[]{:S(2)}) collective-permute-start(bf16[128,1536]{1,0:T(8,128)(2,1)} %get-tuple-element.92), channel_id=1, source_target_pairs={{0,2},{1,3},{2,0},{3,1},{4,6},{5,7},{6,4},{7,5},{8,10},{9,11},{10,... | collective-permute-start | bytes 1179656 | tf_op jit(solution)/shard_map/ppermute | solution.py:55
  205.6 34.8 %collective-permute-start.31 = (bf16[128,1536]{1,0:T(8,128)(2,1)}, bf16[128,1536]{1,0:T(8,128)(2,1)S(1)}, u32[]{:S(2)}, u32[]{:S(2)}) collective-permute-start(bf16[128,1536]{1,0:T(8,128)(2,1)} %get-tuple-element.93), channel_id=1, source_target_pairs={{0,3},{1,2},{2,1},{3,0},{4,7},{5,6},{6,5},{7,4},{8,11},{9,10},{10,... | collective-permute-start | bytes 1179656 | tf_op jit(solution)/shard_map/ppermute | solution.py:55
  206.4 37.8 %collective-permute-start.38 = (bf16[192,512]{1,0:T(8,128)(2,1)S(1)}, bf16[192,512]{1,0:T(8,128)(2,1)S(1)}, u32[]{:S(2)}, u32[]{:S(2)}) collective-permute-start(bf16[192,512]{1,0:T(8,128)(2,1)S(1)} %pad_maximum_fusion.4.rest_4_), channel_id=1, source_target_pairs={{0,16},{4,20},{8,24},{12,28},{16,0},{20,4},{24,8},{28,12},{1,17},{... | collective-permute-start | bytes 589832 | tf_op jit(solution)/shard_map/ppermute | solution.py:55
  210.5 70.4 %copy-start.15 = (bf16[192,512]{1,0:T(8,128)(2,1)}, bf16[192,512]{1,0:T(8,128)(2,1)S(1)}, u32[]{:S(2)}) copy-start(bf16[192,512]{1,0:T(8,128)(2,1)S(1)} %collective-permute-done.40.rest_10_) | copy-start | bytes 589828
  210.5 36.7 %collective-permute-start.36 = (bf16[192,512]{1,0:T(8,128)(2,1)S(1)}, bf16[192,512]{1,0:T(8,128)(2,1)S(1)}, u32[]{:S(2)}, u32[]{:S(2)}) collective-permute-start(bf16[192,512]{1,0:T(8,128)(2,1)S(1)} %pad_maximum_fusion.4.rest_4_), channel_id=1, source_target_pairs={{0,8},{4,12},{8,0},{12,4},{16,24},{20,28},{24,16},{28,20},{1,9},{5... | collective-permute-start | bytes 589832 | tf_op jit(solution)/shard_map/ppermute | solution.py:55
  219.7 20.8 %copy-start.7 = (bf16[128,1536]{1,0:T(8,128)(2,1)}, bf16[128,1536]{1,0:T(8,128)(2,1)S(1)}, u32[]{:S(2)}) copy-start(bf16[128,1536]{1,0:T(8,128)(2,1)S(1)} %collective-permute-done.29.rest_1_) | copy-start | bytes 1179652
  219.7 31.2 %collective-permute-start.35 = (bf16[192,512]{1,0:T(8,128)(2,1)S(1)}, bf16[192,512]{1,0:T(8,128)(2,1)}, u32[]{:S(2)}, u32[]{:S(2)}) collective-permute-start(bf16[192,512]{1,0:T(8,128)(2,1)S(1)} %pad_maximum_fusion.4.rest_4_), channel_id=1, source_target_pairs={{0,4},{4,0},{8,12},{12,8},{16,20},{20,16},{24,28},{28,24},{1,5},{5... | collective-permute-start | bytes 589832 | tf_op jit(solution)/shard_map/ppermute | solution.py:55
  232.3 8.2 %copy-start.8 = (bf16[128,1536]{1,0:T(8,128)(2,1)}, bf16[128,1536]{1,0:T(8,128)(2,1)S(1)}, u32[]{:S(2)}) copy-start(bf16[128,1536]{1,0:T(8,128)(2,1)S(1)} %collective-permute-done.30.rest_2_) | copy-start | bytes 1179652
  232.3 18.7 %collective-permute-start.41 = (bf16[192,512]{1,0:T(8,128)(2,1)S(1)}, bf16[192,512]{1,0:T(8,128)(2,1)}, u32[]{:S(2)}, u32[]{:S(2)}) collective-permute-start(bf16[192,512]{1,0:T(8,128)(2,1)S(1)} %collective-permute-done.40.rest_10_), channel_id=1, source_target_pairs={{0,4},{4,0},{8,12},{12,8},{16,20},{20,16},{24,28},{28,24},{1,5},{5... | collective-permute-start | bytes 589832 | tf_op jit(solution)/shard_map/ppermute | solution.py:55
  244.1 15.4 %collective-permute-start.32 = (bf16[128,1536]{1,0:T(8,128)(2,1)}, bf16[128,1536]{1,0:T(8,128)(2,1)S(1)}, u32[]{:S(2)}, u32[]{:S(2)}) collective-permute-start(bf16[128,1536]{1,0:T(8,128)(2,1)} %get-tuple-element.95), channel_id=1, source_target_pairs={{0,1},{1,0},{2,3},{3,2},{4,5},{5,4},{6,7},{7,6},{8,9},{9,8},{10,11... | collective-permute-start | bytes 1179656 | tf_op jit(solution)/shard_map/ppermute | solution.py:55
  244.1 36.8 %copy-start.16 = (bf16[192,512]{1,0:T(8,128)(2,1)}, bf16[192,512]{1,0:T(8,128)(2,1)S(1)}, u32[]{:S(2)}) copy-start(bf16[192,512]{1,0:T(8,128)(2,1)S(1)} %collective-permute-done.38.rest_8_) | copy-start | bytes 589828
  244.1 29.7 %collective-permute-start.33 = (bf16[128,1536]{1,0:T(8,128)(2,1)}, bf16[128,1536]{1,0:T(8,128)(2,1)S(1)}, u32[]{:S(2)}, u32[]{:S(2)}) collective-permute-start(bf16[128,1536]{1,0:T(8,128)(2,1)} %get-tuple-element.96), channel_id=1, source_target_pairs={{0,2},{1,3},{2,0},{3,1},{4,6},{5,7},{6,4},{7,5},{8,10},{9,11},{10,... | collective-permute-start | bytes 1179656 | tf_op jit(solution)/shard_map/ppermute | solution.py:55
  247.1 33.8 %copy-start.17 = (bf16[192,512]{1,0:T(8,128)(2,1)}, bf16[192,512]{1,0:T(8,128)(2,1)S(1)}, u32[]{:S(2)}) copy-start(bf16[192,512]{1,0:T(8,128)(2,1)S(1)} %collective-permute-done.36.rest_6_) | copy-start | bytes 589828
  247.1 33.7 %collective-permute-start.34 = (bf16[128,1536]{1,0:T(8,128)(2,1)}, bf16[128,1536]{1,0:T(8,128)(2,1)S(1)}, u32[]{:S(2)}, u32[]{:S(2)}) collective-permute-start(bf16[128,1536]{1,0:T(8,128)(2,1)} %get-tuple-element.97), channel_id=1, source_target_pairs={{0,3},{1,2},{2,1},{3,0},{4,7},{5,6},{6,5},{7,4},{8,11},{9,10},{10,... | collective-permute-start | bytes 1179656 | tf_op jit(solution)/shard_map/ppermute | solution.py:55
  250.9 1.5 collective-permute-start.39
  251.0 1.7 collective-permute-start.37
  252.4 28.5 %copy-start.18 = (bf16[192,512]{1,0:T(8,128)(2,1)}, bf16[192,512]{1,0:T(8,128)(2,1)S(1)}, u32[]{:S(2)}) copy-start(bf16[192,512]{1,0:T(8,128)(2,1)S(1)} %collective-permute-done.39.rest_9_) | copy-start | bytes 589828
  252.7 28.2 %copy-start.19 = (bf16[192,512]{1,0:T(8,128)(2,1)}, bf16[192,512]{1,0:T(8,128)(2,1)S(1)}, u32[]{:S(2)}) copy-start(bf16[192,512]{1,0:T(8,128)(2,1)S(1)} %collective-permute-done.37.rest_7_) | copy-start | bytes 589828
  259.5 21.4 %copy-start.12 = (bf16[128,1536]{1,0:T(8,128)(2,1)}, bf16[128,1536]{1,0:T(8,128)(2,1)S(1)}, u32[]{:S(2)}) copy-start(bf16[128,1536]{1,0:T(8,128)(2,1)S(1)} %collective-permute-done.32.rest_1_) | copy-start | bytes 1179652
  273.9 7.1 %copy-start.13 = (bf16[128,1536]{1,0:T(8,128)(2,1)}, bf16[128,1536]{1,0:T(8,128)(2,1)S(1)}, u32[]{:S(2)}) copy-start(bf16[128,1536]{1,0:T(8,128)(2,1)S(1)} %collective-permute-done.33.rest_2_) | copy-start | bytes 1179652
  (6 other events, 9.8 us)

commit v5 on v4

--- a/solution.py
+++ b/solution.py
@@ -66,28 +66,6 @@
 
 def after(values, *tokens):
     return lax.optimization_barrier((tuple(values), tokens))[0]
-
-
-class Relay:
-    def __init__(self, value, size):
-        self.size = size
-        if size != 8:
-            self.pieces = [(m, 0, piece) for m, piece in enumerate(wide_pieces(value, size))]
-            return
-        self.across = exchange(value, "wide", 8, 2)
-        self.along = exchange(value, "wide", 8, 4)
-        self.pieces = [(0, 0, value), (1, 0, exchange(value, "wide", 8, 1))]
-
-    def pass_on(self, *tokens):
-        if self.size != 8:
-            return
-        across, along = after([self.across, self.along], *tokens)
-        half = across.shape[0] // 2
-        top = exchange(across[:half], "wide", 8, 4)
-        low = exchange(along[half:], "wide", 8, 2)
-        for mask, offset, piece in ((2, 0, across), (4, 0, along), (6, 0, top), (6, half, low)):
-            self.pieces.append((mask, offset, piece))
-            self.pieces.append((mask | 1, offset, exchange(piece, "wide", 8, 1)))
 
 
 def narrow_swap(pieces, size):
@@ -133,72 +111,73 @@
     out_ref[...] = weight[:, heads * HD :]
 
 
-def attend_kernel(wide, narrow, key_block, wide_ref, narrow_ref, spots_ref, starts_ref, q_ref, w_out, *rest):
-    kv_pieces, rest = rest[:wide], rest[wide:]
-    part_refs, (kv_out, keyvals, mix, kv_sems, flush_sem) = rest[:narrow], rest[narrow:]
+def attend_kernel(wide, shares, wide_ref, narrow_ref, spots_ref, starts_ref, q_ref, w_out, *rest):
+    first_call = len(rest) > 4
     wide_index, narrow_index = wide_ref[0], narrow_ref[0]
-    kv_copies = place_copies(kv_pieces, keyvals, kv_sems, wide_index)
-    for c in kv_copies:
-        c.start()
-    for c in kv_copies:
-        c.wait()
-    flush = pltpu.make_async_copy(keyvals, kv_out, flush_sem)
-    flush.start()
+    if first_call:
+        kv_pieces, rest = rest[:wide], rest[wide:]
+        part_refs, (kv_out, keyvals, mix, kv_sems, flush_sem) = rest[:2], rest[2:]
+        kv_copies = place_copies(kv_pieces, keyvals, kv_sems, wide_index)
+        for c in kv_copies:
+            c.start()
+        for c in kv_copies:
+            c.wait()
+        flush = pltpu.make_async_copy(keyvals, kv_out, flush_sem)
+        flush.start()
+    else:
+        keyvals, *part_refs, mix = rest
+    share = part_refs[0].shape[0]
+    tile = 2 * share
     tok_rows = q_ref.shape[0]
     heads = q_ref.shape[1] // HD
-    tile = key_block
     row_base = wide_index * tok_rows
     factor = HD ** (-0.5) * math.log2(math.e)
-    for t in range(tok_rows // tile):
-        rows = slice(t * tile, (t + 1) * tile)
-        stacked = jnp.concatenate(
-            [q_ref[rows, h * HD : (h + 1) * HD] for h in range(heads)], axis=0
-        )
-        first = row_base + t * tile
-        diagonal = first // tile
-        lowest = spots_ref[t * tile] // tile
-        whole_from = (spots_ref[(t + 1) * tile - 1] + tile - 1) // tile
-        starts = jnp.concatenate([starts_ref[rows, :]] * heads, axis=0)
-        own = first + lax.broadcasted_iota(jnp.int32, (tile, 1), 0)
-        own = jnp.concatenate([own] * heads, axis=0)
-
-        def visit(block, state, masked, stacked=stacked, starts=starts, own=own):
-            top, total, mixed = state
-            begin = pl.multiple_of(block * tile, tile)
-            keys = keyvals[pl.ds(begin, tile), :HD]
-            values = keyvals[pl.ds(begin, tile), HD:]
-            scores = contract_last(stacked, keys) * factor
-            if masked:
-                spot = begin + lax.broadcasted_iota(jnp.int32, (1, tile), 1)
-                scores = jnp.where((spot >= starts) & (spot <= own), scores, masked_score)
-            new_top = jnp.maximum(top, jnp.max(scores, axis=1, keepdims=True))
-            weights = jnp.exp2(scores - new_top)
-            scale = jnp.exp2(top - new_top)
-            total = total * scale + jnp.sum(weights, axis=1, keepdims=True)
-            mixed = mixed * scale + jnp.dot(
-                weights.astype(bf16), values, preferred_element_type=f32
-            )
-            return new_top, total, mixed
-
-        count = heads * tile
-        state = (
-            jnp.full((count, 1), masked_score, f32),
-            jnp.zeros((count, 1), f32),
-            jnp.zeros((count, HD), f32),
-        )
-        state = visit(diagonal, state, True)
-        split = jnp.minimum(whole_from, diagonal)
-        state = lax.fori_loop(lowest, split, lambda b, s: visit(b, s, True), state)
-        split = jnp.maximum(split, lowest)
-        _, total, mixed = lax.fori_loop(split, diagonal, lambda b, s: visit(b, s, False), state)
-        mixed = (mixed / total).astype(bf16)
-        for h in range(heads):
-            mix[rows, h * HD : (h + 1) * HD] = mixed[h * tile : (h + 1) * tile]
-    share = tok_rows // narrow
-    for k in range(narrow):
-        start = pl.multiple_of((narrow_index ^ k) * share, share)
-        part_refs[k][...] = contract_last(mix[pl.ds(start, share), :], w_out[...]).astype(bf16)
-    flush.wait()
+    begin_row = pl.multiple_of(((narrow_index ^ shares[0]) // 2) * tile, tile)
+    rows = pl.ds(begin_row, tile)
+    stacked = jnp.concatenate([q_ref[rows, h * HD : (h + 1) * HD] for h in range(heads)], axis=0)
+    first = row_base + begin_row
+    diagonal = first // tile
+    lowest = spots_ref[begin_row] // tile
+    whole_from = (spots_ref[begin_row + tile - 1] + tile - 1) // tile
+    starts = jnp.concatenate([starts_ref[rows, :]] * heads, axis=0)
+    own = first + lax.broadcasted_iota(jnp.int32, (tile, 1), 0)
+    own = jnp.concatenate([own] * heads, axis=0)
+
+    def visit(block, state, masked):
+        top, total, mixed = state
+        begin = pl.multiple_of(block * tile, tile)
+        keys = keyvals[pl.ds(begin, tile), :HD]
+        values = keyvals[pl.ds(begin, tile), HD:]
+        scores = contract_last(stacked, keys) * factor
+        if masked:
+            spot = begin + lax.broadcasted_iota(jnp.int32, (1, tile), 1)
+            scores = jnp.where((spot >= starts) & (spot <= own), scores, masked_score)
+        new_top = jnp.maximum(top, jnp.max(scores, axis=1, keepdims=True))
+        weights = jnp.exp2(scores - new_top)
+        scale = jnp.exp2(top - new_top)
+        total = total * scale + jnp.sum(weights, axis=1, keepdims=True)
+        mixed = mixed * scale + jnp.dot(weights.astype(bf16), values, preferred_element_type=f32)
+        return new_top, total, mixed
+
+    count = heads * tile
+    state = (
+        jnp.full((count, 1), masked_score, f32),
+        jnp.zeros((count, 1), f32),
+        jnp.zeros((count, HD), f32),
+    )
+    state = visit(diagonal, state, True)
+    split = jnp.minimum(whole_from, diagonal)
+    state = lax.fori_loop(lowest, split, lambda b, s: visit(b, s, True), state)
+    split = jnp.maximum(split, lowest)
+    _, total, mixed = lax.fori_loop(split, diagonal, lambda b, s: visit(b, s, False), state)
+    mixed = (mixed / total).astype(bf16)
+    for h in range(heads):
+        mix[:, h * HD : (h + 1) * HD] = mixed[h * tile : (h + 1) * tile]
+    for k, part_ref in zip(shares, part_refs):
+        start = pl.multiple_of(((narrow_index ^ k) % 2) * share, share)
+        part_ref[...] = contract_last(mix[pl.ds(start, share), :], w_out[...]).astype(bf16)
+    if first_call:
+        flush.wait()
 
 
 def join_kernel(narrow, base_ref, gain_ref, *rest):
@@ -214,34 +193,20 @@
         out[...] = rounded
 
 
-def ffn_kernel(narrow, piece_rows, spots, wide_ref, *rest):
-    x_refs, rest = rest[:narrow], rest[narrow:]
-    piece_refs, rest = rest[: len(spots)], rest[len(spots) :]
-    part_refs, (x, held, gate, hidden, sems) = rest[:narrow], rest[narrow:]
-    copies = [[], [], []]
-    for j in range(3):
-        for (mask, offset), piece in zip(spots, piece_refs):
-            low = max(offset, j * piece_rows)
-            high = min(offset + piece.shape[0], (j + 1) * piece_rows)
-            if low >= high:
-                continue
-            start = (wide_ref[0] ^ mask) * piece_rows + low - j * piece_rows
-            target = held.at[j, pl.ds(pl.multiple_of(start, 16), high - low)]
-            source = piece.at[pl.ds(low - offset, high - low)]
-            sem = sems.at[j, len(copies[j])]
-            copies[j].append(pltpu.make_async_copy(source, target, sem))
-    for c in copies[0] + copies[1] + copies[2]:
+def ffn_kernel(count, *rest):
+    x_refs, weights_ref, rest = rest[:count], rest[count], rest[count + 1 :]
+    part_refs, (x, held, gate, hidden, sems) = rest[:count], rest[count:]
+    copies = [
+        pltpu.make_async_copy(weights_ref.at[:, j], held.at[j], sems.at[j]) for j in range(3)
+    ]
+    for c in copies:
         c.start()
     share = x_refs[0].shape[0]
-    for k in range(narrow):
+    for k in range(len(x_refs)):
         x[k * share : (k + 1) * share, :] = x_refs[k][...]
-    depth, width = held.shape[1:]
+    depth, width = x.shape[1], hidden.shape[1]
     tile = 256
     whole = width // tile
-
-    def arrive(j):
-        for c in copies[j]:
-            c.wait()
 
     def each_tile(body):
         @pl.loop(0, whole)
@@ -251,24 +216,30 @@
         if width % tile:
             body(slice(whole * tile, width))
 
+    def block(j, lanes):
+        part = held[j, :, :, lanes]
+        return part.reshape(depth, part.shape[-1])
+
     def gate_tile(lanes):
-        gate[:, lanes] = jnp.dot(x[...], held[0, :, lanes], preferred_element_type=f32)
+        gate[:, lanes] = jnp.dot(x[...], block(0, lanes), preferred_element_type=f32)
 
     def up_tile(lanes):
-        up = jnp.dot(x[...], held[1, :, lanes], preferred_element_type=f32)
+        up = jnp.dot(x[...], block(1, lanes), preferred_element_type=f32)
         value = gate[:, lanes]
         hidden[:, lanes] = (value / (1.0 + jnp.exp(-value)) * up).astype(bf16)
 
-    arrive(0)
+    copies[0].wait()
     each_tile(gate_tile)
-    arrive(1)
+    copies[1].wait()
     each_tile(up_tile)
-    arrive(2)
-    group = 768
-    for g in range(depth // group):
-        lanes = slice(g * group, (g + 1) * group)
-        product = contract_last(hidden[...], held[2, lanes, :])
-        for k in range(narrow):
+    copies[2].wait()
+    pieces, rows = held.shape[1], held.shape[2]
+    group = 768 // rows
+    for g in range(pieces // group):
+        lanes = slice(g * group * rows, (g + 1) * group * rows)
+        down = held[2, g * group : (g + 1) * group].reshape(group * rows, width)
+        product = contract_last(hidden[...], down)
+        for k in range(len(x_refs)):
             part_refs[k][:, lanes] = product[k * share : (k + 1) * share].astype(bf16)
 
 
@@ -377,9 +348,10 @@
     mlp_row = mlp_gain.astype(f32)[None]
     next_row = next_gain.astype(f32)[None]
     starts_column = token_start[:, None]
-    packed = jnp.concatenate([w_gate, w_up, w_down.T])
+    packed = jnp.stack([w_gate, w_up, w_down.T])
+    (packed,) = after([packed], *qkv_pieces[2::2])
+    ffn_weights = lax.all_gather(packed, "wide", axis=0, tiled=False)
     early = (
-        packed,
         cosine,
         sine,
         qkv_bias,
@@ -391,8 +363,8 @@
         starts_column,
     )
     early, qkv_pieces = lax.optimization_barrier((early, qkv_pieces))
-    packed, cosine, sine, qkv_bias, next_weight, next_bias, base_rows = early[:7]
-    mlp_row, next_row, starts_column = early[7:]
+    cosine, sine, qkv_bias, next_weight, next_bias, base_rows = early[:6]
+    mlp_row, next_row, starts_column = early[6:]
 
     qkv_width = query_width + 2 * HD
     queries, keyvals, out_weight = pl.pallas_call(
@@ -424,39 +396,45 @@
 
     kv_pieces = wide_pieces(keyvals, wide)
 
-    (packed,) = after([packed], *kv_pieces[2::2])
-    relay = Relay(packed, wide)
-
-    tile = 256
     total_rows = wide * tok_rows
-    *parts, kv_all = pl.pallas_call(
-        functools.partial(attend_kernel, wide, narrow, tile),
-        out_shape=[jax.ShapeDtypeStruct((share, depth), bf16)] * narrow
-        + [jax.ShapeDtypeStruct((total_rows, 2 * HD), bf16)],
-        in_specs=[smem_spec()] * 3 + [vmem_spec()] * 3 + [any_spec()] * wide,
-        out_specs=[vmem_spec()] * narrow + [hbm_spec()],
-        scratch_shapes=[
+    share_shape = jax.ShapeDtypeStruct((share, depth), bf16)
+
+    def attend(shares, first_call, sources):
+        kv_shape = jax.ShapeDtypeStruct((total_rows, 2 * HD), bf16)
+        mix = VMEM((2 * share, query_width), bf16)
+        gather_scratch = [
             VMEM((total_rows, 2 * HD), bf16),
-            VMEM((tok_rows, query_width), bf16),
+            mix,
             pltpu.SemaphoreType.DMA((wide,)),
             pltpu.SemaphoreType.DMA,
-        ],
-        compiler_params=params(60),
-        cost_estimate=pl.CostEstimate(
-            flops=8 * tok_rows * query_width * depth,
-            bytes_accessed=4 * total_rows * HD,
-            transcendentals=tok_rows * depth,
-        ),
-        name="attend",
-    )(
-        wide_index[None],
-        narrow_index[None],
-        token_start,
-        starts_column,
-        queries,
-        out_weight,
-        *kv_pieces,
-    )
+        ]
+        source_specs = [any_spec()] * wide if first_call else [vmem_spec()]
+        return pl.pallas_call(
+            functools.partial(attend_kernel, wide, shares),
+            out_shape=[share_shape] * 2 + [kv_shape] * first_call,
+            in_specs=[smem_spec()] * 3 + [vmem_spec()] * 3 + source_specs,
+            out_specs=[vmem_spec()] * 2 + [hbm_spec()] * first_call,
+            scratch_shapes=gather_scratch if first_call else [mix],
+            compiler_params=params(60 if first_call else 24),
+            cost_estimate=pl.CostEstimate(
+                flops=4 * tok_rows * query_width * depth,
+                bytes_accessed=4 * total_rows * HD,
+                transcendentals=tok_rows * depth,
+            ),
+            name="attend",
+        )(
+            wide_index[None],
+            narrow_index[None],
+            token_start,
+            starts_column,
+            queries,
+            out_weight,
+            *sources,
+        )
+
+    far_two, far_three, kv_all = attend((2, 3), True, kv_pieces)
+    near_zero, near_one = attend((0, 1), False, [kv_all])
+    parts = [near_zero, near_one, far_two, far_three]
 
     def join(parts, base_rows, gain, with_norm):
         shape = jax.ShapeDtypeStruct((share, depth), bf16)
@@ -478,35 +456,38 @@
     cache_block = fill_pages(
         source, seg_lengths, seg_offsets, block_table, wide_index * page_count, page_count
     )
-    relay.pass_on(normed_pieces[1])
-    normed_pieces = after(normed_pieces, cache_block)
-    spots = [(mask, offset) for mask, offset, _ in relay.pieces]
-    bulk = [piece for _, _, piece in relay.pieces]
-    parts = pl.pallas_call(
-        functools.partial(ffn_kernel, narrow, piece_rows, spots),
-        out_shape=[jax.ShapeDtypeStruct((share, depth), bf16)] * narrow,
-        in_specs=[smem_spec()] + [vmem_spec()] * narrow + [hbm_spec()] * len(bulk),
-        out_specs=[vmem_spec()] * narrow,
-        scratch_shapes=[
-            VMEM((tok_rows, depth), bf16),
-            VMEM((3, depth, width), bf16),
-            VMEM((tok_rows, width), f32),
-            VMEM((tok_rows, width), bf16),
-            pltpu.SemaphoreType.DMA((3, len(spots))),
-        ],
-        compiler_params=params(60),
-        cost_estimate=pl.CostEstimate(
-            flops=6 * tok_rows * depth * width,
-            bytes_accessed=6 * depth * width,
-            transcendentals=tok_rows * width,
-        ),
-        name="ffn",
-    )(wide_index[None], *normed_pieces, *bulk)
+    def feed_forward(x_shares):
+        count = len(x_shares)
+        return pl.pallas_call(
+            functools.partial(ffn_kernel, count),
+            out_shape=[share_shape] * count,
+            in_specs=[vmem_spec()] * count + [hbm_spec()],
+            out_specs=[vmem_spec()] * count,
+            scratch_shapes=[
+                VMEM((count * share, depth), bf16),
+                VMEM((3, wide, piece_rows, width), bf16),
+                VMEM((count * share, width), f32),
+                VMEM((count * share, width), bf16),
+                pltpu.SemaphoreType.DMA((3,)),
+            ],
+            compiler_params=params(60 if x_shares is far else 44),
+            cost_estimate=pl.CostEstimate(
+                flops=6 * count * share * depth * width,
+                bytes_accessed=6 * depth * width,
+                transcendentals=count * share * width,
+            ),
+            name="ffn",
+        )(*x_shares, ffn_weights)
+
+    far = normed_pieces[2:]
+    far_two, far_three = feed_forward(far)
+    near_zero, near_one = feed_forward(list(after(normed_pieces[:2], far_two)))
+    parts = [near_zero, near_one, far_two, far_three]
 
     hidden_rows = join(narrow_swap(parts, narrow), residual, mlp_row, False)
     hidden_pieces = narrow_swap(hidden_rows, narrow)
 
-    (next_weight,) = after([next_weight], parts[0])
+    (next_weight,) = after([next_weight], far_two)
     next_pieces = wide_pieces(next_weight, wide)
     next_width = query_width + HD
     hidden_out, next_query, next_keyval = pl.pallas_call(
@@ -519,7 +500,7 @@
         in_specs=[smem_spec()] * 2 + [vmem_spec()] * (2 + narrow) + [any_spec()] * wide,
         out_specs=(vmem_spec(),) * 3,
         scratch_shapes=[VMEM((depth, next_width), bf16), pltpu.SemaphoreType.DMA((wide,))],
-        compiler_params=params(60),
+        compiler_params=params(40),
         cost_estimate=pl.CostEstimate(
             flops=2 * tok_rows * depth * next_width,
             bytes_accessed=2 * depth * (2 * tok_rows + next_width),

time: 290 us -> 272 us (0.938)
  waiting for transfers between devices: 173 us -> 141 us
  between operations: 1.18 us -> 14.6 us
  Pallas kernels: 47.5 us -> 56.2 us
  starting transfers between devices: 35.9 us -> 29.8 us
    ppermute x42 -> x33, waiting for transfers between devices: 173 us -> 141 us  [exchange(): return lax.ppermute(value, axis, [(i, i ^ mask) for i in range(size)])]
    pallas_call x2 -> x4, Pallas kernels: 30 us -> 37.7 us  [the longest x2 25.7 us: feed_forward(): pl.pallas_call(functools.partial(ffn_kernel, count), out_shape=[share_sha...]
    ppermute x42 -> x33, starting transfers between devices: 35.9 us -> 29.8 us  [exchange(): return lax.ppermute(value, axis, [(i, i ^ mask) for i in range(size)])]
    unnamed x56 -> x88, local copies, waits for them, and re-layouts: 3.25 us -> 9.06 us
    another operation x0 -> x1, other arithmetic: none -> 3.49 us  [local(): packed = jnp.stack([w_gate, w_up, w_down.T])]
  transfers between devices with their start and end apart: 42 -> 34, of which waited for: 25 -> 18; matrix products, arithmetic and copies ran while one was open for 9% -> 7% of each run, Pallas kernels for 6% -> 19%
where the time goes in v5:
time: 272 us; the launch traced here: 271 us
  waiting for transfers between devices  141 us (52%)
  Pallas kernels  56.2 us (21%)
  starting transfers between devices  29.8 us (11%)
  local copies, waits for them, and re-layouts  20.1 us (7%)
  between operations  14.6 us (5%)
  other arithmetic  9.11 us (3%)
    ppermute x33, waiting for transfers between devices, exchange(): return lax.ppermute(value, axis, [(i, i ^ mask) for i in range(size)])  141 us
    ppermute x33, starting transfers between devices, exchange(): return lax.ppermute(value, axis, [(i, i ^ mask) for i in range(size)])  29.8 us
    pallas_call x2, Pallas kernels, feed_forward(): pl.pallas_call(functools.partial(ffn_kernel, count), out_shape=[share_sha...  25.7 us
    pallas_call x2, Pallas kernels, attend(): pl.pallas_call(functools.partial(attend_kernel, wide, shares), out_shape=...  12 us
    unnamed x88, local copies, waits for them, and re-layouts  9.06 us
    pallas_call x1, Pallas kernels, local(): pl.pallas_call(functools.partial(qkv_kernel, wide), out_shape=(jax.ShapeD...  6.68 us
    pallas_call x2, Pallas kernels, join(): pl.pallas_call(functools.partial(join_kernel, narrow), out_shape=[shape]...  6.09 us
    pallas_call x1, Pallas kernels, local(): pl.pallas_call(functools.partial(next_kernel, wide, narrow), out_shape=(j...  5.74 us
  transfers between devices with their start and end apart: 34, of which 18 were waited for; matrix products, arithmetic and copies ran while one was open for 7% of the time, Pallas kernels for 19%

profile of v5, /device:TPU:10, one launch (start us, length us, event | category | flops | bytes accessed | tf_op | source)
XLA Modules:
  0.0 271.1 jit_solution(272831355733152048)
XLA Ops:
  7.2 0.8 copy-done
  8.1 1.0 pad_maximum_fusion.1.rest_0_
  9.1 1.6 collective-permute-start.5
  11.2 1.5 collective-permute-start.1
  12.7 3.5 %pad_maximum_fusion = bf16[3,192,2240]{2,1,0:T(8,128)(2,1)} fusion(bf16[1,192,2240]{2,1,0:T(8,128)(2,1)} %bitcast.22, bf16[1,192,2240]{2,1,0:T(8,128)(2,1)} %bitcast.23, bf16[1,192,2240]{2,1,0:T(8,128)(2,1)} %bitcast.24), kind=kLoop, calls=%fused_computation.1 | loop fusion | flops 2580480 | bytes 5160960 | tf_op jit(solution)/shard_map/stack | solution.py:351
  16.2 5.9 %collective-permute-done.5.rest_6_ = bf16[192,1024]{1,0:T(8,128)(2,1)S(1)} collective-permute-done((bf16[192,1024]{1,0:T(8,128)(2,1)S(1)}, bf16[192,1024]{1,0:T(8,128)(2,1)S(1)}, u32[]{:S(2)}, u32[]{:S(2)}) %collective-permute-start.5) | collective-permute-done | bytes 393248 | tf_op jit(solution)/shard_map/ppermute | solution.py:55
  22.2 7.2 %collective-permute-done.3.rest_4_ = bf16[192,1024]{1,0:T(8,128)(2,1)S(1)} collective-permute-done((bf16[192,1024]{1,0:T(8,128)(2,1)S(1)}, bf16[192,1024]{1,0:T(8,128)(2,1)S(1)}, u32[]{:S(2)}, u32[]{:S(2)}) %collective-permute-start.3) | collective-permute-done | bytes 393248 | tf_op jit(solution)/shard_map/ppermute | solution.py:55
  29.9 0.6 maximum_convert_fusion.bias_ref
  30.5 0.8 constant_dynamic-slice_fusion.2
  31.4 1.0 fusion
  33.4 1.3 reshape.200.gain_ref
  34.7 1.3 reshape.198.gain_ref
  36.0 0.7 reshape.199.gain_ref
  36.7 1.0 pad_maximum_fusion.2
  37.7 1.9 constant_dynamic-slice_fusion.1.base_ref
  39.6 0.7 copy-done.20
  40.5 6.7 %qkv.1 = (bf16[512,384]{1,0:T(8,128)(2,1)}, bf16[512,256]{1,0:T(8,128)(2,1)}, bf16[1536,384]{1,0:T(8,128)(2,1)}) custom-call(s32[1]{0:T(128)} %bitcast.index_ref.wide_ref, bf16[512,1536]{1,0:T(8,128)(2,1)} %hidden_ref.1, f32[1,1536]{1,0:T(1,128)} %reshape.200.gain_ref, f32[1,640]{1,0:T(1,128)} %maximum_convert_fusion.bias_ref, ...), custom_call_target="tpu_custom_call" | custom-call | flops 1006632960 | bytes 3538944 | tf_op jit(solution)/shard_map/qkv/pallas_call | solution.py:370
  47.2 1.5 collective-permute-start.12
  48.7 0.6 collective-permute-start.10
  49.3 1.5 collective-permute-start.8
  50.7 12.4 %collective-permute-done.12.rest_6_ = bf16[512,256]{1,0:T(8,128)(2,1)S(1)} collective-permute-done((bf16[512,256]{1,0:T(8,128)(2,1)}, bf16[512,256]{1,0:T(8,128)(2,1)S(1)}, u32[]{:S(2)}, u32[]{:S(2)}) %collective-permute-start.12) | collective-permute-done | bytes 262176 | tf_op jit(solution)/shard_map/ppermute | solution.py:55
  63.1 5.4 %collective-permute-done.10.rest_4_ = bf16[512,256]{1,0:T(8,128)(2,1)S(1)} collective-permute-done((bf16[512,256]{1,0:T(8,128)(2,1)}, bf16[512,256]{1,0:T(8,128)(2,1)S(1)}, u32[]{:S(2)}, u32[]{:S(2)}) %collective-permute-start.10) | collective-permute-done | bytes 262176 | tf_op jit(solution)/shard_map/ppermute | solution.py:55
  68.5 5.2 %collective-permute-done.8.rest_2_ = bf16[512,256]{1,0:T(8,128)(2,1)S(1)} collective-permute-done((bf16[512,256]{1,0:T(8,128)(2,1)}, bf16[512,256]{1,0:T(8,128)(2,1)S(1)}, u32[]{:S(2)}, u32[]{:S(2)}) %collective-permute-start.8) | collective-permute-done | bytes 262176 | tf_op jit(solution)/shard_map/ppermute | solution.py:55
  73.7 0.9 copy.29.starts_ref
  74.7 0.7 collective-permute-done.9.rest_3_
  75.4 7.9 %attend.2 = (bf16[128,1536]{1,0:T(8,128)(2,1)}, bf16[128,1536]{1,0:T(8,128)(2,1)}, bf16[4096,256]{1,0:T(8,128)(2,1)}) custom-call(s32[1]{0:T(128)} %bitcast.index_ref.wide_ref, s32[1]{0:T(128)} %bitcast.1.narrow_ref, s32[512]{0:T(512)} %copy-done.12, s32[512,1]{1,0:T(8,128)} %copy.29.starts_ref, bf16[512,384]{1,0:T(8,128)(2,1)} %get-tuple-element.65.q_ref, ...), custom_call_target="tpu_custom_call" | custom-call | flops 1207959552 | bytes 2097152 | tf_op jit(solution)/shard_map/attend/pallas_call | solution.py:412
  83.4 1.9 collective-permute-start.15
  85.3 1.6 copy-done.1
  86.9 4.1 %attend.3 = (bf16[128,1536]{1,0:T(8,128)(2,1)S(1)}, bf16[128,1536]{1,0:T(8,128)(2,1)S(1)}) custom-call(s32[1]{0:T(128)} %bitcast.index_ref.wide_ref, s32[1]{0:T(128)} %bitcast.1.narrow_ref, s32[512]{0:T(512)S(1)} %copy-done.13, s32[512,1]{1,0:T(8,128)S(1)} %copy-done.7, bf16[512,384]{1,0:T(8,128)(2,1)S(1)} %copy-done.15, bf16[1536,384]{1,0:T(8,128)(2,1)S(1)} %copy-done.14, ...), custom_call_target="tpu_custom_call" | custom-call | flops 1207959552 | bytes 2097152 | tf_op jit(solution)/shard_map/attend/pallas_call | solution.py:412
  91.0 0.7 copy-done.4
  91.7 0.7 collective-permute-start.16
  92.4 2.5 collective-permute-start.14
  95.5 16.4 %collective-permute-done.15.rest_2_ = bf16[128,1536]{1,0:T(8,128)(2,1)S(1)} collective-permute-done((bf16[128,1536]{1,0:T(8,128)(2,1)}, bf16[128,1536]{1,0:T(8,128)(2,1)S(1)}, u32[]{:S(2)}, u32[]{:S(2)}) %collective-permute-start.15) | collective-permute-done | bytes 393248 | tf_op jit(solution)/shard_map/ppermute | solution.py:55
  111.9 8.3 %collective-permute-done.16.rest_3_ = bf16[128,1536]{1,0:T(8,128)(2,1)S(1)} collective-permute-done((bf16[128,1536]{1,0:T(8,128)(2,1)S(1)}, bf16[128,1536]{1,0:T(8,128)(2,1)S(1)}, u32[]{:S(2)}, u32[]{:S(2)}) %collective-permute-start.16) | collective-permute-done | bytes 393248 | tf_op jit(solution)/shard_map/ppermute | solution.py:55
  120.2 0.7 copy-done.24
  121.1 3.2 %join.2 = (bf16[128,1536]{1,0:T(8,128)(2,1)}, bf16[128,1536]{1,0:T(8,128)(2,1)}, bf16[128,1536]{1,0:T(8,128)(2,1)}, bf16[128,1536]{1,0:T(8,128)(2,1)}, bf16[128,1536]{1,0:T(8,128)(2,1)}) custom-call(bf16[128,1536]{1,0:T(8,128)(2,1)} %constant_dynamic-slice_fusion.1.base_ref, f32[1,1536]{1,0:T(1,128)} %reshape.198.gain_ref, bf16[128,1536]{1,0:T(8,128)(2,1)} %copy-done.4, ...), custom_call_target="tpu_custom_call" | custom-call | tf_op jit(solution)/shard_map/join/pallas_call | solution.py:442
  124.3 2.5 collective-permute-start.18
  126.8 0.7 collective-permute-start.19
  127.6 1.3 collective-permute-start.17
  128.8 24.7 %collective-permute-done.18.rest_0_ = bf16[128,1536]{1,0:T(8,128)(2,1)S(1)} collective-permute-done((bf16[128,1536]{1,0:T(8,128)(2,1)}, bf16[128,1536]{1,0:T(8,128)(2,1)S(1)}, u32[]{:S(2)}, u32[]{:S(2)}) %collective-permute-start.18) | collective-permute-done | bytes 393248 | tf_op jit(solution)/shard_map/ppermute | solution.py:55
  153.5 8.8 %collective-permute-done.19.rest_1_ = bf16[128,1536]{1,0:T(8,128)(2,1)S(1)} collective-permute-done((bf16[128,1536]{1,0:T(8,128)(2,1)}, bf16[128,1536]{1,0:T(8,128)(2,1)S(1)}, u32[]{:S(2)}, u32[]{:S(2)}) %collective-permute-start.19) | collective-permute-done | bytes 393248 | tf_op jit(solution)/shard_map/ppermute | solution.py:55
  162.4 0.7 copy-done.27
  163.1 13.8 %ffn.2 = (bf16[128,1536]{1,0:T(8,128)(2,1)}, bf16[128,1536]{1,0:T(8,128)(2,1)}) custom-call(bf16[128,1536]{1,0:T(8,128)(2,1)} %copy-done.26, bf16[128,1536]{1,0:T(8,128)(2,1)} %copy-done.27, bf16[8,3,192,2240]{3,2,1,0:T(8,128)(2,1)} %bitcast.20), custom_call_target="tpu_custom_call" | custom-call | flops 5284823040 | bytes 20643840 | tf_op jit(solution)/shard_map/ffn/pallas_call | solution.py:461
  177.0 3.8 %collective-permute-start.31 = (bf16[192,512]{1,0:T(8,128)(2,1)S(1)}, bf16[192,512]{1,0:T(8,128)(2,1)S(1)}, u32[]{:S(2)}, u32[]{:S(2)}) collective-permute-start(bf16[192,512]{1,0:T(8,128)(2,1)S(1)} %pad_maximum_fusion.4.rest_4_), channel_id=1, source_target_pairs={{0,24},{4,28},{8,16},{12,20},{16,8},{20,12},{24,0},{28,4},{1,25},{... | collective-permute-start | bytes 589832 | tf_op jit(solution)/shard_map/ppermute | solution.py:55
  180.8 11.9 %ffn.3 = (bf16[128,1536]{1,0:T(8,128)(2,1)S(1)}, bf16[128,1536]{1,0:T(8,128)(2,1)S(1)}) custom-call(bf16[128,1536]{1,0:T(8,128)(2,1)S(1)} %copy-done.6, bf16[128,1536]{1,0:T(8,128)(2,1)S(1)} %collective-permute-done.17.rest_1_, bf16[8,3,192,2240]{3,2,1,0:T(8,128)(2,1)} %bitcast.21), custom_call_target="tpu_custom_call" | custom-call | flops 5284823040 | bytes 20643840 | tf_op jit(solution)/shard_map/ffn/pallas_call | solution.py:461
  192.7 0.7 copy-done.3
  193.5 3.2 %collective-permute-start.20 = (bf16[128,1536]{1,0:T(8,128)(2,1)S(1)}, bf16[128,1536]{1,0:T(8,128)(2,1)S(1)}, u32[]{:S(2)}, u32[]{:S(2)}) collective-permute-start(bf16[128,1536]{1,0:T(8,128)(2,1)S(1)} %get-tuple-element.83), channel_id=1, source_target_pairs={{0,1},{1,0},{2,3},{3,2},{4,5},{5,4},{6,7},{7,6},{8,9},{9,8},{10,11... | collective-permute-start | bytes 1179656 | tf_op jit(solution)/shard_map/ppermute | solution.py:55
  197.2 0.6 collective-permute-start.27
  197.9 8.8 %collective-permute-done.20.rest_1_ = bf16[128,1536]{1,0:T(8,128)(2,1)S(1)} collective-permute-done((bf16[128,1536]{1,0:T(8,128)(2,1)S(1)}, bf16[128,1536]{1,0:T(8,128)(2,1)S(1)}, u32[]{:S(2)}, u32[]{:S(2)}) %collective-permute-start.20) | collective-permute-done | bytes 393248 | tf_op jit(solution)/shard_map/ppermute | solution.py:55
  206.7 8.7 %collective-permute-done.22.rest_3_ = bf16[128,1536]{1,0:T(8,128)(2,1)} collective-permute-done((bf16[128,1536]{1,0:T(8,128)(2,1)}, bf16[128,1536]{1,0:T(8,128)(2,1)}, u32[]{:S(2)}, u32[]{:S(2)}) %collective-permute-start.22) | collective-permute-done | bytes 393248 | tf_op jit(solution)/shard_map/ppermute | solution.py:55
  215.4 2.9 %join.3 = (bf16[128,1536]{1,0:T(8,128)(2,1)}, bf16[128,1536]{1,0:T(8,128)(2,1)}, bf16[128,1536]{1,0:T(8,128)(2,1)}, bf16[128,1536]{1,0:T(8,128)(2,1)}) custom-call(bf16[128,1536]{1,0:T(8,128)(2,1)} %get-tuple-element.73.base_ref, f32[1,1536]{1,0:T(1,128)} %reshape.198.gain_ref, bf16[128,1536]{1,0:T(8,128)(2,1)} %copy-done.3, bf16[128,1536]{1,0:T(8,128)(2,1)} %copy-done.22, ...), custom_call_target="tpu_custom_call" | custom-call | tf_op jit(solution)/shard_map/join/pallas_call | solution.py:442
  218.3 0.7 collective-permute-start.23
  219.0 1.1 collective-permute-start.24
  220.1 0.7 copy-done.10
  220.8 1.7 collective-permute-start.25
  222.5 1.0 constant_dynamic-slice_fusion.3
  223.5 3.1 %gather_fusion = bf16[640,128]{1,0:T(8,128)(2,1)S(1)} fusion(bf16[4096,128]{1,0:T(8,128)(2,1)} %constant_dynamic-slice_fusion.3, s32[1024]{0:T(1024)S(1)} %pad_clamp_fusion), kind=kCustom, calls=%fused_computation | custom fusion | bytes 330240 | tf_op jit(solution)/shard_map/jit(_take)/gather | solution.py:280
  227.2 0.9 select_select_fusion
  228.6 6.4 %collective-permute-done.23.rest_1_ = bf16[128,1536]{1,0:T(8,128)(2,1)S(1)} collective-permute-done((bf16[128,1536]{1,0:T(8,128)(2,1)}, bf16[128,1536]{1,0:T(8,128)(2,1)S(1)}, u32[]{:S(2)}, u32[]{:S(2)}) %collective-permute-start.23) | collective-permute-done | bytes 393248 | tf_op jit(solution)/shard_map/ppermute | solution.py:55
  235.0 11.6 %collective-permute-done.24.rest_2_ = bf16[128,1536]{1,0:T(8,128)(2,1)} collective-permute-done((bf16[128,1536]{1,0:T(8,128)(2,1)}, bf16[128,1536]{1,0:T(8,128)(2,1)}, u32[]{:S(2)}, u32[]{:S(2)}) %collective-permute-start.24) | collective-permute-done | bytes 393248 | tf_op jit(solution)/shard_map/ppermute | solution.py:55
  246.6 10.0 %collective-permute-done.25.rest_3_ = bf16[128,1536]{1,0:T(8,128)(2,1)} collective-permute-done((bf16[128,1536]{1,0:T(8,128)(2,1)}, bf16[128,1536]{1,0:T(8,128)(2,1)}, u32[]{:S(2)}, u32[]{:S(2)}) %collective-permute-start.25) | collective-permute-done | bytes 393248 | tf_op jit(solution)/shard_map/ppermute | solution.py:55
  256.7 0.9 copy-done.9
  257.6 0.9 copy-done.11
  258.5 5.7 %next.1 = (bf16[512,1536]{1,0:T(8,128)(2,1)}, bf16[512,384]{1,0:T(8,128)(2,1)}, bf16[512,128]{1,0:T(8,128)(2,1)}) custom-call(s32[1]{0:T(128)} %bitcast.index_ref.wide_ref, s32[1]{0:T(128)} %bitcast.1.narrow_ref, f32[1,1536]{1,0:T(1,128)S(1)} %reshape.199.gain_ref, f32[1,512]{1,0:T(1,128)S(1)} %maximum_convert_fusion.1.bias_ref, ...), custom_call_target="tpu_custom_call" | custom-call | flops 805306368 | bytes 4718592 | tf_op jit(solution)/shard_map/next/pallas_call | solution.py:493
  (135 shorter events, 4.9 us)
Async XLA Ops:
  7.2 155.2 %all-gather.3.cloned.1.call-start = ((), (), s32[]{:S(2)}) async-start(), calls=%async_computation | async-start | bytes 23887872 | tf_op jit(solution)/shard_map/all_gather | solution.py:353
  9.1 20.4 %copy-start.16 = (bf16[192,1024]{1,0:T(8,128)(2,1)}, bf16[192,1024]{1,0:T(8,128)(2,1)S(1)}, u32[]{:S(2)}) copy-start(bf16[192,1024]{1,0:T(8,128)(2,1)S(1)} %pad_maximum_fusion.1.rest_0_) | copy-start | bytes 1179652
  9.1 13.0 %collective-permute-start.5 = (bf16[192,1024]{1,0:T(8,128)(2,1)S(1)}, bf16[192,1024]{1,0:T(8,128)(2,1)S(1)}, u32[]{:S(2)}, u32[]{:S(2)}) collective-permute-start(bf16[192,1024]{1,0:T(8,128)(2,1)S(1)} %pad_maximum_fusion.1.rest_0_), channel_id=1, source_target_pairs={{0,24},{4,28},{8,16},{12,20},{16,8},{20,12},{24,0},{28,4},{1,25},{... | collective-permute-start | bytes 1179656 | tf_op jit(solution)/shard_map/ppermute | solution.py:55
  10.7 18.7 %collective-permute-start.3 = (bf16[192,1024]{1,0:T(8,128)(2,1)S(1)}, bf16[192,1024]{1,0:T(8,128)(2,1)S(1)}, u32[]{:S(2)}, u32[]{:S(2)}) collective-permute-start(bf16[192,1024]{1,0:T(8,128)(2,1)S(1)} %pad_maximum_fusion.1.rest_0_), channel_id=1, source_target_pairs={{0,16},{4,20},{8,24},{12,28},{16,0},{20,4},{24,8},{28,12},{1,17},{... | collective-permute-start | bytes 1179656 | tf_op jit(solution)/shard_map/ppermute | solution.py:55
  11.2 18.3 %collective-permute-start.1 = (bf16[192,1024]{1,0:T(8,128)(2,1)S(1)}, bf16[192,1024]{1,0:T(8,128)(2,1)S(1)}, u32[]{:S(2)}, u32[]{:S(2)}) collective-permute-start(bf16[192,1024]{1,0:T(8,128)(2,1)S(1)} %pad_maximum_fusion.1.rest_0_), channel_id=1, source_target_pairs={{0,8},{4,12},{8,0},{12,4},{16,24},{20,28},{24,16},{28,20},{1,9},{5... | collective-permute-start | bytes 1179656 | tf_op jit(solution)/shard_map/ppermute | solution.py:55
  16.2 13.4 %copy-start.42 = (bf16[512]{0:T(512)(128)(2,1)S(1)}, bf16[512]{0:T(512)(128)(2,1)}, u32[]{:S(2)}) copy-start(bf16[512]{0:T(512)(128)(2,1)} %param.29) | copy-start | bytes 3076
  16.2 13.5 %copy-start.33 = (bf16[384]{0:T(512)(128)(2,1)S(1)}, bf16[384]{0:T(512)(128)(2,1)}, u32[]{:S(2)}) copy-start(bf16[384]{0:T(512)(128)(2,1)} %param.27) | copy-start | bytes 2308
  16.2 13.5 %copy-start.34 = (bf16[384]{0:T(512)(128)(2,1)S(1)}, bf16[384]{0:T(512)(128)(2,1)}, u32[]{:S(2)}) copy-start(bf16[384]{0:T(512)(128)(2,1)} %param.37) | copy-start | bytes 2308
  16.2 13.6 %copy-start.43 = (bf16[512]{0:T(512)(128)(2,1)S(1)}, bf16[512]{0:T(512)(128)(2,1)}, u32[]{:S(2)}) copy-start(bf16[512]{0:T(512)(128)(2,1)} %param.39) | copy-start | bytes 3076
  16.2 15.1 %copy-start.30 = (s32[8]{0:T(128)S(1)}, s32[8]{0:T(128)}, u32[]{:S(2)}) copy-start(s32[8]{0:T(128)} %param.23) | copy-start | bytes 100
  16.2 15.1 %copy-start.32 = (s32[512]{0:T(512)S(1)}, s32[512]{0:T(512)}, u32[]{:S(2)}) copy-start(s32[512]{0:T(512)} %param.21) | copy-start | bytes 6148
  16.2 15.1 %copy-start.28 = (bf16[192,384]{1,0:T(8,128)(2,1)S(1)}, bf16[192,384]{1,0:T(8,128)(2,1)}, u32[]{:S(2)}) copy-start(bf16[192,384]{1,0:T(8,128)(2,1)} %param.36) | copy-start | bytes 442372
  22.2 15.6 %copy-start.17 = (bf16[192,1024]{1,0:T(8,128)(2,1)}, bf16[192,1024]{1,0:T(8,128)(2,1)S(1)}, u32[]{:S(2)}) copy-start(bf16[192,1024]{1,0:T(8,128)(2,1)S(1)} %collective-permute-done.5.rest_6_) | copy-start | bytes 1179652
  29.4 8.3 %copy-start.18 = (bf16[192,1024]{1,0:T(8,128)(2,1)}, bf16[192,1024]{1,0:T(8,128)(2,1)S(1)}, u32[]{:S(2)}) copy-start(bf16[192,1024]{1,0:T(8,128)(2,1)S(1)} %collective-permute-done.3.rest_4_) | copy-start | bytes 1179652
  29.5 8.2 %copy-start.19 = (bf16[192,1024]{1,0:T(8,128)(2,1)}, bf16[192,1024]{1,0:T(8,128)(2,1)S(1)}, u32[]{:S(2)}) copy-start(bf16[192,1024]{1,0:T(8,128)(2,1)S(1)} %collective-permute-done.1.rest_2_) | copy-start | bytes 1179652
  29.5 10.1 %collective-permute-start = (bf16[192,1024]{1,0:T(8,128)(2,1)S(1)}, bf16[192,1024]{1,0:T(8,128)(2,1)S(1)}, u32[]{:S(2)}, u32[]{:S(2)}) collective-permute-start(bf16[192,1024]{1,0:T(8,128)(2,1)S(1)} %pad_maximum_fusion.1.rest_0_), channel_id=1, source_target_pairs={{0,4},{4,0},{8,12},{12,8},{16,20},{20,16},{24,28},{28,24},{1,5},{5... | collective-permute-start | bytes 1179656 | tf_op jit(solution)/shard_map/ppermute | solution.py:55
  31.4 42.4 %copy-start.12 = (s32[512]{0:T(512)}, s32[512]{0:T(512)S(1)}, u32[]{:S(2)}) copy-start(s32[512]{0:T(512)S(1)} %select_reduce_fusion.spots_ref) | copy-start | bytes 6148
  32.4 7.2 %collective-permute-start.6 = (bf16[192,1024]{1,0:T(8,128)(2,1)S(1)}, bf16[192,1024]{1,0:T(8,128)(2,1)S(1)}, u32[]{:S(2)}, u32[]{:S(2)}) collective-permute-start(bf16[192,1024]{1,0:T(8,128)(2,1)S(1)} %collective-permute-done.5.rest_6_), channel_id=1, source_target_pairs={{0,4},{4,0},{8,12},{12,8},{16,20},{20,16},{24,28},{28,24},{1,5},{5... | collective-permute-start | bytes 1179656 | tf_op jit(solution)/shard_map/ppermute | solution.py:55
  32.9 6.7 %collective-permute-start.4 = (bf16[192,1024]{1,0:T(8,128)(2,1)S(1)}, bf16[192,1024]{1,0:T(8,128)(2,1)}, u32[]{:S(2)}, u32[]{:S(2)}) collective-permute-start(bf16[192,1024]{1,0:T(8,128)(2,1)S(1)} %collective-permute-done.3.rest_4_), channel_id=1, source_target_pairs={{0,4},{4,0},{8,12},{12,8},{16,20},{20,16},{24,28},{28,24},{1,5},{5... | collective-permute-start | bytes 1179656 | tf_op jit(solution)/shard_map/ppermute | solution.py:55
  33.0 6.6 %collective-permute-start.2 = (bf16[192,1024]{1,0:T(8,128)(2,1)S(1)}, bf16[192,1024]{1,0:T(8,128)(2,1)}, u32[]{:S(2)}, u32[]{:S(2)}) collective-permute-start(bf16[192,1024]{1,0:T(8,128)(2,1)S(1)} %collective-permute-done.1.rest_2_), channel_id=1, source_target_pairs={{0,4},{4,0},{8,12},{12,8},{16,20},{20,16},{24,28},{28,24},{1,5},{5... | collective-permute-start | bytes 1179656 | tf_op jit(solution)/shard_map/ppermute | solution.py:55
  47.2 38.1 %copy-start.14 = (bf16[1536,384]{1,0:T(8,128)(2,1)S(1)}, bf16[1536,384]{1,0:T(8,128)(2,1)}, u32[]{:S(2)}) copy-start(bf16[1536,384]{1,0:T(8,128)(2,1)} %get-tuple-element.66.w_out) | copy-start | bytes 3538948
  47.2 38.1 %copy-start.15 = (bf16[512,384]{1,0:T(8,128)(2,1)S(1)}, bf16[512,384]{1,0:T(8,128)(2,1)}, u32[]{:S(2)}) copy-start(bf16[512,384]{1,0:T(8,128)(2,1)} %get-tuple-element.65.q_ref) | copy-start | bytes 1179652
  47.2 15.9 %collective-permute-start.12 = (bf16[512,256]{1,0:T(8,128)(2,1)}, bf16[512,256]{1,0:T(8,128)(2,1)S(1)}, u32[]{:S(2)}, u32[]{:S(2)}) collective-permute-start(bf16[512,256]{1,0:T(8,128)(2,1)} %get-tuple-element.67.rest_0_), channel_id=1, source_target_pairs={{0,24},{4,28},{8,16},{12,20},{16,8},{20,12},{24,0},{28,4},{1,25},{... | collective-permute-start | bytes 786440 | tf_op jit(solution)/shard_map/ppermute | solution.py:55
  48.7 19.8 %collective-permute-start.10 = (bf16[512,256]{1,0:T(8,128)(2,1)}, bf16[512,256]{1,0:T(8,128)(2,1)S(1)}, u32[]{:S(2)}, u32[]{:S(2)}) collective-permute-start(bf16[512,256]{1,0:T(8,128)(2,1)} %get-tuple-element.67.rest_0_), channel_id=1, source_target_pairs={{0,16},{4,20},{8,24},{12,28},{16,0},{20,4},{24,8},{28,12},{1,17},{... | collective-permute-start | bytes 786440 | tf_op jit(solution)/shard_map/ppermute | solution.py:55
  49.3 24.5 %collective-permute-start.8 = (bf16[512,256]{1,0:T(8,128)(2,1)}, bf16[512,256]{1,0:T(8,128)(2,1)S(1)}, u32[]{:S(2)}, u32[]{:S(2)}) collective-permute-start(bf16[512,256]{1,0:T(8,128)(2,1)} %get-tuple-element.67.rest_0_), channel_id=1, source_target_pairs={{0,8},{4,12},{8,0},{12,4},{16,24},{20,28},{24,16},{28,20},{1,9},{5... | collective-permute-start | bytes 786440 | tf_op jit(solution)/shard_map/ppermute | solution.py:55
  50.7 23.9 %collective-permute-start.7 = (bf16[512,256]{1,0:T(8,128)(2,1)}, bf16[512,256]{1,0:T(8,128)(2,1)S(1)}, u32[]{:S(2)}, u32[]{:S(2)}) collective-permute-start(bf16[512,256]{1,0:T(8,128)(2,1)} %get-tuple-element.67.rest_0_), channel_id=1, source_target_pairs={{0,4},{4,0},{8,12},{12,8},{16,20},{20,16},{24,28},{28,24},{1,5},{5... | collective-permute-start | bytes 786440 | tf_op jit(solution)/shard_map/ppermute | solution.py:55
  63.1 12.3 %copy-start.37 = (bf16[512,256]{1,0:T(8,128)(2,1)}, bf16[512,256]{1,0:T(8,128)(2,1)S(1)}, u32[]{:S(2)}) copy-start(bf16[512,256]{1,0:T(8,128)(2,1)S(1)} %collective-permute-done.12.rest_6_) | copy-start | bytes 786436
  63.1 11.5 %collective-permute-start.13 = (bf16[512,256]{1,0:T(8,128)(2,1)S(1)}, bf16[512,256]{1,0:T(8,128)(2,1)S(1)}, u32[]{:S(2)}, u32[]{:S(2)}) collective-permute-start(bf16[512,256]{1,0:T(8,128)(2,1)S(1)} %collective-permute-done.12.rest_6_), channel_id=1, source_target_pairs={{0,4},{4,0},{8,12},{12,8},{16,20},{20,16},{24,28},{28,24},{1,5},{5... | collective-permute-start | bytes 786440 | tf_op jit(solution)/shard_map/ppermute | solution.py:55
  68.5 6.9 %copy-start.38 = (bf16[512,256]{1,0:T(8,128)(2,1)}, bf16[512,256]{1,0:T(8,128)(2,1)S(1)}, u32[]{:S(2)}) copy-start(bf16[512,256]{1,0:T(8,128)(2,1)S(1)} %collective-permute-done.10.rest_4_) | copy-start | bytes 786436
  68.5 6.2 %collective-permute-start.11 = (bf16[512,256]{1,0:T(8,128)(2,1)S(1)}, bf16[512,256]{1,0:T(8,128)(2,1)}, u32[]{:S(2)}, u32[]{:S(2)}) collective-permute-start(bf16[512,256]{1,0:T(8,128)(2,1)S(1)} %collective-permute-done.10.rest_4_), channel_id=1, source_target_pairs={{0,4},{4,0},{8,12},{12,8},{16,20},{20,16},{24,28},{28,24},{1,5},{5... | collective-permute-start | bytes 786440 | tf_op jit(solution)/shard_map/ppermute | solution.py:55
  73.7 1.7 copy-start.39
  73.7 1.7 collective-permute-start.9
  74.6 10.7 %copy-start.7 = (s32[512,1]{1,0:T(8,128)S(1)}, s32[512,1]{1,0:T(8,128)}, u32[]{:S(2)}) copy-start(s32[512,1]{1,0:T(8,128)} %copy.29.starts_ref) | copy-start | bytes 6148
  74.6 10.7 %copy-start.13 = (s32[512]{0:T(512)S(1)}, s32[512]{0:T(512)}, u32[]{:S(2)}) copy-start(s32[512]{0:T(512)} %copy-done.12) | copy-start | bytes 6148
  75.4 19.5 %copy-start.29 = (s32[8,16]{1,0:T(8,128)S(1)}, s32[8,16]{1,0:T(8,128)}, u32[]{:S(2)}) copy-start(s32[8,16]{1,0:T(8,128)} %param.24) | copy-start | bytes 1540
  83.4 11.9 %copy-start.31 = (s32[8]{0:T(128)S(1)}, s32[8]{0:T(128)}, u32[]{:S(2)}) copy-start(s32[8]{0:T(128)} %param.23) | copy-start | bytes 100
  83.4 11.9 %copy-start.35 = (s32[8]{0:T(128)S(1)}, s32[8]{0:T(128)}, u32[]{:S(2)}) copy-start(s32[8]{0:T(128)} %param.22) | copy-start | bytes 100
  83.4 28.5 %collective-permute-start.15 = (bf16[128,1536]{1,0:T(8,128)(2,1)}, bf16[128,1536]{1,0:T(8,128)(2,1)S(1)}, u32[]{:S(2)}, u32[]{:S(2)}) collective-permute-start(bf16[128,1536]{1,0:T(8,128)(2,1)} %get-tuple-element.71), channel_id=1, source_target_pairs={{0,2},{1,3},{2,0},{3,1},{4,6},{5,7},{6,4},{7,5},{8,10},{9,11},{10,... | collective-permute-start | bytes 1179656 | tf_op jit(solution)/shard_map/ppermute | solution.py:55
  85.3 1.6 copy-start.1
  86.9 4.8 %copy-start.36 = (bf16[128,1536]{1,0:T(8,128)(2,1)S(1)}, bf16[128,1536]{1,0:T(8,128)(2,1)}, u32[]{:S(2)}) copy-start(bf16[128,1536]{1,0:T(8,128)(2,1)} %get-tuple-element.72) | copy-start | bytes 1179652
  91.7 28.5 %collective-permute-start.16 = (bf16[128,1536]{1,0:T(8,128)(2,1)S(1)}, bf16[128,1536]{1,0:T(8,128)(2,1)S(1)}, u32[]{:S(2)}, u32[]{:S(2)}) collective-permute-start(bf16[128,1536]{1,0:T(8,128)(2,1)S(1)} %copy-done.36), channel_id=1, source_target_pairs={{0,3},{1,2},{2,1},{3,0},{4,7},{5,6},{6,5},{7,4},{8,11},{9,10},{10,... | collective-permute-start | bytes 1179656 | tf_op jit(solution)/shard_map/ppermute | solution.py:55
  92.4 27.8 %collective-permute-start.14 = (bf16[128,1536]{1,0:T(8,128)(2,1)S(1)}, bf16[128,1536]{1,0:T(8,128)(2,1)S(1)}, u32[]{:S(2)}, u32[]{:S(2)}) collective-permute-start(bf16[128,1536]{1,0:T(8,128)(2,1)S(1)} %get-tuple-element.70), channel_id=1, source_target_pairs={{0,1},{1,0},{2,3},{3,2},{4,5},{5,4},{6,7},{7,6},{8,9},{9,8},{10,11... | collective-permute-start | bytes 1179656 | tf_op jit(solution)/shard_map/ppermute | solution.py:55
  111.9 8.3 %copy-start.23 = (bf16[128,1536]{1,0:T(8,128)(2,1)}, bf16[128,1536]{1,0:T(8,128)(2,1)S(1)}, u32[]{:S(2)}) copy-start(bf16[128,1536]{1,0:T(8,128)(2,1)S(1)} %collective-permute-done.15.rest_2_) | copy-start | bytes 1179652
  124.3 29.2 %collective-permute-start.18 = (bf16[128,1536]{1,0:T(8,128)(2,1)}, bf16[128,1536]{1,0:T(8,128)(2,1)S(1)}, u32[]{:S(2)}, u32[]{:S(2)}) collective-permute-start(bf16[128,1536]{1,0:T(8,128)(2,1)} %get-tuple-element.76), channel_id=1, source_target_pairs={{0,2},{1,3},{2,0},{3,1},{4,6},{5,7},{6,4},{7,5},{8,10},{9,11},{10,... | collective-permute-start | bytes 1179656 | tf_op jit(solution)/shard_map/ppermute | solution.py:55
  126.8 35.6 %collective-permute-start.19 = (bf16[128,1536]{1,0:T(8,128)(2,1)}, bf16[128,1536]{1,0:T(8,128)(2,1)S(1)}, u32[]{:S(2)}, u32[]{:S(2)}) collective-permute-start(bf16[128,1536]{1,0:T(8,128)(2,1)} %get-tuple-element.77), channel_id=1, source_target_pairs={{0,3},{1,2},{2,1},{3,0},{4,7},{5,6},{6,5},{7,4},{8,11},{9,10},{10,... | collective-permute-start | bytes 1179656 | tf_op jit(solution)/shard_map/ppermute | solution.py:55
  127.6 49.4 %collective-permute-start.17 = (bf16[128,1536]{1,0:T(8,128)(2,1)}, bf16[128,1536]{1,0:T(8,128)(2,1)S(1)}, u32[]{:S(2)}, u32[]{:S(2)}) collective-permute-start(bf16[128,1536]{1,0:T(8,128)(2,1)} %get-tuple-element.75), channel_id=1, source_target_pairs={{0,1},{1,0},{2,3},{3,2},{4,5},{5,4},{6,7},{7,6},{8,9},{9,8},{10,11... | collective-permute-start | bytes 1179656 | tf_op jit(solution)/shard_map/ppermute | solution.py:55
  153.5 8.8 %copy-start.26 = (bf16[128,1536]{1,0:T(8,128)(2,1)}, bf16[128,1536]{1,0:T(8,128)(2,1)S(1)}, u32[]{:S(2)}) copy-start(bf16[128,1536]{1,0:T(8,128)(2,1)S(1)} %collective-permute-done.18.rest_0_) | copy-start | bytes 1179652
  163.1 17.7 %copy-start.6 = (bf16[128,1536]{1,0:T(8,128)(2,1)S(1)}, bf16[128,1536]{1,0:T(8,128)(2,1)}, u32[]{:S(2)}) copy-start(bf16[128,1536]{1,0:T(8,128)(2,1)} %get-tuple-element.80.rest_0_) | copy-start | bytes 1179652
  176.9 38.5 %collective-permute-start.21 = (bf16[128,1536]{1,0:T(8,128)(2,1)}, bf16[128,1536]{1,0:T(8,128)(2,1)}, u32[]{:S(2)}, u32[]{:S(2)}) collective-permute-start(bf16[128,1536]{1,0:T(8,128)(2,1)} %get-tuple-element.79), channel_id=1, source_target_pairs={{0,2},{1,3},{2,0},{3,1},{4,6},{5,7},{6,4},{7,5},{8,10},{9,11},{10,... | collective-permute-start | bytes 1179656 | tf_op jit(solution)/shard_map/ppermute | solution.py:55
  177.0 20.2 %collective-permute-start.31 = (bf16[192,512]{1,0:T(8,128)(2,1)S(1)}, bf16[192,512]{1,0:T(8,128)(2,1)S(1)}, u32[]{:S(2)}, u32[]{:S(2)}) collective-permute-start(bf16[192,512]{1,0:T(8,128)(2,1)S(1)} %pad_maximum_fusion.4.rest_4_), channel_id=1, source_target_pairs={{0,24},{4,28},{8,16},{12,20},{16,8},{20,12},{24,0},{28,4},{1,25},{... | collective-permute-start | bytes 589832 | tf_op jit(solution)/shard_map/ppermute | solution.py:55
  180.8 41.7 %copy-start.2 = (bf16[4096,256]{1,0:T(8,128)(2,1)S(1)}, bf16[4096,256]{1,0:T(8,128)(2,1)}, u32[]{:S(2)}) copy-start(bf16[4096,256]{1,0:T(8,128)(2,1)} %get-tuple-element.68.rest_0_) | copy-start | bytes 6291460
  193.5 13.2 %collective-permute-start.20 = (bf16[128,1536]{1,0:T(8,128)(2,1)S(1)}, bf16[128,1536]{1,0:T(8,128)(2,1)S(1)}, u32[]{:S(2)}, u32[]{:S(2)}) collective-permute-start(bf16[128,1536]{1,0:T(8,128)(2,1)S(1)} %get-tuple-element.83), channel_id=1, source_target_pairs={{0,1},{1,0},{2,3},{3,2},{4,5},{5,4},{6,7},{7,6},{8,9},{9,8},{10,11... | collective-permute-start | bytes 1179656 | tf_op jit(solution)/shard_map/ppermute | solution.py:55
  196.7 18.7 %collective-permute-start.22 = (bf16[128,1536]{1,0:T(8,128)(2,1)}, bf16[128,1536]{1,0:T(8,128)(2,1)}, u32[]{:S(2)}, u32[]{:S(2)}) collective-permute-start(bf16[128,1536]{1,0:T(8,128)(2,1)} %get-tuple-element.84), channel_id=1, source_target_pairs={{0,3},{1,2},{2,1},{3,0},{4,7},{5,6},{6,5},{7,4},{8,11},{9,10},{10,... | collective-permute-start | bytes 1179656 | tf_op jit(solution)/shard_map/ppermute | solution.py:55
  197.1 21.9 %collective-permute-start.29 = (bf16[192,512]{1,0:T(8,128)(2,1)S(1)}, bf16[192,512]{1,0:T(8,128)(2,1)S(1)}, u32[]{:S(2)}, u32[]{:S(2)}) collective-permute-start(bf16[192,512]{1,0:T(8,128)(2,1)S(1)} %pad_maximum_fusion.4.rest_4_), channel_id=1, source_target_pairs={{0,16},{4,20},{8,24},{12,28},{16,0},{20,4},{24,8},{28,12},{1,17},{... | collective-permute-start | bytes 589832 | tf_op jit(solution)/shard_map/ppermute | solution.py:55
  197.2 22.9 %collective-permute-start.27 = (bf16[192,512]{1,0:T(8,128)(2,1)S(1)}, bf16[192,512]{1,0:T(8,128)(2,1)S(1)}, u32[]{:S(2)}, u32[]{:S(2)}) collective-permute-start(bf16[192,512]{1,0:T(8,128)(2,1)S(1)} %pad_maximum_fusion.4.rest_4_), channel_id=1, source_target_pairs={{0,8},{4,12},{8,0},{12,4},{16,24},{20,28},{24,16},{28,20},{1,9},{5... | collective-permute-start | bytes 589832 | tf_op jit(solution)/shard_map/ppermute | solution.py:55
  206.7 8.7 %copy-start.22 = (bf16[128,1536]{1,0:T(8,128)(2,1)}, bf16[128,1536]{1,0:T(8,128)(2,1)S(1)}, u32[]{:S(2)}) copy-start(bf16[128,1536]{1,0:T(8,128)(2,1)S(1)} %collective-permute-done.20.rest_1_) | copy-start | bytes 1179652
  206.7 19.9 %collective-permute-start.26 = (bf16[192,512]{1,0:T(8,128)(2,1)S(1)}, bf16[192,512]{1,0:T(8,128)(2,1)}, u32[]{:S(2)}, u32[]{:S(2)}) collective-permute-start(bf16[192,512]{1,0:T(8,128)(2,1)S(1)} %pad_maximum_fusion.4.rest_4_), channel_id=1, source_target_pairs={{0,4},{4,0},{8,12},{12,8},{16,20},{20,16},{24,28},{28,24},{1,5},{5... | collective-permute-start | bytes 589832 | tf_op jit(solution)/shard_map/ppermute | solution.py:55
  215.4 11.3 %collective-permute-start.32 = (bf16[192,512]{1,0:T(8,128)(2,1)S(1)}, bf16[192,512]{1,0:T(8,128)(2,1)}, u32[]{:S(2)}, u32[]{:S(2)}) collective-permute-start(bf16[192,512]{1,0:T(8,128)(2,1)S(1)} %collective-permute-done.31.rest_10_), channel_id=1, source_target_pairs={{0,4},{4,0},{8,12},{12,8},{16,20},{20,16},{24,28},{28,24},{1,5},{5... | collective-permute-start | bytes 589832 | tf_op jit(solution)/shard_map/ppermute | solution.py:55
  218.3 38.4 %copy-start.5 = (bf16[128,1536]{1,0:T(8,128)(2,1)S(1)}, bf16[128,1536]{1,0:T(8,128)(2,1)}, u32[]{:S(2)}) copy-start(bf16[128,1536]{1,0:T(8,128)(2,1)} %get-tuple-element.85.rest_0_) | copy-start | bytes 1179652
  218.3 16.7 %collective-permute-start.23 = (bf16[128,1536]{1,0:T(8,128)(2,1)}, bf16[128,1536]{1,0:T(8,128)(2,1)S(1)}, u32[]{:S(2)}, u32[]{:S(2)}) collective-permute-start(bf16[128,1536]{1,0:T(8,128)(2,1)} %get-tuple-element.86), channel_id=1, source_target_pairs={{0,1},{1,0},{2,3},{3,2},{4,5},{5,4},{6,7},{7,6},{8,9},{9,8},{10,11... | collective-permute-start | bytes 1179656 | tf_op jit(solution)/shard_map/ppermute | solution.py:55
  219.0 27.6 %collective-permute-start.24 = (bf16[128,1536]{1,0:T(8,128)(2,1)}, bf16[128,1536]{1,0:T(8,128)(2,1)}, u32[]{:S(2)}, u32[]{:S(2)}) collective-permute-start(bf16[128,1536]{1,0:T(8,128)(2,1)} %get-tuple-element.87), channel_id=1, source_target_pairs={{0,2},{1,3},{2,0},{3,1},{4,6},{5,7},{6,4},{7,5},{8,10},{9,11},{10,... | collective-permute-start | bytes 1179656 | tf_op jit(solution)/shard_map/ppermute | solution.py:55
  220.8 35.9 %collective-permute-start.25 = (bf16[128,1536]{1,0:T(8,128)(2,1)}, bf16[128,1536]{1,0:T(8,128)(2,1)}, u32[]{:S(2)}, u32[]{:S(2)}) collective-permute-start(bf16[128,1536]{1,0:T(8,128)(2,1)} %get-tuple-element.88), channel_id=1, source_target_pairs={{0,3},{1,2},{2,1},{3,0},{4,7},{5,6},{6,5},{7,4},{8,11},{9,10},{10,... | collective-permute-start | bytes 1179656 | tf_op jit(solution)/shard_map/ppermute | solution.py:55
  226.6 1.7 collective-permute-start.30
  226.7 1.9 collective-permute-start.28
  (14 other events, 11.6 us)
Sparse Core Ops, SparseCore 0:
  29.6 120.2 all-gather.2

commit v6 on v5

--- a/solution.py
+++ b/solution.py
@@ -70,6 +70,12 @@
 
 def narrow_swap(pieces, size):
     return [pieces[0]] + [exchange(pieces[k], "narrow", size, k) for k in range(1, size)]
+
+
+def narrow_spread(copies, size):
+    near = exchange(copies[1], "narrow", size, 1)
+    far = exchange(copies[2], "narrow", size, 3)
+    return [copies[0], near, exchange(far, "narrow", size, 1), far]
 
 
 def place_copies(piece_refs, target, sems, wide_index):
@@ -186,10 +192,10 @@
     for part in parts[1:]:
         total = total + part[...].astype(f32)
     rounded = (base_ref[...].astype(f32) + total).astype(bf16)
-    if len(outs) > narrow:
-        outs[narrow][...] = rounded
+    if len(outs) > 3:
+        outs[3][...] = rounded
         rounded = norm_rows(rounded.astype(f32), gain_ref[...])
-    for out in outs[:narrow]:
+    for out in outs[:3]:
         out[...] = rounded
 
 
@@ -243,25 +249,38 @@
             part_refs[k][:, lanes] = product[k * share : (k + 1) * share].astype(bf16)
 
 
-def next_kernel(wide, narrow, wide_ref, narrow_ref, gain_ref, bias_ref, *rest):
-    h_refs, pieces = rest[:narrow], rest[narrow : narrow + wide]
-    out_ref, query_ref, keyval_ref, weight, sems = rest[narrow + wide :]
-    wide_index, narrow_index = wide_ref[0], narrow_ref[0]
-    copies = place_copies(pieces, weight, sems, wide_index)
+def next_kernel(wide, shares, wide_ref, narrow_ref, gain_ref, bias_ref, *rest):
+    count = len(shares)
+    h_refs, pieces = rest[:count], rest[count : count + wide]
+    *outs, weight, query, keyval, sems, out_sems = rest[-8:]
+    copies = place_copies(pieces, weight, sems, wide_ref[0])
     for c in copies:
         c.start()
     share = h_refs[0].shape[0]
-    queries = query_ref.shape[1]
+    width = query.shape[1]
+    flushes = []
+
+    def flush(source, k, j):
+        begin = pl.multiple_of((narrow_ref[0] ^ k) * share, share)
+        target = outs[j].at[pl.ds(begin, share)]
+        copy = pltpu.make_async_copy(source, target, out_sems.at[len(flushes)])
+        copy.start()
+        flushes.append(copy)
+
+    for i, k in enumerate(shares):
+        flush(h_refs[i], k, 0)
     for c in copies:
         c.wait()
-    for k in range(narrow):
-        rows = pl.ds(pl.multiple_of((narrow_index ^ k) * share, share), share)
-        value = h_refs[k][...]
-        out_ref[rows, :] = value
-        normed = norm_rows(value.astype(f32), gain_ref[...])
+    for i, k in enumerate(shares):
+        rows = slice(i * share, (i + 1) * share)
+        normed = norm_rows(h_refs[i][...].astype(f32), gain_ref[...])
         product = jnp.dot(normed, weight[...], preferred_element_type=f32) + bias_ref[...]
-        query_ref[rows, :] = product[:, :queries].astype(bf16)
-        keyval_ref[rows, :] = product[:, queries:].astype(bf16)
+        query[rows, :] = product[:, :width].astype(bf16)
+        keyval[rows, :] = product[:, width:].astype(bf16)
+        flush(query.at[pl.ds(i * share, share)], k, 1)
+        flush(keyval.at[pl.ds(i * share, share)], k, 2)
+    for c in flushes:
+        c.wait()
 
 
 def fill_pages(source, seg_lengths, seg_offsets, block_table, first_page, page_count):
@@ -349,7 +368,7 @@
     next_row = next_gain.astype(f32)[None]
     starts_column = token_start[:, None]
     packed = jnp.stack([w_gate, w_up, w_down.T])
-    (packed,) = after([packed], *qkv_pieces[2::2])
+    (packed,) = after([packed], qkv_pieces[1])
     ffn_weights = lax.all_gather(packed, "wide", axis=0, tiled=False)
     early = (
         cosine,
@@ -438,7 +457,7 @@
 
     def join(parts, base_rows, gain, with_norm):
         shape = jax.ShapeDtypeStruct((share, depth), bf16)
-        count = narrow + 1 if with_norm else narrow
+        count = 4 if with_norm else 3
         return pl.pallas_call(
             functools.partial(join_kernel, narrow),
             out_shape=[shape] * count,
@@ -449,7 +468,7 @@
         )(base_rows, gain, *parts)
 
     *normed, residual = join(narrow_swap(parts, narrow), base_rows, mlp_row, True)
-    normed_pieces = narrow_swap(normed, narrow)
+    normed_pieces = narrow_spread(normed, narrow)
 
     source = lax.dynamic_slice_in_dim(kv_all, kind_index * HD, HD, 1)
     page_count = tok_rows // PAGE_LEN + 1
@@ -479,42 +498,60 @@
             name="ffn",
         )(*x_shares, ffn_weights)
 
-    far = normed_pieces[2:]
-    far_two, far_three = feed_forward(far)
-    near_zero, near_one = feed_forward(list(after(normed_pieces[:2], far_two)))
-    parts = [near_zero, near_one, far_two, far_three]
-
+    far = [normed_pieces[3], normed_pieces[0]]
+    part_three, part_zero = feed_forward(far)
+    part_one, part_two = feed_forward(list(after(normed_pieces[1:3], part_three)))
+    parts = [part_zero, part_one, part_two, part_three]
+
+    (next_weight,) = after([next_weight], part_three)
+    next_pieces = wide_pieces(next_weight, wide)
+    (residual,) = after([residual], *next_pieces)
     hidden_rows = join(narrow_swap(parts, narrow), residual, mlp_row, False)
-    hidden_pieces = narrow_swap(hidden_rows, narrow)
-
-    (next_weight,) = after([next_weight], far_two)
-    next_pieces = wide_pieces(next_weight, wide)
+    hidden_pieces = narrow_spread(hidden_rows, narrow)
+
     next_width = query_width + HD
-    hidden_out, next_query, next_keyval = pl.pallas_call(
-        functools.partial(next_kernel, wide, narrow),
-        out_shape=(
-            jax.ShapeDtypeStruct((tok_rows, depth), bf16),
-            jax.ShapeDtypeStruct((tok_rows, query_width), bf16),
-            jax.ShapeDtypeStruct((tok_rows, HD), bf16),
-        ),
-        in_specs=[smem_spec()] * 2 + [vmem_spec()] * (2 + narrow) + [any_spec()] * wide,
-        out_specs=(vmem_spec(),) * 3,
-        scratch_shapes=[VMEM((depth, next_width), bf16), pltpu.SemaphoreType.DMA((wide,))],
-        compiler_params=params(40),
-        cost_estimate=pl.CostEstimate(
-            flops=2 * tok_rows * depth * next_width,
-            bytes_accessed=2 * depth * (2 * tok_rows + next_width),
-            transcendentals=0,
-        ),
-        name="next",
-    )(
-        wide_index[None],
-        narrow_index[None],
-        next_row,
-        next_bias,
-        *hidden_pieces,
-        *next_pieces,
-    )
+    def project(shares, outputs):
+        count = len(shares)
+        operands = 4 + count + wide
+        return pl.pallas_call(
+            functools.partial(next_kernel, wide, shares),
+            out_shape=(
+                jax.ShapeDtypeStruct((tok_rows, depth), bf16),
+                jax.ShapeDtypeStruct((tok_rows, query_width), bf16),
+                jax.ShapeDtypeStruct((tok_rows, HD), bf16),
+            ),
+            in_specs=[smem_spec()] * 2
+            + [vmem_spec()] * (2 + count)
+            + [any_spec()] * wide
+            + [hbm_spec()] * len(outputs),
+            out_specs=(hbm_spec(),) * 3,
+            scratch_shapes=[
+                VMEM((depth, next_width), bf16),
+                VMEM((count * share, query_width), bf16),
+                VMEM((count * share, HD), bf16),
+                pltpu.SemaphoreType.DMA((wide,)),
+                pltpu.SemaphoreType.DMA((3 * count,)),
+            ],
+            input_output_aliases={operands + i: i for i in range(len(outputs))},
+            compiler_params=params(40),
+            cost_estimate=pl.CostEstimate(
+                flops=2 * count * share * depth * next_width,
+                bytes_accessed=2 * depth * (2 * tok_rows + next_width),
+                transcendentals=0,
+            ),
+            name="next",
+        )(
+            wide_index[None],
+            narrow_index[None],
+            next_row,
+            next_bias,
+            *[hidden_pieces[k] for k in shares],
+            *next_pieces,
+            *outputs,
+        )
+
+    outputs = project((0, 1, 3), ())
+    hidden_out, next_query, next_keyval = project((2,), outputs)
 
     return (hidden_out, next_query, next_keyval, cache_block[None])
 

time: 272 us -> 247 us (0.908)
  waiting for transfers between devices: 141 us -> 114 us
    ppermute x33, waiting for transfers between devices: 141 us -> 114 us  [exchange(): return lax.ppermute(value, axis, [(i, i ^ mask) for i in range(size)])]
    unnamed x88 -> x80, local copies, waits for them, and re-layouts: 9.06 us -> 6.83 us
    pallas_call x1 -> x2, Pallas kernels: 5.74 us -> 7.05 us  [project(): pl.pallas_call(functools.partial(next_kernel, wide, shares), out_shape=(j...]
  transfers between devices with their start and end apart: 34 -> 34, of which waited for: 18 -> 17; matrix products, arithmetic and copies ran while one was open for 7% -> 8% of each run, Pallas kernels for 19% -> 21%
where the time goes in v6:
time: 247 us; the launch traced here: 245 us
  waiting for transfers between devices  114 us (46%)
  Pallas kernels  58.6 us (24%)
  starting transfers between devices  30 us (12%)
  local copies, waits for them, and re-layouts  18.4 us (7%)
  between operations  14.5 us (6%)
  other arithmetic  9.18 us (4%)
    ppermute x33, waiting for transfers between devices, exchange(): return lax.ppermute(value, axis, [(i, i ^ mask) for i in range(size)])  114 us
    ppermute x33, starting transfers between devices, exchange(): return lax.ppermute(value, axis, [(i, i ^ mask) for i in range(size)])  30 us
    pallas_call x2, Pallas kernels, feed_forward(): pl.pallas_call(functools.partial(ffn_kernel, count), out_shape=[share_sha...  25.5 us
    pallas_call x2, Pallas kernels, attend(): pl.pallas_call(functools.partial(attend_kernel, wide, shares), out_shape=...  14 us
    pallas_call x2, Pallas kernels, project(): pl.pallas_call(functools.partial(next_kernel, wide, shares), out_shape=(j...  7.05 us
    unnamed x80, local copies, waits for them, and re-layouts  6.83 us
    pallas_call x1, Pallas kernels, local(): pl.pallas_call(functools.partial(qkv_kernel, wide), out_shape=(jax.ShapeD...  6.17 us
    pallas_call x2, Pallas kernels, join(): pl.pallas_call(functools.partial(join_kernel, narrow), out_shape=[shape]...  5.93 us
  transfers between devices with their start and end apart: 34, of which 17 were waited for; matrix products, arithmetic and copies ran while one was open for 8% of the time, Pallas kernels for 21%

profile of v6, /device:TPU:10, one launch (start us, length us, event | category | flops | bytes accessed | tf_op | source)
XLA Modules:
  0.0 245.0 jit_solution(8622004129261188044)
XLA Ops:
  7.2 0.8 copy-done
  8.1 1.0 pad_maximum_fusion.1.rest_0_
  9.2 3.6 %pad_maximum_fusion = bf16[3,192,2240]{2,1,0:T(8,128)(2,1)} fusion(bf16[1,192,2240]{2,1,0:T(8,128)(2,1)} %bitcast.22, bf16[1,192,2240]{2,1,0:T(8,128)(2,1)} %bitcast.23, bf16[1,192,2240]{2,1,0:T(8,128)(2,1)} %bitcast.24), kind=kLoop, calls=%fused_computation.1 | loop fusion | flops 2580480 | bytes 5160960 | tf_op jit(solution)/shard_map/stack | solution.py:370
  12.9 1.6 collective-permute-start.5
  14.4 0.5 collective-permute-start.3
  15.0 1.5 collective-permute-start.1
  16.6 0.6 maximum_convert_fusion.bias_ref
  17.2 0.8 constant_dynamic-slice_fusion.2
  18.2 1.0 fusion
  19.2 6.6 %collective-permute-done.5.rest_6_ = bf16[192,1024]{1,0:T(8,128)(2,1)S(1)} collective-permute-done((bf16[192,1024]{1,0:T(8,128)(2,1)S(1)}, bf16[192,1024]{1,0:T(8,128)(2,1)S(1)}, u32[]{:S(2)}, u32[]{:S(2)}) %collective-permute-start.5) | collective-permute-done | bytes 393248 | tf_op jit(solution)/shard_map/ppermute | solution.py:55
  25.8 14.5 %collective-permute-done.3.rest_4_ = bf16[192,1024]{1,0:T(8,128)(2,1)S(1)} collective-permute-done((bf16[192,1024]{1,0:T(8,128)(2,1)S(1)}, bf16[192,1024]{1,0:T(8,128)(2,1)S(1)}, u32[]{:S(2)}, u32[]{:S(2)}) %collective-permute-start.3) | collective-permute-done | bytes 393248 | tf_op jit(solution)/shard_map/ppermute | solution.py:55
  40.3 2.0 collective-permute-done.1.rest_2_
  42.3 0.7 reshape.200.gain_ref
  43.0 1.3 reshape.198.gain_ref
  44.3 0.7 reshape.199.gain_ref
  45.0 1.0 pad_maximum_fusion.2
  46.0 1.8 constant_dynamic-slice_fusion.1.base_ref
  47.8 0.7 copy-done.14
  48.6 6.2 %qkv.1 = (bf16[512,384]{1,0:T(8,128)(2,1)}, bf16[512,256]{1,0:T(8,128)(2,1)}, bf16[1536,384]{1,0:T(8,128)(2,1)}) custom-call(s32[1]{0:T(128)} %bitcast.index_ref.wide_ref, bf16[512,1536]{1,0:T(8,128)(2,1)} %hidden_ref.1, f32[1,1536]{1,0:T(1,128)} %reshape.200.gain_ref, f32[1,640]{1,0:T(1,128)} %maximum_convert_fusion.bias_ref, ...), custom_call_target="tpu_custom_call" | custom-call | flops 1006632960 | bytes 3538944 | tf_op jit(solution)/shard_map/qkv/pallas_call | solution.py:389
  54.8 0.9 collective-permute-start.12
  55.9 2.4 collective-permute-start.8
  58.4 9.6 %collective-permute-done.12.rest_6_ = bf16[512,256]{1,0:T(8,128)(2,1)S(1)} collective-permute-done((bf16[512,256]{1,0:T(8,128)(2,1)}, bf16[512,256]{1,0:T(8,128)(2,1)S(1)}, u32[]{:S(2)}, u32[]{:S(2)}) %collective-permute-start.12) | collective-permute-done | bytes 262176 | tf_op jit(solution)/shard_map/ppermute | solution.py:55
  68.0 5.4 %collective-permute-done.10.rest_4_ = bf16[512,256]{1,0:T(8,128)(2,1)S(1)} collective-permute-done((bf16[512,256]{1,0:T(8,128)(2,1)}, bf16[512,256]{1,0:T(8,128)(2,1)S(1)}, u32[]{:S(2)}, u32[]{:S(2)}) %collective-permute-start.10) | collective-permute-done | bytes 262176 | tf_op jit(solution)/shard_map/ppermute | solution.py:55
  73.5 0.4 collective-permute-start.9
  73.9 0.9 copy.32.starts_ref
  75.0 0.5 collective-permute-done.9.rest_3_
  75.7 9.2 %attend.2 = (bf16[128,1536]{1,0:T(8,128)(2,1)}, bf16[128,1536]{1,0:T(8,128)(2,1)}, bf16[4096,256]{1,0:T(8,128)(2,1)}) custom-call(s32[1]{0:T(128)} %bitcast.index_ref.wide_ref, s32[1]{0:T(128)} %bitcast.1.narrow_ref, s32[512]{0:T(512)} %copy-done.5, s32[512,1]{1,0:T(8,128)} %copy.32.starts_ref, bf16[512,384]{1,0:T(8,128)(2,1)} %get-tuple-element.67.q_ref, ...), custom_call_target="tpu_custom_call" | custom-call | flops 1207959552 | bytes 2097152 | tf_op jit(solution)/shard_map/attend/pallas_call | solution.py:431
  85.0 2.0 collective-permute-start.15
  87.0 1.7 copy-done.1
  88.7 4.7 %attend.3 = (bf16[128,1536]{1,0:T(8,128)(2,1)S(1)}, bf16[128,1536]{1,0:T(8,128)(2,1)S(1)}) custom-call(s32[1]{0:T(128)} %bitcast.index_ref.wide_ref, s32[1]{0:T(128)} %bitcast.1.narrow_ref, s32[512]{0:T(512)S(1)} %copy-done.6, s32[512,1]{1,0:T(8,128)S(1)} %copy-done.4, bf16[512,384]{1,0:T(8,128)(2,1)S(1)} %copy-done.8, bf16[1536,384]{1,0:T(8,128)(2,1)S(1)} %copy-done.7, ...), custom_call_target="tpu_custom_call" | custom-call | flops 1207959552 | bytes 2097152 | tf_op jit(solution)/shard_map/attend/pallas_call | solution.py:431
  93.4 0.7 copy-done.3
  94.1 0.6 collective-permute-start.16
  94.7 2.5 %collective-permute-start.14 = (bf16[128,1536]{1,0:T(8,128)(2,1)S(1)}, bf16[128,1536]{1,0:T(8,128)(2,1)S(1)}, u32[]{:S(2)}, u32[]{:S(2)}) collective-permute-start(bf16[128,1536]{1,0:T(8,128)(2,1)S(1)} %get-tuple-element.72), channel_id=1, source_target_pairs={{0,1},{1,0},{2,3},{3,2},{4,5},{5,4},{6,7},{7,6},{8,9},{9,8},{10,11... | collective-permute-start | bytes 1179656 | tf_op jit(solution)/shard_map/ppermute | solution.py:55
  97.2 16.3 %collective-permute-done.15.rest_2_ = bf16[128,1536]{1,0:T(8,128)(2,1)S(1)} collective-permute-done((bf16[128,1536]{1,0:T(8,128)(2,1)}, bf16[128,1536]{1,0:T(8,128)(2,1)S(1)}, u32[]{:S(2)}, u32[]{:S(2)}) %collective-permute-start.15) | collective-permute-done | bytes 393248 | tf_op jit(solution)/shard_map/ppermute | solution.py:55
  113.5 8.6 %collective-permute-done.16.rest_3_ = bf16[128,1536]{1,0:T(8,128)(2,1)S(1)} collective-permute-done((bf16[128,1536]{1,0:T(8,128)(2,1)S(1)}, bf16[128,1536]{1,0:T(8,128)(2,1)S(1)}, u32[]{:S(2)}, u32[]{:S(2)}) %collective-permute-start.16) | collective-permute-done | bytes 393248 | tf_op jit(solution)/shard_map/ppermute | solution.py:55
  122.2 0.7 copy-done.19
  123.0 3.2 %join.2 = (bf16[128,1536]{1,0:T(8,128)(2,1)}, bf16[128,1536]{1,0:T(8,128)(2,1)}, bf16[128,1536]{1,0:T(8,128)(2,1)}, bf16[128,1536]{1,0:T(8,128)(2,1)}) custom-call(bf16[128,1536]{1,0:T(8,128)(2,1)} %constant_dynamic-slice_fusion.1.base_ref, f32[1,1536]{1,0:T(1,128)} %reshape.198.gain_ref, bf16[128,1536]{1,0:T(8,128)(2,1)} %copy-done.3, ...), custom_call_target="tpu_custom_call" | custom-call | tf_op jit(solution)/shard_map/join/pallas_call | solution.py:461
  126.2 1.9 collective-permute-start.17
  128.2 0.3 fusion.2
  128.7 2.2 collective-permute-start.25
  130.9 15.5 %collective-permute-done.17.rest_0_ = bf16[128,1536]{1,0:T(8,128)(2,1)S(1)} collective-permute-done((bf16[128,1536]{1,0:T(8,128)(2,1)}, bf16[128,1536]{1,0:T(8,128)(2,1)S(1)}, u32[]{:S(2)}, u32[]{:S(2)}) %collective-permute-start.17) | collective-permute-done | bytes 393248 | tf_op jit(solution)/shard_map/ppermute | solution.py:55
  146.3 0.7 copy-done.21
  147.1 13.7 %ffn.2 = (bf16[128,1536]{1,0:T(8,128)(2,1)}, bf16[128,1536]{1,0:T(8,128)(2,1)}) custom-call(bf16[128,1536]{1,0:T(8,128)(2,1)} %copy-done.21, bf16[128,1536]{1,0:T(8,128)(2,1)} %get-tuple-element.78.rest_1_, bf16[8,3,192,2240]{3,2,1,0:T(8,128)(2,1)} %bitcast.20), custom_call_target="tpu_custom_call" | custom-call | flops 5284823040 | bytes 20643840 | tf_op jit(solution)/shard_map/ffn/pallas_call | solution.py:480
  161.0 3.4 %collective-permute-start.19 = (bf16[192,512]{1,0:T(8,128)(2,1)S(1)}, bf16[192,512]{1,0:T(8,128)(2,1)S(1)}, u32[]{:S(2)}, u32[]{:S(2)}) collective-permute-start(bf16[192,512]{1,0:T(8,128)(2,1)S(1)} %pad_maximum_fusion.4.rest_3_.rest_1_), channel_id=1, source_target_pairs={{0,8},{4,12},{8,0},{12,4},{16,24},{20,28},{24,16},{28,20},{1,9},{5... | collective-permute-start | bytes 589832 | tf_op jit(solution)/shard_map/ppermute | solution.py:55
  164.4 1.8 collective-permute-start.29
  166.2 11.8 %ffn.3 = (bf16[128,1536]{1,0:T(8,128)(2,1)S(1)}, bf16[128,1536]{1,0:T(8,128)(2,1)S(1)}) custom-call(bf16[128,1536]{1,0:T(8,128)(2,1)S(1)} %collective-permute-done.25.rest_0_, bf16[128,1536]{1,0:T(8,128)(2,1)S(1)} %collective-permute-done.26.rest_1_, bf16[8,3,192,2240]{3,2,1,0:T(8,128)(2,1)} %bitcast.21), custom_call_target="tpu_custom_call" | custom-call | flops 5284823040 | bytes 20643840 | tf_op jit(solution)/shard_map/ffn/pallas_call | solution.py:480
  178.0 2.2 collective-permute-start.27
  180.3 0.5 collective-permute-start.22
  180.8 0.9 collective-permute-done.24.rest_10_.rest_8_
  182.0 1.2 collective-permute-done.20.rest_6_.rest_4_
  183.2 10.6 %collective-permute-done.27.rest_1_ = bf16[128,1536]{1,0:T(8,128)(2,1)S(1)} collective-permute-done((bf16[128,1536]{1,0:T(8,128)(2,1)S(1)}, bf16[128,1536]{1,0:T(8,128)(2,1)S(1)}, u32[]{:S(2)}, u32[]{:S(2)}) %collective-permute-start.27) | collective-permute-done | bytes 393248 | tf_op jit(solution)/shard_map/ppermute | solution.py:55
  193.8 6.9 %collective-permute-done.28.rest_2_ = bf16[128,1536]{1,0:T(8,128)(2,1)} collective-permute-done((bf16[128,1536]{1,0:T(8,128)(2,1)S(1)}, bf16[128,1536]{1,0:T(8,128)(2,1)}, u32[]{:S(2)}, u32[]{:S(2)}) %collective-permute-start.28) | collective-permute-done | bytes 393248 | tf_op jit(solution)/shard_map/ppermute | solution.py:55
  200.7 0.7 copy-done.16
  201.4 2.7 %join.3 = (bf16[128,1536]{1,0:T(8,128)(2,1)}, bf16[128,1536]{1,0:T(8,128)(2,1)}, bf16[128,1536]{1,0:T(8,128)(2,1)}) custom-call(bf16[128,1536]{1,0:T(8,128)(2,1)} %get-tuple-element.82.base_ref, f32[1,1536]{1,0:T(1,128)} %reshape.198.gain_ref, bf16[128,1536]{1,0:T(8,128)(2,1)} %get-tuple-element.83.rest_0_, bf16[128,1536]{1,0:T(8,128)(2,1)} %copy-done.17, ...), custom_call_target="tpu_custom_call" | custom-call | tf_op jit(solution)/shard_map/join/pallas_call | solution.py:461
  204.2 0.3 collective-permute-start.30
  204.5 0.3 compare_reduce_fusion
  204.8 4.7 %collective-permute-start.32 = (bf16[128,1536]{1,0:T(8,128)(2,1)}, bf16[128,1536]{1,0:T(8,128)(2,1)S(1)}, u32[]{:S(2)}, u32[]{:S(2)}) collective-permute-start(bf16[128,1536]{1,0:T(8,128)(2,1)} %get-tuple-element.91), channel_id=1, source_target_pairs={{0,1},{1,0},{2,3},{3,2},{4,5},{5,4},{6,7},{7,6},{8,9},{9,8},{10,11... | collective-permute-start | bytes 1179656 | tf_op jit(solution)/shard_map/ppermute | solution.py:55
  209.5 14.0 %collective-permute-done.30.rest_2_ = bf16[128,1536]{1,0:T(8,128)(2,1)S(1)} collective-permute-done((bf16[128,1536]{1,0:T(8,128)(2,1)}, bf16[128,1536]{1,0:T(8,128)(2,1)S(1)}, u32[]{:S(2)}, u32[]{:S(2)}) %collective-permute-start.30) | collective-permute-done | bytes 393248 | tf_op jit(solution)/shard_map/ppermute | solution.py:55
  223.5 2.3 constant_dynamic-slice_fusion.3
  225.8 3.1 %gather_fusion = bf16[640,128]{1,0:T(8,128)(2,1)S(1)} fusion(bf16[4096,128]{1,0:T(8,128)(2,1)} %constant_dynamic-slice_fusion.3, s32[1024]{0:T(1024)S(1)} %pad_clamp_fusion), kind=kCustom, calls=%fused_computation | custom fusion | bytes 330240 | tf_op jit(solution)/shard_map/jit(_take)/gather | solution.py:299
  228.8 0.9 select_select_fusion
  229.7 3.8 %next.2 = (bf16[512,1536]{1,0:T(8,128)(2,1)}, bf16[512,384]{1,0:T(8,128)(2,1)}, bf16[512,128]{1,0:T(8,128)(2,1)}) custom-call(s32[1]{0:T(128)} %bitcast.index_ref.wide_ref, s32[1]{0:T(128)} %bitcast.1.narrow_ref, f32[1,1536]{1,0:T(1,128)S(1)} %reshape.199.gain_ref, f32[1,512]{1,0:T(1,128)S(1)} %maximum_convert_fusion.1.bias_ref, ...), custom_call_target="tpu_custom_call" | custom-call | flops 603979776 | bytes 4718592 | tf_op jit(solution)/shard_map/next/pallas_call | solution.py:516
  233.6 1.3 collective-permute-done.31.rest_0_
  234.9 3.2 %next.3 = (bf16[512,1536]{1,0:T(8,128)(2,1)}, bf16[512,384]{1,0:T(8,128)(2,1)}, bf16[512,128]{1,0:T(8,128)(2,1)}) custom-call(s32[1]{0:T(128)} %bitcast.index_ref.wide_ref, s32[1]{0:T(128)} %bitcast.1.narrow_ref, f32[1,1536]{1,0:T(1,128)S(1)} %reshape.199.gain_ref, ...), custom_call_target="tpu_custom_call", output_to_operand_aliasing={{0}: (13, {}), {1}: (14, {}), {2}: (15, {})} | custom-call | flops 201326592 | bytes 4718592 | tf_op jit(solution)/shard_map/next/pallas_call | solution.py:516
  (128 shorter events, 2.3 us)
Async XLA Ops:
  7.2 0.9 copy-start
  7.2 139.2 %all-gather.3.cloned.1.call-start = ((), (), s32[]{:S(2)}) async-start(), calls=%async_computation | async-start | bytes 23887872 | tf_op jit(solution)/shard_map/all_gather | solution.py:372
  9.1 5.8 %copy-start.9 = (bf16[192,1024]{1,0:T(8,128)(2,1)}, bf16[192,1024]{1,0:T(8,128)(2,1)S(1)}, u32[]{:S(2)}) copy-start(bf16[192,1024]{1,0:T(8,128)(2,1)S(1)} %pad_maximum_fusion.1.rest_0_) | copy-start | bytes 1179652
  9.1 3.7 %collective-permute-start = (bf16[192,1024]{1,0:T(8,128)(2,1)S(1)}, bf16[192,1024]{1,0:T(8,128)(2,1)S(1)}, u32[]{:S(2)}, u32[]{:S(2)}) collective-permute-start(bf16[192,1024]{1,0:T(8,128)(2,1)S(1)} %pad_maximum_fusion.1.rest_0_), channel_id=1, source_target_pairs={{0,4},{4,0},{8,12},{12,8},{16,20},{20,16},{24,28},{28,24},{1,5},{5... | collective-permute-start | bytes 1179656 | tf_op jit(solution)/shard_map/ppermute | solution.py:55
  12.8 3.7 %copy-start.38 = (bf16[512]{0:T(512)(128)(2,1)S(1)}, bf16[512]{0:T(512)(128)(2,1)}, u32[]{:S(2)}) copy-start(bf16[512]{0:T(512)(128)(2,1)} %param.29) | copy-start | bytes 3076
  12.8 3.8 %copy-start.28 = (bf16[384]{0:T(512)(128)(2,1)S(1)}, bf16[384]{0:T(512)(128)(2,1)}, u32[]{:S(2)}) copy-start(bf16[384]{0:T(512)(128)(2,1)} %param.27) | copy-start | bytes 2308
  12.8 5.2 %copy-start.25 = (s32[8]{0:T(128)S(1)}, s32[8]{0:T(128)}, u32[]{:S(2)}) copy-start(s32[8]{0:T(128)} %param.23) | copy-start | bytes 100
  12.8 5.2 %copy-start.27 = (s32[512]{0:T(512)S(1)}, s32[512]{0:T(512)}, u32[]{:S(2)}) copy-start(s32[512]{0:T(512)} %param.21) | copy-start | bytes 6148
  12.8 5.3 %copy-start.39 = (bf16[512]{0:T(512)(128)(2,1)S(1)}, bf16[512]{0:T(512)(128)(2,1)}, u32[]{:S(2)}) copy-start(bf16[512]{0:T(512)(128)(2,1)} %param.39) | copy-start | bytes 3076
  12.8 5.3 %copy-start.29 = (bf16[384]{0:T(512)(128)(2,1)S(1)}, bf16[384]{0:T(512)(128)(2,1)}, u32[]{:S(2)}) copy-start(bf16[384]{0:T(512)(128)(2,1)} %param.37) | copy-start | bytes 2308
  12.8 5.3 %copy-start.22 = (bf16[192,384]{1,0:T(8,128)(2,1)S(1)}, bf16[192,384]{1,0:T(8,128)(2,1)}, u32[]{:S(2)}) copy-start(bf16[192,384]{1,0:T(8,128)(2,1)} %param.36) | copy-start | bytes 442372
  12.8 29.5 %copy-start.24 = (bf16[1536]{0:T(1024)(128)(2,1)S(1)}, bf16[1536]{0:T(1024)(128)(2,1)}, u32[]{:S(2)}) copy-start(bf16[1536]{0:T(1024)(128)(2,1)} %param.25) | copy-start | bytes 9220
  12.9 33.1 %copy-start.10 = (bf16[192,1024]{1,0:T(8,128)(2,1)}, bf16[192,1024]{1,0:T(8,128)(2,1)S(1)}, u32[]{:S(2)}) copy-start(bf16[192,1024]{1,0:T(8,128)(2,1)S(1)} %collective-permute-done.rest_1_) | copy-start | bytes 1179652
  12.9 12.9 %collective-permute-start.5 = (bf16[192,1024]{1,0:T(8,128)(2,1)S(1)}, bf16[192,1024]{1,0:T(8,128)(2,1)S(1)}, u32[]{:S(2)}, u32[]{:S(2)}) collective-permute-start(bf16[192,1024]{1,0:T(8,128)(2,1)S(1)} %pad_maximum_fusion.1.rest_0_), channel_id=1, source_target_pairs={{0,24},{4,28},{8,16},{12,20},{16,8},{20,12},{24,0},{28,4},{1,25},{... | collective-permute-start | bytes 1179656 | tf_op jit(solution)/shard_map/ppermute | solution.py:55
  14.4 25.9 %collective-permute-start.3 = (bf16[192,1024]{1,0:T(8,128)(2,1)S(1)}, bf16[192,1024]{1,0:T(8,128)(2,1)S(1)}, u32[]{:S(2)}, u32[]{:S(2)}) collective-permute-start(bf16[192,1024]{1,0:T(8,128)(2,1)S(1)} %pad_maximum_fusion.1.rest_0_), channel_id=1, source_target_pairs={{0,16},{4,20},{8,24},{12,28},{16,0},{20,4},{24,8},{28,12},{1,17},{... | collective-permute-start | bytes 1179656 | tf_op jit(solution)/shard_map/ppermute | solution.py:55
  15.0 27.3 %collective-permute-start.1 = (bf16[192,1024]{1,0:T(8,128)(2,1)S(1)}, bf16[192,1024]{1,0:T(8,128)(2,1)S(1)}, u32[]{:S(2)}, u32[]{:S(2)}) collective-permute-start(bf16[192,1024]{1,0:T(8,128)(2,1)S(1)} %pad_maximum_fusion.1.rest_0_), channel_id=1, source_target_pairs={{0,8},{4,12},{8,0},{12,4},{16,24},{20,28},{24,16},{28,20},{1,9},{5... | collective-permute-start | bytes 1179656 | tf_op jit(solution)/shard_map/ppermute | solution.py:55
  18.1 55.9 %copy-start.5 = (s32[512]{0:T(512)}, s32[512]{0:T(512)S(1)}, u32[]{:S(2)}) copy-start(s32[512]{0:T(512)S(1)} %select_reduce_fusion.spots_ref) | copy-start | bytes 6148
  25.8 22.0 %copy-start.11 = (bf16[192,1024]{1,0:T(8,128)(2,1)}, bf16[192,1024]{1,0:T(8,128)(2,1)S(1)}, u32[]{:S(2)}) copy-start(bf16[192,1024]{1,0:T(8,128)(2,1)S(1)} %collective-permute-done.5.rest_6_) | copy-start | bytes 1179652
  25.8 21.9 %collective-permute-start.6 = (bf16[192,1024]{1,0:T(8,128)(2,1)S(1)}, bf16[192,1024]{1,0:T(8,128)(2,1)S(1)}, u32[]{:S(2)}, u32[]{:S(2)}) collective-permute-start(bf16[192,1024]{1,0:T(8,128)(2,1)S(1)} %collective-permute-done.5.rest_6_), channel_id=1, source_target_pairs={{0,4},{4,0},{8,12},{12,8},{16,20},{20,16},{24,28},{28,24},{1,5},{5... | collective-permute-start | bytes 1179656 | tf_op jit(solution)/shard_map/ppermute | solution.py:55
  40.3 7.5 %copy-start.12 = (bf16[192,1024]{1,0:T(8,128)(2,1)}, bf16[192,1024]{1,0:T(8,128)(2,1)S(1)}, u32[]{:S(2)}) copy-start(bf16[192,1024]{1,0:T(8,128)(2,1)S(1)} %collective-permute-done.3.rest_4_) | copy-start | bytes 1179652
  40.3 7.4 %collective-permute-start.4 = (bf16[192,1024]{1,0:T(8,128)(2,1)S(1)}, bf16[192,1024]{1,0:T(8,128)(2,1)}, u32[]{:S(2)}, u32[]{:S(2)}) collective-permute-start(bf16[192,1024]{1,0:T(8,128)(2,1)S(1)} %collective-permute-done.3.rest_4_), channel_id=1, source_target_pairs={{0,4},{4,0},{8,12},{12,8},{16,20},{20,16},{24,28},{28,24},{1,5},{5... | collective-permute-start | bytes 1179656 | tf_op jit(solution)/shard_map/ppermute | solution.py:55
  42.3 5.5 %copy-start.13 = (bf16[192,1024]{1,0:T(8,128)(2,1)}, bf16[192,1024]{1,0:T(8,128)(2,1)S(1)}, u32[]{:S(2)}) copy-start(bf16[192,1024]{1,0:T(8,128)(2,1)S(1)} %collective-permute-done.1.rest_2_) | copy-start | bytes 1179652
  42.3 5.5 %collective-permute-start.2 = (bf16[192,1024]{1,0:T(8,128)(2,1)S(1)}, bf16[192,1024]{1,0:T(8,128)(2,1)S(1)}, u32[]{:S(2)}, u32[]{:S(2)}) collective-permute-start(bf16[192,1024]{1,0:T(8,128)(2,1)S(1)} %collective-permute-done.1.rest_2_), channel_id=1, source_target_pairs={{0,4},{4,0},{8,12},{12,8},{16,20},{20,16},{24,28},{28,24},{1,5},{5... | collective-permute-start | bytes 1179656 | tf_op jit(solution)/shard_map/ppermute | solution.py:55
  54.8 32.2 %copy-start.7 = (bf16[1536,384]{1,0:T(8,128)(2,1)S(1)}, bf16[1536,384]{1,0:T(8,128)(2,1)}, u32[]{:S(2)}) copy-start(bf16[1536,384]{1,0:T(8,128)(2,1)} %get-tuple-element.68.w_out) | copy-start | bytes 3538948
  54.8 32.2 %copy-start.8 = (bf16[512,384]{1,0:T(8,128)(2,1)S(1)}, bf16[512,384]{1,0:T(8,128)(2,1)}, u32[]{:S(2)}) copy-start(bf16[512,384]{1,0:T(8,128)(2,1)} %get-tuple-element.67.q_ref) | copy-start | bytes 1179652
  54.8 13.2 %collective-permute-start.12 = (bf16[512,256]{1,0:T(8,128)(2,1)}, bf16[512,256]{1,0:T(8,128)(2,1)S(1)}, u32[]{:S(2)}, u32[]{:S(2)}) collective-permute-start(bf16[512,256]{1,0:T(8,128)(2,1)} %get-tuple-element.69.rest_0_), channel_id=1, source_target_pairs={{0,24},{4,28},{8,16},{12,20},{16,8},{20,12},{24,0},{28,4},{1,25},{... | collective-permute-start | bytes 786440 | tf_op jit(solution)/shard_map/ppermute | solution.py:55
  55.8 17.7 %collective-permute-start.10 = (bf16[512,256]{1,0:T(8,128)(2,1)}, bf16[512,256]{1,0:T(8,128)(2,1)S(1)}, u32[]{:S(2)}, u32[]{:S(2)}) collective-permute-start(bf16[512,256]{1,0:T(8,128)(2,1)} %get-tuple-element.69.rest_0_), channel_id=1, source_target_pairs={{0,16},{4,20},{8,24},{12,28},{16,0},{20,4},{24,8},{28,12},{1,17},{... | collective-permute-start | bytes 786440 | tf_op jit(solution)/shard_map/ppermute | solution.py:55
  55.9 17.6 %collective-permute-start.8 = (bf16[512,256]{1,0:T(8,128)(2,1)}, bf16[512,256]{1,0:T(8,128)(2,1)S(1)}, u32[]{:S(2)}, u32[]{:S(2)}) collective-permute-start(bf16[512,256]{1,0:T(8,128)(2,1)} %get-tuple-element.69.rest_0_), channel_id=1, source_target_pairs={{0,8},{4,12},{8,0},{12,4},{16,24},{20,28},{24,16},{28,20},{1,9},{5... | collective-permute-start | bytes 786440 | tf_op jit(solution)/shard_map/ppermute | solution.py:55
  58.4 16.4 %collective-permute-start.7 = (bf16[512,256]{1,0:T(8,128)(2,1)}, bf16[512,256]{1,0:T(8,128)(2,1)S(1)}, u32[]{:S(2)}, u32[]{:S(2)}) collective-permute-start(bf16[512,256]{1,0:T(8,128)(2,1)} %get-tuple-element.69.rest_0_), channel_id=1, source_target_pairs={{0,4},{4,0},{8,12},{12,8},{16,20},{20,16},{24,28},{28,24},{1,5},{5... | collective-permute-start | bytes 786440 | tf_op jit(solution)/shard_map/ppermute | solution.py:55
  68.0 7.4 %copy-start.32 = (bf16[512,256]{1,0:T(8,128)(2,1)}, bf16[512,256]{1,0:T(8,128)(2,1)S(1)}, u32[]{:S(2)}) copy-start(bf16[512,256]{1,0:T(8,128)(2,1)S(1)} %collective-permute-done.12.rest_6_) | copy-start | bytes 786436
  68.0 6.8 %collective-permute-start.13 = (bf16[512,256]{1,0:T(8,128)(2,1)S(1)}, bf16[512,256]{1,0:T(8,128)(2,1)S(1)}, u32[]{:S(2)}, u32[]{:S(2)}) collective-permute-start(bf16[512,256]{1,0:T(8,128)(2,1)S(1)} %collective-permute-done.12.rest_6_), channel_id=1, source_target_pairs={{0,4},{4,0},{8,12},{12,8},{16,20},{20,16},{24,28},{28,24},{1,5},{5... | collective-permute-start | bytes 786440 | tf_op jit(solution)/shard_map/ppermute | solution.py:55
  73.4 2.0 copy-start.33
  73.4 1.5 collective-permute-start.11
  73.5 2.0 copy-start.34
  73.5 1.9 collective-permute-start.9
  74.8 12.2 %copy-start.4 = (s32[512,1]{1,0:T(8,128)S(1)}, s32[512,1]{1,0:T(8,128)}, u32[]{:S(2)}) copy-start(s32[512,1]{1,0:T(8,128)} %copy.32.starts_ref) | copy-start | bytes 6148
  74.8 12.2 %copy-start.6 = (s32[512]{0:T(512)S(1)}, s32[512]{0:T(512)}, u32[]{:S(2)}) copy-start(s32[512]{0:T(512)} %copy-done.5) | copy-start | bytes 6148
  85.0 28.5 %collective-permute-start.15 = (bf16[128,1536]{1,0:T(8,128)(2,1)}, bf16[128,1536]{1,0:T(8,128)(2,1)S(1)}, u32[]{:S(2)}, u32[]{:S(2)}) collective-permute-start(bf16[128,1536]{1,0:T(8,128)(2,1)} %get-tuple-element.73), channel_id=1, source_target_pairs={{0,2},{1,3},{2,0},{3,1},{4,6},{5,7},{6,4},{7,5},{8,10},{9,11},{10,... | collective-permute-start | bytes 1179656 | tf_op jit(solution)/shard_map/ppermute | solution.py:55
  87.0 1.7 copy-start.1
  88.6 5.5 %copy-start.31 = (bf16[128,1536]{1,0:T(8,128)(2,1)S(1)}, bf16[128,1536]{1,0:T(8,128)(2,1)}, u32[]{:S(2)}) copy-start(bf16[128,1536]{1,0:T(8,128)(2,1)} %get-tuple-element.74) | copy-start | bytes 1179652
  88.7 39.5 %copy-start.23 = (s32[8,16]{1,0:T(8,128)S(1)}, s32[8,16]{1,0:T(8,128)}, u32[]{:S(2)}) copy-start(s32[8,16]{1,0:T(8,128)} %param.24) | copy-start | bytes 1540
  88.7 39.8 %copy-start.26 = (s32[8]{0:T(128)S(1)}, s32[8]{0:T(128)}, u32[]{:S(2)}) copy-start(s32[8]{0:T(128)} %param.23) | copy-start | bytes 100
  88.7 39.8 %copy-start.30 = (s32[8]{0:T(128)S(1)}, s32[8]{0:T(128)}, u32[]{:S(2)}) copy-start(s32[8]{0:T(128)} %param.22) | copy-start | bytes 100
  94.1 28.0 %collective-permute-start.16 = (bf16[128,1536]{1,0:T(8,128)(2,1)S(1)}, bf16[128,1536]{1,0:T(8,128)(2,1)S(1)}, u32[]{:S(2)}, u32[]{:S(2)}) collective-permute-start(bf16[128,1536]{1,0:T(8,128)(2,1)S(1)} %copy-done.31), channel_id=1, source_target_pairs={{0,3},{1,2},{2,1},{3,0},{4,7},{5,6},{6,5},{7,4},{8,11},{9,10},{10,... | collective-permute-start | bytes 1179656 | tf_op jit(solution)/shard_map/ppermute | solution.py:55
  94.7 27.4 %collective-permute-start.14 = (bf16[128,1536]{1,0:T(8,128)(2,1)S(1)}, bf16[128,1536]{1,0:T(8,128)(2,1)S(1)}, u32[]{:S(2)}, u32[]{:S(2)}) collective-permute-start(bf16[128,1536]{1,0:T(8,128)(2,1)S(1)} %get-tuple-element.72), channel_id=1, source_target_pairs={{0,1},{1,0},{2,3},{3,2},{4,5},{5,4},{6,7},{7,6},{8,9},{9,8},{10,11... | collective-permute-start | bytes 1179656 | tf_op jit(solution)/shard_map/ppermute | solution.py:55
  113.5 8.6 %copy-start.18 = (bf16[128,1536]{1,0:T(8,128)(2,1)}, bf16[128,1536]{1,0:T(8,128)(2,1)S(1)}, u32[]{:S(2)}) copy-start(bf16[128,1536]{1,0:T(8,128)(2,1)S(1)} %collective-permute-done.15.rest_2_) | copy-start | bytes 1179652
  126.2 20.1 %collective-permute-start.17 = (bf16[128,1536]{1,0:T(8,128)(2,1)}, bf16[128,1536]{1,0:T(8,128)(2,1)S(1)}, u32[]{:S(2)}, u32[]{:S(2)}) collective-permute-start(bf16[128,1536]{1,0:T(8,128)(2,1)} %get-tuple-element.77), channel_id=1, source_target_pairs={{0,3},{1,2},{2,1},{3,0},{4,7},{5,6},{6,5},{7,4},{8,11},{9,10},{10,... | collective-permute-start | bytes 1179656 | tf_op jit(solution)/shard_map/ppermute | solution.py:55
  128.7 35.7 %collective-permute-start.25 = (bf16[128,1536]{1,0:T(8,128)(2,1)}, bf16[128,1536]{1,0:T(8,128)(2,1)S(1)}, u32[]{:S(2)}, u32[]{:S(2)}) collective-permute-start(bf16[128,1536]{1,0:T(8,128)(2,1)} %get-tuple-element.84), channel_id=1, source_target_pairs={{0,1},{1,0},{2,3},{3,2},{4,5},{5,4},{6,7},{7,6},{8,9},{9,8},{10,11... | collective-permute-start | bytes 1179656 | tf_op jit(solution)/shard_map/ppermute | solution.py:55
  146.3 18.0 %collective-permute-start.26 = (bf16[128,1536]{1,0:T(8,128)(2,1)S(1)}, bf16[128,1536]{1,0:T(8,128)(2,1)S(1)}, u32[]{:S(2)}, u32[]{:S(2)}) collective-permute-start(bf16[128,1536]{1,0:T(8,128)(2,1)S(1)} %collective-permute-done.17.rest_0_), channel_id=1, source_target_pairs={{0,1},{1,0},{2,3},{3,2},{4,5},{5,4},{6,7},{7,6},{8,9},{9,8},{10,11... | collective-permute-start | bytes 1179656 | tf_op jit(solution)/shard_map/ppermute | solution.py:55
  160.8 17.1 %collective-permute-start.23 = (bf16[192,512]{1,0:T(8,128)(2,1)S(1)}, bf16[192,512]{1,0:T(8,128)(2,1)S(1)}, u32[]{:S(2)}, u32[]{:S(2)}) collective-permute-start(bf16[192,512]{1,0:T(8,128)(2,1)S(1)} %pad_maximum_fusion.4.rest_3_.rest_1_), channel_id=1, source_target_pairs={{0,24},{4,28},{8,16},{12,20},{16,8},{20,12},{24,0},{28,4},{1,25},{... | collective-permute-start | bytes 589832 | tf_op jit(solution)/shard_map/ppermute | solution.py:55
  160.9 19.3 %collective-permute-start.21 = (bf16[192,512]{1,0:T(8,128)(2,1)S(1)}, bf16[192,512]{1,0:T(8,128)(2,1)S(1)}, u32[]{:S(2)}, u32[]{:S(2)}) collective-permute-start(bf16[192,512]{1,0:T(8,128)(2,1)S(1)} %pad_maximum_fusion.4.rest_3_.rest_1_), channel_id=1, source_target_pairs={{0,16},{4,20},{8,24},{12,28},{16,0},{20,4},{24,8},{28,12},{1,17},{... | collective-permute-start | bytes 589832 | tf_op jit(solution)/shard_map/ppermute | solution.py:55
  161.0 19.2 %collective-permute-start.19 = (bf16[192,512]{1,0:T(8,128)(2,1)S(1)}, bf16[192,512]{1,0:T(8,128)(2,1)S(1)}, u32[]{:S(2)}, u32[]{:S(2)}) collective-permute-start(bf16[192,512]{1,0:T(8,128)(2,1)S(1)} %pad_maximum_fusion.4.rest_3_.rest_1_), channel_id=1, source_target_pairs={{0,8},{4,12},{8,0},{12,4},{16,24},{20,28},{24,16},{28,20},{1,9},{5... | collective-permute-start | bytes 589832 | tf_op jit(solution)/shard_map/ppermute | solution.py:55
  164.4 15.9 %collective-permute-start.18 = (bf16[192,512]{1,0:T(8,128)(2,1)S(1)}, bf16[192,512]{1,0:T(8,128)(2,1)S(1)}, u32[]{:S(2)}, u32[]{:S(2)}) collective-permute-start(bf16[192,512]{1,0:T(8,128)(2,1)S(1)} %pad_maximum_fusion.4.rest_3_.rest_1_), channel_id=1, source_target_pairs={{0,4},{4,0},{8,12},{12,8},{16,20},{20,16},{24,28},{28,24},{1,5},{5... | collective-permute-start | bytes 589832 | tf_op jit(solution)/shard_map/ppermute | solution.py:55
  164.4 36.3 %collective-permute-start.29 = (bf16[128,1536]{1,0:T(8,128)(2,1)}, bf16[128,1536]{1,0:T(8,128)(2,1)S(1)}, u32[]{:S(2)}, u32[]{:S(2)}) collective-permute-start(bf16[128,1536]{1,0:T(8,128)(2,1)} %get-tuple-element.80), channel_id=1, source_target_pairs={{0,3},{1,2},{2,1},{3,0},{4,7},{5,6},{6,5},{7,4},{8,11},{9,10},{10,... | collective-permute-start | bytes 1179656 | tf_op jit(solution)/shard_map/ppermute | solution.py:55
  178.0 15.8 %collective-permute-start.27 = (bf16[128,1536]{1,0:T(8,128)(2,1)S(1)}, bf16[128,1536]{1,0:T(8,128)(2,1)S(1)}, u32[]{:S(2)}, u32[]{:S(2)}) collective-permute-start(bf16[128,1536]{1,0:T(8,128)(2,1)S(1)} %get-tuple-element.87), channel_id=1, source_target_pairs={{0,1},{1,0},{2,3},{3,2},{4,5},{5,4},{6,7},{7,6},{8,9},{9,8},{10,11... | collective-permute-start | bytes 1179656 | tf_op jit(solution)/shard_map/ppermute | solution.py:55
  180.2 20.5 %collective-permute-start.28 = (bf16[128,1536]{1,0:T(8,128)(2,1)S(1)}, bf16[128,1536]{1,0:T(8,128)(2,1)}, u32[]{:S(2)}, u32[]{:S(2)}) collective-permute-start(bf16[128,1536]{1,0:T(8,128)(2,1)S(1)} %get-tuple-element.88), channel_id=1, source_target_pairs={{0,2},{1,3},{2,0},{3,1},{4,6},{5,7},{6,4},{7,5},{8,10},{9,11},{10,... | collective-permute-start | bytes 1179656 | tf_op jit(solution)/shard_map/ppermute | solution.py:55
  180.2 1.5 collective-permute-start.24
  180.3 1.7 collective-permute-start.22
  181.7 1.4 collective-permute-start.20
  193.8 6.9 %copy-start.17 = (bf16[128,1536]{1,0:T(8,128)(2,1)}, bf16[128,1536]{1,0:T(8,128)(2,1)S(1)}, u32[]{:S(2)}) copy-start(bf16[128,1536]{1,0:T(8,128)(2,1)S(1)} %collective-permute-done.27.rest_1_) | copy-start | bytes 1179652
  204.2 25.6 %copy-start.2 = (bf16[128,1536]{1,0:T(8,128)(2,1)S(1)}, bf16[128,1536]{1,0:T(8,128)(2,1)}, u32[]{:S(2)}) copy-start(bf16[128,1536]{1,0:T(8,128)(2,1)} %get-tuple-element.90.rest_0_) | copy-start | bytes 1179652
  204.2 19.3 %collective-permute-start.30 = (bf16[128,1536]{1,0:T(8,128)(2,1)}, bf16[128,1536]{1,0:T(8,128)(2,1)S(1)}, u32[]{:S(2)}, u32[]{:S(2)}) collective-permute-start(bf16[128,1536]{1,0:T(8,128)(2,1)} %get-tuple-element.89), channel_id=1, source_target_pairs={{0,3},{1,2},{2,1},{3,0},{4,7},{5,6},{6,5},{7,4},{8,11},{9,10},{10,... | collective-permute-start | bytes 1179656 | tf_op jit(solution)/shard_map/ppermute | solution.py:55
  204.8 24.9 %collective-permute-start.32 = (bf16[128,1536]{1,0:T(8,128)(2,1)}, bf16[128,1536]{1,0:T(8,128)(2,1)S(1)}, u32[]{:S(2)}, u32[]{:S(2)}) collective-permute-start(bf16[128,1536]{1,0:T(8,128)(2,1)} %get-tuple-element.91), channel_id=1, source_target_pairs={{0,1},{1,0},{2,3},{3,2},{4,5},{5,4},{6,7},{7,6},{8,9},{9,8},{10,11... | collective-permute-start | bytes 1179656 | tf_op jit(solution)/shard_map/ppermute | solution.py:55
  223.5 11.4 %collective-permute-start.31 = (bf16[128,1536]{1,0:T(8,128)(2,1)S(1)}, bf16[128,1536]{1,0:T(8,128)(2,1)S(1)}, u32[]{:S(2)}, u32[]{:S(2)}) collective-permute-start(bf16[128,1536]{1,0:T(8,128)(2,1)S(1)} %collective-permute-done.30.rest_2_), channel_id=1, source_target_pairs={{0,1},{1,0},{2,3},{3,2},{4,5},{5,4},{6,7},{7,6},{8,9},{9,8},{10,11... | collective-permute-start | bytes 1179656 | tf_op jit(solution)/shard_map/ppermute | solution.py:55
  (10 other events, 7.8 us)
Sparse Core Ops, SparseCore 0:
  13.0 126.3 all-gather.2

commit v7 on v6

--- a/solution.py
+++ b/solution.py
@@ -55,12 +55,15 @@
     return lax.ppermute(value, axis, [(i, i ^ mask) for i in range(size)])
 
 
-def wide_pieces(value, size):
+def wide_pieces(value, size, *tokens):
     pieces = {0: value}
     for mask in range(2, size, 2):
         pieces[mask] = exchange(value, "wide", size, mask)
     for mask in range(0, size, 2):
-        pieces[mask + 1] = exchange(pieces[mask], "wide", size, 1)
+        source = pieces[mask]
+        if tokens and mask:
+            (source,) = after([source], *tokens)
+        pieces[mask + 1] = exchange(source, "wide", size, 1)
     return [pieces[m] for m in range(size)]
 
 
@@ -203,15 +206,20 @@
     x_refs, weights_ref, rest = rest[:count], rest[count], rest[count + 1 :]
     part_refs, (x, held, gate, hidden, sems) = rest[:count], rest[count:]
     copies = [
-        pltpu.make_async_copy(weights_ref.at[:, j], held.at[j], sems.at[j]) for j in range(3)
+        [
+            pltpu.make_async_copy(weights_ref.at[p, j], held.at[j, p], sems.at[j, p])
+            for p in range(held.shape[1])
+        ]
+        for j in range(3)
     ]
-    for c in copies:
-        c.start()
+    for group in copies:
+        for c in group:
+            c.start()
     share = x_refs[0].shape[0]
     for k in range(len(x_refs)):
         x[k * share : (k + 1) * share, :] = x_refs[k][...]
     depth, width = x.shape[1], hidden.shape[1]
-    tile = 256
+    tile = 1024
     whole = width // tile
 
     def each_tile(body):
@@ -234,11 +242,14 @@
         value = gate[:, lanes]
         hidden[:, lanes] = (value / (1.0 + jnp.exp(-value)) * up).astype(bf16)
 
-    copies[0].wait()
+    for c in copies[0]:
+        c.wait()
     each_tile(gate_tile)
-    copies[1].wait()
+    for c in copies[1]:
+        c.wait()
     each_tile(up_tile)
-    copies[2].wait()
+    for c in copies[2]:
+        c.wait()
     pieces, rows = held.shape[1], held.shape[2]
     group = 768 // rows
     for g in range(pieces // group):
@@ -249,13 +260,9 @@
             part_refs[k][:, lanes] = product[k * share : (k + 1) * share].astype(bf16)
 
 
-def next_kernel(wide, shares, wide_ref, narrow_ref, gain_ref, bias_ref, *rest):
-    count = len(shares)
-    h_refs, pieces = rest[:count], rest[count : count + wide]
-    *outs, weight, query, keyval, sems, out_sems = rest[-8:]
-    copies = place_copies(pieces, weight, sems, wide_ref[0])
-    for c in copies:
-        c.start()
+def next_kernel(shares, narrow_ref, gain_ref, bias_ref, weight, *rest):
+    h_refs = rest[: len(shares)]
+    *outs, query, keyval, out_sems = rest[-6:]
     share = h_refs[0].shape[0]
     width = query.shape[1]
     flushes = []
@@ -269,8 +276,6 @@
 
     for i, k in enumerate(shares):
         flush(h_refs[i], k, 0)
-    for c in copies:
-        c.wait()
     for i, k in enumerate(shares):
         rows = slice(i * share, (i + 1) * share)
         normed = norm_rows(h_refs[i][...].astype(f32), gain_ref[...])
@@ -344,7 +349,6 @@
     qkv_bias = jnp.concatenate(
         [b_query, lax.dynamic_slice_in_dim(b_keyval, pair_offset, 2 * HD, 0)]
     ).astype(f32)[None]
-    qkv_pieces = wide_pieces(qkv_weight, wide)
 
 
     token_start = lookup(seg_offsets, segment_ids)
@@ -368,7 +372,6 @@
     next_row = next_gain.astype(f32)[None]
     starts_column = token_start[:, None]
     packed = jnp.stack([w_gate, w_up, w_down.T])
-    (packed,) = after([packed], qkv_pieces[1])
     ffn_weights = lax.all_gather(packed, "wide", axis=0, tiled=False)
     early = (
         cosine,
@@ -381,7 +384,8 @@
         next_row,
         starts_column,
     )
-    early, qkv_pieces = lax.optimization_barrier((early, qkv_pieces))
+    early = lax.optimization_barrier(early)
+    qkv_pieces = wide_pieces(qkv_weight, wide, *early)
     cosine, sine, qkv_bias, next_weight, next_bias, base_rows = early[:6]
     mlp_row, next_row, starts_column = early[6:]
 
@@ -487,7 +491,7 @@
                 VMEM((3, wide, piece_rows, width), bf16),
                 VMEM((count * share, width), f32),
                 VMEM((count * share, width), bf16),
-                pltpu.SemaphoreType.DMA((3,)),
+                pltpu.SemaphoreType.DMA((3, wide)),
             ],
             compiler_params=params(60 if x_shares is far else 44),
             cost_estimate=pl.CostEstimate(
@@ -503,33 +507,29 @@
     part_one, part_two = feed_forward(list(after(normed_pieces[1:3], part_three)))
     parts = [part_zero, part_one, part_two, part_three]
 
-    (next_weight,) = after([next_weight], part_three)
-    next_pieces = wide_pieces(next_weight, wide)
-    (residual,) = after([residual], *next_pieces)
+    (next_weight,) = after([next_weight], residual)
+    next_weight = lax.all_gather(next_weight, "wide", axis=0, tiled=True)
     hidden_rows = join(narrow_swap(parts, narrow), residual, mlp_row, False)
     hidden_pieces = narrow_spread(hidden_rows, narrow)
 
     next_width = query_width + HD
     def project(shares, outputs):
         count = len(shares)
-        operands = 4 + count + wide
+        operands = 4 + count
         return pl.pallas_call(
-            functools.partial(next_kernel, wide, shares),
+            functools.partial(next_kernel, shares),
             out_shape=(
                 jax.ShapeDtypeStruct((tok_rows, depth), bf16),
                 jax.ShapeDtypeStruct((tok_rows, query_width), bf16),
                 jax.ShapeDtypeStruct((tok_rows, HD), bf16),
             ),
-            in_specs=[smem_spec()] * 2
-            + [vmem_spec()] * (2 + count)
-            + [any_spec()] * wide
+            in_specs=[smem_spec()]
+            + [vmem_spec()] * (3 + count)
             + [hbm_spec()] * len(outputs),
             out_specs=(hbm_spec(),) * 3,
             scratch_shapes=[
-                VMEM((depth, next_width), bf16),
                 VMEM((count * share, query_width), bf16),
                 VMEM((count * share, HD), bf16),
-                pltpu.SemaphoreType.DMA((wide,)),
                 pltpu.SemaphoreType.DMA((3 * count,)),
             ],
             input_output_aliases={operands + i: i for i in range(len(outputs))},
@@ -541,12 +541,11 @@
             ),
             name="next",
         )(
-            wide_index[None],
             narrow_index[None],
             next_row,
             next_bias,
+            next_weight,
             *[hidden_pieces[k] for k in shares],
-            *next_pieces,
             *outputs,
         )
 

time: 247 us -> 237 us (0.960)
  Pallas kernels: 58.6 us -> 52.4 us
  starting transfers between devices: 30 us -> 26.7 us
    ppermute x33 -> x26, starting transfers between devices: 30 us -> 26.6 us  [exchange(): return lax.ppermute(value, axis, [(i, i ^ mask) for i in range(size)])]
    pallas_call x2, Pallas kernels: 7.05 us -> 4.05 us  [project(): pl.pallas_call(functools.partial(next_kernel, shares), out_shape=(jax.Sha...]
    pallas_call x2, Pallas kernels: 25.5 us -> 23 us  [feed_forward(): pl.pallas_call(functools.partial(ffn_kernel, count), out_shape=[share_sha...]
    unnamed x80 -> x96, local copies, waits for them, and re-layouts: 6.83 us -> 8.44 us
    ppermute x33 -> x26, waiting for transfers between devices: 114 us -> 114 us  [exchange(): return lax.ppermute(value, axis, [(i, i ^ mask) for i in range(size)])]
  transfers between devices with their start and end apart: 34 -> 28, of which waited for: 17 -> 19; matrix products, arithmetic and copies ran while one was open for 8% -> 6% of each run, Pallas kernels for 21% -> 22%
where the time goes in v7:
time: 237 us; the launch traced here: 234 us
  waiting for transfers between devices  114 us (48%)
  Pallas kernels  52.4 us (22%)
  starting transfers between devices  26.7 us (11%)
  local copies, waits for them, and re-layouts  17.5 us (7%)
  between operations  14.5 us (6%)
  other arithmetic  8.82 us (4%)
    ppermute x26, waiting for transfers between devices, exchange(): return lax.ppermute(value, axis, [(i, i ^ mask) for i in range(size)])  114 us
    ppermute x26, starting transfers between devices, exchange(): return lax.ppermute(value, axis, [(i, i ^ mask) for i in range(size)])  26.6 us
    pallas_call x2, Pallas kernels, feed_forward(): pl.pallas_call(functools.partial(ffn_kernel, count), out_shape=[share_sha...  23 us
    pallas_call x2, Pallas kernels, attend(): pl.pallas_call(functools.partial(attend_kernel, wide, shares), out_shape=...  13.5 us
    unnamed x96, local copies, waits for them, and re-layouts  8.44 us
    pallas_call x1, Pallas kernels, local(): pl.pallas_call(functools.partial(qkv_kernel, wide), out_shape=(jax.ShapeD...  6.16 us
    pallas_call x2, Pallas kernels, join(): pl.pallas_call(functools.partial(join_kernel, narrow), out_shape=[shape]...  5.72 us
  transfers between devices with their start and end apart: 28, of which 19 were waited for; matrix products, arithmetic and copies ran while one was open for 6% of the time, Pallas kernels for 22%

profile of v7, /device:TPU:10, one launch (start us, length us, event | category | flops | bytes accessed | tf_op | source)
XLA Modules:
  0.0 234.0 jit_solution(4125762465424136632)
XLA Ops:
  7.2 3.5 %pad_maximum_fusion = bf16[3,192,2240]{2,1,0:T(8,128)(2,1)} fusion(bf16[1,192,2240]{2,1,0:T(8,128)(2,1)} %bitcast.22, bf16[1,192,2240]{2,1,0:T(8,128)(2,1)} %bitcast.23, bf16[1,192,2240]{2,1,0:T(8,128)(2,1)} %bitcast.24), kind=kLoop, calls=%fused_computation.1 | loop fusion | flops 2580480 | bytes 5160960 | tf_op jit(solution)/shard_map/stack | solution.py:374
  11.0 0.7 copy-done.27
  11.8 1.6 collective-permute-start.5
  13.4 0.5 collective-permute-start.3
  13.9 1.5 collective-permute-start.1
  15.6 0.5 maximum_convert_fusion.bias_ref
  16.1 0.8 constant_dynamic-slice_fusion.2
  17.0 0.7 pad_maximum_fusion.4
  17.7 1.0 fusion
  18.8 0.6 reshape.198.gain_ref
  19.4 1.0 pad_maximum_fusion.2
  20.4 1.9 constant_dynamic-slice_fusion.1.base_ref
  22.3 2.6 %collective-permute-done.5.rest_6_ = bf16[192,1024]{1,0:T(8,128)(2,1)S(1)} collective-permute-done((bf16[192,1024]{1,0:T(8,128)(2,1)S(1)}, bf16[192,1024]{1,0:T(8,128)(2,1)S(1)}, u32[]{:S(2)}, u32[]{:S(2)}) %collective-permute-start.5) | collective-permute-done | bytes 393248 | tf_op jit(solution)/shard_map/ppermute | solution.py:55
  24.9 14.1 %collective-permute-done.3.rest_4_ = bf16[192,1024]{1,0:T(8,128)(2,1)S(1)} collective-permute-done((bf16[192,1024]{1,0:T(8,128)(2,1)S(1)}, bf16[192,1024]{1,0:T(8,128)(2,1)S(1)}, u32[]{:S(2)}, u32[]{:S(2)}) %collective-permute-start.3) | collective-permute-done | bytes 393248 | tf_op jit(solution)/shard_map/ppermute | solution.py:55
  39.0 2.6 %collective-permute-done.1.rest_2_ = bf16[192,1024]{1,0:T(8,128)(2,1)S(1)} collective-permute-done((bf16[192,1024]{1,0:T(8,128)(2,1)S(1)}, bf16[192,1024]{1,0:T(8,128)(2,1)S(1)}, u32[]{:S(2)}, u32[]{:S(2)}) %collective-permute-start.1) | collective-permute-done | bytes 393248 | tf_op jit(solution)/shard_map/ppermute | solution.py:55
  41.6 0.5 collective-permute-start.4
  42.2 0.6 reshape.200.gain_ref
  42.8 0.6 collective-permute-done.2.rest_3_
  43.4 0.6 collective-permute-done.4.rest_5_
  43.9 0.6 collective-permute-done.6.rest_7_
  44.7 0.6 copy-done.19
  45.2 6.2 %qkv.1 = (bf16[512,384]{1,0:T(8,128)(2,1)}, bf16[512,256]{1,0:T(8,128)(2,1)}, bf16[1536,384]{1,0:T(8,128)(2,1)}) custom-call(s32[1]{0:T(128)} %bitcast.3.index_ref.wide_ref, bf16[512,1536]{1,0:T(8,128)(2,1)} %hidden_ref.1, f32[1,1536]{1,0:T(1,128)} %reshape.200.gain_ref, f32[1,640]{1,0:T(1,128)} %maximum_convert_fusion.bias_ref, ...), custom_call_target="tpu_custom_call" | custom-call | flops 1006632960 | bytes 3538944 | tf_op jit(solution)/shard_map/qkv/pallas_call | solution.py:393
  51.5 1.1 collective-permute-start.10
  52.6 2.4 %collective-permute-start.8 = (bf16[512,256]{1,0:T(8,128)(2,1)}, bf16[512,256]{1,0:T(8,128)(2,1)S(1)}, u32[]{:S(2)}, u32[]{:S(2)}) collective-permute-start(bf16[512,256]{1,0:T(8,128)(2,1)} %get-tuple-element.58.rest_0_), channel_id=1, source_target_pairs={{0,8},{4,12},{8,0},{12,4},{16,24},{20,28},{24,16},{28,20},{1,9},{5... | collective-permute-start | bytes 786440 | tf_op jit(solution)/shard_map/ppermute | solution.py:55
  54.9 11.5 %collective-permute-done.12.rest_6_ = bf16[512,256]{1,0:T(8,128)(2,1)S(1)} collective-permute-done((bf16[512,256]{1,0:T(8,128)(2,1)}, bf16[512,256]{1,0:T(8,128)(2,1)S(1)}, u32[]{:S(2)}, u32[]{:S(2)}) %collective-permute-start.12) | collective-permute-done | bytes 262176 | tf_op jit(solution)/shard_map/ppermute | solution.py:55
  66.4 5.3 %collective-permute-done.10.rest_4_ = bf16[512,256]{1,0:T(8,128)(2,1)S(1)} collective-permute-done((bf16[512,256]{1,0:T(8,128)(2,1)}, bf16[512,256]{1,0:T(8,128)(2,1)S(1)}, u32[]{:S(2)}, u32[]{:S(2)}) %collective-permute-start.10) | collective-permute-done | bytes 262176 | tf_op jit(solution)/shard_map/ppermute | solution.py:55
  71.8 0.4 collective-permute-start.9
  72.3 0.8 copy.32.starts_ref
  73.3 0.4 collective-permute-done.9.rest_3_
  74.0 0.4 copy-done.45
  74.4 8.8 %attend.2 = (bf16[128,1536]{1,0:T(8,128)(2,1)}, bf16[128,1536]{1,0:T(8,128)(2,1)}, bf16[4096,256]{1,0:T(8,128)(2,1)}) custom-call(s32[1]{0:T(128)} %bitcast.3.index_ref.wide_ref, s32[1]{0:T(128)} %bitcast.narrow_ref, s32[512]{0:T(512)} %copy-done.8, s32[512,1]{1,0:T(8,128)} %copy.32.starts_ref, bf16[512,384]{1,0:T(8,128)(2,1)} %get-tuple-element.56.q_ref, ...), custom_call_target="tpu_custom_call" | custom-call | flops 1207959552 | bytes 2097152 | tf_op jit(solution)/shard_map/attend/pallas_call | solution.py:435
  83.1 2.0 collective-permute-start.15
  85.1 1.6 copy-done.3
  86.7 4.7 %attend.3 = (bf16[128,1536]{1,0:T(8,128)(2,1)S(1)}, bf16[128,1536]{1,0:T(8,128)(2,1)S(1)}) custom-call(s32[1]{0:T(128)} %bitcast.3.index_ref.wide_ref, s32[1]{0:T(128)} %bitcast.narrow_ref, s32[512]{0:T(512)S(1)} %copy-done.9, s32[512,1]{1,0:T(8,128)S(1)} %copy-done.7, bf16[512,384]{1,0:T(8,128)(2,1)S(1)} %copy-done.11, bf16[1536,384]{1,0:T(8,128)(2,1)S(1)} %copy-done.10, ...), custom_call_target="tpu_custom_call" | custom-call | flops 1207959552 | bytes 2097152 | tf_op jit(solution)/shard_map/attend/pallas_call | solution.py:435
  91.5 0.7 copy-done.6
  92.2 0.7 collective-permute-start.16
  92.9 2.5 %collective-permute-start.14 = (bf16[128,1536]{1,0:T(8,128)(2,1)S(1)}, bf16[128,1536]{1,0:T(8,128)(2,1)S(1)}, u32[]{:S(2)}, u32[]{:S(2)}) collective-permute-start(bf16[128,1536]{1,0:T(8,128)(2,1)S(1)} %get-tuple-element.61), channel_id=1, source_target_pairs={{0,1},{1,0},{2,3},{3,2},{4,5},{5,4},{6,7},{7,6},{8,9},{9,8},{10,11... | collective-permute-start | bytes 1179656 | tf_op jit(solution)/shard_map/ppermute | solution.py:55
  95.4 16.3 %collective-permute-done.15.rest_2_ = bf16[128,1536]{1,0:T(8,128)(2,1)S(1)} collective-permute-done((bf16[128,1536]{1,0:T(8,128)(2,1)}, bf16[128,1536]{1,0:T(8,128)(2,1)S(1)}, u32[]{:S(2)}, u32[]{:S(2)}) %collective-permute-start.15) | collective-permute-done | bytes 393248 | tf_op jit(solution)/shard_map/ppermute | solution.py:55
  111.7 8.5 %collective-permute-done.16.rest_3_ = bf16[128,1536]{1,0:T(8,128)(2,1)S(1)} collective-permute-done((bf16[128,1536]{1,0:T(8,128)(2,1)S(1)}, bf16[128,1536]{1,0:T(8,128)(2,1)S(1)}, u32[]{:S(2)}, u32[]{:S(2)}) %collective-permute-start.16) | collective-permute-done | bytes 393248 | tf_op jit(solution)/shard_map/ppermute | solution.py:55
  120.2 0.7 copy-done.23
  121.1 3.0 %join.2 = (bf16[128,1536]{1,0:T(8,128)(2,1)}, bf16[128,1536]{1,0:T(8,128)(2,1)}, bf16[128,1536]{1,0:T(8,128)(2,1)}, bf16[128,1536]{1,0:T(8,128)(2,1)}) custom-call(bf16[128,1536]{1,0:T(8,128)(2,1)} %constant_dynamic-slice_fusion.1.base_ref, f32[1,1536]{1,0:T(1,128)} %reshape.198.gain_ref, bf16[128,1536]{1,0:T(8,128)(2,1)} %copy-done.6, ...), custom_call_target="tpu_custom_call" | custom-call | tf_op jit(solution)/shard_map/join/pallas_call | solution.py:465
  124.1 2.3 collective-permute-start.17
  126.4 0.3 fusion.2
  127.0 2.2 collective-permute-start.18
  129.1 15.5 %collective-permute-done.17.rest_0_ = bf16[128,1536]{1,0:T(8,128)(2,1)S(1)} collective-permute-done((bf16[128,1536]{1,0:T(8,128)(2,1)}, bf16[128,1536]{1,0:T(8,128)(2,1)S(1)}, u32[]{:S(2)}, u32[]{:S(2)}) %collective-permute-start.17) | collective-permute-done | bytes 393248 | tf_op jit(solution)/shard_map/ppermute | solution.py:55
  144.7 0.7 copy-done.25
  145.4 12.1 %ffn.2 = (bf16[128,1536]{1,0:T(8,128)(2,1)}, bf16[128,1536]{1,0:T(8,128)(2,1)}) custom-call(bf16[128,1536]{1,0:T(8,128)(2,1)} %copy-done.25, bf16[128,1536]{1,0:T(8,128)(2,1)} %get-tuple-element.67.rest_1_, bf16[8,3,192,2240]{3,2,1,0:T(8,128)(2,1)} %bitcast.20), custom_call_target="tpu_custom_call" | custom-call | flops 5284823040 | bytes 20643840 | tf_op jit(solution)/shard_map/ffn/pallas_call | solution.py:484
  157.5 1.8 collective-permute-start.22
  159.4 10.9 %ffn.3 = (bf16[128,1536]{1,0:T(8,128)(2,1)}, bf16[128,1536]{1,0:T(8,128)(2,1)S(1)}) custom-call(bf16[128,1536]{1,0:T(8,128)(2,1)S(1)} %collective-permute-done.18.rest_0_, bf16[128,1536]{1,0:T(8,128)(2,1)S(1)} %collective-permute-done.19.rest_1_, bf16[8,3,192,2240]{3,2,1,0:T(8,128)(2,1)} %bitcast.21), custom_call_target="tpu_custom_call" | custom-call | flops 5284823040 | bytes 20643840 | tf_op jit(solution)/shard_map/ffn/pallas_call | solution.py:484
  170.2 2.3 collective-permute-start.20
  172.6 11.8 %collective-permute-done.20.rest_1_ = bf16[128,1536]{1,0:T(8,128)(2,1)S(1)} collective-permute-done((bf16[128,1536]{1,0:T(8,128)(2,1)}, bf16[128,1536]{1,0:T(8,128)(2,1)S(1)}, u32[]{:S(2)}, u32[]{:S(2)}) %collective-permute-start.20) | collective-permute-done | bytes 393248 | tf_op jit(solution)/shard_map/ppermute | solution.py:55
  184.5 8.4 %collective-permute-done.21.rest_2_ = bf16[128,1536]{1,0:T(8,128)(2,1)S(1)} collective-permute-done((bf16[128,1536]{1,0:T(8,128)(2,1)S(1)}, bf16[128,1536]{1,0:T(8,128)(2,1)S(1)}, u32[]{:S(2)}, u32[]{:S(2)}) %collective-permute-start.21) | collective-permute-done | bytes 393248 | tf_op jit(solution)/shard_map/ppermute | solution.py:55
  192.8 0.7 copy-done.21
  193.6 2.7 %join.3 = (bf16[128,1536]{1,0:T(8,128)(2,1)}, bf16[128,1536]{1,0:T(8,128)(2,1)}, bf16[128,1536]{1,0:T(8,128)(2,1)}) custom-call(bf16[128,1536]{1,0:T(8,128)(2,1)} %get-tuple-element.64.base_ref, f32[1,1536]{1,0:T(1,128)} %reshape.198.gain_ref, bf16[128,1536]{1,0:T(8,128)(2,1)} %get-tuple-element.68.rest_0_, bf16[128,1536]{1,0:T(8,128)(2,1)} %copy-done.20, ...), custom_call_target="tpu_custom_call" | custom-call | tf_op jit(solution)/shard_map/join/pallas_call | solution.py:465
  196.3 0.7 collective-permute-start.23
  197.3 4.2 %collective-permute-start.25 = (bf16[128,1536]{1,0:T(8,128)(2,1)}, bf16[128,1536]{1,0:T(8,128)(2,1)}, u32[]{:S(2)}, u32[]{:S(2)}) collective-permute-start(bf16[128,1536]{1,0:T(8,128)(2,1)} %get-tuple-element.77), channel_id=1, source_target_pairs={{0,1},{1,0},{2,3},{3,2},{4,5},{5,4},{6,7},{7,6},{8,9},{9,8},{10,11... | collective-permute-start | bytes 1179656 | tf_op jit(solution)/shard_map/ppermute | solution.py:55
  201.5 13.1 %collective-permute-done.23.rest_2_ = bf16[128,1536]{1,0:T(8,128)(2,1)S(1)} collective-permute-done((bf16[128,1536]{1,0:T(8,128)(2,1)}, bf16[128,1536]{1,0:T(8,128)(2,1)S(1)}, u32[]{:S(2)}, u32[]{:S(2)}) %collective-permute-start.23) | collective-permute-done | bytes 393248 | tf_op jit(solution)/shard_map/ppermute | solution.py:55
  214.6 1.0 constant_dynamic-slice_fusion.3
  215.7 3.1 %gather_fusion = bf16[640,128]{1,0:T(8,128)(2,1)S(1)} fusion(bf16[4096,128]{1,0:T(8,128)(2,1)} %constant_dynamic-slice_fusion.3, s32[1024]{0:T(1024)S(1)} %pad_clamp_fusion), kind=kCustom, calls=%fused_computation | custom fusion | bytes 330240 | tf_op jit(solution)/shard_map/jit(_take)/gather | solution.py:304
  218.7 0.9 select_select_fusion
  219.9 1.4 copy-done.1
  221.3 2.9 %next.2 = (bf16[512,1536]{1,0:T(8,128)(2,1)}, bf16[512,384]{1,0:T(8,128)(2,1)}, bf16[512,128]{1,0:T(8,128)(2,1)}) custom-call(s32[1]{0:T(128)} %bitcast.narrow_ref, f32[1,1536]{1,0:T(1,128)S(1)} %reshape.199.gain_ref, f32[1,512]{1,0:T(1,128)S(1)} %maximum_convert_fusion.1.bias_ref, bf16[1536,512]{1,0:T(8,128)(2,1)S(1)} %copy-done.1, ...), custom_call_target="tpu_custom_call" | custom-call | flops 603979776 | bytes 4718592 | tf_op jit(solution)/shard_map/next/pallas_call | solution.py:519
  224.2 1.7 collective-permute-done.24.rest_0_
  226.0 1.2 next.3
  (133 shorter events, 2.7 us)
Async XLA Ops:
  7.2 3.8 %copy-start = (bf16[192,512]{1,0:T(8,128)(2,1)S(1)}, bf16[192,512]{1,0:T(8,128)(2,1)}, u32[]{:S(2)}) copy-start(bf16[192,512]{1,0:T(8,128)(2,1)} %param.28) | copy-start | bytes 589828
  7.2 137.5 %all-gather.6.cloned.1.call-start = ((), (), s32[]{:S(2)}) async-start(), calls=%async_computation.1 | async-start | bytes 23887872 | tf_op jit(solution)/shard_map/all_gather | solution.py:375
  10.8 1.0 copy-start.28
  10.8 4.6 %copy-start.46 = (bf16[512]{0:T(512)(128)(2,1)S(1)}, bf16[512]{0:T(512)(128)(2,1)}, u32[]{:S(2)}) copy-start(bf16[512]{0:T(512)(128)(2,1)} %param.29) | copy-start | bytes 3076
  10.8 4.7 %copy-start.35 = (bf16[384]{0:T(512)(128)(2,1)S(1)}, bf16[384]{0:T(512)(128)(2,1)}, u32[]{:S(2)}) copy-start(bf16[384]{0:T(512)(128)(2,1)} %param.27) | copy-start | bytes 2308
  10.8 4.7 %copy-start.36 = (bf16[384]{0:T(512)(128)(2,1)S(1)}, bf16[384]{0:T(512)(128)(2,1)}, u32[]{:S(2)}) copy-start(bf16[384]{0:T(512)(128)(2,1)} %param.37) | copy-start | bytes 2308
  10.8 4.7 %copy-start.47 = (bf16[512]{0:T(512)(128)(2,1)S(1)}, bf16[512]{0:T(512)(128)(2,1)}, u32[]{:S(2)}) copy-start(bf16[512]{0:T(512)(128)(2,1)} %param.39) | copy-start | bytes 3076
  10.8 6.1 %copy-start.33 = (s32[8]{0:T(128)S(1)}, s32[8]{0:T(128)}, u32[]{:S(2)}) copy-start(s32[8]{0:T(128)} %param.23) | copy-start | bytes 100
  10.8 6.1 %copy-start.34 = (s32[512]{0:T(512)S(1)}, s32[512]{0:T(512)}, u32[]{:S(2)}) copy-start(s32[512]{0:T(512)} %param.21) | copy-start | bytes 6148
  10.8 6.2 %copy-start.26 = (bf16[192,384]{1,0:T(8,128)(2,1)S(1)}, bf16[192,384]{1,0:T(8,128)(2,1)}, u32[]{:S(2)}) copy-start(bf16[192,384]{1,0:T(8,128)(2,1)} %param.36) | copy-start | bytes 442372
  10.8 7.9 %copy-start.30 = (bf16[1536]{0:T(1024)(128)(2,1)S(1)}, bf16[1536]{0:T(1024)(128)(2,1)}, u32[]{:S(2)}) copy-start(bf16[1536]{0:T(1024)(128)(2,1)} %param.31) | copy-start | bytes 9220
  10.9 8.5 %copy-start.31 = (bf16[1536]{0:T(1024)(128)(2,1)S(1)}, bf16[1536]{0:T(1024)(128)(2,1)}, u32[]{:S(2)}) copy-start(bf16[1536]{0:T(1024)(128)(2,1)} %param.35) | copy-start | bytes 9220
  10.9 208.8 %all-gather.4.cloned.1.call-start = ((), (), s32[]{:S(2)}) async-start(), calls=%async_computation | async-start | bytes 1769472 | tf_op jit(solution)/shard_map/all_gather | solution.py:511
  11.8 30.4 %copy-start.32 = (bf16[1536]{0:T(1024)(128)(2,1)S(1)}, bf16[1536]{0:T(1024)(128)(2,1)}, u32[]{:S(2)}) copy-start(bf16[1536]{0:T(1024)(128)(2,1)} %param.25) | copy-start | bytes 9220
  11.8 32.7 %copy-start.12 = (bf16[192,1024]{1,0:T(8,128)(2,1)}, bf16[192,1024]{1,0:T(8,128)(2,1)S(1)}, u32[]{:S(2)}) copy-start(bf16[192,1024]{1,0:T(8,128)(2,1)S(1)} %pad_maximum_fusion.1.rest_0_) | copy-start | bytes 1179652
  11.8 13.1 %collective-permute-start.5 = (bf16[192,1024]{1,0:T(8,128)(2,1)S(1)}, bf16[192,1024]{1,0:T(8,128)(2,1)S(1)}, u32[]{:S(2)}, u32[]{:S(2)}) collective-permute-start(bf16[192,1024]{1,0:T(8,128)(2,1)S(1)} %pad_maximum_fusion.1.rest_0_), channel_id=1, source_target_pairs={{0,24},{4,28},{8,16},{12,20},{16,8},{20,12},{24,0},{28,4},{1,25},{... | collective-permute-start | bytes 1179656 | tf_op jit(solution)/shard_map/ppermute | solution.py:55
  13.4 25.7 %collective-permute-start.3 = (bf16[192,1024]{1,0:T(8,128)(2,1)S(1)}, bf16[192,1024]{1,0:T(8,128)(2,1)S(1)}, u32[]{:S(2)}, u32[]{:S(2)}) collective-permute-start(bf16[192,1024]{1,0:T(8,128)(2,1)S(1)} %pad_maximum_fusion.1.rest_0_), channel_id=1, source_target_pairs={{0,16},{4,20},{8,24},{12,28},{16,0},{20,4},{24,8},{28,12},{1,17},{... | collective-permute-start | bytes 1179656 | tf_op jit(solution)/shard_map/ppermute | solution.py:55
  13.9 27.8 %collective-permute-start.1 = (bf16[192,1024]{1,0:T(8,128)(2,1)S(1)}, bf16[192,1024]{1,0:T(8,128)(2,1)S(1)}, u32[]{:S(2)}, u32[]{:S(2)}) collective-permute-start(bf16[192,1024]{1,0:T(8,128)(2,1)S(1)} %pad_maximum_fusion.1.rest_0_), channel_id=1, source_target_pairs={{0,8},{4,12},{8,0},{12,4},{16,24},{20,28},{24,16},{28,20},{1,9},{5... | collective-permute-start | bytes 1179656 | tf_op jit(solution)/shard_map/ppermute | solution.py:55
  15.4 27.4 %collective-permute-start = (bf16[192,1024]{1,0:T(8,128)(2,1)S(1)}, bf16[192,1024]{1,0:T(8,128)(2,1)S(1)}, u32[]{:S(2)}, u32[]{:S(2)}) collective-permute-start(bf16[192,1024]{1,0:T(8,128)(2,1)S(1)} %pad_maximum_fusion.1.rest_0_), channel_id=1, source_target_pairs={{0,4},{4,0},{8,12},{12,8},{16,20},{20,16},{24,28},{28,24},{1,5},{5... | collective-permute-start | bytes 1179656 | tf_op jit(solution)/shard_map/ppermute | solution.py:55
  17.0 55.2 %copy-start.8 = (s32[512]{0:T(512)}, s32[512]{0:T(512)S(1)}, u32[]{:S(2)}) copy-start(s32[512]{0:T(512)S(1)} %select_reduce_fusion.spots_ref) | copy-start | bytes 6148
  24.9 19.6 %copy-start.13 = (bf16[192,1024]{1,0:T(8,128)(2,1)}, bf16[192,1024]{1,0:T(8,128)(2,1)S(1)}, u32[]{:S(2)}) copy-start(bf16[192,1024]{1,0:T(8,128)(2,1)S(1)} %collective-permute-done.5.rest_6_) | copy-start | bytes 1179652
  39.0 5.5 %copy-start.14 = (bf16[192,1024]{1,0:T(8,128)(2,1)}, bf16[192,1024]{1,0:T(8,128)(2,1)S(1)}, u32[]{:S(2)}) copy-start(bf16[192,1024]{1,0:T(8,128)(2,1)S(1)} %collective-permute-done.3.rest_4_) | copy-start | bytes 1179652
  41.6 2.9 %copy-start.15 = (bf16[192,1024]{1,0:T(8,128)(2,1)}, bf16[192,1024]{1,0:T(8,128)(2,1)S(1)}, u32[]{:S(2)}) copy-start(bf16[192,1024]{1,0:T(8,128)(2,1)S(1)} %collective-permute-done.1.rest_2_) | copy-start | bytes 1179652
  41.6 1.7 collective-permute-start.2
  41.6 2.3 collective-permute-start.4
  42.1 2.3 collective-permute-start.6
  42.8 1.8 copy-start.16
  43.4 1.2 copy-start.17
  51.4 15.0 %collective-permute-start.12 = (bf16[512,256]{1,0:T(8,128)(2,1)}, bf16[512,256]{1,0:T(8,128)(2,1)S(1)}, u32[]{:S(2)}, u32[]{:S(2)}) collective-permute-start(bf16[512,256]{1,0:T(8,128)(2,1)} %get-tuple-element.58.rest_0_), channel_id=1, source_target_pairs={{0,24},{4,28},{8,16},{12,20},{16,8},{20,12},{24,0},{28,4},{1,25},{... | collective-permute-start | bytes 786440 | tf_op jit(solution)/shard_map/ppermute | solution.py:55
  51.5 20.3 %collective-permute-start.10 = (bf16[512,256]{1,0:T(8,128)(2,1)}, bf16[512,256]{1,0:T(8,128)(2,1)S(1)}, u32[]{:S(2)}, u32[]{:S(2)}) collective-permute-start(bf16[512,256]{1,0:T(8,128)(2,1)} %get-tuple-element.58.rest_0_), channel_id=1, source_target_pairs={{0,16},{4,20},{8,24},{12,28},{16,0},{20,4},{24,8},{28,12},{1,17},{... | collective-permute-start | bytes 786440 | tf_op jit(solution)/shard_map/ppermute | solution.py:55
  52.6 19.3 %collective-permute-start.8 = (bf16[512,256]{1,0:T(8,128)(2,1)}, bf16[512,256]{1,0:T(8,128)(2,1)S(1)}, u32[]{:S(2)}, u32[]{:S(2)}) collective-permute-start(bf16[512,256]{1,0:T(8,128)(2,1)} %get-tuple-element.58.rest_0_), channel_id=1, source_target_pairs={{0,8},{4,12},{8,0},{12,4},{16,24},{20,28},{24,16},{28,20},{1,9},{5... | collective-permute-start | bytes 786440 | tf_op jit(solution)/shard_map/ppermute | solution.py:55
  54.9 18.2 %collective-permute-start.7 = (bf16[512,256]{1,0:T(8,128)(2,1)}, bf16[512,256]{1,0:T(8,128)(2,1)S(1)}, u32[]{:S(2)}, u32[]{:S(2)}) collective-permute-start(bf16[512,256]{1,0:T(8,128)(2,1)} %get-tuple-element.58.rest_0_), channel_id=1, source_target_pairs={{0,4},{4,0},{8,12},{12,8},{16,20},{20,16},{24,28},{28,24},{1,5},{5... | collective-permute-start | bytes 786440 | tf_op jit(solution)/shard_map/ppermute | solution.py:55
  66.4 7.2 %copy-start.39 = (bf16[512,256]{1,0:T(8,128)(2,1)}, bf16[512,256]{1,0:T(8,128)(2,1)S(1)}, u32[]{:S(2)}) copy-start(bf16[512,256]{1,0:T(8,128)(2,1)S(1)} %collective-permute-done.12.rest_6_) | copy-start | bytes 786436
  66.4 6.7 %collective-permute-start.13 = (bf16[512,256]{1,0:T(8,128)(2,1)S(1)}, bf16[512,256]{1,0:T(8,128)(2,1)S(1)}, u32[]{:S(2)}, u32[]{:S(2)}) collective-permute-start(bf16[512,256]{1,0:T(8,128)(2,1)S(1)} %collective-permute-done.12.rest_6_), channel_id=1, source_target_pairs={{0,4},{4,0},{8,12},{12,8},{16,20},{20,16},{24,28},{28,24},{1,5},{5... | collective-permute-start | bytes 786440 | tf_op jit(solution)/shard_map/ppermute | solution.py:55
  71.7 1.9 copy-start.40
  71.7 1.5 collective-permute-start.11
  71.8 1.8 copy-start.41
  71.8 1.8 collective-permute-start.9
  74.4 10.8 %copy-start.7 = (s32[512,1]{1,0:T(8,128)S(1)}, s32[512,1]{1,0:T(8,128)}, u32[]{:S(2)}) copy-start(s32[512,1]{1,0:T(8,128)} %copy.32.starts_ref) | copy-start | bytes 6148
  74.4 10.8 %copy-start.9 = (s32[512]{0:T(512)S(1)}, s32[512]{0:T(512)}, u32[]{:S(2)}) copy-start(s32[512]{0:T(512)} %copy-done.8) | copy-start | bytes 6148
  74.4 10.8 %copy-start.10 = (bf16[1536,384]{1,0:T(8,128)(2,1)S(1)}, bf16[1536,384]{1,0:T(8,128)(2,1)}, u32[]{:S(2)}) copy-start(bf16[1536,384]{1,0:T(8,128)(2,1)} %get-tuple-element.57.w_out) | copy-start | bytes 3538948
  74.4 10.8 %copy-start.11 = (bf16[512,384]{1,0:T(8,128)(2,1)S(1)}, bf16[512,384]{1,0:T(8,128)(2,1)}, u32[]{:S(2)}) copy-start(bf16[512,384]{1,0:T(8,128)(2,1)} %get-tuple-element.56.q_ref) | copy-start | bytes 1179652
  83.1 28.5 %collective-permute-start.15 = (bf16[128,1536]{1,0:T(8,128)(2,1)}, bf16[128,1536]{1,0:T(8,128)(2,1)S(1)}, u32[]{:S(2)}, u32[]{:S(2)}) collective-permute-start(bf16[128,1536]{1,0:T(8,128)(2,1)} %get-tuple-element.62), channel_id=1, source_target_pairs={{0,2},{1,3},{2,0},{3,1},{4,6},{5,7},{6,4},{7,5},{8,10},{9,11},{10,... | collective-permute-start | bytes 1179656 | tf_op jit(solution)/shard_map/ppermute | solution.py:55
  85.1 1.6 copy-start.3
  86.7 5.5 %copy-start.38 = (bf16[128,1536]{1,0:T(8,128)(2,1)S(1)}, bf16[128,1536]{1,0:T(8,128)(2,1)}, u32[]{:S(2)}) copy-start(bf16[128,1536]{1,0:T(8,128)(2,1)} %get-tuple-element.63) | copy-start | bytes 1179652
  86.7 39.7 %copy-start.29 = (s32[8,16]{1,0:T(8,128)S(1)}, s32[8,16]{1,0:T(8,128)}, u32[]{:S(2)}) copy-start(s32[8,16]{1,0:T(8,128)} %param.24) | copy-start | bytes 1540
  92.2 34.6 %copy-start.37 = (s32[8]{0:T(128)S(1)}, s32[8]{0:T(128)}, u32[]{:S(2)}) copy-start(s32[8]{0:T(128)} %param.22) | copy-start | bytes 100
  92.2 28.0 %collective-permute-start.16 = (bf16[128,1536]{1,0:T(8,128)(2,1)S(1)}, bf16[128,1536]{1,0:T(8,128)(2,1)S(1)}, u32[]{:S(2)}, u32[]{:S(2)}) collective-permute-start(bf16[128,1536]{1,0:T(8,128)(2,1)S(1)} %copy-done.38), channel_id=1, source_target_pairs={{0,3},{1,2},{2,1},{3,0},{4,7},{5,6},{6,5},{7,4},{8,11},{9,10},{10,... | collective-permute-start | bytes 1179656 | tf_op jit(solution)/shard_map/ppermute | solution.py:55
  92.9 27.3 %collective-permute-start.14 = (bf16[128,1536]{1,0:T(8,128)(2,1)S(1)}, bf16[128,1536]{1,0:T(8,128)(2,1)S(1)}, u32[]{:S(2)}, u32[]{:S(2)}) collective-permute-start(bf16[128,1536]{1,0:T(8,128)(2,1)S(1)} %get-tuple-element.61), channel_id=1, source_target_pairs={{0,1},{1,0},{2,3},{3,2},{4,5},{5,4},{6,7},{7,6},{8,9},{9,8},{10,11... | collective-permute-start | bytes 1179656 | tf_op jit(solution)/shard_map/ppermute | solution.py:55
  111.7 8.5 %copy-start.22 = (bf16[128,1536]{1,0:T(8,128)(2,1)}, bf16[128,1536]{1,0:T(8,128)(2,1)S(1)}, u32[]{:S(2)}) copy-start(bf16[128,1536]{1,0:T(8,128)(2,1)S(1)} %collective-permute-done.15.rest_2_) | copy-start | bytes 1179652
  124.1 20.5 %collective-permute-start.17 = (bf16[128,1536]{1,0:T(8,128)(2,1)}, bf16[128,1536]{1,0:T(8,128)(2,1)S(1)}, u32[]{:S(2)}, u32[]{:S(2)}) collective-permute-start(bf16[128,1536]{1,0:T(8,128)(2,1)} %get-tuple-element.66), channel_id=1, source_target_pairs={{0,3},{1,2},{2,1},{3,0},{4,7},{5,6},{6,5},{7,4},{8,11},{9,10},{10,... | collective-permute-start | bytes 1179656 | tf_op jit(solution)/shard_map/ppermute | solution.py:55
  127.0 32.4 %collective-permute-start.18 = (bf16[128,1536]{1,0:T(8,128)(2,1)}, bf16[128,1536]{1,0:T(8,128)(2,1)S(1)}, u32[]{:S(2)}, u32[]{:S(2)}) collective-permute-start(bf16[128,1536]{1,0:T(8,128)(2,1)} %get-tuple-element.69), channel_id=1, source_target_pairs={{0,1},{1,0},{2,3},{3,2},{4,5},{5,4},{6,7},{7,6},{8,9},{9,8},{10,11... | collective-permute-start | bytes 1179656 | tf_op jit(solution)/shard_map/ppermute | solution.py:55
  144.6 14.7 %collective-permute-start.19 = (bf16[128,1536]{1,0:T(8,128)(2,1)S(1)}, bf16[128,1536]{1,0:T(8,128)(2,1)S(1)}, u32[]{:S(2)}, u32[]{:S(2)}) collective-permute-start(bf16[128,1536]{1,0:T(8,128)(2,1)S(1)} %collective-permute-done.17.rest_0_), channel_id=1, source_target_pairs={{0,1},{1,0},{2,3},{3,2},{4,5},{5,4},{6,7},{7,6},{8,9},{9,8},{10,11... | collective-permute-start | bytes 1179656 | tf_op jit(solution)/shard_map/ppermute | solution.py:55
  157.5 35.3 %collective-permute-start.22 = (bf16[128,1536]{1,0:T(8,128)(2,1)}, bf16[128,1536]{1,0:T(8,128)(2,1)}, u32[]{:S(2)}, u32[]{:S(2)}) collective-permute-start(bf16[128,1536]{1,0:T(8,128)(2,1)} %get-tuple-element.70), channel_id=1, source_target_pairs={{0,3},{1,2},{2,1},{3,0},{4,7},{5,6},{6,5},{7,4},{8,11},{9,10},{10,... | collective-permute-start | bytes 1179656 | tf_op jit(solution)/shard_map/ppermute | solution.py:55
  159.3 55.3 %copy-start.4 = (bf16[4096,256]{1,0:T(8,128)(2,1)S(1)}, bf16[4096,256]{1,0:T(8,128)(2,1)}, u32[]{:S(2)}) copy-start(bf16[4096,256]{1,0:T(8,128)(2,1)} %get-tuple-element.59.rest_0_) | copy-start | bytes 6291460
  170.2 14.2 %collective-permute-start.20 = (bf16[128,1536]{1,0:T(8,128)(2,1)}, bf16[128,1536]{1,0:T(8,128)(2,1)S(1)}, u32[]{:S(2)}, u32[]{:S(2)}) collective-permute-start(bf16[128,1536]{1,0:T(8,128)(2,1)} %get-tuple-element.73), channel_id=1, source_target_pairs={{0,1},{1,0},{2,3},{3,2},{4,5},{5,4},{6,7},{7,6},{8,9},{9,8},{10,11... | collective-permute-start | bytes 1179656 | tf_op jit(solution)/shard_map/ppermute | solution.py:55
  172.5 20.3 %collective-permute-start.21 = (bf16[128,1536]{1,0:T(8,128)(2,1)S(1)}, bf16[128,1536]{1,0:T(8,128)(2,1)S(1)}, u32[]{:S(2)}, u32[]{:S(2)}) collective-permute-start(bf16[128,1536]{1,0:T(8,128)(2,1)S(1)} %get-tuple-element.74), channel_id=1, source_target_pairs={{0,2},{1,3},{2,0},{3,1},{4,6},{5,7},{6,4},{7,5},{8,10},{9,11},{10,... | collective-permute-start | bytes 1179656 | tf_op jit(solution)/shard_map/ppermute | solution.py:55
  184.5 8.4 %copy-start.20 = (bf16[128,1536]{1,0:T(8,128)(2,1)}, bf16[128,1536]{1,0:T(8,128)(2,1)S(1)}, u32[]{:S(2)}) copy-start(bf16[128,1536]{1,0:T(8,128)(2,1)S(1)} %collective-permute-done.20.rest_1_) | copy-start | bytes 1179652
  196.3 23.6 %copy-start.5 = (bf16[128,1536]{1,0:T(8,128)(2,1)S(1)}, bf16[128,1536]{1,0:T(8,128)(2,1)}, u32[]{:S(2)}) copy-start(bf16[128,1536]{1,0:T(8,128)(2,1)} %get-tuple-element.76.rest_0_) | copy-start | bytes 1179652
  196.3 18.3 %collective-permute-start.23 = (bf16[128,1536]{1,0:T(8,128)(2,1)}, bf16[128,1536]{1,0:T(8,128)(2,1)S(1)}, u32[]{:S(2)}, u32[]{:S(2)}) collective-permute-start(bf16[128,1536]{1,0:T(8,128)(2,1)} %get-tuple-element.75), channel_id=1, source_target_pairs={{0,3},{1,2},{2,1},{3,0},{4,7},{5,6},{6,5},{7,4},{8,11},{9,10},{10,... | collective-permute-start | bytes 1179656 | tf_op jit(solution)/shard_map/ppermute | solution.py:55
  197.3 22.6 %collective-permute-start.25 = (bf16[128,1536]{1,0:T(8,128)(2,1)}, bf16[128,1536]{1,0:T(8,128)(2,1)}, u32[]{:S(2)}, u32[]{:S(2)}) collective-permute-start(bf16[128,1536]{1,0:T(8,128)(2,1)} %get-tuple-element.77), channel_id=1, source_target_pairs={{0,1},{1,0},{2,3},{3,2},{4,5},{5,4},{6,7},{7,6},{8,9},{9,8},{10,11... | collective-permute-start | bytes 1179656 | tf_op jit(solution)/shard_map/ppermute | solution.py:55
  214.6 11.3 %collective-permute-start.24 = (bf16[128,1536]{1,0:T(8,128)(2,1)S(1)}, bf16[128,1536]{1,0:T(8,128)(2,1)S(1)}, u32[]{:S(2)}, u32[]{:S(2)}) collective-permute-start(bf16[128,1536]{1,0:T(8,128)(2,1)S(1)} %collective-permute-done.23.rest_2_), channel_id=1, source_target_pairs={{0,1},{1,0},{2,3},{3,2},{4,5},{5,4},{6,7},{7,6},{8,9},{9,8},{10,11... | collective-permute-start | bytes 1179656 | tf_op jit(solution)/shard_map/ppermute | solution.py:55
  219.9 1.4 copy-start.1
  221.3 4.6 %copy-start.2 = (bf16[1536,512]{1,0:T(8,128)(2,1)S(1)}, bf16[1536,512]{1,0:T(8,128)(2,1)}, u32[]{:S(2)}) copy-start(bf16[1536,512]{1,0:T(8,128)(2,1)} %all-gather.4.cloned.1.call-done.weight) | copy-start | bytes 4718596
  (12 other events, 9.3 us)
Sparse Core Ops, SparseCore 0:
  11.0 128.5 all-gather.5
  141.5 25.7 all-gather.3

commit v8 on v7

--- a/solution.py
+++ b/solution.py
@@ -509,7 +509,11 @@
 
     (next_weight,) = after([next_weight], residual)
     next_weight = lax.all_gather(next_weight, "wide", axis=0, tiled=True)
-    hidden_rows = join(narrow_swap(parts, narrow), residual, mlp_row, False)
+    summed = residual.astype(f32)
+    swapped = narrow_swap(parts, narrow)
+    for part in [swapped[k] for k in (0, 2, 3, 1)]:
+        summed = summed + part.astype(f32)
+    hidden_rows = [summed.astype(bf16)] * 3
     hidden_pieces = narrow_spread(hidden_rows, narrow)
 
     next_width = query_width + HD

time: 237 us -> 234 us (0.987)
  the two profiles are of different devices: /device:TPU:10 before, /device:TPU:5 now
where the time goes in v8:
time: 234 us; the launch traced here: 232 us
  waiting for transfers between devices  105 us (45%)
  Pallas kernels  48.8 us (21%)
  starting transfers between devices  37.2 us (16%)
  local copies, waits for them, and re-layouts  15.8 us (7%)
  between operations  14.5 us (6%)
  other arithmetic  10.5 us (4%)
    ppermute x26, waiting for transfers between devices, exchange(): return lax.ppermute(value, axis, [(i, i ^ mask) for i in range(size)])  105 us
    ppermute x26, starting transfers between devices, exchange(): return lax.ppermute(value, axis, [(i, i ^ mask) for i in range(size)])  37.2 us
    pallas_call x2, Pallas kernels, feed_forward(): pl.pallas_call(functools.partial(ffn_kernel, count), out_shape=[share_sha...  22.3 us
    pallas_call x2, Pallas kernels, attend(): pl.pallas_call(functools.partial(attend_kernel, wide, shares), out_shape=...  13.5 us
    unnamed x90, local copies, waits for them, and re-layouts  6.79 us
    pallas_call x1, Pallas kernels, local(): pl.pallas_call(functools.partial(qkv_kernel, wide), out_shape=(jax.ShapeD...  6.16 us
  transfers between devices with their start and end apart: 28, of which 14 were waited for; matrix products, arithmetic and copies ran while one was open for 7% of the time, Pallas kernels for 21%

profile of v8, /device:TPU:5, one launch (start us, length us, event | category | flops | bytes accessed | tf_op | source)
XLA Modules:
  0.0 232.3 jit_solution(15838385446738657165)
XLA Ops:
  7.2 3.5 %pad_maximum_fusion = bf16[3,192,2240]{2,1,0:T(8,128)(2,1)} fusion(bf16[1,192,2240]{2,1,0:T(8,128)(2,1)} %bitcast.22, bf16[1,192,2240]{2,1,0:T(8,128)(2,1)} %bitcast.23, bf16[1,192,2240]{2,1,0:T(8,128)(2,1)} %bitcast.24), kind=kLoop, calls=%fused_computation.1 | loop fusion | flops 2580480 | bytes 5160960 | tf_op jit(solution)/shard_map/stack | solution.py:374
  11.0 0.7 copy-done.24
  11.8 1.2 collective-permute-start.5
  13.0 1.2 collective-permute-start.3
  14.3 0.3 collective-permute-start.1
  14.5 1.5 collective-permute-start
  16.3 0.6 maximum_convert_fusion.bias_ref
  16.9 0.8 constant_dynamic-slice_fusion.2
  17.8 0.7 pad_maximum_fusion.4
  18.5 1.0 fusion
  19.5 0.6 reshape.198.gain_ref
  20.1 1.0 pad_maximum_fusion.2
  21.1 1.8 constant_dynamic-slice_fusion.1.base_ref
  22.9 17.0 %collective-permute-done.3.rest_4_ = bf16[192,1024]{1,0:T(8,128)(2,1)S(1)} collective-permute-done((bf16[192,1024]{1,0:T(8,128)(2,1)S(1)}, bf16[192,1024]{1,0:T(8,128)(2,1)S(1)}, u32[]{:S(2)}, u32[]{:S(2)}) %collective-permute-start.3) | collective-permute-done | bytes 393248 | tf_op jit(solution)/shard_map/ppermute | solution.py:55
  39.9 0.6 collective-permute-start.2
  40.6 0.4 collective-permute-start.6
  41.1 0.6 reshape.200.gain_ref
  41.7 0.2 collective-permute-done.2.rest_3_
  41.9 0.6 collective-permute-done.4.rest_5_
  42.5 0.6 collective-permute-done.6.rest_7_
  43.2 0.5 copy-done.18
  43.8 6.2 %qkv.1 = (bf16[512,384]{1,0:T(8,128)(2,1)}, bf16[512,256]{1,0:T(8,128)(2,1)}, bf16[1536,384]{1,0:T(8,128)(2,1)}) custom-call(s32[1]{0:T(128)} %bitcast.3.index_ref.wide_ref, bf16[512,1536]{1,0:T(8,128)(2,1)} %hidden_ref.1, f32[1,1536]{1,0:T(1,128)} %reshape.200.gain_ref, f32[1,640]{1,0:T(1,128)} %maximum_convert_fusion.bias_ref, ...), custom_call_target="tpu_custom_call" | custom-call | flops 1006632960 | bytes 3538944 | tf_op jit(solution)/shard_map/qkv/pallas_call | solution.py:393
  49.9 3.1 %collective-permute-start.12 = (bf16[512,256]{1,0:T(8,128)(2,1)}, bf16[512,256]{1,0:T(8,128)(2,1)S(1)}, u32[]{:S(2)}, u32[]{:S(2)}) collective-permute-start(bf16[512,256]{1,0:T(8,128)(2,1)} %get-tuple-element.55.rest_0_), channel_id=1, source_target_pairs={{0,24},{4,28},{8,16},{12,20},{16,8},{20,12},{24,0},{28,4},{1,25},{... | collective-permute-start | bytes 786440 | tf_op jit(solution)/shard_map/ppermute | solution.py:55
  53.0 0.4 collective-permute-start.8
  53.4 0.9 collective-permute-start.7
  54.3 11.2 %collective-permute-done.12.rest_6_ = bf16[512,256]{1,0:T(8,128)(2,1)S(1)} collective-permute-done((bf16[512,256]{1,0:T(8,128)(2,1)}, bf16[512,256]{1,0:T(8,128)(2,1)S(1)}, u32[]{:S(2)}, u32[]{:S(2)}) %collective-permute-start.12) | collective-permute-done | bytes 262176 | tf_op jit(solution)/shard_map/ppermute | solution.py:55
  65.5 1.1 collective-permute-start.13
  66.6 5.3 %collective-permute-done.10.rest_4_ = bf16[512,256]{1,0:T(8,128)(2,1)S(1)} collective-permute-done((bf16[512,256]{1,0:T(8,128)(2,1)}, bf16[512,256]{1,0:T(8,128)(2,1)S(1)}, u32[]{:S(2)}, u32[]{:S(2)}) %collective-permute-start.10) | collective-permute-done | bytes 262176 | tf_op jit(solution)/shard_map/ppermute | solution.py:55
  71.9 0.5 collective-permute-start.11
  72.5 0.9 copy.32.starts_ref
  73.6 0.4 collective-permute-done.9.rest_3_
  74.3 0.4 copy-done.42
  74.7 8.8 %attend.2 = (bf16[128,1536]{1,0:T(8,128)(2,1)}, bf16[128,1536]{1,0:T(8,128)(2,1)}, bf16[4096,256]{1,0:T(8,128)(2,1)}) custom-call(s32[1]{0:T(128)} %bitcast.3.index_ref.wide_ref, s32[1]{0:T(128)} %bitcast.narrow_ref, s32[512]{0:T(512)} %copy-done.6, s32[512,1]{1,0:T(8,128)} %copy.32.starts_ref, bf16[512,384]{1,0:T(8,128)(2,1)} %get-tuple-element.53.q_ref, ...), custom_call_target="tpu_custom_call" | custom-call | flops 1207959552 | bytes 2097152 | tf_op jit(solution)/shard_map/attend/pallas_call | solution.py:435
  83.5 1.7 collective-permute-start.15
  85.2 1.6 copy-done.2
  86.8 4.7 %attend.3 = (bf16[128,1536]{1,0:T(8,128)(2,1)S(1)}, bf16[128,1536]{1,0:T(8,128)(2,1)S(1)}) custom-call(s32[1]{0:T(128)} %bitcast.3.index_ref.wide_ref, s32[1]{0:T(128)} %bitcast.narrow_ref, s32[512]{0:T(512)S(1)} %copy-done.7, s32[512,1]{1,0:T(8,128)S(1)} %copy-done.5, bf16[512,384]{1,0:T(8,128)(2,1)S(1)} %copy-done.9, bf16[1536,384]{1,0:T(8,128)(2,1)S(1)} %copy-done.8, ...), custom_call_target="tpu_custom_call" | custom-call | flops 1207959552 | bytes 2097152 | tf_op jit(solution)/shard_map/attend/pallas_call | solution.py:435
  91.5 0.7 copy-done.4
  92.3 2.4 %collective-permute-start.16 = (bf16[128,1536]{1,0:T(8,128)(2,1)S(1)}, bf16[128,1536]{1,0:T(8,128)(2,1)S(1)}, u32[]{:S(2)}, u32[]{:S(2)}) collective-permute-start(bf16[128,1536]{1,0:T(8,128)(2,1)S(1)} %copy-done.35), channel_id=1, source_target_pairs={{0,3},{1,2},{2,1},{3,0},{4,7},{5,6},{6,5},{7,4},{8,11},{9,10},{10,... | collective-permute-start | bytes 1179656 | tf_op jit(solution)/shard_map/ppermute | solution.py:55
  94.7 17.7 %collective-permute-done.15.rest_2_ = bf16[128,1536]{1,0:T(8,128)(2,1)S(1)} collective-permute-done((bf16[128,1536]{1,0:T(8,128)(2,1)}, bf16[128,1536]{1,0:T(8,128)(2,1)S(1)}, u32[]{:S(2)}, u32[]{:S(2)}) %collective-permute-start.15) | collective-permute-done | bytes 393248 | tf_op jit(solution)/shard_map/ppermute | solution.py:55
  112.3 7.9 %collective-permute-done.14.rest_1_ = bf16[128,1536]{1,0:T(8,128)(2,1)S(1)} collective-permute-done((bf16[128,1536]{1,0:T(8,128)(2,1)S(1)}, bf16[128,1536]{1,0:T(8,128)(2,1)S(1)}, u32[]{:S(2)}, u32[]{:S(2)}) %collective-permute-start.14) | collective-permute-done | bytes 393248 | tf_op jit(solution)/shard_map/ppermute | solution.py:55
  120.3 0.8 copy-done.21
  121.0 3.0 %join.1 = (bf16[128,1536]{1,0:T(8,128)(2,1)}, bf16[128,1536]{1,0:T(8,128)(2,1)}, bf16[128,1536]{1,0:T(8,128)(2,1)}, bf16[128,1536]{1,0:T(8,128)(2,1)}) custom-call(bf16[128,1536]{1,0:T(8,128)(2,1)} %constant_dynamic-slice_fusion.1.base_ref, f32[1,1536]{1,0:T(1,128)} %reshape.198.gain_ref, bf16[128,1536]{1,0:T(8,128)(2,1)} %copy-done.4, ...), custom_call_target="tpu_custom_call" | custom-call | tf_op jit(solution)/shard_map/join/pallas_call | solution.py:465
  124.0 1.7 collective-permute-start.17
  125.7 0.3 fusion.2
  126.3 0.7 collective-permute-start.18
  127.0 10.0 %collective-permute-done.17.rest_0_ = bf16[128,1536]{1,0:T(8,128)(2,1)S(1)} collective-permute-done((bf16[128,1536]{1,0:T(8,128)(2,1)}, bf16[128,1536]{1,0:T(8,128)(2,1)S(1)}, u32[]{:S(2)}, u32[]{:S(2)}) %collective-permute-start.17) | collective-permute-done | bytes 393248 | tf_op jit(solution)/shard_map/ppermute | solution.py:55
  137.0 7.3 %collective-permute-start.19 = (bf16[128,1536]{1,0:T(8,128)(2,1)S(1)}, bf16[128,1536]{1,0:T(8,128)(2,1)S(1)}, u32[]{:S(2)}, u32[]{:S(2)}) collective-permute-start(bf16[128,1536]{1,0:T(8,128)(2,1)S(1)} %collective-permute-done.17.rest_0_), channel_id=1, source_target_pairs={{0,1},{1,0},{2,3},{3,2},{4,5},{5,4},{6,7},{7,6},{8,9},{9,8},{10,11... | collective-permute-start | bytes 1179656 | tf_op jit(solution)/shard_map/ppermute | solution.py:55
  144.3 12.0 %ffn.2 = (bf16[128,1536]{1,0:T(8,128)(2,1)}, bf16[128,1536]{1,0:T(8,128)(2,1)}) custom-call(bf16[128,1536]{1,0:T(8,128)(2,1)} %copy-done.22, bf16[128,1536]{1,0:T(8,128)(2,1)} %get-tuple-element.64.rest_1_, bf16[8,3,192,2240]{3,2,1,0:T(8,128)(2,1)} %bitcast.20), custom_call_target="tpu_custom_call" | custom-call | flops 5284823040 | bytes 20643840 | tf_op jit(solution)/shard_map/ffn/pallas_call | solution.py:484
  156.3 2.6 %collective-permute-start.21 = (bf16[128,1536]{1,0:T(8,128)(2,1)}, bf16[128,1536]{1,0:T(8,128)(2,1)}, u32[]{:S(2)}, u32[]{:S(2)}) collective-permute-start(bf16[128,1536]{1,0:T(8,128)(2,1)} %get-tuple-element.67), channel_id=1, source_target_pairs={{0,3},{1,2},{2,1},{3,0},{4,7},{5,6},{6,5},{7,4},{8,11},{9,10},{10,... | collective-permute-start | bytes 1179656 | tf_op jit(solution)/shard_map/ppermute | solution.py:55
  158.9 10.3 %ffn.3 = (bf16[128,1536]{1,0:T(8,128)(2,1)S(1)}, bf16[128,1536]{1,0:T(8,128)(2,1)S(1)}) custom-call(bf16[128,1536]{1,0:T(8,128)(2,1)S(1)} %collective-permute-done.18.rest_0_, bf16[128,1536]{1,0:T(8,128)(2,1)S(1)} %collective-permute-done.19.rest_1_, bf16[8,3,192,2240]{3,2,1,0:T(8,128)(2,1)} %bitcast.21), custom_call_target="tpu_custom_call" | custom-call | flops 5284823040 | bytes 20643840 | tf_op jit(solution)/shard_map/ffn/pallas_call | solution.py:484
  169.3 0.8 collective-permute-start.22
  170.2 22.5 %collective-permute-done.20 = bf16[128,1536]{1,0:T(8,128)(2,1)} collective-permute-done((bf16[128,1536]{1,0:T(8,128)(2,1)S(1)}, bf16[128,1536]{1,0:T(8,128)(2,1)}, u32[]{:S(2)}, u32[]{:S(2)}) %collective-permute-start.20) | collective-permute-done | bytes 393248 | tf_op jit(solution)/shard_map/ppermute | solution.py:55
  192.7 1.6 add_convert_fusion.rest_0_
  194.4 2.4 %collective-permute-start.23 = (bf16[128,1536]{1,0:T(8,128)(2,1)S(1)}, bf16[128,1536]{1,0:T(8,128)(2,1)S(1)}, u32[]{:S(2)}, u32[]{:S(2)}) collective-permute-start(bf16[128,1536]{1,0:T(8,128)(2,1)S(1)} %add_convert_fusion.rest_0_), channel_id=1, source_target_pairs={{0,3},{1,2},{2,1},{3,0},{4,7},{5,6},{6,5},{7,4},{8,11},{9,10},{10,... | collective-permute-start | bytes 1179656 | tf_op jit(solution)/shard_map/ppermute | solution.py:55
  196.8 0.3 compare_reduce_fusion
  197.1 8.4 %collective-permute-done.23.rest_2_ = bf16[128,1536]{1,0:T(8,128)(2,1)S(1)} collective-permute-done((bf16[128,1536]{1,0:T(8,128)(2,1)S(1)}, bf16[128,1536]{1,0:T(8,128)(2,1)S(1)}, u32[]{:S(2)}, u32[]{:S(2)}) %collective-permute-start.23) | collective-permute-done | bytes 393248 | tf_op jit(solution)/shard_map/ppermute | solution.py:55
  205.5 6.0 %collective-permute-start.24 = (bf16[128,1536]{1,0:T(8,128)(2,1)S(1)}, bf16[128,1536]{1,0:T(8,128)(2,1)S(1)}, u32[]{:S(2)}, u32[]{:S(2)}) collective-permute-start(bf16[128,1536]{1,0:T(8,128)(2,1)S(1)} %collective-permute-done.23.rest_2_), channel_id=1, source_target_pairs={{0,1},{1,0},{2,3},{3,2},{4,5},{5,4},{6,7},{7,6},{8,9},{9,8},{10,11... | collective-permute-start | bytes 1179656 | tf_op jit(solution)/shard_map/ppermute | solution.py:55
  211.5 1.0 constant_dynamic-slice_fusion.3
  212.6 3.1 %gather_fusion = bf16[640,128]{1,0:T(8,128)(2,1)S(1)} fusion(bf16[4096,128]{1,0:T(8,128)(2,1)} %constant_dynamic-slice_fusion.3, s32[1024]{0:T(1024)S(1)} %pad_clamp_fusion), kind=kCustom, calls=%fused_computation | custom fusion | bytes 330240 | tf_op jit(solution)/shard_map/jit(_take)/gather | solution.py:304
  215.7 0.9 select_select_fusion
  216.6 1.4 copy-done.1
  218.0 2.8 %next.2 = (bf16[512,1536]{1,0:T(8,128)(2,1)}, bf16[512,384]{1,0:T(8,128)(2,1)}, bf16[512,128]{1,0:T(8,128)(2,1)}) custom-call(s32[1]{0:T(128)} %bitcast.narrow_ref, f32[1,1536]{1,0:T(1,128)S(1)} %reshape.199.gain_ref, f32[1,512]{1,0:T(1,128)S(1)} %maximum_convert_fusion.1.bias_ref, bf16[1536,512]{1,0:T(8,128)(2,1)S(1)} %copy-done.1, ...), custom_call_target="tpu_custom_call" | custom-call | flops 603979776 | bytes 4718592 | tf_op jit(solution)/shard_map/next/pallas_call | solution.py:523
  220.7 3.5 %collective-permute-done.24.rest_0_ = bf16[128,1536]{1,0:T(8,128)(2,1)S(1)} collective-permute-done((bf16[128,1536]{1,0:T(8,128)(2,1)S(1)}, bf16[128,1536]{1,0:T(8,128)(2,1)S(1)}, u32[]{:S(2)}, u32[]{:S(2)}) %collective-permute-start.24) | collective-permute-done | bytes 393248 | tf_op jit(solution)/shard_map/ppermute | solution.py:55
  224.2 1.2 next.3
  (127 shorter events, 2.0 us)
Async XLA Ops:
  7.2 3.8 %copy-start = (bf16[192,512]{1,0:T(8,128)(2,1)S(1)}, bf16[192,512]{1,0:T(8,128)(2,1)}, u32[]{:S(2)}) copy-start(bf16[192,512]{1,0:T(8,128)(2,1)} %param.28) | copy-start | bytes 589828
  7.2 137.2 %all-gather.6.cloned.1.call-start = ((), (), s32[]{:S(2)}) async-start(), calls=%async_computation.1 | async-start | bytes 23887872 | tf_op jit(solution)/shard_map/all_gather | solution.py:375
  10.8 1.0 copy-start.25
  10.8 5.3 %copy-start.43 = (bf16[512]{0:T(512)(128)(2,1)S(1)}, bf16[512]{0:T(512)(128)(2,1)}, u32[]{:S(2)}) copy-start(bf16[512]{0:T(512)(128)(2,1)} %param.29) | copy-start | bytes 3076
  10.8 5.4 %copy-start.32 = (bf16[384]{0:T(512)(128)(2,1)S(1)}, bf16[384]{0:T(512)(128)(2,1)}, u32[]{:S(2)}) copy-start(bf16[384]{0:T(512)(128)(2,1)} %param.27) | copy-start | bytes 2308
  10.8 5.4 %copy-start.33 = (bf16[384]{0:T(512)(128)(2,1)S(1)}, bf16[384]{0:T(512)(128)(2,1)}, u32[]{:S(2)}) copy-start(bf16[384]{0:T(512)(128)(2,1)} %param.37) | copy-start | bytes 2308
  10.8 5.4 %copy-start.44 = (bf16[512]{0:T(512)(128)(2,1)S(1)}, bf16[512]{0:T(512)(128)(2,1)}, u32[]{:S(2)}) copy-start(bf16[512]{0:T(512)(128)(2,1)} %param.39) | copy-start | bytes 3076
  10.8 6.9 %copy-start.30 = (s32[8]{0:T(128)S(1)}, s32[8]{0:T(128)}, u32[]{:S(2)}) copy-start(s32[8]{0:T(128)} %param.23) | copy-start | bytes 100
  10.8 6.8 %copy-start.31 = (s32[512]{0:T(512)S(1)}, s32[512]{0:T(512)}, u32[]{:S(2)}) copy-start(s32[512]{0:T(512)} %param.21) | copy-start | bytes 6148
  10.8 6.9 %copy-start.23 = (bf16[192,384]{1,0:T(8,128)(2,1)S(1)}, bf16[192,384]{1,0:T(8,128)(2,1)}, u32[]{:S(2)}) copy-start(bf16[192,384]{1,0:T(8,128)(2,1)} %param.36) | copy-start | bytes 442372
  10.8 8.6 %copy-start.27 = (bf16[1536]{0:T(1024)(128)(2,1)S(1)}, bf16[1536]{0:T(1024)(128)(2,1)}, u32[]{:S(2)}) copy-start(bf16[1536]{0:T(1024)(128)(2,1)} %param.31) | copy-start | bytes 9220
  10.9 9.2 %copy-start.28 = (bf16[1536]{0:T(1024)(128)(2,1)S(1)}, bf16[1536]{0:T(1024)(128)(2,1)}, u32[]{:S(2)}) copy-start(bf16[1536]{0:T(1024)(128)(2,1)} %param.35) | copy-start | bytes 9220
  10.9 205.7 %all-gather.4.cloned.1.call-start = ((), (), s32[]{:S(2)}) async-start(), calls=%async_computation | async-start | bytes 1769472 | tf_op jit(solution)/shard_map/all_gather | solution.py:511
  11.8 29.3 %copy-start.29 = (bf16[1536]{0:T(1024)(128)(2,1)S(1)}, bf16[1536]{0:T(1024)(128)(2,1)}, u32[]{:S(2)}) copy-start(bf16[1536]{0:T(1024)(128)(2,1)} %param.25) | copy-start | bytes 9220
  11.8 31.2 %copy-start.10 = (bf16[192,1024]{1,0:T(8,128)(2,1)}, bf16[192,1024]{1,0:T(8,128)(2,1)S(1)}, u32[]{:S(2)}) copy-start(bf16[192,1024]{1,0:T(8,128)(2,1)S(1)} %pad_maximum_fusion.1.rest_0_) | copy-start | bytes 1179652
  11.8 11.1 %collective-permute-start.5 = (bf16[192,1024]{1,0:T(8,128)(2,1)S(1)}, bf16[192,1024]{1,0:T(8,128)(2,1)S(1)}, u32[]{:S(2)}, u32[]{:S(2)}) collective-permute-start(bf16[192,1024]{1,0:T(8,128)(2,1)S(1)} %pad_maximum_fusion.1.rest_0_), channel_id=1, source_target_pairs={{0,24},{4,28},{8,16},{12,20},{16,8},{20,12},{24,0},{28,4},{1,25},{... | collective-permute-start | bytes 1179656 | tf_op jit(solution)/shard_map/ppermute | solution.py:55
  13.0 26.9 %collective-permute-start.3 = (bf16[192,1024]{1,0:T(8,128)(2,1)S(1)}, bf16[192,1024]{1,0:T(8,128)(2,1)S(1)}, u32[]{:S(2)}, u32[]{:S(2)}) collective-permute-start(bf16[192,1024]{1,0:T(8,128)(2,1)S(1)} %pad_maximum_fusion.1.rest_0_), channel_id=1, source_target_pairs={{0,16},{4,20},{8,24},{12,28},{16,0},{20,4},{24,8},{28,12},{1,17},{... | collective-permute-start | bytes 1179656 | tf_op jit(solution)/shard_map/ppermute | solution.py:55
  14.3 25.6 %collective-permute-start.1 = (bf16[192,1024]{1,0:T(8,128)(2,1)S(1)}, bf16[192,1024]{1,0:T(8,128)(2,1)S(1)}, u32[]{:S(2)}, u32[]{:S(2)}) collective-permute-start(bf16[192,1024]{1,0:T(8,128)(2,1)S(1)} %pad_maximum_fusion.1.rest_0_), channel_id=1, source_target_pairs={{0,8},{4,12},{8,0},{12,4},{16,24},{20,28},{24,16},{28,20},{1,9},{5... | collective-permute-start | bytes 1179656 | tf_op jit(solution)/shard_map/ppermute | solution.py:55
  14.5 27.1 %collective-permute-start = (bf16[192,1024]{1,0:T(8,128)(2,1)S(1)}, bf16[192,1024]{1,0:T(8,128)(2,1)S(1)}, u32[]{:S(2)}, u32[]{:S(2)}) collective-permute-start(bf16[192,1024]{1,0:T(8,128)(2,1)S(1)} %pad_maximum_fusion.1.rest_0_), channel_id=1, source_target_pairs={{0,4},{4,0},{8,12},{12,8},{16,20},{20,16},{24,28},{28,24},{1,5},{5... | collective-permute-start | bytes 1179656 | tf_op jit(solution)/shard_map/ppermute | solution.py:55
  17.8 54.7 %copy-start.6 = (s32[512]{0:T(512)}, s32[512]{0:T(512)S(1)}, u32[]{:S(2)}) copy-start(s32[512]{0:T(512)S(1)} %select_reduce_fusion.spots_ref) | copy-start | bytes 6148
  22.9 20.1 %copy-start.11 = (bf16[192,1024]{1,0:T(8,128)(2,1)}, bf16[192,1024]{1,0:T(8,128)(2,1)S(1)}, u32[]{:S(2)}) copy-start(bf16[192,1024]{1,0:T(8,128)(2,1)S(1)} %collective-permute-done.5.rest_6_) | copy-start | bytes 1179652
  39.9 3.1 %copy-start.12 = (bf16[192,1024]{1,0:T(8,128)(2,1)}, bf16[192,1024]{1,0:T(8,128)(2,1)S(1)}, u32[]{:S(2)}) copy-start(bf16[192,1024]{1,0:T(8,128)(2,1)S(1)} %collective-permute-done.3.rest_4_) | copy-start | bytes 1179652
  39.9 3.1 %copy-start.13 = (bf16[192,1024]{1,0:T(8,128)(2,1)}, bf16[192,1024]{1,0:T(8,128)(2,1)S(1)}, u32[]{:S(2)}) copy-start(bf16[192,1024]{1,0:T(8,128)(2,1)S(1)} %collective-permute-done.1.rest_2_) | copy-start | bytes 1179652
  39.9 2.0 collective-permute-start.2
  40.6 1.9 collective-permute-start.4
  40.6 2.4 %collective-permute-start.6 = (bf16[192,1024]{1,0:T(8,128)(2,1)S(1)}, bf16[192,1024]{1,0:T(8,128)(2,1)S(1)}, u32[]{:S(2)}, u32[]{:S(2)}) collective-permute-start(bf16[192,1024]{1,0:T(8,128)(2,1)S(1)} %collective-permute-done.5.rest_6_), channel_id=1, source_target_pairs={{0,4},{4,0},{8,12},{12,8},{16,20},{20,16},{24,28},{28,24},{1,5},{5... | collective-permute-start | bytes 1179656 | tf_op jit(solution)/shard_map/ppermute | solution.py:55
  41.7 1.4 copy-start.14
  41.9 1.2 copy-start.16
  49.9 15.6 %collective-permute-start.12 = (bf16[512,256]{1,0:T(8,128)(2,1)}, bf16[512,256]{1,0:T(8,128)(2,1)S(1)}, u32[]{:S(2)}, u32[]{:S(2)}) collective-permute-start(bf16[512,256]{1,0:T(8,128)(2,1)} %get-tuple-element.55.rest_0_), channel_id=1, source_target_pairs={{0,24},{4,28},{8,16},{12,20},{16,8},{20,12},{24,0},{28,4},{1,25},{... | collective-permute-start | bytes 786440 | tf_op jit(solution)/shard_map/ppermute | solution.py:55
  53.0 18.9 %collective-permute-start.10 = (bf16[512,256]{1,0:T(8,128)(2,1)}, bf16[512,256]{1,0:T(8,128)(2,1)S(1)}, u32[]{:S(2)}, u32[]{:S(2)}) collective-permute-start(bf16[512,256]{1,0:T(8,128)(2,1)} %get-tuple-element.55.rest_0_), channel_id=1, source_target_pairs={{0,16},{4,20},{8,24},{12,28},{16,0},{20,4},{24,8},{28,12},{1,17},{... | collective-permute-start | bytes 786440 | tf_op jit(solution)/shard_map/ppermute | solution.py:55
  53.0 19.4 %collective-permute-start.8 = (bf16[512,256]{1,0:T(8,128)(2,1)}, bf16[512,256]{1,0:T(8,128)(2,1)S(1)}, u32[]{:S(2)}, u32[]{:S(2)}) collective-permute-start(bf16[512,256]{1,0:T(8,128)(2,1)} %get-tuple-element.55.rest_0_), channel_id=1, source_target_pairs={{0,8},{4,12},{8,0},{12,4},{16,24},{20,28},{24,16},{28,20},{1,9},{5... | collective-permute-start | bytes 786440 | tf_op jit(solution)/shard_map/ppermute | solution.py:55
  53.4 20.0 %collective-permute-start.7 = (bf16[512,256]{1,0:T(8,128)(2,1)}, bf16[512,256]{1,0:T(8,128)(2,1)S(1)}, u32[]{:S(2)}, u32[]{:S(2)}) collective-permute-start(bf16[512,256]{1,0:T(8,128)(2,1)} %get-tuple-element.55.rest_0_), channel_id=1, source_target_pairs={{0,4},{4,0},{8,12},{12,8},{16,20},{20,16},{24,28},{28,24},{1,5},{5... | collective-permute-start | bytes 786440 | tf_op jit(solution)/shard_map/ppermute | solution.py:55
  65.5 8.5 %copy-start.36 = (bf16[512,256]{1,0:T(8,128)(2,1)}, bf16[512,256]{1,0:T(8,128)(2,1)S(1)}, u32[]{:S(2)}) copy-start(bf16[512,256]{1,0:T(8,128)(2,1)S(1)} %collective-permute-done.12.rest_6_) | copy-start | bytes 786436
  65.5 7.8 %collective-permute-start.13 = (bf16[512,256]{1,0:T(8,128)(2,1)S(1)}, bf16[512,256]{1,0:T(8,128)(2,1)S(1)}, u32[]{:S(2)}, u32[]{:S(2)}) collective-permute-start(bf16[512,256]{1,0:T(8,128)(2,1)S(1)} %collective-permute-done.12.rest_6_), channel_id=1, source_target_pairs={{0,4},{4,0},{8,12},{12,8},{16,20},{20,16},{24,28},{28,24},{1,5},{5... | collective-permute-start | bytes 786440 | tf_op jit(solution)/shard_map/ppermute | solution.py:55
  71.9 2.0 copy-start.37
  71.9 1.7 collective-permute-start.11
  72.4 1.5 copy-start.38
  72.4 1.5 collective-permute-start.9
  74.7 10.5 %copy-start.5 = (s32[512,1]{1,0:T(8,128)S(1)}, s32[512,1]{1,0:T(8,128)}, u32[]{:S(2)}) copy-start(s32[512,1]{1,0:T(8,128)} %copy.32.starts_ref) | copy-start | bytes 6148
  74.7 10.5 %copy-start.7 = (s32[512]{0:T(512)S(1)}, s32[512]{0:T(512)}, u32[]{:S(2)}) copy-start(s32[512]{0:T(512)} %copy-done.6) | copy-start | bytes 6148
  74.7 10.5 %copy-start.8 = (bf16[1536,384]{1,0:T(8,128)(2,1)S(1)}, bf16[1536,384]{1,0:T(8,128)(2,1)}, u32[]{:S(2)}) copy-start(bf16[1536,384]{1,0:T(8,128)(2,1)} %get-tuple-element.54.w_out) | copy-start | bytes 3538948
  74.7 10.5 %copy-start.9 = (bf16[512,384]{1,0:T(8,128)(2,1)S(1)}, bf16[512,384]{1,0:T(8,128)(2,1)}, u32[]{:S(2)}) copy-start(bf16[512,384]{1,0:T(8,128)(2,1)} %get-tuple-element.53.q_ref) | copy-start | bytes 1179652
  83.5 28.9 %collective-permute-start.15 = (bf16[128,1536]{1,0:T(8,128)(2,1)}, bf16[128,1536]{1,0:T(8,128)(2,1)S(1)}, u32[]{:S(2)}, u32[]{:S(2)}) collective-permute-start(bf16[128,1536]{1,0:T(8,128)(2,1)} %get-tuple-element.59), channel_id=1, source_target_pairs={{0,2},{1,3},{2,0},{3,1},{4,6},{5,7},{6,4},{7,5},{8,10},{9,11},{10,... | collective-permute-start | bytes 1179656 | tf_op jit(solution)/shard_map/ppermute | solution.py:55
  85.2 1.6 copy-start.2
  86.8 5.5 %copy-start.35 = (bf16[128,1536]{1,0:T(8,128)(2,1)S(1)}, bf16[128,1536]{1,0:T(8,128)(2,1)}, u32[]{:S(2)}) copy-start(bf16[128,1536]{1,0:T(8,128)(2,1)} %get-tuple-element.60) | copy-start | bytes 1179652
  86.8 39.0 %copy-start.26 = (s32[8,16]{1,0:T(8,128)S(1)}, s32[8,16]{1,0:T(8,128)}, u32[]{:S(2)}) copy-start(s32[8,16]{1,0:T(8,128)} %param.24) | copy-start | bytes 1540
  86.8 39.3 %copy-start.34 = (s32[8]{0:T(128)S(1)}, s32[8]{0:T(128)}, u32[]{:S(2)}) copy-start(s32[8]{0:T(128)} %param.22) | copy-start | bytes 100
  92.3 20.1 %collective-permute-start.16 = (bf16[128,1536]{1,0:T(8,128)(2,1)S(1)}, bf16[128,1536]{1,0:T(8,128)(2,1)S(1)}, u32[]{:S(2)}, u32[]{:S(2)}) collective-permute-start(bf16[128,1536]{1,0:T(8,128)(2,1)S(1)} %copy-done.35), channel_id=1, source_target_pairs={{0,3},{1,2},{2,1},{3,0},{4,7},{5,6},{6,5},{7,4},{8,11},{9,10},{10,... | collective-permute-start | bytes 1179656 | tf_op jit(solution)/shard_map/ppermute | solution.py:55
  94.7 25.6 %collective-permute-start.14 = (bf16[128,1536]{1,0:T(8,128)(2,1)S(1)}, bf16[128,1536]{1,0:T(8,128)(2,1)S(1)}, u32[]{:S(2)}, u32[]{:S(2)}) collective-permute-start(bf16[128,1536]{1,0:T(8,128)(2,1)S(1)} %get-tuple-element.58), channel_id=1, source_target_pairs={{0,1},{1,0},{2,3},{3,2},{4,5},{5,4},{6,7},{7,6},{8,9},{9,8},{10,11... | collective-permute-start | bytes 1179656 | tf_op jit(solution)/shard_map/ppermute | solution.py:55
  112.3 7.9 %copy-start.19 = (bf16[128,1536]{1,0:T(8,128)(2,1)}, bf16[128,1536]{1,0:T(8,128)(2,1)S(1)}, u32[]{:S(2)}) copy-start(bf16[128,1536]{1,0:T(8,128)(2,1)S(1)} %collective-permute-done.15.rest_2_) | copy-start | bytes 1179652
  112.3 7.9 %copy-start.20 = (bf16[128,1536]{1,0:T(8,128)(2,1)}, bf16[128,1536]{1,0:T(8,128)(2,1)S(1)}, u32[]{:S(2)}) copy-start(bf16[128,1536]{1,0:T(8,128)(2,1)S(1)} %collective-permute-done.16.rest_3_) | copy-start | bytes 1179652
  124.0 13.0 %collective-permute-start.17 = (bf16[128,1536]{1,0:T(8,128)(2,1)}, bf16[128,1536]{1,0:T(8,128)(2,1)S(1)}, u32[]{:S(2)}, u32[]{:S(2)}) collective-permute-start(bf16[128,1536]{1,0:T(8,128)(2,1)} %get-tuple-element.63), channel_id=1, source_target_pairs={{0,3},{1,2},{2,1},{3,0},{4,7},{5,6},{6,5},{7,4},{8,11},{9,10},{10,... | collective-permute-start | bytes 1179656 | tf_op jit(solution)/shard_map/ppermute | solution.py:55
  126.3 32.7 %collective-permute-start.18 = (bf16[128,1536]{1,0:T(8,128)(2,1)}, bf16[128,1536]{1,0:T(8,128)(2,1)S(1)}, u32[]{:S(2)}, u32[]{:S(2)}) collective-permute-start(bf16[128,1536]{1,0:T(8,128)(2,1)} %get-tuple-element.66), channel_id=1, source_target_pairs={{0,1},{1,0},{2,3},{3,2},{4,5},{5,4},{6,7},{7,6},{8,9},{9,8},{10,11... | collective-permute-start | bytes 1179656 | tf_op jit(solution)/shard_map/ppermute | solution.py:55
  137.0 7.3 %copy-start.22 = (bf16[128,1536]{1,0:T(8,128)(2,1)}, bf16[128,1536]{1,0:T(8,128)(2,1)S(1)}, u32[]{:S(2)}) copy-start(bf16[128,1536]{1,0:T(8,128)(2,1)S(1)} %collective-permute-done.17.rest_0_) | copy-start | bytes 1179652
  137.0 21.9 %collective-permute-start.19 = (bf16[128,1536]{1,0:T(8,128)(2,1)S(1)}, bf16[128,1536]{1,0:T(8,128)(2,1)S(1)}, u32[]{:S(2)}, u32[]{:S(2)}) collective-permute-start(bf16[128,1536]{1,0:T(8,128)(2,1)S(1)} %collective-permute-done.17.rest_0_), channel_id=1, source_target_pairs={{0,1},{1,0},{2,3},{3,2},{4,5},{5,4},{6,7},{7,6},{8,9},{9,8},{10,11... | collective-permute-start | bytes 1179656 | tf_op jit(solution)/shard_map/ppermute | solution.py:55
  156.3 36.4 %copy-start.15 = (bf16[128,1536]{1,0:T(8,128)(2,1)S(1)}, bf16[128,1536]{1,0:T(8,128)(2,1)}, u32[]{:S(2)}) copy-start(bf16[128,1536]{1,0:T(8,128)(2,1)} %get-tuple-element.61) | copy-start | bytes 1179652
  156.3 36.4 %collective-permute-start.21 = (bf16[128,1536]{1,0:T(8,128)(2,1)}, bf16[128,1536]{1,0:T(8,128)(2,1)}, u32[]{:S(2)}, u32[]{:S(2)}) collective-permute-start(bf16[128,1536]{1,0:T(8,128)(2,1)} %get-tuple-element.67), channel_id=1, source_target_pairs={{0,3},{1,2},{2,1},{3,0},{4,7},{5,6},{6,5},{7,4},{8,11},{9,10},{10,... | collective-permute-start | bytes 1179656 | tf_op jit(solution)/shard_map/ppermute | solution.py:55
  169.2 42.3 %copy-start.3 = (bf16[4096,256]{1,0:T(8,128)(2,1)S(1)}, bf16[4096,256]{1,0:T(8,128)(2,1)}, u32[]{:S(2)}) copy-start(bf16[4096,256]{1,0:T(8,128)(2,1)} %get-tuple-element.56.rest_0_) | copy-start | bytes 6291460
  169.2 23.5 %collective-permute-start.20 = (bf16[128,1536]{1,0:T(8,128)(2,1)S(1)}, bf16[128,1536]{1,0:T(8,128)(2,1)}, u32[]{:S(2)}, u32[]{:S(2)}) collective-permute-start(bf16[128,1536]{1,0:T(8,128)(2,1)S(1)} %get-tuple-element.70), channel_id=1, source_target_pairs={{0,2},{1,3},{2,0},{3,1},{4,6},{5,7},{6,4},{7,5},{8,10},{9,11},{10,... | collective-permute-start | bytes 1179656 | tf_op jit(solution)/shard_map/ppermute | solution.py:55
  169.3 23.4 %collective-permute-start.22 = (bf16[128,1536]{1,0:T(8,128)(2,1)S(1)}, bf16[128,1536]{1,0:T(8,128)(2,1)}, u32[]{:S(2)}, u32[]{:S(2)}) collective-permute-start(bf16[128,1536]{1,0:T(8,128)(2,1)S(1)} %get-tuple-element.71), channel_id=1, source_target_pairs={{0,1},{1,0},{2,3},{3,2},{4,5},{5,4},{6,7},{7,6},{8,9},{9,8},{10,11... | collective-permute-start | bytes 1179656 | tf_op jit(solution)/shard_map/ppermute | solution.py:55
  194.4 11.2 %collective-permute-start.23 = (bf16[128,1536]{1,0:T(8,128)(2,1)S(1)}, bf16[128,1536]{1,0:T(8,128)(2,1)S(1)}, u32[]{:S(2)}, u32[]{:S(2)}) collective-permute-start(bf16[128,1536]{1,0:T(8,128)(2,1)S(1)} %add_convert_fusion.rest_0_), channel_id=1, source_target_pairs={{0,3},{1,2},{2,1},{3,0},{4,7},{5,6},{6,5},{7,4},{8,11},{9,10},{10,... | collective-permute-start | bytes 1179656 | tf_op jit(solution)/shard_map/ppermute | solution.py:55
  197.1 19.5 %collective-permute-start.25 = (bf16[128,1536]{1,0:T(8,128)(2,1)S(1)}, bf16[128,1536]{1,0:T(8,128)(2,1)}, u32[]{:S(2)}, u32[]{:S(2)}) collective-permute-start(bf16[128,1536]{1,0:T(8,128)(2,1)S(1)} %add_convert_fusion.rest_0_), channel_id=1, source_target_pairs={{0,1},{1,0},{2,3},{3,2},{4,5},{5,4},{6,7},{7,6},{8,9},{9,8},{10,11... | collective-permute-start | bytes 1179656 | tf_op jit(solution)/shard_map/ppermute | solution.py:55
  205.5 18.7 %collective-permute-start.24 = (bf16[128,1536]{1,0:T(8,128)(2,1)S(1)}, bf16[128,1536]{1,0:T(8,128)(2,1)S(1)}, u32[]{:S(2)}, u32[]{:S(2)}) collective-permute-start(bf16[128,1536]{1,0:T(8,128)(2,1)S(1)} %collective-permute-done.23.rest_2_), channel_id=1, source_target_pairs={{0,1},{1,0},{2,3},{3,2},{4,5},{5,4},{6,7},{7,6},{8,9},{9,8},{10,11... | collective-permute-start | bytes 1179656 | tf_op jit(solution)/shard_map/ppermute | solution.py:55
  216.6 1.4 copy-start.1
  (9 other events, 6.8 us)
Sparse Core Ops, SparseCore 0:
  11.0 128.0 all-gather.5
  141.0 26.5 all-gather.3

commit v9 on v8

--- a/solution.py
+++ b/solution.py
@@ -219,16 +219,9 @@
     for k in range(len(x_refs)):
         x[k * share : (k + 1) * share, :] = x_refs[k][...]
     depth, width = x.shape[1], hidden.shape[1]
-    tile = 1024
-    whole = width // tile
 
     def each_tile(body):
-        @pl.loop(0, whole)
-        def _(j):
-            body(pl.ds(pl.multiple_of(j * tile, tile), tile))
-
-        if width % tile:
-            body(slice(whole * tile, width))
+        body(slice(0, width))
 
     def block(j, lanes):
         part = held[j, :, :, lanes]

time: 234 us -> 235 us (level)
  the two profiles are of different devices: /device:TPU:5 before, /device:TPU:7 now
where the time goes in v9:
time: 235 us; the launch traced here: 233 us
  waiting for transfers between devices  98 us (42%)
  Pallas kernels  53.3 us (23%)
  starting transfers between devices  41.1 us (17%)
  local copies, waits for them, and re-layouts  15.8 us (7%)
  between operations  14.5 us (6%)
  other arithmetic  10.7 us (5%)
    ppermute x26, waiting for transfers between devices, exchange(): return lax.ppermute(value, axis, [(i, i ^ mask) for i in range(size)])  98 us
    ppermute x26, starting transfers between devices, exchange(): return lax.ppermute(value, axis, [(i, i ^ mask) for i in range(size)])  41.1 us
    pallas_call x2, Pallas kernels, feed_forward(): pl.pallas_call(functools.partial(ffn_kernel, count), out_shape=[share_sha...  21.5 us
    pallas_call x2, Pallas kernels, attend(): pl.pallas_call(functools.partial(attend_kernel, wide, shares), out_shape=...  18.8 us
    unnamed x90, local copies, waits for them, and re-layouts  6.79 us
    pallas_call x1, Pallas kernels, local(): pl.pallas_call(functools.partial(qkv_kernel, wide), out_shape=(jax.ShapeD...  6.16 us
  transfers between devices with their start and end apart: 28, of which 14 were waited for; matrix products, arithmetic and copies ran while one was open for 7% of the time, Pallas kernels for 22%

profile of v9, /device:TPU:7, one launch (start us, length us, event | category | flops | bytes accessed | tf_op | source)
XLA Modules:
  0.0 233.5 jit_solution(5104823665663322598)
XLA Ops:
  7.2 3.5 %pad_maximum_fusion = bf16[3,192,2240]{2,1,0:T(8,128)(2,1)} fusion(bf16[1,192,2240]{2,1,0:T(8,128)(2,1)} %bitcast.22, bf16[1,192,2240]{2,1,0:T(8,128)(2,1)} %bitcast.23, bf16[1,192,2240]{2,1,0:T(8,128)(2,1)} %bitcast.24), kind=kLoop, calls=%fused_computation.1 | loop fusion | flops 2580480 | bytes 5160960 | tf_op jit(solution)/shard_map/stack | solution.py:367
  11.0 0.7 copy-done.24
  11.9 1.4 collective-permute-start.3
  13.3 1.2 collective-permute-start.1
  14.5 1.5 collective-permute-start
  16.3 0.6 maximum_convert_fusion.bias_ref
  16.9 0.8 constant_dynamic-slice_fusion.2
  17.8 0.7 pad_maximum_fusion.4
  18.5 1.0 fusion
  19.5 0.6 reshape.198.gain_ref
  20.1 1.0 pad_maximum_fusion.2
  21.1 1.8 constant_dynamic-slice_fusion.1.base_ref
  22.9 14.0 %collective-permute-done.3.rest_4_ = bf16[192,1024]{1,0:T(8,128)(2,1)S(1)} collective-permute-done((bf16[192,1024]{1,0:T(8,128)(2,1)S(1)}, bf16[192,1024]{1,0:T(8,128)(2,1)S(1)}, u32[]{:S(2)}, u32[]{:S(2)}) %collective-permute-start.3) | collective-permute-done | bytes 393248 | tf_op jit(solution)/shard_map/ppermute | solution.py:55
  37.0 3.3 %collective-permute-start.2 = (bf16[192,1024]{1,0:T(8,128)(2,1)S(1)}, bf16[192,1024]{1,0:T(8,128)(2,1)S(1)}, u32[]{:S(2)}, u32[]{:S(2)}) collective-permute-start(bf16[192,1024]{1,0:T(8,128)(2,1)S(1)} %collective-permute-done.1.rest_2_), channel_id=1, source_target_pairs={{0,4},{4,0},{8,12},{12,8},{16,20},{20,16},{24,28},{28,24},{1,5},{5... | collective-permute-start | bytes 1179656 | tf_op jit(solution)/shard_map/ppermute | solution.py:55
  40.3 0.5 collective-permute-start.6
  40.8 0.6 reshape.200.gain_ref
  41.4 0.2 collective-permute-done.2.rest_3_
  41.6 0.6 collective-permute-done.4.rest_5_
  42.2 0.6 collective-permute-done.6.rest_7_
  43.0 0.5 copy-done.18
  43.5 6.2 %qkv.1 = (bf16[512,384]{1,0:T(8,128)(2,1)}, bf16[512,256]{1,0:T(8,128)(2,1)}, bf16[1536,384]{1,0:T(8,128)(2,1)}) custom-call(s32[1]{0:T(128)} %bitcast.3.index_ref.wide_ref, bf16[512,1536]{1,0:T(8,128)(2,1)} %hidden_ref.1, f32[1,1536]{1,0:T(1,128)} %reshape.200.gain_ref, f32[1,640]{1,0:T(1,128)} %maximum_convert_fusion.bias_ref, ...), custom_call_target="tpu_custom_call" | custom-call | flops 1006632960 | bytes 3538944 | tf_op jit(solution)/shard_map/qkv/pallas_call | solution.py:386
  49.7 1.4 collective-permute-start.12
  51.1 1.1 collective-permute-start.10
  52.2 1.1 collective-permute-start.8
  53.3 0.9 collective-permute-start.7
  54.2 10.2 %collective-permute-done.12.rest_6_ = bf16[512,256]{1,0:T(8,128)(2,1)S(1)} collective-permute-done((bf16[512,256]{1,0:T(8,128)(2,1)}, bf16[512,256]{1,0:T(8,128)(2,1)S(1)}, u32[]{:S(2)}, u32[]{:S(2)}) %collective-permute-start.12) | collective-permute-done | bytes 262176 | tf_op jit(solution)/shard_map/ppermute | solution.py:55
  64.5 1.5 collective-permute-start.13
  66.0 4.6 %collective-permute-done.10.rest_4_ = bf16[512,256]{1,0:T(8,128)(2,1)S(1)} collective-permute-done((bf16[512,256]{1,0:T(8,128)(2,1)}, bf16[512,256]{1,0:T(8,128)(2,1)S(1)}, u32[]{:S(2)}, u32[]{:S(2)}) %collective-permute-start.10) | collective-permute-done | bytes 262176 | tf_op jit(solution)/shard_map/ppermute | solution.py:55
  70.6 0.9 collective-permute-start.11
  71.6 0.9 copy.32.starts_ref
  72.6 0.4 collective-permute-done.9.rest_3_
  73.3 0.4 copy-done.42
  73.7 11.4 %attend.2 = (bf16[128,1536]{1,0:T(8,128)(2,1)}, bf16[128,1536]{1,0:T(8,128)(2,1)}, bf16[4096,256]{1,0:T(8,128)(2,1)}) custom-call(s32[1]{0:T(128)} %bitcast.3.index_ref.wide_ref, s32[1]{0:T(128)} %bitcast.narrow_ref, s32[512]{0:T(512)} %copy-done.6, s32[512,1]{1,0:T(8,128)} %copy.32.starts_ref, bf16[512,384]{1,0:T(8,128)(2,1)} %get-tuple-element.53.q_ref, ...), custom_call_target="tpu_custom_call" | custom-call | flops 1207959552 | bytes 2097152 | tf_op jit(solution)/shard_map/attend/pallas_call | solution.py:428
  85.1 1.9 collective-permute-start.15
  87.0 1.6 copy-done.2
  88.6 7.4 %attend.3 = (bf16[128,1536]{1,0:T(8,128)(2,1)S(1)}, bf16[128,1536]{1,0:T(8,128)(2,1)S(1)}) custom-call(s32[1]{0:T(128)} %bitcast.3.index_ref.wide_ref, s32[1]{0:T(128)} %bitcast.narrow_ref, s32[512]{0:T(512)S(1)} %copy-done.7, s32[512,1]{1,0:T(8,128)S(1)} %copy-done.5, bf16[512,384]{1,0:T(8,128)(2,1)S(1)} %copy-done.9, bf16[1536,384]{1,0:T(8,128)(2,1)S(1)} %copy-done.8, ...), custom_call_target="tpu_custom_call" | custom-call | flops 1207959552 | bytes 2097152 | tf_op jit(solution)/shard_map/attend/pallas_call | solution.py:428
  96.0 0.7 copy-done.4
  96.8 2.2 collective-permute-start.16
  99.0 15.0 %collective-permute-done.15.rest_2_ = bf16[128,1536]{1,0:T(8,128)(2,1)S(1)} collective-permute-done((bf16[128,1536]{1,0:T(8,128)(2,1)}, bf16[128,1536]{1,0:T(8,128)(2,1)S(1)}, u32[]{:S(2)}, u32[]{:S(2)}) %collective-permute-start.15) | collective-permute-done | bytes 393248 | tf_op jit(solution)/shard_map/ppermute | solution.py:55
  114.0 8.4 %collective-permute-done.14.rest_1_ = bf16[128,1536]{1,0:T(8,128)(2,1)S(1)} collective-permute-done((bf16[128,1536]{1,0:T(8,128)(2,1)S(1)}, bf16[128,1536]{1,0:T(8,128)(2,1)S(1)}, u32[]{:S(2)}, u32[]{:S(2)}) %collective-permute-start.14) | collective-permute-done | bytes 393248 | tf_op jit(solution)/shard_map/ppermute | solution.py:55
  122.4 0.8 copy-done.21
  123.2 3.0 %join.1 = (bf16[128,1536]{1,0:T(8,128)(2,1)}, bf16[128,1536]{1,0:T(8,128)(2,1)}, bf16[128,1536]{1,0:T(8,128)(2,1)}, bf16[128,1536]{1,0:T(8,128)(2,1)}) custom-call(bf16[128,1536]{1,0:T(8,128)(2,1)} %constant_dynamic-slice_fusion.1.base_ref, f32[1,1536]{1,0:T(1,128)} %reshape.198.gain_ref, bf16[128,1536]{1,0:T(8,128)(2,1)} %copy-done.4, ...), custom_call_target="tpu_custom_call" | custom-call | tf_op jit(solution)/shard_map/join/pallas_call | solution.py:458
  126.1 2.7 %collective-permute-start.17 = (bf16[128,1536]{1,0:T(8,128)(2,1)}, bf16[128,1536]{1,0:T(8,128)(2,1)S(1)}, u32[]{:S(2)}, u32[]{:S(2)}) collective-permute-start(bf16[128,1536]{1,0:T(8,128)(2,1)} %get-tuple-element.63), channel_id=1, source_target_pairs={{0,3},{1,2},{2,1},{3,0},{4,7},{5,6},{6,5},{7,4},{8,11},{9,10},{10,... | collective-permute-start | bytes 1179656 | tf_op jit(solution)/shard_map/ppermute | solution.py:55
  128.8 0.3 fusion.2
  129.4 9.3 %collective-permute-done.17.rest_0_ = bf16[128,1536]{1,0:T(8,128)(2,1)S(1)} collective-permute-done((bf16[128,1536]{1,0:T(8,128)(2,1)}, bf16[128,1536]{1,0:T(8,128)(2,1)S(1)}, u32[]{:S(2)}, u32[]{:S(2)}) %collective-permute-start.17) | collective-permute-done | bytes 393248 | tf_op jit(solution)/shard_map/ppermute | solution.py:55
  138.7 7.4 %collective-permute-start.19 = (bf16[128,1536]{1,0:T(8,128)(2,1)S(1)}, bf16[128,1536]{1,0:T(8,128)(2,1)S(1)}, u32[]{:S(2)}, u32[]{:S(2)}) collective-permute-start(bf16[128,1536]{1,0:T(8,128)(2,1)S(1)} %collective-permute-done.17.rest_0_), channel_id=1, source_target_pairs={{0,1},{1,0},{2,3},{3,2},{4,5},{5,4},{6,7},{7,6},{8,9},{9,8},{10,11... | collective-permute-start | bytes 1179656 | tf_op jit(solution)/shard_map/ppermute | solution.py:55
  146.2 11.8 %ffn.2 = (bf16[128,1536]{1,0:T(8,128)(2,1)}, bf16[128,1536]{1,0:T(8,128)(2,1)}) custom-call(bf16[128,1536]{1,0:T(8,128)(2,1)} %copy-done.22, bf16[128,1536]{1,0:T(8,128)(2,1)} %get-tuple-element.64.rest_1_, bf16[8,3,192,2240]{3,2,1,0:T(8,128)(2,1)} %bitcast.20), custom_call_target="tpu_custom_call" | custom-call | flops 5284823040 | bytes 20643840 | tf_op jit(solution)/shard_map/ffn/pallas_call | solution.py:477
  158.0 2.0 collective-permute-start.21
  160.0 9.7 %ffn.3 = (bf16[128,1536]{1,0:T(8,128)(2,1)S(1)}, bf16[128,1536]{1,0:T(8,128)(2,1)S(1)}) custom-call(bf16[128,1536]{1,0:T(8,128)(2,1)S(1)} %collective-permute-done.18.rest_0_, bf16[128,1536]{1,0:T(8,128)(2,1)S(1)} %collective-permute-done.19.rest_1_, bf16[8,3,192,2240]{3,2,1,0:T(8,128)(2,1)} %bitcast.21), custom_call_target="tpu_custom_call" | custom-call | flops 5284823040 | bytes 20643840 | tf_op jit(solution)/shard_map/ffn/pallas_call | solution.py:477
  169.7 0.2 collective-permute-start.20
  169.9 1.7 collective-permute-start.22
  171.7 22.0 %collective-permute-done.20 = bf16[128,1536]{1,0:T(8,128)(2,1)} collective-permute-done((bf16[128,1536]{1,0:T(8,128)(2,1)S(1)}, bf16[128,1536]{1,0:T(8,128)(2,1)}, u32[]{:S(2)}, u32[]{:S(2)}) %collective-permute-start.20) | collective-permute-done | bytes 393248 | tf_op jit(solution)/shard_map/ppermute | solution.py:55
  193.7 1.8 add_convert_fusion.rest_0_
  195.6 2.1 collective-permute-start.23
  197.7 0.3 compare_reduce_fusion
  198.0 8.3 %collective-permute-done.23.rest_2_ = bf16[128,1536]{1,0:T(8,128)(2,1)S(1)} collective-permute-done((bf16[128,1536]{1,0:T(8,128)(2,1)S(1)}, bf16[128,1536]{1,0:T(8,128)(2,1)S(1)}, u32[]{:S(2)}, u32[]{:S(2)}) %collective-permute-start.23) | collective-permute-done | bytes 393248 | tf_op jit(solution)/shard_map/ppermute | solution.py:55
  206.3 5.7 %collective-permute-start.24 = (bf16[128,1536]{1,0:T(8,128)(2,1)S(1)}, bf16[128,1536]{1,0:T(8,128)(2,1)S(1)}, u32[]{:S(2)}, u32[]{:S(2)}) collective-permute-start(bf16[128,1536]{1,0:T(8,128)(2,1)S(1)} %collective-permute-done.23.rest_2_), channel_id=1, source_target_pairs={{0,1},{1,0},{2,3},{3,2},{4,5},{5,4},{6,7},{7,6},{8,9},{9,8},{10,11... | collective-permute-start | bytes 1179656 | tf_op jit(solution)/shard_map/ppermute | solution.py:55
  212.0 1.0 constant_dynamic-slice_fusion.3
  213.1 3.1 %gather_fusion = bf16[640,128]{1,0:T(8,128)(2,1)S(1)} fusion(bf16[4096,128]{1,0:T(8,128)(2,1)} %constant_dynamic-slice_fusion.3, s32[1024]{0:T(1024)S(1)} %pad_clamp_fusion), kind=kCustom, calls=%fused_computation | custom fusion | bytes 330240 | tf_op jit(solution)/shard_map/jit(_take)/gather | solution.py:297
  216.2 0.9 select_select_fusion
  217.1 1.4 copy-done.1
  218.5 2.8 %next.2 = (bf16[512,1536]{1,0:T(8,128)(2,1)}, bf16[512,384]{1,0:T(8,128)(2,1)}, bf16[512,128]{1,0:T(8,128)(2,1)}) custom-call(s32[1]{0:T(128)} %bitcast.narrow_ref, f32[1,1536]{1,0:T(1,128)S(1)} %reshape.199.gain_ref, f32[1,512]{1,0:T(1,128)S(1)} %maximum_convert_fusion.1.bias_ref, bf16[1536,512]{1,0:T(8,128)(2,1)S(1)} %copy-done.1, ...), custom_call_target="tpu_custom_call" | custom-call | flops 603979776 | bytes 4718592 | tf_op jit(solution)/shard_map/next/pallas_call | solution.py:516
  221.3 4.2 %collective-permute-done.24.rest_0_ = bf16[128,1536]{1,0:T(8,128)(2,1)S(1)} collective-permute-done((bf16[128,1536]{1,0:T(8,128)(2,1)S(1)}, bf16[128,1536]{1,0:T(8,128)(2,1)S(1)}, u32[]{:S(2)}, u32[]{:S(2)}) %collective-permute-start.24) | collective-permute-done | bytes 393248 | tf_op jit(solution)/shard_map/ppermute | solution.py:55
  225.4 1.2 next.3
  (127 shorter events, 2.0 us)
Async XLA Ops:
  7.2 3.8 %copy-start = (bf16[192,512]{1,0:T(8,128)(2,1)S(1)}, bf16[192,512]{1,0:T(8,128)(2,1)}, u32[]{:S(2)}) copy-start(bf16[192,512]{1,0:T(8,128)(2,1)} %param.28) | copy-start | bytes 589828
  7.2 139.0 %all-gather.6.cloned.1.call-start = ((), (), s32[]{:S(2)}) async-start(), calls=%async_computation.1 | async-start | bytes 23887872 | tf_op jit(solution)/shard_map/all_gather | solution.py:368
  10.8 1.0 copy-start.25
  10.8 5.3 %copy-start.43 = (bf16[512]{0:T(512)(128)(2,1)S(1)}, bf16[512]{0:T(512)(128)(2,1)}, u32[]{:S(2)}) copy-start(bf16[512]{0:T(512)(128)(2,1)} %param.29) | copy-start | bytes 3076
  10.8 5.4 %copy-start.32 = (bf16[384]{0:T(512)(128)(2,1)S(1)}, bf16[384]{0:T(512)(128)(2,1)}, u32[]{:S(2)}) copy-start(bf16[384]{0:T(512)(128)(2,1)} %param.27) | copy-start | bytes 2308
  10.8 5.4 %copy-start.33 = (bf16[384]{0:T(512)(128)(2,1)S(1)}, bf16[384]{0:T(512)(128)(2,1)}, u32[]{:S(2)}) copy-start(bf16[384]{0:T(512)(128)(2,1)} %param.37) | copy-start | bytes 2308
  10.8 5.4 %copy-start.44 = (bf16[512]{0:T(512)(128)(2,1)S(1)}, bf16[512]{0:T(512)(128)(2,1)}, u32[]{:S(2)}) copy-start(bf16[512]{0:T(512)(128)(2,1)} %param.39) | copy-start | bytes 3076
  10.8 6.9 %copy-start.30 = (s32[8]{0:T(128)S(1)}, s32[8]{0:T(128)}, u32[]{:S(2)}) copy-start(s32[8]{0:T(128)} %param.23) | copy-start | bytes 100
  10.8 6.8 %copy-start.31 = (s32[512]{0:T(512)S(1)}, s32[512]{0:T(512)}, u32[]{:S(2)}) copy-start(s32[512]{0:T(512)} %param.21) | copy-start | bytes 6148
  10.8 6.9 %copy-start.23 = (bf16[192,384]{1,0:T(8,128)(2,1)S(1)}, bf16[192,384]{1,0:T(8,128)(2,1)}, u32[]{:S(2)}) copy-start(bf16[192,384]{1,0:T(8,128)(2,1)} %param.36) | copy-start | bytes 442372
  10.8 8.6 %copy-start.27 = (bf16[1536]{0:T(1024)(128)(2,1)S(1)}, bf16[1536]{0:T(1024)(128)(2,1)}, u32[]{:S(2)}) copy-start(bf16[1536]{0:T(1024)(128)(2,1)} %param.31) | copy-start | bytes 9220
  10.9 9.2 %copy-start.28 = (bf16[1536]{0:T(1024)(128)(2,1)S(1)}, bf16[1536]{0:T(1024)(128)(2,1)}, u32[]{:S(2)}) copy-start(bf16[1536]{0:T(1024)(128)(2,1)} %param.35) | copy-start | bytes 9220
  10.9 206.2 %all-gather.4.cloned.1.call-start = ((), (), s32[]{:S(2)}) async-start(), calls=%async_computation | async-start | bytes 1769472 | tf_op jit(solution)/shard_map/all_gather | solution.py:504
  11.8 29.0 %copy-start.29 = (bf16[1536]{0:T(1024)(128)(2,1)S(1)}, bf16[1536]{0:T(1024)(128)(2,1)}, u32[]{:S(2)}) copy-start(bf16[1536]{0:T(1024)(128)(2,1)} %param.25) | copy-start | bytes 9220
  11.8 31.0 %copy-start.10 = (bf16[192,1024]{1,0:T(8,128)(2,1)}, bf16[192,1024]{1,0:T(8,128)(2,1)S(1)}, u32[]{:S(2)}) copy-start(bf16[192,1024]{1,0:T(8,128)(2,1)S(1)} %pad_maximum_fusion.1.rest_0_) | copy-start | bytes 1179652
  11.8 11.1 %collective-permute-start.5 = (bf16[192,1024]{1,0:T(8,128)(2,1)S(1)}, bf16[192,1024]{1,0:T(8,128)(2,1)S(1)}, u32[]{:S(2)}, u32[]{:S(2)}) collective-permute-start(bf16[192,1024]{1,0:T(8,128)(2,1)S(1)} %pad_maximum_fusion.1.rest_0_), channel_id=1, source_target_pairs={{0,24},{4,28},{8,16},{12,20},{16,8},{20,12},{24,0},{28,4},{1,25},{... | collective-permute-start | bytes 1179656 | tf_op jit(solution)/shard_map/ppermute | solution.py:55
  11.9 25.1 %collective-permute-start.3 = (bf16[192,1024]{1,0:T(8,128)(2,1)S(1)}, bf16[192,1024]{1,0:T(8,128)(2,1)S(1)}, u32[]{:S(2)}, u32[]{:S(2)}) collective-permute-start(bf16[192,1024]{1,0:T(8,128)(2,1)S(1)} %pad_maximum_fusion.1.rest_0_), channel_id=1, source_target_pairs={{0,16},{4,20},{8,24},{12,28},{16,0},{20,4},{24,8},{28,12},{1,17},{... | collective-permute-start | bytes 1179656 | tf_op jit(solution)/shard_map/ppermute | solution.py:55
  13.3 23.6 %collective-permute-start.1 = (bf16[192,1024]{1,0:T(8,128)(2,1)S(1)}, bf16[192,1024]{1,0:T(8,128)(2,1)S(1)}, u32[]{:S(2)}, u32[]{:S(2)}) collective-permute-start(bf16[192,1024]{1,0:T(8,128)(2,1)S(1)} %pad_maximum_fusion.1.rest_0_), channel_id=1, source_target_pairs={{0,8},{4,12},{8,0},{12,4},{16,24},{20,28},{24,16},{28,20},{1,9},{5... | collective-permute-start | bytes 1179656 | tf_op jit(solution)/shard_map/ppermute | solution.py:55
  14.5 26.9 %collective-permute-start = (bf16[192,1024]{1,0:T(8,128)(2,1)S(1)}, bf16[192,1024]{1,0:T(8,128)(2,1)S(1)}, u32[]{:S(2)}, u32[]{:S(2)}) collective-permute-start(bf16[192,1024]{1,0:T(8,128)(2,1)S(1)} %pad_maximum_fusion.1.rest_0_), channel_id=1, source_target_pairs={{0,4},{4,0},{8,12},{12,8},{16,20},{20,16},{24,28},{28,24},{1,5},{5... | collective-permute-start | bytes 1179656 | tf_op jit(solution)/shard_map/ppermute | solution.py:55
  17.8 53.8 %copy-start.6 = (s32[512]{0:T(512)}, s32[512]{0:T(512)S(1)}, u32[]{:S(2)}) copy-start(s32[512]{0:T(512)S(1)} %select_reduce_fusion.spots_ref) | copy-start | bytes 6148
  22.9 19.8 %copy-start.11 = (bf16[192,1024]{1,0:T(8,128)(2,1)}, bf16[192,1024]{1,0:T(8,128)(2,1)S(1)}, u32[]{:S(2)}) copy-start(bf16[192,1024]{1,0:T(8,128)(2,1)S(1)} %collective-permute-done.5.rest_6_) | copy-start | bytes 1179652
  37.0 5.8 %copy-start.12 = (bf16[192,1024]{1,0:T(8,128)(2,1)}, bf16[192,1024]{1,0:T(8,128)(2,1)S(1)}, u32[]{:S(2)}) copy-start(bf16[192,1024]{1,0:T(8,128)(2,1)S(1)} %collective-permute-done.3.rest_4_) | copy-start | bytes 1179652
  37.0 5.8 %copy-start.13 = (bf16[192,1024]{1,0:T(8,128)(2,1)}, bf16[192,1024]{1,0:T(8,128)(2,1)S(1)}, u32[]{:S(2)}) copy-start(bf16[192,1024]{1,0:T(8,128)(2,1)S(1)} %collective-permute-done.1.rest_2_) | copy-start | bytes 1179652
  37.0 4.7 %collective-permute-start.2 = (bf16[192,1024]{1,0:T(8,128)(2,1)S(1)}, bf16[192,1024]{1,0:T(8,128)(2,1)S(1)}, u32[]{:S(2)}, u32[]{:S(2)}) collective-permute-start(bf16[192,1024]{1,0:T(8,128)(2,1)S(1)} %collective-permute-done.1.rest_2_), channel_id=1, source_target_pairs={{0,4},{4,0},{8,12},{12,8},{16,20},{20,16},{24,28},{28,24},{1,5},{5... | collective-permute-start | bytes 1179656 | tf_op jit(solution)/shard_map/ppermute | solution.py:55
  40.3 1.9 collective-permute-start.4
  40.3 2.5 %collective-permute-start.6 = (bf16[192,1024]{1,0:T(8,128)(2,1)S(1)}, bf16[192,1024]{1,0:T(8,128)(2,1)S(1)}, u32[]{:S(2)}, u32[]{:S(2)}) collective-permute-start(bf16[192,1024]{1,0:T(8,128)(2,1)S(1)} %collective-permute-done.5.rest_6_), channel_id=1, source_target_pairs={{0,4},{4,0},{8,12},{12,8},{16,20},{20,16},{24,28},{28,24},{1,5},{5... | collective-permute-start | bytes 1179656 | tf_op jit(solution)/shard_map/ppermute | solution.py:55
  41.4 1.4 copy-start.14
  41.6 1.2 copy-start.16
  49.7 14.8 %collective-permute-start.12 = (bf16[512,256]{1,0:T(8,128)(2,1)}, bf16[512,256]{1,0:T(8,128)(2,1)S(1)}, u32[]{:S(2)}, u32[]{:S(2)}) collective-permute-start(bf16[512,256]{1,0:T(8,128)(2,1)} %get-tuple-element.55.rest_0_), channel_id=1, source_target_pairs={{0,24},{4,28},{8,16},{12,20},{16,8},{20,12},{24,0},{28,4},{1,25},{... | collective-permute-start | bytes 786440 | tf_op jit(solution)/shard_map/ppermute | solution.py:55
  51.1 19.5 %collective-permute-start.10 = (bf16[512,256]{1,0:T(8,128)(2,1)}, bf16[512,256]{1,0:T(8,128)(2,1)S(1)}, u32[]{:S(2)}, u32[]{:S(2)}) collective-permute-start(bf16[512,256]{1,0:T(8,128)(2,1)} %get-tuple-element.55.rest_0_), channel_id=1, source_target_pairs={{0,16},{4,20},{8,24},{12,28},{16,0},{20,4},{24,8},{28,12},{1,17},{... | collective-permute-start | bytes 786440 | tf_op jit(solution)/shard_map/ppermute | solution.py:55
  52.2 19.3 %collective-permute-start.8 = (bf16[512,256]{1,0:T(8,128)(2,1)}, bf16[512,256]{1,0:T(8,128)(2,1)S(1)}, u32[]{:S(2)}, u32[]{:S(2)}) collective-permute-start(bf16[512,256]{1,0:T(8,128)(2,1)} %get-tuple-element.55.rest_0_), channel_id=1, source_target_pairs={{0,8},{4,12},{8,0},{12,4},{16,24},{20,28},{24,16},{28,20},{1,9},{5... | collective-permute-start | bytes 786440 | tf_op jit(solution)/shard_map/ppermute | solution.py:55
  53.3 19.1 %collective-permute-start.7 = (bf16[512,256]{1,0:T(8,128)(2,1)}, bf16[512,256]{1,0:T(8,128)(2,1)S(1)}, u32[]{:S(2)}, u32[]{:S(2)}) collective-permute-start(bf16[512,256]{1,0:T(8,128)(2,1)} %get-tuple-element.55.rest_0_), channel_id=1, source_target_pairs={{0,4},{4,0},{8,12},{12,8},{16,20},{20,16},{24,28},{28,24},{1,5},{5... | collective-permute-start | bytes 786440 | tf_op jit(solution)/shard_map/ppermute | solution.py:55
  64.5 8.5 %copy-start.36 = (bf16[512,256]{1,0:T(8,128)(2,1)}, bf16[512,256]{1,0:T(8,128)(2,1)S(1)}, u32[]{:S(2)}) copy-start(bf16[512,256]{1,0:T(8,128)(2,1)S(1)} %collective-permute-done.12.rest_6_) | copy-start | bytes 786436
  64.5 7.9 %collective-permute-start.13 = (bf16[512,256]{1,0:T(8,128)(2,1)S(1)}, bf16[512,256]{1,0:T(8,128)(2,1)S(1)}, u32[]{:S(2)}, u32[]{:S(2)}) collective-permute-start(bf16[512,256]{1,0:T(8,128)(2,1)S(1)} %collective-permute-done.12.rest_6_), channel_id=1, source_target_pairs={{0,4},{4,0},{8,12},{12,8},{16,20},{20,16},{24,28},{28,24},{1,5},{5... | collective-permute-start | bytes 786440 | tf_op jit(solution)/shard_map/ppermute | solution.py:55
  70.6 2.4 %copy-start.37 = (bf16[512,256]{1,0:T(8,128)(2,1)}, bf16[512,256]{1,0:T(8,128)(2,1)S(1)}, u32[]{:S(2)}) copy-start(bf16[512,256]{1,0:T(8,128)(2,1)S(1)} %collective-permute-done.10.rest_4_) | copy-start | bytes 786436
  70.6 2.1 collective-permute-start.11
  71.5 1.5 copy-start.38
  71.5 1.5 collective-permute-start.9
  73.7 13.3 %copy-start.5 = (s32[512,1]{1,0:T(8,128)S(1)}, s32[512,1]{1,0:T(8,128)}, u32[]{:S(2)}) copy-start(s32[512,1]{1,0:T(8,128)} %copy.32.starts_ref) | copy-start | bytes 6148
  73.7 13.3 %copy-start.7 = (s32[512]{0:T(512)S(1)}, s32[512]{0:T(512)}, u32[]{:S(2)}) copy-start(s32[512]{0:T(512)} %copy-done.6) | copy-start | bytes 6148
  73.7 13.3 %copy-start.8 = (bf16[1536,384]{1,0:T(8,128)(2,1)S(1)}, bf16[1536,384]{1,0:T(8,128)(2,1)}, u32[]{:S(2)}) copy-start(bf16[1536,384]{1,0:T(8,128)(2,1)} %get-tuple-element.54.w_out) | copy-start | bytes 3538948
  73.7 13.3 %copy-start.9 = (bf16[512,384]{1,0:T(8,128)(2,1)S(1)}, bf16[512,384]{1,0:T(8,128)(2,1)}, u32[]{:S(2)}) copy-start(bf16[512,384]{1,0:T(8,128)(2,1)} %get-tuple-element.53.q_ref) | copy-start | bytes 1179652
  85.1 28.9 %collective-permute-start.15 = (bf16[128,1536]{1,0:T(8,128)(2,1)}, bf16[128,1536]{1,0:T(8,128)(2,1)S(1)}, u32[]{:S(2)}, u32[]{:S(2)}) collective-permute-start(bf16[128,1536]{1,0:T(8,128)(2,1)} %get-tuple-element.59), channel_id=1, source_target_pairs={{0,2},{1,3},{2,0},{3,1},{4,6},{5,7},{6,4},{7,5},{8,10},{9,11},{10,... | collective-permute-start | bytes 1179656 | tf_op jit(solution)/shard_map/ppermute | solution.py:55
  87.0 1.6 copy-start.2
  88.6 8.2 %copy-start.35 = (bf16[128,1536]{1,0:T(8,128)(2,1)S(1)}, bf16[128,1536]{1,0:T(8,128)(2,1)}, u32[]{:S(2)}) copy-start(bf16[128,1536]{1,0:T(8,128)(2,1)} %get-tuple-element.60) | copy-start | bytes 1179652
  88.6 40.2 %copy-start.26 = (s32[8,16]{1,0:T(8,128)S(1)}, s32[8,16]{1,0:T(8,128)}, u32[]{:S(2)}) copy-start(s32[8,16]{1,0:T(8,128)} %param.24) | copy-start | bytes 1540
  88.6 40.5 %copy-start.34 = (s32[8]{0:T(128)S(1)}, s32[8]{0:T(128)}, u32[]{:S(2)}) copy-start(s32[8]{0:T(128)} %param.22) | copy-start | bytes 100
  96.8 17.2 %collective-permute-start.16 = (bf16[128,1536]{1,0:T(8,128)(2,1)S(1)}, bf16[128,1536]{1,0:T(8,128)(2,1)S(1)}, u32[]{:S(2)}, u32[]{:S(2)}) collective-permute-start(bf16[128,1536]{1,0:T(8,128)(2,1)S(1)} %copy-done.35), channel_id=1, source_target_pairs={{0,3},{1,2},{2,1},{3,0},{4,7},{5,6},{6,5},{7,4},{8,11},{9,10},{10,... | collective-permute-start | bytes 1179656 | tf_op jit(solution)/shard_map/ppermute | solution.py:55
  99.0 23.4 %collective-permute-start.14 = (bf16[128,1536]{1,0:T(8,128)(2,1)S(1)}, bf16[128,1536]{1,0:T(8,128)(2,1)S(1)}, u32[]{:S(2)}, u32[]{:S(2)}) collective-permute-start(bf16[128,1536]{1,0:T(8,128)(2,1)S(1)} %get-tuple-element.58), channel_id=1, source_target_pairs={{0,1},{1,0},{2,3},{3,2},{4,5},{5,4},{6,7},{7,6},{8,9},{9,8},{10,11... | collective-permute-start | bytes 1179656 | tf_op jit(solution)/shard_map/ppermute | solution.py:55
  114.0 8.4 %copy-start.19 = (bf16[128,1536]{1,0:T(8,128)(2,1)}, bf16[128,1536]{1,0:T(8,128)(2,1)S(1)}, u32[]{:S(2)}) copy-start(bf16[128,1536]{1,0:T(8,128)(2,1)S(1)} %collective-permute-done.15.rest_2_) | copy-start | bytes 1179652
  114.0 8.4 %copy-start.20 = (bf16[128,1536]{1,0:T(8,128)(2,1)}, bf16[128,1536]{1,0:T(8,128)(2,1)S(1)}, u32[]{:S(2)}) copy-start(bf16[128,1536]{1,0:T(8,128)(2,1)S(1)} %collective-permute-done.16.rest_3_) | copy-start | bytes 1179652
  126.1 12.6 %collective-permute-start.17 = (bf16[128,1536]{1,0:T(8,128)(2,1)}, bf16[128,1536]{1,0:T(8,128)(2,1)S(1)}, u32[]{:S(2)}, u32[]{:S(2)}) collective-permute-start(bf16[128,1536]{1,0:T(8,128)(2,1)} %get-tuple-element.63), channel_id=1, source_target_pairs={{0,3},{1,2},{2,1},{3,0},{4,7},{5,6},{6,5},{7,4},{8,11},{9,10},{10,... | collective-permute-start | bytes 1179656 | tf_op jit(solution)/shard_map/ppermute | solution.py:55
  129.3 30.6 %collective-permute-start.18 = (bf16[128,1536]{1,0:T(8,128)(2,1)}, bf16[128,1536]{1,0:T(8,128)(2,1)S(1)}, u32[]{:S(2)}, u32[]{:S(2)}) collective-permute-start(bf16[128,1536]{1,0:T(8,128)(2,1)} %get-tuple-element.66), channel_id=1, source_target_pairs={{0,1},{1,0},{2,3},{3,2},{4,5},{5,4},{6,7},{7,6},{8,9},{9,8},{10,11... | collective-permute-start | bytes 1179656 | tf_op jit(solution)/shard_map/ppermute | solution.py:55
  138.7 7.4 %copy-start.22 = (bf16[128,1536]{1,0:T(8,128)(2,1)}, bf16[128,1536]{1,0:T(8,128)(2,1)S(1)}, u32[]{:S(2)}) copy-start(bf16[128,1536]{1,0:T(8,128)(2,1)S(1)} %collective-permute-done.17.rest_0_) | copy-start | bytes 1179652
  138.7 21.3 %collective-permute-start.19 = (bf16[128,1536]{1,0:T(8,128)(2,1)S(1)}, bf16[128,1536]{1,0:T(8,128)(2,1)S(1)}, u32[]{:S(2)}, u32[]{:S(2)}) collective-permute-start(bf16[128,1536]{1,0:T(8,128)(2,1)S(1)} %collective-permute-done.17.rest_0_), channel_id=1, source_target_pairs={{0,1},{1,0},{2,3},{3,2},{4,5},{5,4},{6,7},{7,6},{8,9},{9,8},{10,11... | collective-permute-start | bytes 1179656 | tf_op jit(solution)/shard_map/ppermute | solution.py:55
  157.9 35.8 %copy-start.15 = (bf16[128,1536]{1,0:T(8,128)(2,1)S(1)}, bf16[128,1536]{1,0:T(8,128)(2,1)}, u32[]{:S(2)}) copy-start(bf16[128,1536]{1,0:T(8,128)(2,1)} %get-tuple-element.61) | copy-start | bytes 1179652
  158.0 35.8 %collective-permute-start.21 = (bf16[128,1536]{1,0:T(8,128)(2,1)}, bf16[128,1536]{1,0:T(8,128)(2,1)}, u32[]{:S(2)}, u32[]{:S(2)}) collective-permute-start(bf16[128,1536]{1,0:T(8,128)(2,1)} %get-tuple-element.67), channel_id=1, source_target_pairs={{0,3},{1,2},{2,1},{3,0},{4,7},{5,6},{6,5},{7,4},{8,11},{9,10},{10,... | collective-permute-start | bytes 1179656 | tf_op jit(solution)/shard_map/ppermute | solution.py:55
  169.7 42.4 %copy-start.3 = (bf16[4096,256]{1,0:T(8,128)(2,1)S(1)}, bf16[4096,256]{1,0:T(8,128)(2,1)}, u32[]{:S(2)}) copy-start(bf16[4096,256]{1,0:T(8,128)(2,1)} %get-tuple-element.56.rest_0_) | copy-start | bytes 6291460
  169.7 24.0 %collective-permute-start.20 = (bf16[128,1536]{1,0:T(8,128)(2,1)S(1)}, bf16[128,1536]{1,0:T(8,128)(2,1)}, u32[]{:S(2)}, u32[]{:S(2)}) collective-permute-start(bf16[128,1536]{1,0:T(8,128)(2,1)S(1)} %get-tuple-element.70), channel_id=1, source_target_pairs={{0,2},{1,3},{2,0},{3,1},{4,6},{5,7},{6,4},{7,5},{8,10},{9,11},{10,... | collective-permute-start | bytes 1179656 | tf_op jit(solution)/shard_map/ppermute | solution.py:55
  169.9 23.8 %collective-permute-start.22 = (bf16[128,1536]{1,0:T(8,128)(2,1)S(1)}, bf16[128,1536]{1,0:T(8,128)(2,1)}, u32[]{:S(2)}, u32[]{:S(2)}) collective-permute-start(bf16[128,1536]{1,0:T(8,128)(2,1)S(1)} %get-tuple-element.71), channel_id=1, source_target_pairs={{0,1},{1,0},{2,3},{3,2},{4,5},{5,4},{6,7},{7,6},{8,9},{9,8},{10,11... | collective-permute-start | bytes 1179656 | tf_op jit(solution)/shard_map/ppermute | solution.py:55
  195.6 10.8 %collective-permute-start.23 = (bf16[128,1536]{1,0:T(8,128)(2,1)S(1)}, bf16[128,1536]{1,0:T(8,128)(2,1)S(1)}, u32[]{:S(2)}, u32[]{:S(2)}) collective-permute-start(bf16[128,1536]{1,0:T(8,128)(2,1)S(1)} %add_convert_fusion.rest_0_), channel_id=1, source_target_pairs={{0,3},{1,2},{2,1},{3,0},{4,7},{5,6},{6,5},{7,4},{8,11},{9,10},{10,... | collective-permute-start | bytes 1179656 | tf_op jit(solution)/shard_map/ppermute | solution.py:55
  198.0 19.1 %collective-permute-start.25 = (bf16[128,1536]{1,0:T(8,128)(2,1)S(1)}, bf16[128,1536]{1,0:T(8,128)(2,1)}, u32[]{:S(2)}, u32[]{:S(2)}) collective-permute-start(bf16[128,1536]{1,0:T(8,128)(2,1)S(1)} %add_convert_fusion.rest_0_), channel_id=1, source_target_pairs={{0,1},{1,0},{2,3},{3,2},{4,5},{5,4},{6,7},{7,6},{8,9},{9,8},{10,11... | collective-permute-start | bytes 1179656 | tf_op jit(solution)/shard_map/ppermute | solution.py:55
  206.3 19.1 %collective-permute-start.24 = (bf16[128,1536]{1,0:T(8,128)(2,1)S(1)}, bf16[128,1536]{1,0:T(8,128)(2,1)S(1)}, u32[]{:S(2)}, u32[]{:S(2)}) collective-permute-start(bf16[128,1536]{1,0:T(8,128)(2,1)S(1)} %collective-permute-done.23.rest_2_), channel_id=1, source_target_pairs={{0,1},{1,0},{2,3},{3,2},{4,5},{5,4},{6,7},{7,6},{8,9},{9,8},{10,11... | collective-permute-start | bytes 1179656 | tf_op jit(solution)/shard_map/ppermute | solution.py:55
  217.1 1.4 copy-start.1
  (9 other events, 6.8 us)
Sparse Core Ops, SparseCore 0:
  11.0 128.0 all-gather.5
  141.0 25.6 all-gather.3
